TPU v7x, 128 devices: a whole 4x4x4 slice. The times are simulated.
128 devices in a mesh: lat: 32 (over y, z, core), lon: 4 (over x).
Axes of the slice: x: 4, y: 4, z: 4, core: 2. Of those that a mesh axis runs over, the one named last changes fastest.
Arguments:
- adjoint_state: float32 [4, 75, 256, 1024], P(None, None, 'lat', 'lon'), may hold values from -6 to 6
- mixing_base: float32 [74, 256, 1024], P(None, 'lat', 'lon'), may hold values from 0.05 to 5
- atm_flux: float32 [4, 512, 128], P(None, 'lat'), may hold values from -6 to 6
- send_count: int32 [32, 128], P('lat', 'lon'), may hold values from 0 to 2, as said below
- send_segment: int32 [32, 256], P('lat', 'lon'), may hold values from 0 to 15, as said below
- cover_index: int32 [4, 256, 1024], P(None, 'lat', 'lon'), may hold values from 0 to 8191, as said below
- cover_weight: float32 [4, 256, 1024], P(None, 'lat', 'lon'), may hold values from 0.1 to 1
- land_mask: int32 [256, 1024], P('lat', 'lon'), may hold values 0 or 1
Outputs:
- state_adjoint: float32 [4, 75, 256, 1024], P(None, None, 'lat', 'lon')
- flux_adjoint: float32 [4, 512, 128], P(None, 'lat')
Inputs may be any that keep to these rules, and one draw needn't show every extreme that they name: `send_count`: for every longitude column one ocean latitude index receives 2 segments from every owner, and every ocean device receives at least one segment from the owner of its own latitude index. `send_segment`: for each owner and longitude column, the first entries list the segments for destination 0, then destination 1 and so on, as many as send_count gives; entries past their total are unused. `cover_index`: equals src * 2 * 128 + slot * 128 + lane, where slot is below the count that owner src sends to the cell's device in the cell's longitude column.
All inputs are finite; a program needn't handle non-finite values. No bound on the sum of `land_mask` on one device may be relied on, other than what follows from the above.
Results may differ from a plain program's by a relative error of at most 0.0003.
Values sent between devices are 32-bit elements; how exact they have to be, the bound alone decides.
A program may use at most 64 MiB of HBM per device.

v0:
```python
import math

import jax
import jax.numpy as jnp
import numpy as np
from jax import lax
from jax.experimental import pallas as pl
from jax.experimental.pallas import tpu as pltpu
from jax.sharding import PartitionSpec as P

SMOOTHING = 0.02
WIND_GAIN = 1.0
DEPTH_SCALE = 12.0
FIELD_MIX = (1.0, 1.0, 2.0, 2.0)


HALO = 4


def from_neighbours(block, axis, dim, width):
    count = lax.axis_size(axis)
    to_prev = [(i, (i - 1) % count) for i in range(count)]
    to_next = [(i, (i + 1) % count) for i in range(count)]
    size = block.shape[dim]
    from_next = lax.ppermute(lax.slice_in_dim(block, 0, width, axis=dim), axis, to_prev)
    from_prev = lax.ppermute(lax.slice_in_dim(block, size - width, size, axis=dim), axis, to_next)
    return from_next, from_prev


def extended_planes(values, land_mask, width):
    fields, levels, rows, cols = values.shape
    planes = values.reshape(fields * levels, rows, cols)
    coast = land_mask.astype(jnp.float32)[None]
    stack = jnp.concatenate([planes, coast], axis=0)
    south, north = from_neighbours(stack, "lat", 1, width)
    tall = jnp.concatenate([stack, south, north], axis=1)
    east, west = from_neighbours(tall, "lon", 2, width)
    wide = -(-(cols + 2 * width) // 128) * 128
    gap = jnp.zeros(tall.shape[:2] + (wide - cols - 2 * width,), jnp.float32)
    ext = jnp.concatenate([tall, east, gap, west], axis=2)
    lat_count = lax.axis_size("lat")
    where_lat = lax.axis_index("lat")
    row = lax.broadcasted_iota(jnp.int32, ext.shape[1:], 0)
    outside = jnp.logical_or(
        jnp.logical_and(where_lat == 0, row >= rows + width),
        jnp.logical_and(where_lat == lat_count - 1, jnp.logical_and(row >= rows, row < rows + width)),
    )
    mask = jnp.where(outside, 0.0, ext[-1])
    return ext, mask


def with_halo(block, sides, width):
    for axis, dim in sides:
        count = lax.axis_size(axis)
        forward = [(i, i + 1) for i in range(count - 1)]
        forward.append((count - 1, 0))
        backward = [(target, source) for source, target in forward]
        low = lax.ppermute(
            lax.slice_in_dim(block, block.shape[dim] - width, None, axis=dim), axis, forward
        )
        high = lax.ppermute(lax.slice_in_dim(block, 0, width, axis=dim), axis, backward)
        block = jnp.concatenate([low, block, high], axis=dim)
    return block


def laplace(values, marks):
    centre = values[..., 1:-1, 1:-1]
    north = marks[:-2, 1:-1] * (values[..., :-2, 1:-1] - centre)
    south = marks[2:, 1:-1] * (values[..., 2:, 1:-1] - centre)
    west = marks[1:-1, :-2] * (values[..., 1:-1, :-2] - centre)
    east = marks[1:-1, 2:] * (values[..., 1:-1, 2:] - centre)
    return marks[1:-1, 1:-1] * (north + south + west + east)


def tridiagonal_kernel(
    decay_ref, ext_ref, mask_ref, base_ref, surf_ref, land_ref, out_ref, back_ref, ratio_ref, marks_ref
):
    fields, levels = out_ref.shape[0], out_ref.shape[1]
    rows, cols = out_ref.shape[2], out_ref.shape[3]
    tall, wide = mask_ref.shape
    marks = mask_ref[...]
    marks_ref[0] = marks
    marks_ref[1] = pltpu.roll(marks, 1, 0)
    marks_ref[2] = pltpu.roll(marks, tall - 1, 0)
    marks_ref[3] = pltpu.roll(marks, 1, 1)
    marks_ref[4] = pltpu.roll(marks, wide - 1, 1)

    def laplace_ext(values):
        north = marks_ref[1] * (pltpu.roll(values, 1, 0) - values)
        south = marks_ref[2] * (pltpu.roll(values, tall - 1, 0) - values)
        west = marks_ref[3] * (pltpu.roll(values, 1, 1) - values)
        east = marks_ref[4] * (pltpu.roll(values, wide - 1, 1) - values)
        return marks_ref[0] * (((north + south) + west) + east)

    def smoothed(f, level):
        values = ext_ref[f * levels + level]
        for turn in range(2):
            inner = laplace_ext(values)
            values = values - SMOOTHING * laplace_ext(inner)
        return values[:rows, :cols]

    gains = sorted(set(FIELD_MIX))
    groups = [[f for f in range(fields) if FIELD_MIX[f] == g] for g in gains]
    surf = surf_ref[...]
    zero = jnp.zeros_like(surf)

    def step(level, below_mix, above_mix, ratios, parts):
        new_ratios, new_parts = [], list(parts)
        for gi, gain in enumerate(gains):
            below = gain * below_mix
            above = gain * above_mix
            pivot = ((1.0 + below) + above) - below * ratios[gi]
            if level is not None:
                ratio = above / pivot
                ratio_ref[gi, level] = ratio
                new_ratios.append(ratio)
            for f in groups[gi]:
                value = (smoothed(f, level if level is not None else levels - 1) + below * parts[f]) / pivot
                out_ref[f, level if level is not None else levels - 1] = value
                new_parts[f] = value
        return tuple(new_ratios), tuple(new_parts)

    def forward(level, carry):
        below_mix, ratios, parts = carry
        mix = base_ref[level] + surf * decay_ref[level]
        ratios, parts = step(level, below_mix, mix, ratios, parts)
        return (mix, ratios, parts)

    carry = (zero, tuple(zero for _ in gains), tuple(zero for _ in range(fields)))
    last_mix, ratios, parts = lax.fori_loop(0, levels - 1, forward, carry)
    step(None, last_mix, zero, ratios, parts)

    def backward(i, later):
        level = levels - 2 - i
        result = []
        for gi in range(len(gains)):
            ratio = ratio_ref[gi, level]
            for f in groups[gi]:
                value = out_ref[f, level] + ratio * later[f]
                out_ref[f, level] = value
                result.append((f, value))
        result.sort(key=lambda item: item[0])
        return tuple(v for _, v in result)

    final = tuple(out_ref[f, levels - 1] for f in range(fields))
    lax.fori_loop(0, levels - 1, backward, final)
    land = land_ref[...]
    for f in range(fields):
        back_ref[f] = land * out_ref[f, 0]


def tridiagonal(ext, mask, shape, mixing_base, surface, land):
    fields, levels = shape[0], shape[1]
    decay_table = np.array(
        [math.exp(-level / DEPTH_SCALE) for level in range(levels)], dtype=np.float32
    )
    vmem = pltpu.MemorySpace.VMEM
    return pl.pallas_call(
        tridiagonal_kernel,
        out_shape=(
            jax.ShapeDtypeStruct(shape, jnp.float32),
            jax.ShapeDtypeStruct((fields,) + shape[2:], jnp.float32),
        ),
        in_specs=[pl.BlockSpec(memory_space=pltpu.MemorySpace.SMEM)]
        + [pl.BlockSpec(memory_space=vmem)] * 5,
        out_specs=(pl.BlockSpec(memory_space=vmem), pl.BlockSpec(memory_space=vmem)),
        scratch_shapes=[
            pltpu.VMEM((len(set(FIELD_MIX)), levels) + shape[2:], jnp.float32),
            pltpu.VMEM((5,) + mask.shape, jnp.float32),
        ],
    )(jnp.asarray(decay_table), ext, mask, mixing_base, surface, land)


def lat_edges(marks, width):
    lat_count = lax.axis_size("lat")
    where_lat = lax.axis_index("lat")
    rows = lax.broadcasted_iota(jnp.int32, marks.shape, 0)
    keep_top = jnp.logical_or(where_lat > 0, rows >= width)
    keep_bottom = jnp.logical_or(where_lat < lat_count - 1, rows < marks.shape[0] - width)
    return jnp.where(jnp.logical_and(keep_top, keep_bottom), marks, 0.0)


def single_rim(values):
    return with_halo(values, (("lat", 2), ("lon", 3)), 1)


def shards(
    adjoint_state,
    mixing_base,
    atm_flux,
    send_count,
    send_segment,
    cover_index,
    cover_weight,
    land_mask,
):
    lat_count = lax.axis_size("lat")
    owned = atm_flux.shape[1]
    counts = send_count[0]
    capacity = send_segment.shape[1] // lat_count
    starts = jnp.cumsum(counts) - counts
    column = jnp.arange(capacity, dtype=jnp.int32)
    places = jnp.minimum(starts[:, None] + column[None, :], send_segment.shape[1] - 1)
    chosen = send_segment[0][places]
    live_slot = column[None, :] < counts[:, None]
    whole = lax.all_gather(atm_flux, "lat", axis=1, tiled=True)
    global_ids = lax.axis_index("lat") * owned + chosen
    arrived = lax.all_to_all(global_ids, "lat", split_axis=0, concat_axis=0, tiled=True)
    received = whole[:, arrived, :]
    flat_recv = received.reshape(4, -1)
    picked = flat_recv[:, cover_index]
    forcing = cover_weight[0] * picked[:, 0]
    for item in range(1, cover_index.shape[0]):
        forcing = forcing + cover_weight[item] * picked[:, item]
    surface = WIND_GAIN * (forcing[2] * forcing[2] + forcing[3] * forcing[3]) + jax.nn.softplus(
        forcing[1] - forcing[0]
    )
    land = land_mask.astype(jnp.float32)
    ext, mask = extended_planes(adjoint_state, land_mask, HALO)
    state_adjoint, flux_back = tridiagonal(ext, mask, adjoint_state.shape, mixing_base, surface, land)
    weighted = cover_weight[None] * flux_back[:, None]
    buffer = jnp.zeros_like(flat_recv).at[:, cover_index].add(weighted)
    returned = lax.all_to_all(
        buffer.reshape(received.shape), "lat", split_axis=1, concat_axis=1, tiled=True
    )
    kept = jnp.where(live_slot[None, :, :, None], returned, 0.0).reshape(4, -1, 128)
    owner_sum = jnp.zeros_like(atm_flux).at[:, chosen.reshape(-1), :].add(kept)
    flux_adjoint = lax.psum(owner_sum, "lon")
    return (state_adjoint, flux_adjoint)


def solution(mesh):
    in_specs = (
        P(None, None, "lat", "lon"),
        P(None, "lat", "lon"),
        P(None, "lat", None),
        P("lat", "lon"),
        P("lat", "lon"),
        P(None, "lat", "lon"),
        P(None, "lat", "lon"),
        P("lat", "lon"),
    )
    out_specs = (P(None, None, "lat", "lon"), P(None, "lat", None))
    return jax.shard_map(shards, mesh=mesh, in_specs=in_specs, out_specs=out_specs, check_vma=False)
```

profile of v0, /device:TPU:0, one launch (start us, length us, event | category | flops | bytes accessed | tf_op | source)
XLA Modules:
  0.0 244.3 jit_solution(1381790562849896656)
XLA Ops:
  10.5 8.4 %all-to-all-start = ((s32[32,1,2]{2,1,0:T(1,128)}), s32[32,1,2]{2,1,0:T(1,128)S(1)}, u32[]{:S(2)}, u32[]{:S(2)}) async-start(s32[32,1,2]{2,1,0:T(1,128)} %bitcast.7), calls=%async_computation | async-start | bytes 32768 | tf_op jit(solution)/shard_map/all_to_all | solution.py:208
  22.2 4.9 %collective-permute-start = (f32[301,4,256]{2,1,0:T(4,128)}, f32[301,4,256]{2,1,0:T(4,128)}, u32[]{:S(2)}, u32[]{:S(2)}) collective-permute-start(f32[301,4,256]{2,1,0:T(4,128)} %get-tuple-element.14), channel_id=1, source_target_pairs={{0,124},{4,0},{8,4},{12,8},{16,12},{20,16},{24,20},{28,24},{32,28}... | collective-permute-start | bytes 3698696 | tf_op jit(solution)/shard_map/ppermute | solution.py:25
  27.6 14.4 %collective-permute-done = f32[301,4,256]{2,1,0:T(4,128)} collective-permute-done((f32[301,4,256]{2,1,0:T(4,128)}, f32[301,4,256]{2,1,0:T(4,128)}, u32[]{:S(2)}, u32[]{:S(2)}) %collective-permute-start) | collective-permute-done | bytes 1232928 | tf_op jit(solution)/shard_map/ppermute | solution.py:25
  42.0 5.2 %collective-permute-done.1 = f32[301,4,256]{2,1,0:T(4,128)} collective-permute-done((f32[301,4,256]{2,1,0:T(4,128)}, f32[301,4,256]{2,1,0:T(4,128)}, u32[]{:S(2)}, u32[]{:S(2)}) %collective-permute-start.1) | collective-permute-done | bytes 1232928 | tf_op jit(solution)/shard_map/ppermute | solution.py:26
  47.3 2.4 pad_maximum_fusion.1
  49.7 3.1 %fusion.17 = (f32[301,16,4]{2,1,0:T(8,128)}, f32[301,16,4]{2,1,0:T(8,128)}) fusion(f32[301,16,256]{2,1,0:T(8,128)S(1)} %pad_maximum_fusion.1), kind=kLoop, calls=%fused_computation.54 | loop fusion | bytes 308224 | tf_op jit(solution)/shard_map/slice | solution.py:25
  52.8 2.8 %copy.30 = f32[301,16,4]{0,1,2:T(8,128)S(1)} copy(f32[301,16,4]{2,1,0:T(8,128)} %get-tuple-element.12) | data formatting | bytes 154112 | tf_op jit(solution)/shard_map/slice | solution.py:25
  55.6 2.9 %copy.31 = f32[301,16,4]{0,1,2:T(8,128)S(1)} copy(f32[301,16,4]{2,1,0:T(8,128)} %get-tuple-element.13) | data formatting | bytes 154112 | tf_op jit(solution)/shard_map/slice | solution.py:26
  61.8 2.9 %collective-permute-done.2 = f32[301,16,4]{0,1,2:T(8,128)S(1)} collective-permute-done((f32[301,16,4]{0,1,2:T(8,128)S(1)}, f32[301,16,4]{0,1,2:T(8,128)S(1)}, u32[]{:S(2)}, u32[]{:S(2)}) %collective-permute-start.2) | collective-permute-done | bytes 77088 | tf_op jit(solution)/shard_map/ppermute | solution.py:25
  64.7 2.9 %copy.32 = f32[301,16,4]{2,1,0:T(8,128)} copy(f32[301,16,4]{0,1,2:T(8,128)S(1)} %collective-permute-done.2) | data formatting | bytes 154112 | tf_op jit(solution)/shard_map/ppermute | solution.py:25
  67.6 2.8 %copy.33 = f32[301,16,4]{2,1,0:T(8,128)} copy(f32[301,16,4]{0,1,2:T(8,128)S(1)} %collective-permute-done.3) | data formatting | bytes 154112 | tf_op jit(solution)/shard_map/ppermute | solution.py:26
  70.4 4.1 %pad_maximum_fusion.ext_ref = f32[301,16,384]{2,1,0:T(8,128)S(1)} fusion(f32[301,16,4]{2,1,0:T(8,128)} %copy.33, f32[301,16,4]{2,1,0:T(8,128)} %copy.32, f32[301,4,256]{2,1,0:T(4,128)} %collective-permute-done.1, f32[301,4,256]{2,1,0:T(4,128)} %collective-permute-done, f32[1,8,256]{2,1,0:T(8,128)S(1)} %get-tuple-element.21, f32[300,8,256]{2,1,0:T(8,128)S(1)} %bitcast.85, ...), kind=kLoop, calls=%fused_computation.5 | loop fusion | flops 11096064 | bytes 12484608 | tf_op jit(solution)/shard_map/concatenate | solution.py:40
  74.5 2.9 %copy-done.1 = f32[301,16,384]{2,1,0:T(8,128)} copy-done((f32[301,16,384]{2,1,0:T(8,128)}, f32[301,16,384]{2,1,0:T(8,128)S(1)}, u32[]{:S(2)}) %copy-start.1) | copy-done | bytes 7397400
  80.0 2.7 %copy.40 = f32[4,32,2,128]{0,3,2,1:T(8,128)} copy(f32[4,32,2,128]{3,0,2,1:T(4,128)S(1)} %bitcast.91) | data formatting | bytes 262144 | tf_op jit(solution)/shard_map/gather | solution.py:209
  82.8 29.9 %gather_fusion.2 = f32[8192,4]{1,0:T(8,128)} fusion(f32[4,8192]{0,1:T(8,128)} %bitcast.87, s32[8192]{0:T(1024)S(1)} %broadcast_clamp_fusion), kind=kCustom, calls=%fused_computation.2 | custom fusion | bytes 294912 | tf_op jit(solution)/shard_map/gather | solution.py:211
  112.7 2.8 %copy.42 = f32[4,8,256,4]{2,1,3,0:T(8,128)S(1)} copy(f32[4,8,256,4]{3,2,1,0:T(8,128)} %bitcast.88) | data formatting | bytes 262144 | tf_op jit(solution)/shard_map/gather | solution.py:211
  116.2 34.6 %shard_map.104 = (f32[4,75,8,256]{3,2,1,0:T(8,128)}, f32[4,8,256]{2,1,0:T(8,128)}) custom-call(f32[75]{0:T(128)} %constant.9.clone.decay_ref, f32[301,16,384]{2,1,0:T(8,128)} %copy-done.1, f32[16,384]{1,0:T(8,128)} %fusion.11.mask_ref, f32[74,8,256]{2,1,0:T(8,128)} %base_ref.1, f32[8,256]{1,0:T(8,128)} %fusion.12.surf_ref, f32[8,256]{1,0:T(8,128)} %get-tuple-element.20.land_ref), custom_call_target="tpu_custom_call" | custom-call | tf_op jit(solution)/shard_map/pallas_call | solution.py:158
  151.9 3.1 %broadcast_multiply_fusion = f32[4,4,8,256]{0,3,2,1:T(8,128)} fusion(f32[4,8,256]{0,2,1:T(8,128)S(1)} %copy.43, f32[4,8,256]{2,1,0:T(8,128)S(1)} %copy-done.3), kind=kLoop, calls=%fused_computation.9 | loop fusion | flops 32768 | bytes 196608 | tf_op jit(solution)/shard_map/mul | solution.py:221
  155.0 46.5 %scatter_custom_fusion = f32[4,8192]{0,1:T(8,128)} fusion(s32[8192]{0:T(1024)S(1)} %bitcast.94, f32[8192,4]{1,0:T(8,128)} %bitcast.89, f32[]{:T(128)} %constant.13.clone.1), kind=kCustom, calls=%fused_computation.10 | custom fusion | flops 32768 | bytes 131584 | tf_op jit(solution)/shard_map/scatter-add | solution.py:222
  201.4 3.5 %copy.44 = f32[4,32,2,128]{3,0,2,1:T(4,128)} copy(f32[4,32,2,128]{0,3,2,1:T(8,128)} %bitcast.86) | data formatting | bytes 262144 | tf_op jit(solution)/shard_map/reshape | solution.py:224
  204.9 3.9 %all-to-all-start.1 = ((f32[4,32,2,128]{3,0,2,1:T(4,128)}), f32[4,32,2,128]{3,0,2,1:T(4,128)S(1)}, u32[]{:S(2)}, u32[]{:S(2)}) async-start(f32[4,32,2,128]{3,0,2,1:T(4,128)} %copy.44), calls=%async_computation.1 | async-start | bytes 262144 | tf_op jit(solution)/shard_map/all_to_all | solution.py:223
  208.8 7.8 %all-to-all-done.1 = f32[4,32,2,128]{3,0,2,1:T(4,128)S(1)} async-done(((f32[4,32,2,128]{3,0,2,1:T(4,128)}), f32[4,32,2,128]{3,0,2,1:T(4,128)S(1)}, u32[]{:S(2)}, u32[]{:S(2)}) %all-to-all-start.1) | async-done | bytes 131104 | tf_op jit(solution)/shard_map/all_to_all | solution.py:223
  216.7 2.8 %scatter_fusion = f32[4,16,128]{2,0,1:T(4,128)S(1)} fusion(f32[4,16,128]{2,0,1:T(4,128)S(1)} %broadcast_in_dim.45, s32[64]{0:T(128)S(1)} %fusion.16, f32[64,4,128]{2,1,0:T(4,128)S(1)} %bitcast.92), kind=kCustom, calls=%fused_computation.4 | custom fusion | flops 32768 | bytes 393472 | tf_op jit(solution)/shard_map/scatter-add | solution.py:227
  219.6 17.2 %psum.7 = f32[4,16,128]{2,0,1:T(4,128)S(1)} all-reduce(f32[4,16,128]{2,0,1:T(4,128)S(1)} %scatter_fusion), channel_id=1, replica_groups=mesh['lat'=32,'lon'=4] {'lon'}, use_global_device_ids=true, to_apply=%region_3.4 | all-reduce | flops 8192 | bytes 65536 | tf_op jit(solution)/shard_map/psum | solution.py:228
  (59 shorter events, 15.3 us)
Async XLA Ops:
  7.2 1.8 copy-start
  9.0 10.1 %copy-start.4 = (f32[4,16,128]{2,1,0:T(8,128)S(1)}, f32[4,16,128]{2,1,0:T(8,128)}, u32[]{:S(2)}) copy-start(f32[4,16,128]{2,1,0:T(8,128)} %param.11) | copy-start | bytes 98308
  9.0 10.7 %copy-start.6 = (s32[8,256]{1,0:T(8,128)S(1)}, s32[8,256]{1,0:T(8,128)}, u32[]{:S(2)}) copy-start(s32[8,256]{1,0:T(8,128)} %param.16) | copy-start | bytes 24580
  9.0 11.3 %copy-start.2 = (f32[4,75,8,256]{3,2,1,0:T(8,128)S(1)}, f32[4,75,8,256]{3,2,1,0:T(8,128)}, u32[]{:S(2)}) copy-start(f32[4,75,8,256]{3,2,1,0:T(8,128)} %param.9) | copy-start | bytes 7372804
  9.8 17.3 %copy-start.5 = (s32[4,8,256]{2,1,0:T(8,128)S(1)}, s32[4,8,256]{2,1,0:T(8,128)}, u32[]{:S(2)}) copy-start(s32[4,8,256]{2,1,0:T(8,128)} %param.14) | copy-start | bytes 98308
  9.8 17.3 %copy-start.3 = (f32[4,8,256]{2,1,0:T(8,128)S(1)}, f32[4,8,256]{2,1,0:T(8,128)}, u32[]{:S(2)}) copy-start(f32[4,8,256]{2,1,0:T(8,128)} %param.15) | copy-start | bytes 98308
  9.8 17.4 %copy-start.7 = (s32[1,32]{1,0:T(1,128)S(1)}, s32[1,32]{1,0:T(1,128)}, u32[]{:S(2)}) copy-start(s32[1,32]{1,0:T(1,128)} %param.12) | copy-start | bytes 388
  10.5 16.8 %all-to-all-start = ((s32[32,1,2]{2,1,0:T(1,128)}), s32[32,1,2]{2,1,0:T(1,128)S(1)}, u32[]{:S(2)}, u32[]{:S(2)}) async-start(s32[32,1,2]{2,1,0:T(1,128)} %bitcast.7), calls=%async_computation | async-start | bytes 32768 | tf_op jit(solution)/shard_map/all_to_all | solution.py:208
  19.0 59.2 %all-gather.2.cloned.1.call-start = ((), (), s32[]{:S(2)}) async-start(), calls=%async_computation.2 | async-start | bytes 1081344 | tf_op jit(solution)/shard_map/all_gather | solution.py:206
  22.2 19.9 %collective-permute-start = (f32[301,4,256]{2,1,0:T(4,128)}, f32[301,4,256]{2,1,0:T(4,128)}, u32[]{:S(2)}, u32[]{:S(2)}) collective-permute-start(f32[301,4,256]{2,1,0:T(4,128)} %get-tuple-element.14), channel_id=1, source_target_pairs={{0,124},{4,0},{8,4},{12,8},{16,12},{20,16},{24,20},{28,24},{32,28}... | collective-permute-start | bytes 3698696 | tf_op jit(solution)/shard_map/ppermute | solution.py:25
  27.1 20.2 %collective-permute-start.1 = (f32[301,4,256]{2,1,0:T(4,128)}, f32[301,4,256]{2,1,0:T(4,128)}, u32[]{:S(2)}, u32[]{:S(2)}) collective-permute-start(f32[301,4,256]{2,1,0:T(4,128)} %get-tuple-element.15), channel_id=1, source_target_pairs={{0,4},{4,8},{8,12},{12,16},{16,20},{20,24},{24,28},{28,32},{32,36}... | collective-permute-start | bytes 3698696 | tf_op jit(solution)/shard_map/ppermute | solution.py:26
  58.5 9.1 %collective-permute-start.3 = (f32[301,16,4]{0,1,2:T(8,128)S(1)}, f32[301,16,4]{0,1,2:T(8,128)S(1)}, u32[]{:S(2)}, u32[]{:S(2)}) collective-permute-start(f32[301,16,4]{0,1,2:T(8,128)S(1)} %copy.31), channel_id=1, source_target_pairs={{0,1},{1,2},{2,3},{3,0},{4,5},{5,6},{6,7},{7,4},{8,9},{9,10},{10,1... | collective-permute-start | bytes 231176 | tf_op jit(solution)/shard_map/ppermute | solution.py:26
  60.1 4.6 %collective-permute-start.2 = (f32[301,16,4]{0,1,2:T(8,128)S(1)}, f32[301,16,4]{0,1,2:T(8,128)S(1)}, u32[]{:S(2)}, u32[]{:S(2)}) collective-permute-start(f32[301,16,4]{0,1,2:T(8,128)S(1)} %copy.30), channel_id=1, source_target_pairs={{0,3},{1,0},{2,1},{3,2},{4,7},{5,4},{6,5},{7,6},{8,11},{9,8},{10,9... | collective-permute-start | bytes 231176 | tf_op jit(solution)/shard_map/ppermute | solution.py:25
  74.5 3.0 %copy-start.1 = (f32[301,16,384]{2,1,0:T(8,128)}, f32[301,16,384]{2,1,0:T(8,128)S(1)}, u32[]{:S(2)}) copy-start(f32[301,16,384]{2,1,0:T(8,128)S(1)} %pad_maximum_fusion.ext_ref) | copy-start | bytes 22192132
  204.9 11.7 %all-to-all-start.1 = ((f32[4,32,2,128]{3,0,2,1:T(4,128)}), f32[4,32,2,128]{3,0,2,1:T(4,128)S(1)}, u32[]{:S(2)}, u32[]{:S(2)}) async-start(f32[4,32,2,128]{3,0,2,1:T(4,128)} %copy.44), calls=%async_computation.1 | async-start | bytes 262144 | tf_op jit(solution)/shard_map/all_to_all | solution.py:223
Sparse Core Ops, SparseCore 0:
  22.6 46.1 all-gather.1
where the time goes:
time: 245 us; the launch traced here: 244 us
  other arithmetic  63.8 us (26%)
  local copies, waits for them, and re-layouts  63.5 us (26%)
  Pallas kernels  34.6 us (14%)
  waiting for transfers between devices  30.4 us (12%)
  starting transfers between devices  20.5 us (8%)
  blocking collectives  17.2 us (7%)
  between operations  14.3 us (6%)
    scatter-add x1, other arithmetic, shards(): buffer = jnp.zeros_like(flat_recv).at[:, cover_index].add(weighted)  46.5 us
    pallas_call x1, Pallas kernels, tridiagonal(): pl.pallas_call(tridiagonal_kernel, out_shape=(jax.ShapeDtypeStruct(shape,...  34.6 us
    gather x2, local copies, waits for them, and re-layouts, shards(): picked = flat_recv[:, cover_index]  32.8 us
    ppermute x2, waiting for transfers between devices, from_neighbours(): lax.ppermute(lax.slice_in_dim(block, 0, width, axis=dim), axis, to_prev)  17.3 us
    psum x1, blocking collectives, shards(): flux_adjoint = lax.psum(owner_sum, 'lon')  17.2 us
    all_to_all x1, starting transfers between devices, shards(): lax.all_to_all(global_ids, 'lat', split_axis=0, concat_axis=0, tiled=True)  8.44 us
    all_to_all x1, waiting for transfers between devices, shards(): lax.all_to_all(buffer.reshape(received.shape), 'lat', split_axis=1, conca...  7.82 us
    ppermute x2, starting transfers between devices, from_neighbours(): lax.ppermute(lax.slice_in_dim(block, 0, width, axis=dim), axis, to_prev)  6.61 us
  transfers between devices with their start and end apart: 7, of which 4 were waited for; matrix products, arithmetic and copies ran while one was open for 10% of the time, Pallas kernels for 0%

commit v1 on v0

--- a/solution.py
+++ b/solution.py
@@ -169,6 +169,80 @@
             pltpu.VMEM((5,) + mask.shape, jnp.float32),
         ],
     )(jnp.asarray(decay_table), ext, mask, mixing_base, surface, land)
+
+
+def split_three(values):
+    high = values.astype(jnp.bfloat16)
+    rest = values - high.astype(jnp.float32)
+    middle = rest.astype(jnp.bfloat16)
+    low = (rest - middle.astype(jnp.float32)).astype(jnp.bfloat16)
+    return high, middle, low
+
+
+def matmul_exact(parts, other, contract):
+    numbers = (((1,), (contract,)), ((), ()))
+    total = None
+    for part in parts:
+        product = lax.dot_general(part, other, numbers, preferred_element_type=jnp.float32)
+        total = product if total is None else total + product
+    return total
+
+
+def gather_kernel(recv_ref, index_ref, weight_ref, out_ref):
+    stacked, lanes = recv_ref.shape
+    fields, rows, cols = out_ref.shape
+    segments = stacked // fields
+    items = index_ref.shape[0] // rows
+    parts = split_three(recv_ref[...])
+    lane_iota = lax.broadcasted_iota(jnp.int32, (lanes, cols), 0)
+    segment_iota = lax.broadcasted_iota(jnp.int32, (fields, segments, cols), 1)
+
+    def row_step(y, carry):
+        total = None
+        for item in range(items):
+            index = index_ref[pl.ds(item * rows + y, 1), :]
+            onehot = (lane_iota == index % lanes).astype(jnp.bfloat16)
+            chosen = matmul_exact(parts, onehot, 0).reshape(fields, segments, cols)
+            hit = segment_iota == (index // lanes)[None]
+            picked = jnp.sum(jnp.where(hit, chosen, 0.0), axis=1)
+            term = weight_ref[pl.ds(item * rows + y, 1), :] * picked
+            total = term if total is None else total + term
+        out_ref[:, pl.ds(y, 1), :] = total[:, None, :]
+        return carry
+
+    lax.fori_loop(0, rows, row_step, 0)
+
+
+def scatter_kernel(back_ref, index_ref, weight_ref, out_ref):
+    fields, rows, cols = back_ref.shape
+    stacked, lanes = out_ref.shape
+    segments = stacked // fields
+    items = index_ref.shape[0] // rows
+    lane_iota = lax.broadcasted_iota(jnp.int32, (lanes, cols), 0)
+    segment_iota = lax.broadcasted_iota(jnp.int32, (fields, segments, cols), 1)
+
+    def row_step(y, total):
+        back = back_ref[:, pl.ds(y, 1), :]
+        for item in range(items):
+            index = index_ref[pl.ds(item * rows + y, 1), :]
+            onehot = (lane_iota == index % lanes).astype(jnp.bfloat16)
+            weighted = weight_ref[pl.ds(item * rows + y, 1), :][None] * back
+            hit = segment_iota == (index // lanes)[None]
+            spread = jnp.where(hit, weighted, 0.0).reshape(stacked, cols)
+            total = total + matmul_exact(split_three(spread), onehot, 1)
+        return total
+
+    out_ref[...] = lax.fori_loop(0, rows, row_step, jnp.zeros((stacked, lanes), jnp.float32))
+
+
+def remap_call(kernel, out_shape, *operands):
+    vmem = pltpu.MemorySpace.VMEM
+    return pl.pallas_call(
+        kernel,
+        out_shape=jax.ShapeDtypeStruct(out_shape, jnp.float32),
+        in_specs=[pl.BlockSpec(memory_space=vmem)] * len(operands),
+        out_specs=pl.BlockSpec(memory_space=vmem),
+    )(*operands)
 
 
 def lat_edges(marks, width):
@@ -207,19 +281,19 @@
     global_ids = lax.axis_index("lat") * owned + chosen
     arrived = lax.all_to_all(global_ids, "lat", split_axis=0, concat_axis=0, tiled=True)
     received = whole[:, arrived, :]
-    flat_recv = received.reshape(4, -1)
-    picked = flat_recv[:, cover_index]
-    forcing = cover_weight[0] * picked[:, 0]
-    for item in range(1, cover_index.shape[0]):
-        forcing = forcing + cover_weight[item] * picked[:, item]
+    items, rows, cols = cover_index.shape
+    fields = received.shape[0]
+    flat_recv = received.reshape(-1, received.shape[-1])
+    index_rows = cover_index.reshape(items * rows, cols)
+    weight_rows = cover_weight.reshape(items * rows, cols)
+    forcing = remap_call(gather_kernel, (fields, rows, cols), flat_recv, index_rows, weight_rows)
     surface = WIND_GAIN * (forcing[2] * forcing[2] + forcing[3] * forcing[3]) + jax.nn.softplus(
         forcing[1] - forcing[0]
     )
     land = land_mask.astype(jnp.float32)
     ext, mask = extended_planes(adjoint_state, land_mask, HALO)
     state_adjoint, flux_back = tridiagonal(ext, mask, adjoint_state.shape, mixing_base, surface, land)
-    weighted = cover_weight[None] * flux_back[:, None]
-    buffer = jnp.zeros_like(flat_recv).at[:, cover_index].add(weighted)
+    buffer = remap_call(scatter_kernel, flat_recv.shape, flux_back, index_rows, weight_rows)
     returned = lax.all_to_all(
         buffer.reshape(received.shape), "lat", split_axis=1, concat_axis=1, tiled=True
     )

time: 245 us -> 170 us (0.69)
  other arithmetic: 63.8 us -> 17.4 us
  local copies, waits for them, and re-layouts: 63.5 us -> 25.1 us
  Pallas kernels: 34.6 us -> 47.4 us
  waiting for transfers between devices: 30.4 us -> 26.9 us
    scatter-add x1 -> x0, other arithmetic: 46.5 us -> none  [shards(): buffer = jnp.zeros_like(flat_recv).at[:, cover_index].add(weighted)]
    gather x2 -> x0, local copies, waits for them, and re-layouts: 32.8 us -> none  [shards(): picked = flat_recv[:, cover_index]]
    ppermute x2, waiting for transfers between devices: 17.3 us -> 0.01 us  [from_neighbours(): lax.ppermute(lax.slice_in_dim(block, 0, width, axis=dim), axis, to_prev)]
    pallas_call x0 -> x2, Pallas kernels: none -> 12.9 us  [remap_call(): pl.pallas_call(kernel, out_shape=jax.ShapeDtypeStruct(out_shape, jnp.floa...]
    all_to_all x1, waiting for transfers between devices: 0.01 us -> 10.3 us  [shards(): lax.all_to_all(global_ids, 'lat', split_axis=0, concat_axis=0, tiled=True)]
    all_gather x1, waiting for transfers between devices: 0.01 us -> 5.77 us  [shards(): whole = lax.all_gather(atm_flux, 'lat', axis=1, tiled=True)]
    mul x1 -> x0, other arithmetic: 3.09 us -> none  [shards(): weighted = cover_weight[None] * flux_back[:, None]]
    concatenate x1, other arithmetic: 1.82 us -> 4.31 us  [extended_planes(): stack = jnp.concatenate([planes, coast], axis=0)]
  transfers between devices with their start and end apart: 7 -> 7, of which waited for: 4 -> 4; matrix products, arithmetic and copies ran while one was open for 10% -> 15% of each run, Pallas kernels for 0% -> 0%
where the time goes in v1:
time: 170 us; the launch traced here: 169 us
  Pallas kernels  47.4 us (28%)
  waiting for transfers between devices  26.9 us (16%)
  local copies, waits for them, and re-layouts  25.1 us (15%)
  starting transfers between devices  20.9 us (12%)
  other arithmetic  17.4 us (10%)
  blocking collectives  17 us (10%)
  between operations  14.3 us (8%)
    pallas_call x1, Pallas kernels, tridiagonal(): pl.pallas_call(tridiagonal_kernel, out_shape=(jax.ShapeDtypeStruct(shape,...  34.6 us
    psum x1, blocking collectives, shards(): flux_adjoint = lax.psum(owner_sum, 'lon')  17 us
    pallas_call x2, Pallas kernels, remap_call(): pl.pallas_call(kernel, out_shape=jax.ShapeDtypeStruct(out_shape, jnp.floa...  12.9 us
    all_to_all x1, waiting for transfers between devices, shards(): lax.all_to_all(global_ids, 'lat', split_axis=0, concat_axis=0, tiled=True)  10.3 us
    ppermute x2, starting transfers between devices, from_neighbours(): lax.ppermute(lax.slice_in_dim(block, 0, width, axis=dim), axis, to_prev)  8.85 us
    all_to_all x1, waiting for transfers between devices, shards(): lax.all_to_all(buffer.reshape(received.shape), 'lat', split_axis=1, conca...  7.82 us
    all_to_all x1, starting transfers between devices, shards(): lax.all_to_all(global_ids, 'lat', split_axis=0, concat_axis=0, tiled=True)  6.73 us
    slice x2, local copies, waits for them, and re-layouts, from_neighbours(): lax.slice_in_dim(block, 0, width, axis=dim)  5.92 us
  transfers between devices with their start and end apart: 7, of which 4 were waited for; matrix products, arithmetic and copies ran while one was open for 15% of the time, Pallas kernels for 0%

profile of v1, /device:TPU:0, one launch (start us, length us, event | category | flops | bytes accessed | tf_op | source)
XLA Modules:
  0.0 169.1 jit_solution(4117207326642364782)
XLA Ops:
  8.5 4.3 %fusion = (f32[301,4,256]{2,1,0:T(4,128)}, f32[301,4,256]{2,1,0:T(4,128)}) fusion(f32[300,8,256]{2,1,0:T(8,128)} %bitcast.41, f32[1,8,256]{2,1,0:T(8,128)S(1)} %get-tuple-element.19), kind=kLoop, calls=%fused_computation.7 | loop fusion | flops 616448 | bytes 4931584 | tf_op jit(solution)/shard_map/concatenate | solution.py:34
  12.8 6.0 %collective-permute-start = (f32[301,4,256]{2,1,0:T(4,128)}, f32[301,4,256]{2,1,0:T(4,128)}, u32[]{:S(2)}, u32[]{:S(2)}) collective-permute-start(f32[301,4,256]{2,1,0:T(4,128)} %get-tuple-element.16), channel_id=1, source_target_pairs={{0,124},{4,0},{8,4},{12,8},{16,12},{20,16},{24,20},{28,24},{32,28}... | collective-permute-start | bytes 3698696 | tf_op jit(solution)/shard_map/ppermute | solution.py:25
  20.9 6.7 %all-to-all-start = ((s32[32,1,2]{2,1,0:T(1,128)}), s32[32,1,2]{2,1,0:T(1,128)S(1)}, u32[]{:S(2)}, u32[]{:S(2)}) async-start(s32[32,1,2]{2,1,0:T(1,128)} %bitcast.6), calls=%async_computation | async-start | bytes 32768 | tf_op jit(solution)/shard_map/all_to_all | solution.py:282
  28.5 10.3 %all-to-all-done = s32[32,1,2]{2,1,0:T(1,128)S(1)} async-done(((s32[32,1,2]{2,1,0:T(1,128)}), s32[32,1,2]{2,1,0:T(1,128)S(1)}, u32[]{:S(2)}, u32[]{:S(2)}) %all-to-all-start) | async-done | bytes 288 | tf_op jit(solution)/shard_map/all_to_all | solution.py:282
  39.2 2.4 %pad_maximum_fusion.1 = f32[301,16,256]{2,1,0:T(8,128)S(1)} fusion(f32[301,4,256]{2,1,0:T(4,128)} %collective-permute-done.1, f32[301,4,256]{2,1,0:T(4,128)} %collective-permute-done, f32[1,8,256]{2,1,0:T(8,128)S(1)} %get-tuple-element.19, f32[300,8,256]{2,1,0:T(8,128)S(1)} %bitcast.42), kind=kLoop, calls=%fused_computation.4 | loop fusion | flops 3698688 | bytes 9863168 | tf_op jit(solution)/shard_map/concatenate | solution.py:36
  41.6 3.1 %fusion.7 = (f32[301,16,4]{2,1,0:T(8,128)}, f32[301,16,4]{2,1,0:T(8,128)}) fusion(f32[301,16,256]{2,1,0:T(8,128)S(1)} %pad_maximum_fusion.1), kind=kLoop, calls=%fused_computation.31 | loop fusion | bytes 308224 | tf_op jit(solution)/shard_map/slice | solution.py:25
  44.7 2.8 %copy.38 = f32[301,16,4]{0,1,2:T(8,128)S(1)} copy(f32[301,16,4]{2,1,0:T(8,128)} %get-tuple-element.14) | data formatting | bytes 154112 | tf_op jit(solution)/shard_map/slice | solution.py:25
  47.5 2.8 %collective-permute-start.2 = (f32[301,16,4]{0,1,2:T(8,128)S(1)}, f32[301,16,4]{0,1,2:T(8,128)S(1)}, u32[]{:S(2)}, u32[]{:S(2)}) collective-permute-start(f32[301,16,4]{0,1,2:T(8,128)S(1)} %copy.38), channel_id=1, source_target_pairs={{0,3},{1,0},{2,1},{3,2},{4,7},{5,4},{6,5},{7,6},{8,11},{9,8},{10,9... | collective-permute-start | bytes 231176 | tf_op jit(solution)/shard_map/ppermute | solution.py:25
  50.3 2.8 %copy.39 = f32[301,16,4]{0,1,2:T(8,128)S(1)} copy(f32[301,16,4]{2,1,0:T(8,128)} %get-tuple-element.15) | data formatting | bytes 154112 | tf_op jit(solution)/shard_map/slice | solution.py:26
  53.2 2.9 %copy.40 = f32[301,16,4]{2,1,0:T(8,128)} copy(f32[301,16,4]{0,1,2:T(8,128)S(1)} %collective-permute-done.2) | data formatting | bytes 154112 | tf_op jit(solution)/shard_map/ppermute | solution.py:25
  56.1 2.9 %collective-permute-done.3 = f32[301,16,4]{0,1,2:T(8,128)S(1)} collective-permute-done((f32[301,16,4]{0,1,2:T(8,128)S(1)}, f32[301,16,4]{0,1,2:T(8,128)S(1)}, u32[]{:S(2)}, u32[]{:S(2)}) %collective-permute-start.3) | collective-permute-done | bytes 77088 | tf_op jit(solution)/shard_map/ppermute | solution.py:26
  59.0 2.8 %copy.41 = f32[301,16,4]{2,1,0:T(8,128)} copy(f32[301,16,4]{0,1,2:T(8,128)S(1)} %collective-permute-done.3) | data formatting | bytes 154112 | tf_op jit(solution)/shard_map/ppermute | solution.py:26
  61.9 4.1 %pad_maximum_fusion.ext_ref = f32[301,16,384]{2,1,0:T(8,128)S(1)} fusion(f32[301,16,4]{2,1,0:T(8,128)} %copy.41, f32[301,16,4]{2,1,0:T(8,128)} %copy.40, f32[301,4,256]{2,1,0:T(4,128)} %collective-permute-done.1, f32[301,4,256]{2,1,0:T(4,128)} %collective-permute-done, f32[1,8,256]{2,1,0:T(8,128)S(1)} %get-tuple-element.19, f32[300,8,256]{2,1,0:T(8,128)S(1)} %bitcast.43, ...), kind=kLoop, calls=%fused_computation.3 | loop fusion | flops 11096064 | bytes 12484608 | tf_op jit(solution)/shard_map/concatenate | solution.py:40
  66.0 3.0 %copy-done.1 = f32[301,16,384]{2,1,0:T(8,128)} copy-done((f32[301,16,384]{2,1,0:T(8,128)}, f32[301,16,384]{2,1,0:T(8,128)S(1)}, u32[]{:S(2)}) %copy-start.1) | copy-done | bytes 7397400
  69.6 5.8 %all-gather.2.cloned.1.call-done = f32[4,512,128]{2,0,1:T(4,128)} async-done(((f32[4,16,128]{2,0,1:T(4,128)}), f32[4,512,128]{2,0,1:T(4,128)}) %all-gather.2.cloned.1.call-update) | async-done | bytes 1048592 | tf_op jit(solution)/shard_map/all_gather | solution.py:280
  75.4 1.9 %gather_fusion.1 = f32[64,4,128]{2,1,0:T(4,128)S(1)} fusion(f32[4,512,128]{2,0,1:T(4,128)} %all-gather.2.cloned.1.call-done, s32[1024]{0:T(1024)S(1)} %pad_clamp_fusion), kind=kCustom, calls=%fused_computation.1 | custom fusion | bytes 262400 | tf_op jit(solution)/shard_map/gather | solution.py:283
  78.0 6.3 %shard_map.104 = f32[4,8,256]{2,1,0:T(8,128)} custom-call(f32[256,128]{1,0:T(8,128)} %bitcast.44, s32[32,256]{1,0:T(8,128)} %bitcast.48, f32[32,256]{1,0:T(8,128)} %bitcast.50), custom_call_target="tpu_custom_call" | custom-call | tf_op jit(solution)/shard_map/pallas_call | solution.py:240
  85.7 34.6 %shard_map.105 = (f32[4,75,8,256]{3,2,1,0:T(8,128)}, f32[4,8,256]{2,1,0:T(8,128)}) custom-call(f32[75]{0:T(128)} %constant.10.clone.decay_ref, f32[301,16,384]{2,1,0:T(8,128)} %copy-done.1, f32[16,384]{1,0:T(8,128)} %fusion.1.mask_ref, f32[74,8,256]{2,1,0:T(8,128)} %base_ref.1, f32[8,256]{1,0:T(8,128)} %fusion.2.surf_ref, f32[8,256]{1,0:T(8,128)} %get-tuple-element.18.land_ref), custom_call_target="tpu_custom_call" | custom-call | tf_op jit(solution)/shard_map/pallas_call | solution.py:158
  120.2 6.6 %shard_map.106 = f32[256,128]{1,0:T(8,128)} custom-call(f32[4,8,256]{2,1,0:T(8,128)} %get-tuple-element.5.back_ref, s32[32,256]{1,0:T(8,128)} %bitcast.49, f32[32,256]{1,0:T(8,128)} %bitcast.51), custom_call_target="tpu_custom_call" | custom-call | tf_op jit(solution)/shard_map/pallas_call | solution.py:240
  126.8 1.6 copy.49
  128.4 5.2 %all-to-all-start.1 = ((f32[4,32,2,128]{3,2,0,1:T(2,128)}), f32[4,32,2,128]{3,2,0,1:T(2,128)S(1)}, u32[]{:S(2)}, u32[]{:S(2)}) async-start(f32[4,32,2,128]{3,2,0,1:T(2,128)} %copy.49), calls=%async_computation.1 | async-start | bytes 262144 | tf_op jit(solution)/shard_map/all_to_all | solution.py:297
  133.7 7.8 %all-to-all-done.1 = f32[4,32,2,128]{3,2,0,1:T(2,128)S(1)} async-done(((f32[4,32,2,128]{3,2,0,1:T(2,128)}), f32[4,32,2,128]{3,2,0,1:T(2,128)S(1)}, u32[]{:S(2)}, u32[]{:S(2)}) %all-to-all-start.1) | async-done | bytes 131104 | tf_op jit(solution)/shard_map/all_to_all | solution.py:297
  141.8 2.8 %scatter_fusion = f32[4,16,128]{2,0,1:T(4,128)S(1)} fusion(f32[4,16,128]{2,0,1:T(4,128)S(1)} %broadcast_in_dim.35, s32[64]{0:T(128)S(1)} %fusion.6, f32[64,4,128]{2,1,0:T(4,128)S(1)} %copy.51), kind=kCustom, calls=%fused_computation.2 | custom fusion | flops 32768 | bytes 393472 | tf_op jit(solution)/shard_map/scatter-add | solution.py:301
  144.6 17.0 %psum.7 = f32[4,16,128]{2,0,1:T(4,128)S(1)} all-reduce(f32[4,16,128]{2,0,1:T(4,128)S(1)} %scatter_fusion), channel_id=1, replica_groups=mesh['lat'=32,'lon'=4] {'lon'}, use_global_device_ids=true, to_apply=%region_2.3 | all-reduce | flops 8192 | bytes 65536 | tf_op jit(solution)/shard_map/psum | solution.py:302
  (47 shorter events, 8.2 us)
Async XLA Ops:
  7.2 12.2 %copy-start = (s32[1,64]{1,0:T(1,128)S(1)}, s32[1,64]{1,0:T(1,128)}, u32[]{:S(2)}) copy-start(s32[1,64]{1,0:T(1,128)} %param.13) | copy-start | bytes 772
  8.5 10.4 %copy-start.4 = (s32[1,32]{1,0:T(1,128)S(1)}, s32[1,32]{1,0:T(1,128)}, u32[]{:S(2)}) copy-start(s32[1,32]{1,0:T(1,128)} %param.12) | copy-start | bytes 388
  12.8 26.3 %collective-permute-start = (f32[301,4,256]{2,1,0:T(4,128)}, f32[301,4,256]{2,1,0:T(4,128)}, u32[]{:S(2)}, u32[]{:S(2)}) collective-permute-start(f32[301,4,256]{2,1,0:T(4,128)} %get-tuple-element.16), channel_id=1, source_target_pairs={{0,124},{4,0},{8,4},{12,8},{16,12},{20,16},{24,20},{28,24},{32,28}... | collective-permute-start | bytes 3698696 | tf_op jit(solution)/shard_map/ppermute | solution.py:25
  18.8 20.3 %collective-permute-start.1 = (f32[301,4,256]{2,1,0:T(4,128)}, f32[301,4,256]{2,1,0:T(4,128)}, u32[]{:S(2)}, u32[]{:S(2)}) collective-permute-start(f32[301,4,256]{2,1,0:T(4,128)} %get-tuple-element.17), channel_id=1, source_target_pairs={{0,4},{4,8},{8,12},{12,16},{16,20},{20,24},{24,28},{28,32},{32,36}... | collective-permute-start | bytes 3698696 | tf_op jit(solution)/shard_map/ppermute | solution.py:26
  19.3 8.3 %copy-start.3 = (f32[4,16,128]{2,1,0:T(8,128)S(1)}, f32[4,16,128]{2,1,0:T(8,128)}, u32[]{:S(2)}) copy-start(f32[4,16,128]{2,1,0:T(8,128)} %param.11) | copy-start | bytes 98308
  19.4 19.8 %copy-start.2 = (f32[4,75,8,256]{3,2,1,0:T(8,128)S(1)}, f32[4,75,8,256]{3,2,1,0:T(8,128)}, u32[]{:S(2)}) copy-start(f32[4,75,8,256]{3,2,1,0:T(8,128)} %param.9) | copy-start | bytes 7372804
  20.9 18.0 %all-to-all-start = ((s32[32,1,2]{2,1,0:T(1,128)}), s32[32,1,2]{2,1,0:T(1,128)S(1)}, u32[]{:S(2)}, u32[]{:S(2)}) async-start(s32[32,1,2]{2,1,0:T(1,128)} %bitcast.6), calls=%async_computation | async-start | bytes 32768 | tf_op jit(solution)/shard_map/all_to_all | solution.py:282
  27.6 47.8 %all-gather.2.cloned.1.call-start = ((), (), s32[]{:S(2)}) async-start(), calls=%async_computation.2 | async-start | bytes 1081344 | tf_op jit(solution)/shard_map/all_gather | solution.py:280
  47.5 5.7 %collective-permute-start.2 = (f32[301,16,4]{0,1,2:T(8,128)S(1)}, f32[301,16,4]{0,1,2:T(8,128)S(1)}, u32[]{:S(2)}, u32[]{:S(2)}) collective-permute-start(f32[301,16,4]{0,1,2:T(8,128)S(1)} %copy.38), channel_id=1, source_target_pairs={{0,3},{1,0},{2,1},{3,2},{4,7},{5,4},{6,5},{7,6},{8,11},{9,8},{10,9... | collective-permute-start | bytes 231176 | tf_op jit(solution)/shard_map/ppermute | solution.py:25
  53.1 5.9 %collective-permute-start.3 = (f32[301,16,4]{0,1,2:T(8,128)S(1)}, f32[301,16,4]{0,1,2:T(8,128)S(1)}, u32[]{:S(2)}, u32[]{:S(2)}) collective-permute-start(f32[301,16,4]{0,1,2:T(8,128)S(1)} %copy.39), channel_id=1, source_target_pairs={{0,1},{1,2},{2,3},{3,0},{4,5},{5,6},{6,7},{7,4},{8,9},{9,10},{10,1... | collective-permute-start | bytes 231176 | tf_op jit(solution)/shard_map/ppermute | solution.py:26
  66.0 3.0 %copy-start.1 = (f32[301,16,384]{2,1,0:T(8,128)}, f32[301,16,384]{2,1,0:T(8,128)S(1)}, u32[]{:S(2)}) copy-start(f32[301,16,384]{2,1,0:T(8,128)S(1)} %pad_maximum_fusion.ext_ref) | copy-start | bytes 22192132
  128.4 13.1 %all-to-all-start.1 = ((f32[4,32,2,128]{3,2,0,1:T(2,128)}), f32[4,32,2,128]{3,2,0,1:T(2,128)S(1)}, u32[]{:S(2)}, u32[]{:S(2)}) async-start(f32[4,32,2,128]{3,2,0,1:T(2,128)} %copy.49), calls=%async_computation.1 | async-start | bytes 262144 | tf_op jit(solution)/shard_map/all_to_all | solution.py:297
Sparse Core Ops, SparseCore 0:
  31.2 44.1 all-gather.1

commit v2 on v1

--- a/solution.py
+++ b/solution.py
@@ -243,6 +243,18 @@
         in_specs=[pl.BlockSpec(memory_space=vmem)] * len(operands),
         out_specs=pl.BlockSpec(memory_space=vmem),
     )(*operands)
+
+
+def sum_over(values, axis):
+    count = lax.axis_size(axis)
+    if count & (count - 1):
+        return lax.psum(values, axis)
+    step = 1
+    while step < count:
+        pairs = [(i, i ^ step) for i in range(count)]
+        values = values + lax.ppermute(values, axis, pairs)
+        step *= 2
+    return values
 
 
 def lat_edges(marks, width):
@@ -277,10 +289,8 @@
     places = jnp.minimum(starts[:, None] + column[None, :], send_segment.shape[1] - 1)
     chosen = send_segment[0][places]
     live_slot = column[None, :] < counts[:, None]
-    whole = lax.all_gather(atm_flux, "lat", axis=1, tiled=True)
-    global_ids = lax.axis_index("lat") * owned + chosen
-    arrived = lax.all_to_all(global_ids, "lat", split_axis=0, concat_axis=0, tiled=True)
-    received = whole[:, arrived, :]
+    outgoing = atm_flux[:, chosen, :]
+    received = lax.all_to_all(outgoing, "lat", split_axis=1, concat_axis=1, tiled=True)
     items, rows, cols = cover_index.shape
     fields = received.shape[0]
     flat_recv = received.reshape(-1, received.shape[-1])
@@ -299,7 +309,7 @@
     )
     kept = jnp.where(live_slot[None, :, :, None], returned, 0.0).reshape(4, -1, 128)
     owner_sum = jnp.zeros_like(atm_flux).at[:, chosen.reshape(-1), :].add(kept)
-    flux_adjoint = lax.psum(owner_sum, "lon")
+    flux_adjoint = sum_over(owner_sum, "lon")
     return (state_adjoint, flux_adjoint)
 
 

time: 170 us -> 139 us (0.82)
  blocking collectives: 17 us -> 0 us
  between operations: 14.3 us -> 0.85 us
  waiting for transfers between devices: 26.9 us -> 30.5 us
  local copies, waits for them, and re-layouts: 25.1 us -> 23.2 us
    psum x1 -> x0, blocking collectives: 17 us -> none  [shards(): flux_adjoint = lax.psum(owner_sum, 'lon')]
    ppermute x0 -> x2, waiting for transfers between devices: none -> 9.01 us  [sum_over(): values = values + lax.ppermute(values, axis, pairs)]
    all_gather x1 -> x0, waiting for transfers between devices: 5.77 us -> none  [shards(): whole = lax.all_gather(atm_flux, 'lat', axis=1, tiled=True)]
    unnamed x12 -> x13, local copies, waits for them, and re-layouts: 4.23 us -> 3.6 us
  transfers between devices with their start and end apart: 7 -> 8, of which waited for: 4 -> 5; matrix products, arithmetic and copies ran while one was open for 15% -> 7% of each run, Pallas kernels for 0% -> 5%
where the time goes in v2:
time: 139 us
  Pallas kernels  47.3 us (34%)
  waiting for transfers between devices  30.5 us (22%)
  local copies, waits for them, and re-layouts  23.2 us (17%)
  starting transfers between devices  20 us (14%)
  other arithmetic  16.8 us (12%)
    pallas_call x1, Pallas kernels, tridiagonal(): pl.pallas_call(tridiagonal_kernel, out_shape=(jax.ShapeDtypeStruct(shape,...  34.5 us
    pallas_call x2, Pallas kernels, remap_call(): pl.pallas_call(kernel, out_shape=jax.ShapeDtypeStruct(out_shape, jnp.floa...  12.8 us
    all_to_all x1, waiting for transfers between devices, shards(): lax.all_to_all(outgoing, 'lat', split_axis=1, concat_axis=1, tiled=True)  11.3 us
    ppermute x2, waiting for transfers between devices, sum_over(): values = values + lax.ppermute(values, axis, pairs)  9.01 us
    ppermute x2, starting transfers between devices, from_neighbours(): lax.ppermute(lax.slice_in_dim(block, 0, width, axis=dim), axis, to_prev)  8.85 us
    all_to_all x1, waiting for transfers between devices, shards(): lax.all_to_all(buffer.reshape(received.shape), 'lat', split_axis=1, conca...  7.82 us
    all_to_all x1, starting transfers between devices, shards(): lax.all_to_all(outgoing, 'lat', split_axis=1, concat_axis=1, tiled=True)  6.73 us
    slice x2, local copies, waits for them, and re-layouts, from_neighbours(): lax.slice_in_dim(block, 0, width, axis=dim)  5.92 us
  transfers between devices with their start and end apart: 8, of which 5 were waited for; matrix products, arithmetic and copies ran while one was open for 7% of the time, Pallas kernels for 5%

profile of v2, /device:TPU:0, one launch (start us, length us, event | category | flops | bytes accessed | tf_op | source)
XLA Modules:
  0.0 138.6 jit_solution(17089668239252118025)
XLA Ops:
  0.6 1.3 fusion.8
  1.9 4.3 %fusion = (f32[301,4,256]{2,1,0:T(4,128)}, f32[301,4,256]{2,1,0:T(4,128)}) fusion(f32[300,8,256]{2,1,0:T(8,128)} %bitcast.39, f32[1,8,256]{2,1,0:T(8,128)S(1)} %get-tuple-element.19), kind=kLoop, calls=%fused_computation.7 | loop fusion | flops 616448 | bytes 4931584 | tf_op jit(solution)/shard_map/concatenate | solution.py:34
  6.3 6.0 %collective-permute-start = (f32[301,4,256]{2,1,0:T(4,128)}, f32[301,4,256]{2,1,0:T(4,128)}, u32[]{:S(2)}, u32[]{:S(2)}) collective-permute-start(f32[301,4,256]{2,1,0:T(4,128)} %get-tuple-element.16), channel_id=1, source_target_pairs={{0,124},{4,0},{8,4},{12,8},{16,12},{20,16},{24,20},{28,24},{32,28}... | collective-permute-start | bytes 3698696 | tf_op jit(solution)/shard_map/ppermute | solution.py:25
  15.3 6.7 %all-to-all-start = ((f32[4,32,2,128]{3,2,0,1:T(2,128)}), f32[4,32,2,128]{3,2,0,1:T(2,128)S(1)}, u32[]{:S(2)}, u32[]{:S(2)}) async-start(f32[4,32,2,128]{3,2,0,1:T(2,128)} %bitcast.37), calls=%async_computation | async-start | bytes 262144 | tf_op jit(solution)/shard_map/all_to_all | solution.py:293
  22.2 11.3 %all-to-all-done = f32[4,32,2,128]{3,2,0,1:T(2,128)S(1)} async-done(((f32[4,32,2,128]{3,2,0,1:T(2,128)}), f32[4,32,2,128]{3,2,0,1:T(2,128)S(1)}, u32[]{:S(2)}, u32[]{:S(2)}) %all-to-all-start) | async-done | bytes 131104 | tf_op jit(solution)/shard_map/all_to_all | solution.py:293
  34.2 6.3 %shard_map.104 = f32[4,8,256]{2,1,0:T(8,128)} custom-call(f32[256,128]{1,0:T(8,128)} %bitcast.43, s32[32,256]{1,0:T(8,128)} %bitcast.46, f32[32,256]{1,0:T(8,128)} %bitcast.48), custom_call_target="tpu_custom_call" | custom-call | tf_op jit(solution)/shard_map/pallas_call | solution.py:240
  40.5 2.4 %pad_maximum_fusion.1 = f32[301,16,256]{2,1,0:T(8,128)S(1)} fusion(f32[301,4,256]{2,1,0:T(4,128)} %collective-permute-done.1, f32[301,4,256]{2,1,0:T(4,128)} %collective-permute-done, f32[1,8,256]{2,1,0:T(8,128)S(1)} %get-tuple-element.19, f32[300,8,256]{2,1,0:T(8,128)S(1)} %bitcast.40), kind=kLoop, calls=%fused_computation.4 | loop fusion | flops 3698688 | bytes 9863168 | tf_op jit(solution)/shard_map/concatenate | solution.py:36
  42.9 3.1 %fusion.7 = (f32[301,16,4]{2,1,0:T(8,128)}, f32[301,16,4]{2,1,0:T(8,128)}) fusion(f32[301,16,256]{2,1,0:T(8,128)S(1)} %pad_maximum_fusion.1), kind=kLoop, calls=%fused_computation.31 | loop fusion | bytes 308224 | tf_op jit(solution)/shard_map/slice | solution.py:25
  46.0 2.8 %copy.26 = f32[301,16,4]{0,1,2:T(8,128)S(1)} copy(f32[301,16,4]{2,1,0:T(8,128)} %get-tuple-element.14) | data formatting | bytes 154112 | tf_op jit(solution)/shard_map/slice | solution.py:25
  48.8 2.8 %collective-permute-start.2 = (f32[301,16,4]{0,1,2:T(8,128)S(1)}, f32[301,16,4]{0,1,2:T(8,128)S(1)}, u32[]{:S(2)}, u32[]{:S(2)}) collective-permute-start(f32[301,16,4]{0,1,2:T(8,128)S(1)} %copy.26), channel_id=1, source_target_pairs={{0,3},{1,0},{2,1},{3,2},{4,7},{5,4},{6,5},{7,6},{8,11},{9,8},{10,9... | collective-permute-start | bytes 231176 | tf_op jit(solution)/shard_map/ppermute | solution.py:25
  51.6 2.8 %copy.27 = f32[301,16,4]{0,1,2:T(8,128)S(1)} copy(f32[301,16,4]{2,1,0:T(8,128)} %get-tuple-element.15) | data formatting | bytes 154112 | tf_op jit(solution)/shard_map/slice | solution.py:26
  55.2 2.8 %copy.28 = f32[301,16,4]{2,1,0:T(8,128)} copy(f32[301,16,4]{0,1,2:T(8,128)S(1)} %collective-permute-done.2) | data formatting | bytes 154112 | tf_op jit(solution)/shard_map/ppermute | solution.py:25
  58.0 2.3 %collective-permute-done.3 = f32[301,16,4]{0,1,2:T(8,128)S(1)} collective-permute-done((f32[301,16,4]{0,1,2:T(8,128)S(1)}, f32[301,16,4]{0,1,2:T(8,128)S(1)}, u32[]{:S(2)}, u32[]{:S(2)}) %collective-permute-start.3) | collective-permute-done | bytes 77088 | tf_op jit(solution)/shard_map/ppermute | solution.py:26
  60.4 2.8 %copy.29 = f32[301,16,4]{2,1,0:T(8,128)} copy(f32[301,16,4]{0,1,2:T(8,128)S(1)} %collective-permute-done.3) | data formatting | bytes 154112 | tf_op jit(solution)/shard_map/ppermute | solution.py:26
  63.2 4.1 %pad_maximum_fusion.ext_ref = f32[301,16,384]{2,1,0:T(8,128)S(1)} fusion(f32[301,16,4]{2,1,0:T(8,128)} %copy.29, f32[301,16,4]{2,1,0:T(8,128)} %copy.28, f32[301,4,256]{2,1,0:T(4,128)} %collective-permute-done.1, f32[301,4,256]{2,1,0:T(4,128)} %collective-permute-done, f32[1,8,256]{2,1,0:T(8,128)S(1)} %get-tuple-element.19, f32[300,8,256]{2,1,0:T(8,128)S(1)} %bitcast.41, ...), kind=kLoop, calls=%fused_computation.3 | loop fusion | flops 11096064 | bytes 12484608 | tf_op jit(solution)/shard_map/concatenate | solution.py:40
  67.3 3.0 %copy-done.2 = f32[301,16,384]{2,1,0:T(8,128)} copy-done((f32[301,16,384]{2,1,0:T(8,128)}, f32[301,16,384]{2,1,0:T(8,128)S(1)}, u32[]{:S(2)}) %copy-start.2) | copy-done | bytes 7397400
  71.0 34.5 %shard_map.105 = (f32[4,75,8,256]{3,2,1,0:T(8,128)}, f32[4,8,256]{2,1,0:T(8,128)}) custom-call(f32[75]{0:T(128)} %constant.9.clone.decay_ref, f32[301,16,384]{2,1,0:T(8,128)} %copy-done.2, f32[16,384]{1,0:T(8,128)} %fusion.1.mask_ref, f32[74,8,256]{2,1,0:T(8,128)} %base_ref.1, f32[8,256]{1,0:T(8,128)} %fusion.2.surf_ref, f32[8,256]{1,0:T(8,128)} %get-tuple-element.18.land_ref), custom_call_target="tpu_custom_call" | custom-call | tf_op jit(solution)/shard_map/pallas_call | solution.py:158
  105.5 6.5 %shard_map.106 = f32[256,128]{1,0:T(8,128)} custom-call(f32[4,8,256]{2,1,0:T(8,128)} %get-tuple-element.5.back_ref, s32[32,256]{1,0:T(8,128)} %bitcast.47, f32[32,256]{1,0:T(8,128)} %bitcast.49), custom_call_target="tpu_custom_call" | custom-call | tf_op jit(solution)/shard_map/pallas_call | solution.py:240
  112.0 1.6 %copy.33 = f32[4,32,2,128]{3,2,0,1:T(2,128)} copy(f32[4,32,2,128]{3,2,1,0:T(2,128)} %bitcast.44) | data formatting | bytes 262144 | tf_op jit(solution)/shard_map/reshape | solution.py:308
  113.6 3.9 %all-to-all-start.1 = ((f32[4,32,2,128]{3,2,0,1:T(2,128)}), f32[4,32,2,128]{3,2,0,1:T(2,128)S(1)}, u32[]{:S(2)}, u32[]{:S(2)}) async-start(f32[4,32,2,128]{3,2,0,1:T(2,128)} %copy.33), calls=%async_computation.1 | async-start | bytes 262144 | tf_op jit(solution)/shard_map/all_to_all | solution.py:307
  117.5 7.8 %all-to-all-done.1 = f32[4,32,2,128]{3,2,0,1:T(2,128)S(1)} async-done(((f32[4,32,2,128]{3,2,0,1:T(2,128)}), f32[4,32,2,128]{3,2,0,1:T(2,128)S(1)}, u32[]{:S(2)}, u32[]{:S(2)}) %all-to-all-start.1) | async-done | bytes 131104 | tf_op jit(solution)/shard_map/all_to_all | solution.py:307
  125.6 2.8 %scatter_fusion = f32[4,16,128]{2,0,1:T(4,128)S(1)} fusion(f32[4,16,128]{2,0,1:T(4,128)S(1)} %broadcast_in_dim.35, s32[64]{0:T(128)S(1)} %fusion.6, f32[64,4,128]{2,1,0:T(4,128)S(1)} %copy.35), kind=kCustom, calls=%fused_computation.2 | custom fusion | flops 32768 | bytes 393472 | tf_op jit(solution)/shard_map/scatter-add | solution.py:311
  128.5 3.9 %collective-permute-done.4 = f32[4,16,128]{2,0,1:T(4,128)S(1)} collective-permute-done((f32[4,16,128]{2,0,1:T(4,128)S(1)}, f32[4,16,128]{2,0,1:T(4,128)S(1)}, u32[]{:S(2)}, u32[]{:S(2)}) %collective-permute-start.4) | collective-permute-done | bytes 32800 | tf_op jit(solution)/shard_map/ppermute | solution.py:255
  132.8 5.1 %collective-permute-done.5 = f32[4,16,128]{2,0,1:T(4,128)S(1)} collective-permute-done((f32[4,16,128]{2,0,1:T(4,128)S(1)}, f32[4,16,128]{2,0,1:T(4,128)S(1)}, u32[]{:S(2)}, u32[]{:S(2)}) %collective-permute-start.5) | collective-permute-done | bytes 32800 | tf_op jit(solution)/shard_map/ppermute | solution.py:255
  (47 shorter events, 6.5 us)
Async XLA Ops:
  0.6 13.2 %copy-start = (f32[4,16,128]{2,1,0:T(8,128)S(1)}, f32[4,16,128]{2,1,0:T(8,128)}, u32[]{:S(2)}) copy-start(f32[4,16,128]{2,1,0:T(8,128)} %param.11) | copy-start | bytes 98308
  1.9 10.4 %copy-start.5 = (s32[1,32]{1,0:T(1,128)S(1)}, s32[1,32]{1,0:T(1,128)}, u32[]{:S(2)}) copy-start(s32[1,32]{1,0:T(1,128)} %param.12) | copy-start | bytes 388
  1.9 10.9 %copy-start.1 = (s32[1,64]{1,0:T(1,128)S(1)}, s32[1,64]{1,0:T(1,128)}, u32[]{:S(2)}) copy-start(s32[1,64]{1,0:T(1,128)} %param.13) | copy-start | bytes 772
  6.3 34.2 %collective-permute-start = (f32[301,4,256]{2,1,0:T(4,128)}, f32[301,4,256]{2,1,0:T(4,128)}, u32[]{:S(2)}, u32[]{:S(2)}) collective-permute-start(f32[301,4,256]{2,1,0:T(4,128)} %get-tuple-element.16), channel_id=1, source_target_pairs={{0,124},{4,0},{8,4},{12,8},{16,12},{20,16},{24,20},{28,24},{32,28}... | collective-permute-start | bytes 3698696 | tf_op jit(solution)/shard_map/ppermute | solution.py:25
  12.3 28.2 %collective-permute-start.1 = (f32[301,4,256]{2,1,0:T(4,128)}, f32[301,4,256]{2,1,0:T(4,128)}, u32[]{:S(2)}, u32[]{:S(2)}) collective-permute-start(f32[301,4,256]{2,1,0:T(4,128)} %get-tuple-element.17), channel_id=1, source_target_pairs={{0,4},{4,8},{8,12},{12,16},{16,20},{20,24},{24,28},{28,32},{32,36}... | collective-permute-start | bytes 3698696 | tf_op jit(solution)/shard_map/ppermute | solution.py:26
  12.8 27.7 %copy-start.3 = (f32[4,75,8,256]{3,2,1,0:T(8,128)S(1)}, f32[4,75,8,256]{3,2,1,0:T(8,128)}, u32[]{:S(2)}) copy-start(f32[4,75,8,256]{3,2,1,0:T(8,128)} %param.9) | copy-start | bytes 7372804
  15.3 18.2 %all-to-all-start = ((f32[4,32,2,128]{3,2,0,1:T(2,128)}), f32[4,32,2,128]{3,2,0,1:T(2,128)S(1)}, u32[]{:S(2)}, u32[]{:S(2)}) async-start(f32[4,32,2,128]{3,2,0,1:T(2,128)} %bitcast.37), calls=%async_computation | async-start | bytes 262144 | tf_op jit(solution)/shard_map/all_to_all | solution.py:293
  46.0 8.6 %copy-start.4 = (f32[4,8,256]{2,1,0:T(8,128)S(1)}, f32[4,8,256]{2,1,0:T(8,128)}, u32[]{:S(2)}) copy-start(f32[4,8,256]{2,1,0:T(8,128)} %shard_map.104) | copy-start | bytes 98308
  48.8 6.3 %collective-permute-start.2 = (f32[301,16,4]{0,1,2:T(8,128)S(1)}, f32[301,16,4]{0,1,2:T(8,128)S(1)}, u32[]{:S(2)}, u32[]{:S(2)}) collective-permute-start(f32[301,16,4]{0,1,2:T(8,128)S(1)} %copy.26), channel_id=1, source_target_pairs={{0,3},{1,0},{2,1},{3,2},{4,7},{5,4},{6,5},{7,6},{8,11},{9,8},{10,9... | collective-permute-start | bytes 231176 | tf_op jit(solution)/shard_map/ppermute | solution.py:25
  54.5 5.9 %collective-permute-start.3 = (f32[301,16,4]{0,1,2:T(8,128)S(1)}, f32[301,16,4]{0,1,2:T(8,128)S(1)}, u32[]{:S(2)}, u32[]{:S(2)}) collective-permute-start(f32[301,16,4]{0,1,2:T(8,128)S(1)} %copy.27), channel_id=1, source_target_pairs={{0,1},{1,2},{2,3},{3,0},{4,5},{5,6},{6,7},{7,4},{8,9},{9,10},{10,1... | collective-permute-start | bytes 231176 | tf_op jit(solution)/shard_map/ppermute | solution.py:26
  67.3 3.0 %copy-start.2 = (f32[301,16,384]{2,1,0:T(8,128)}, f32[301,16,384]{2,1,0:T(8,128)S(1)}, u32[]{:S(2)}) copy-start(f32[301,16,384]{2,1,0:T(8,128)S(1)} %pad_maximum_fusion.ext_ref) | copy-start | bytes 22192132
  113.6 11.7 %all-to-all-start.1 = ((f32[4,32,2,128]{3,2,0,1:T(2,128)}), f32[4,32,2,128]{3,2,0,1:T(2,128)S(1)}, u32[]{:S(2)}, u32[]{:S(2)}) async-start(f32[4,32,2,128]{3,2,0,1:T(2,128)} %copy.33), calls=%async_computation.1 | async-start | bytes 262144 | tf_op jit(solution)/shard_map/all_to_all | solution.py:307
  128.4 4.0 %collective-permute-start.4 = (f32[4,16,128]{2,0,1:T(4,128)S(1)}, f32[4,16,128]{2,0,1:T(4,128)S(1)}, u32[]{:S(2)}, u32[]{:S(2)}) collective-permute-start(f32[4,16,128]{2,0,1:T(4,128)S(1)} %scatter_fusion), channel_id=1, source_target_pairs={{0,1},{1,0},{2,3},{3,2},{4,5},{5,4},{6,7},{7,6},{8,9},{9,8},{10,11... | collective-permute-start | bytes 98312 | tf_op jit(solution)/shard_map/ppermute | solution.py:255
  132.4 5.5 %collective-permute-start.5 = (f32[4,16,128]{2,0,1:T(4,128)S(1)}, f32[4,16,128]{2,0,1:T(4,128)S(1)}, u32[]{:S(2)}, u32[]{:S(2)}) collective-permute-start(f32[4,16,128]{2,0,1:T(4,128)S(1)} %add.96), channel_id=1, source_target_pairs={{0,2},{1,3},{2,0},{3,1},{4,6},{5,7},{6,4},{7,5},{8,10},{9,11},{10,... | collective-permute-start | bytes 98312 | tf_op jit(solution)/shard_map/ppermute | solution.py:255

commit v3 on v2

--- a/solution.py
+++ b/solution.py
@@ -188,7 +188,7 @@
     return total
 
 
-def gather_kernel(recv_ref, index_ref, weight_ref, out_ref):
+def gather_kernel(recv_ref, index_ref, weight_ref, after_ref, out_ref):
     stacked, lanes = recv_ref.shape
     fields, rows, cols = out_ref.shape
     segments = stacked // fields
@@ -235,14 +235,15 @@
     out_ref[...] = lax.fori_loop(0, rows, row_step, jnp.zeros((stacked, lanes), jnp.float32))
 
 
-def remap_call(kernel, out_shape, *operands):
+def remap_call(kernel, out_shape, *operands, after=()):
     vmem = pltpu.MemorySpace.VMEM
     return pl.pallas_call(
         kernel,
         out_shape=jax.ShapeDtypeStruct(out_shape, jnp.float32),
-        in_specs=[pl.BlockSpec(memory_space=vmem)] * len(operands),
+        in_specs=[pl.BlockSpec(memory_space=vmem)] * len(operands)
+        + [pl.BlockSpec(memory_space=pl.ANY)] * len(after),
         out_specs=pl.BlockSpec(memory_space=vmem),
-    )(*operands)
+    )(*operands, *after)
 
 
 def sum_over(values, axis):
@@ -296,12 +297,14 @@
     flat_recv = received.reshape(-1, received.shape[-1])
     index_rows = cover_index.reshape(items * rows, cols)
     weight_rows = cover_weight.reshape(items * rows, cols)
-    forcing = remap_call(gather_kernel, (fields, rows, cols), flat_recv, index_rows, weight_rows)
+    land = land_mask.astype(jnp.float32)
+    ext, mask = extended_planes(adjoint_state, land_mask, HALO)
+    forcing = remap_call(
+        gather_kernel, (fields, rows, cols), flat_recv, index_rows, weight_rows, after=(ext,)
+    )
     surface = WIND_GAIN * (forcing[2] * forcing[2] + forcing[3] * forcing[3]) + jax.nn.softplus(
         forcing[1] - forcing[0]
     )
-    land = land_mask.astype(jnp.float32)
-    ext, mask = extended_planes(adjoint_state, land_mask, HALO)
     state_adjoint, flux_back = tridiagonal(ext, mask, adjoint_state.shape, mixing_base, surface, land)
     buffer = remap_call(scatter_kernel, flat_recv.shape, flux_back, index_rows, weight_rows)
     returned = lax.all_to_all(

time: 139 us -> 140 us (level)
  other arithmetic: 16.8 us -> 20.2 us
  local copies, waits for them, and re-layouts: 23.2 us -> 20.2 us
    all_to_all x1, waiting for transfers between devices: 11.3 us -> 0.01 us  [shards(): lax.all_to_all(outgoing, 'lat', split_axis=1, concat_axis=1, tiled=True)]
    ppermute x2, waiting for transfers between devices: 0.01 us -> 5.98 us  [from_neighbours(): lax.ppermute(lax.slice_in_dim(block, 0, width, axis=dim), axis, to_prev)]
    ppermute x2, waiting for transfers between devices: 2.35 us -> 7.6 us  [from_neighbours(): lax.ppermute(lax.slice_in_dim(block, size - width, size, axis=dim), axis,...]
    unnamed x13 -> x9, local copies, waits for them, and re-layouts: 3.6 us -> 0.64 us
    concatenate x1, other arithmetic: 4.13 us -> 5.98 us  [extended_planes(): ext = jnp.concatenate([tall, east, gap, west], axis=2)]
  transfers between devices with their start and end apart: 8 -> 8, of which waited for: 5 -> 6; matrix products, arithmetic and copies ran while one was open for 7% -> 13% of each run, Pallas kernels for 5% -> 0%
where the time goes in v3:
time: 140 us; the launch traced here: 139 us
  Pallas kernels  47.3 us (34%)
  waiting for transfers between devices  30.4 us (22%)
  local copies, waits for them, and re-layouts  20.2 us (14%)
  other arithmetic  20.2 us (14%)
  starting transfers between devices  20 us (14%)
    pallas_call x1, Pallas kernels, tridiagonal(): pl.pallas_call(tridiagonal_kernel, out_shape=(jax.ShapeDtypeStruct(shape,...  34.5 us
    pallas_call x2, Pallas kernels, remap_call(): pl.pallas_call(kernel, out_shape=jax.ShapeDtypeStruct(out_shape, jnp.floa...  12.8 us
    ppermute x2, waiting for transfers between devices, sum_over(): values = values + lax.ppermute(values, axis, pairs)  8.96 us
    ppermute x2, starting transfers between devices, from_neighbours(): lax.ppermute(lax.slice_in_dim(block, 0, width, axis=dim), axis, to_prev)  8.85 us
    all_to_all x1, waiting for transfers between devices, shards(): lax.all_to_all(buffer.reshape(received.shape), 'lat', split_axis=1, conca...  7.82 us
    ppermute x2, waiting for transfers between devices, from_neighbours(): lax.ppermute(lax.slice_in_dim(block, size - width, size, axis=dim), axis,...  7.6 us
    all_to_all x1, starting transfers between devices, shards(): lax.all_to_all(outgoing, 'lat', split_axis=1, concat_axis=1, tiled=True)  6.73 us
    ppermute x2, waiting for transfers between devices, from_neighbours(): lax.ppermute(lax.slice_in_dim(block, 0, width, axis=dim), axis, to_prev)  5.98 us
  transfers between devices with their start and end apart: 8, of which 6 were waited for; matrix products, arithmetic and copies ran while one was open for 13% of the time, Pallas kernels for 0%

profile of v3, /device:TPU:0, one launch (start us, length us, event | category | flops | bytes accessed | tf_op | source)
XLA Modules:
  0.0 139.0 jit_solution(5080286589653878119)
XLA Ops:
  1.9 4.4 %fusion = (f32[301,4,256]{2,1,0:T(4,128)}, f32[301,4,256]{2,1,0:T(4,128)}) fusion(f32[300,8,256]{2,1,0:T(8,128)} %bitcast.39, f32[1,8,256]{2,1,0:T(8,128)S(1)} %get-tuple-element.19), kind=kLoop, calls=%fused_computation.7 | loop fusion | flops 616448 | bytes 4931584 | tf_op jit(solution)/shard_map/concatenate | solution.py:34
  6.4 6.0 %collective-permute-start = (f32[301,4,256]{2,1,0:T(4,128)}, f32[301,4,256]{2,1,0:T(4,128)}, u32[]{:S(2)}, u32[]{:S(2)}) collective-permute-start(f32[301,4,256]{2,1,0:T(4,128)} %get-tuple-element.16), channel_id=1, source_target_pairs={{0,124},{4,0},{8,4},{12,8},{16,12},{20,16},{24,20},{28,24},{32,28}... | collective-permute-start | bytes 3698696 | tf_op jit(solution)/shard_map/ppermute | solution.py:25
  15.4 6.7 %all-to-all-start = ((f32[4,32,2,128]{3,2,0,1:T(2,128)}), f32[4,32,2,128]{3,2,0,1:T(2,128)S(1)}, u32[]{:S(2)}, u32[]{:S(2)}) async-start(f32[4,32,2,128]{3,2,0,1:T(2,128)} %bitcast.37), calls=%async_computation | async-start | bytes 262144 | tf_op jit(solution)/shard_map/all_to_all | solution.py:294
  22.3 6.0 %collective-permute-done = f32[301,4,256]{2,1,0:T(4,128)} collective-permute-done((f32[301,4,256]{2,1,0:T(4,128)}, f32[301,4,256]{2,1,0:T(4,128)}, u32[]{:S(2)}, u32[]{:S(2)}) %collective-permute-start) | collective-permute-done | bytes 1232928 | tf_op jit(solution)/shard_map/ppermute | solution.py:25
  28.3 5.3 %collective-permute-done.1 = f32[301,4,256]{2,1,0:T(4,128)} collective-permute-done((f32[301,4,256]{2,1,0:T(4,128)}, f32[301,4,256]{2,1,0:T(4,128)}, u32[]{:S(2)}, u32[]{:S(2)}) %collective-permute-start.1) | collective-permute-done | bytes 1232928 | tf_op jit(solution)/shard_map/ppermute | solution.py:26
  33.6 2.4 %pad_maximum_fusion.1 = f32[301,16,256]{2,1,0:T(8,128)S(1)} fusion(f32[301,4,256]{2,1,0:T(4,128)} %collective-permute-done.1, f32[301,4,256]{2,1,0:T(4,128)} %collective-permute-done, f32[1,8,256]{2,1,0:T(8,128)S(1)} %get-tuple-element.19, f32[300,8,256]{2,1,0:T(8,128)S(1)} %bitcast.40), kind=kLoop, calls=%fused_computation.4 | loop fusion | flops 3698688 | bytes 9863168 | tf_op jit(solution)/shard_map/concatenate | solution.py:36
  36.0 3.1 %fusion.7 = (f32[301,16,4]{2,1,0:T(8,128)}, f32[301,16,4]{2,1,0:T(8,128)}) fusion(f32[301,16,256]{2,1,0:T(8,128)S(1)} %pad_maximum_fusion.1), kind=kLoop, calls=%fused_computation.31 | loop fusion | bytes 308224 | tf_op jit(solution)/shard_map/slice | solution.py:25
  39.0 2.8 %copy.26 = f32[301,16,4]{0,1,2:T(8,128)S(1)} copy(f32[301,16,4]{2,1,0:T(8,128)} %get-tuple-element.14) | data formatting | bytes 154112 | tf_op jit(solution)/shard_map/slice | solution.py:25
  41.9 2.8 %collective-permute-start.2 = (f32[301,16,4]{0,1,2:T(8,128)S(1)}, f32[301,16,4]{0,1,2:T(8,128)S(1)}, u32[]{:S(2)}, u32[]{:S(2)}) collective-permute-start(f32[301,16,4]{0,1,2:T(8,128)S(1)} %copy.26), channel_id=1, source_target_pairs={{0,3},{1,0},{2,1},{3,2},{4,7},{5,4},{6,5},{7,6},{8,11},{9,8},{10,9... | collective-permute-start | bytes 231176 | tf_op jit(solution)/shard_map/ppermute | solution.py:25
  44.7 2.8 %copy.27 = f32[301,16,4]{0,1,2:T(8,128)S(1)} copy(f32[301,16,4]{2,1,0:T(8,128)} %get-tuple-element.15) | data formatting | bytes 154112 | tf_op jit(solution)/shard_map/slice | solution.py:26
  48.3 2.8 %copy.28 = f32[301,16,4]{2,1,0:T(8,128)} copy(f32[301,16,4]{0,1,2:T(8,128)S(1)} %collective-permute-done.2) | data formatting | bytes 154112 | tf_op jit(solution)/shard_map/ppermute | solution.py:25
  51.1 2.3 %collective-permute-done.3 = f32[301,16,4]{0,1,2:T(8,128)S(1)} collective-permute-done((f32[301,16,4]{0,1,2:T(8,128)S(1)}, f32[301,16,4]{0,1,2:T(8,128)S(1)}, u32[]{:S(2)}, u32[]{:S(2)}) %collective-permute-start.3) | collective-permute-done | bytes 77088 | tf_op jit(solution)/shard_map/ppermute | solution.py:26
  53.4 2.9 %copy.29 = f32[301,16,4]{2,1,0:T(8,128)} copy(f32[301,16,4]{0,1,2:T(8,128)S(1)} %collective-permute-done.3) | data formatting | bytes 154112 | tf_op jit(solution)/shard_map/ppermute | solution.py:26
  56.3 6.0 %pad_maximum_fusion.after_ref.ext_ref = f32[301,16,384]{2,1,0:T(8,128)} fusion(f32[301,16,4]{2,1,0:T(8,128)} %copy.29, f32[301,16,4]{2,1,0:T(8,128)} %copy.28, f32[301,4,256]{2,1,0:T(4,128)} %collective-permute-done.1, f32[301,4,256]{2,1,0:T(4,128)} %collective-permute-done, f32[1,8,256]{2,1,0:T(8,128)S(1)} %get-tuple-element.19, ...), kind=kLoop, calls=%fused_computation.3 | loop fusion | flops 11096064 | bytes 12484608 | tf_op jit(solution)/shard_map/concatenate | solution.py:40
  62.3 6.3 %shard_map.104 = f32[4,8,256]{2,1,0:T(8,128)} custom-call(f32[256,128]{1,0:T(8,128)} %bitcast.42, s32[32,256]{1,0:T(8,128)} %bitcast.46, f32[32,256]{1,0:T(8,128)} %bitcast.48, f32[301,16,384]{2,1,0:T(8,128)} %pad_maximum_fusion.after_ref.ext_ref), custom_call_target="tpu_custom_call" | custom-call | tf_op jit(solution)/shard_map/pallas_call | solution.py:240
  69.9 1.4 %fusion.1.mask_ref = f32[16,384]{1,0:T(8,128)} fusion(f32[301,16,384]{2,1,0:T(8,128)} %pad_maximum_fusion.after_ref.ext_ref, pred[16]{0:T(512)(128)(4,1)S(1)} %and_or_fusion), kind=kLoop, calls=%fused_computation.14 | loop fusion | flops 6144 | bytes 49168 | tf_op jit(solution)/shard_map/jit(_where)/select_n | solution.py:48
  71.3 34.5 %shard_map.105 = (f32[4,75,8,256]{3,2,1,0:T(8,128)}, f32[4,8,256]{2,1,0:T(8,128)}) custom-call(f32[75]{0:T(128)} %constant.9.clone.decay_ref, f32[301,16,384]{2,1,0:T(8,128)} %pad_maximum_fusion.after_ref.ext_ref, f32[16,384]{1,0:T(8,128)} %fusion.1.mask_ref, f32[74,8,256]{2,1,0:T(8,128)} %base_ref.1, f32[8,256]{1,0:T(8,128)} %fusion.2.surf_ref, ...), custom_call_target="tpu_custom_call" | custom-call | tf_op jit(solution)/shard_map/pallas_call | solution.py:158
  105.8 6.6 %shard_map.106 = f32[256,128]{1,0:T(8,128)} custom-call(f32[4,8,256]{2,1,0:T(8,128)} %get-tuple-element.5.back_ref, s32[32,256]{1,0:T(8,128)} %bitcast.47, f32[32,256]{1,0:T(8,128)} %bitcast.49), custom_call_target="tpu_custom_call" | custom-call | tf_op jit(solution)/shard_map/pallas_call | solution.py:240
  112.4 1.6 %copy.33 = f32[4,32,2,128]{3,2,0,1:T(2,128)} copy(f32[4,32,2,128]{3,2,1,0:T(2,128)} %bitcast.44) | data formatting | bytes 262144 | tf_op jit(solution)/shard_map/reshape | solution.py:311
  114.0 3.9 %all-to-all-start.1 = ((f32[4,32,2,128]{3,2,0,1:T(2,128)}), f32[4,32,2,128]{3,2,0,1:T(2,128)S(1)}, u32[]{:S(2)}, u32[]{:S(2)}) async-start(f32[4,32,2,128]{3,2,0,1:T(2,128)} %copy.33), calls=%async_computation.1 | async-start | bytes 262144 | tf_op jit(solution)/shard_map/all_to_all | solution.py:310
  117.9 7.8 %all-to-all-done.1 = f32[4,32,2,128]{3,2,0,1:T(2,128)S(1)} async-done(((f32[4,32,2,128]{3,2,0,1:T(2,128)}), f32[4,32,2,128]{3,2,0,1:T(2,128)S(1)}, u32[]{:S(2)}, u32[]{:S(2)}) %all-to-all-start.1) | async-done | bytes 131104 | tf_op jit(solution)/shard_map/all_to_all | solution.py:310
  126.0 2.8 %scatter_fusion = f32[4,16,128]{2,0,1:T(4,128)S(1)} fusion(f32[4,16,128]{2,0,1:T(4,128)S(1)} %broadcast_in_dim.35, s32[64]{0:T(128)S(1)} %fusion.6, f32[64,4,128]{2,1,0:T(4,128)S(1)} %copy.35), kind=kCustom, calls=%fused_computation.2 | custom fusion | flops 32768 | bytes 393472 | tf_op jit(solution)/shard_map/scatter-add | solution.py:314
  128.9 3.9 %collective-permute-done.4 = f32[4,16,128]{2,0,1:T(4,128)S(1)} collective-permute-done((f32[4,16,128]{2,0,1:T(4,128)S(1)}, f32[4,16,128]{2,0,1:T(4,128)S(1)}, u32[]{:S(2)}, u32[]{:S(2)}) %collective-permute-start.4) | collective-permute-done | bytes 32800 | tf_op jit(solution)/shard_map/ppermute | solution.py:256
  133.3 5.1 %collective-permute-done.5 = f32[4,16,128]{2,0,1:T(4,128)S(1)} collective-permute-done((f32[4,16,128]{2,0,1:T(4,128)S(1)}, f32[4,16,128]{2,0,1:T(4,128)S(1)}, u32[]{:S(2)}, u32[]{:S(2)}) %collective-permute-start.5) | collective-permute-done | bytes 32800 | tf_op jit(solution)/shard_map/ppermute | solution.py:256
  (43 shorter events, 7.9 us)
Async XLA Ops:
  0.6 13.3 %copy-start = (f32[4,16,128]{2,1,0:T(8,128)S(1)}, f32[4,16,128]{2,1,0:T(8,128)}, u32[]{:S(2)}) copy-start(f32[4,16,128]{2,1,0:T(8,128)} %param.11) | copy-start | bytes 98308
  1.9 10.5 %copy-start.3 = (s32[1,32]{1,0:T(1,128)S(1)}, s32[1,32]{1,0:T(1,128)}, u32[]{:S(2)}) copy-start(s32[1,32]{1,0:T(1,128)} %param.12) | copy-start | bytes 388
  1.9 10.9 %copy-start.1 = (s32[1,64]{1,0:T(1,128)S(1)}, s32[1,64]{1,0:T(1,128)}, u32[]{:S(2)}) copy-start(s32[1,64]{1,0:T(1,128)} %param.13) | copy-start | bytes 772
  6.4 21.9 %collective-permute-start = (f32[301,4,256]{2,1,0:T(4,128)}, f32[301,4,256]{2,1,0:T(4,128)}, u32[]{:S(2)}, u32[]{:S(2)}) collective-permute-start(f32[301,4,256]{2,1,0:T(4,128)} %get-tuple-element.16), channel_id=1, source_target_pairs={{0,124},{4,0},{8,4},{12,8},{16,12},{20,16},{24,20},{28,24},{32,28}... | collective-permute-start | bytes 3698696 | tf_op jit(solution)/shard_map/ppermute | solution.py:25
  12.4 21.2 %collective-permute-start.1 = (f32[301,4,256]{2,1,0:T(4,128)}, f32[301,4,256]{2,1,0:T(4,128)}, u32[]{:S(2)}, u32[]{:S(2)}) collective-permute-start(f32[301,4,256]{2,1,0:T(4,128)} %get-tuple-element.17), channel_id=1, source_target_pairs={{0,4},{4,8},{8,12},{12,16},{16,20},{20,24},{24,28},{28,32},{32,36}... | collective-permute-start | bytes 3698696 | tf_op jit(solution)/shard_map/ppermute | solution.py:26
  12.9 20.7 %copy-start.2 = (f32[4,75,8,256]{3,2,1,0:T(8,128)S(1)}, f32[4,75,8,256]{3,2,1,0:T(8,128)}, u32[]{:S(2)}) copy-start(f32[4,75,8,256]{3,2,1,0:T(8,128)} %param.9) | copy-start | bytes 7372804
  15.4 32.2 %all-to-all-start = ((f32[4,32,2,128]{3,2,0,1:T(2,128)}), f32[4,32,2,128]{3,2,0,1:T(2,128)S(1)}, u32[]{:S(2)}, u32[]{:S(2)}) async-start(f32[4,32,2,128]{3,2,0,1:T(2,128)} %bitcast.37), calls=%async_computation | async-start | bytes 262144 | tf_op jit(solution)/shard_map/all_to_all | solution.py:294
  41.9 6.5 %collective-permute-start.2 = (f32[301,16,4]{0,1,2:T(8,128)S(1)}, f32[301,16,4]{0,1,2:T(8,128)S(1)}, u32[]{:S(2)}, u32[]{:S(2)}) collective-permute-start(f32[301,16,4]{0,1,2:T(8,128)S(1)} %copy.26), channel_id=1, source_target_pairs={{0,3},{1,0},{2,1},{3,2},{4,7},{5,4},{6,5},{7,6},{8,11},{9,8},{10,9... | collective-permute-start | bytes 231176 | tf_op jit(solution)/shard_map/ppermute | solution.py:25
  47.5 5.9 %collective-permute-start.3 = (f32[301,16,4]{0,1,2:T(8,128)S(1)}, f32[301,16,4]{0,1,2:T(8,128)S(1)}, u32[]{:S(2)}, u32[]{:S(2)}) collective-permute-start(f32[301,16,4]{0,1,2:T(8,128)S(1)} %copy.27), channel_id=1, source_target_pairs={{0,1},{1,2},{2,3},{3,0},{4,5},{5,6},{6,7},{7,4},{8,9},{9,10},{10,1... | collective-permute-start | bytes 231176 | tf_op jit(solution)/shard_map/ppermute | solution.py:26
  114.0 11.7 %all-to-all-start.1 = ((f32[4,32,2,128]{3,2,0,1:T(2,128)}), f32[4,32,2,128]{3,2,0,1:T(2,128)S(1)}, u32[]{:S(2)}, u32[]{:S(2)}) async-start(f32[4,32,2,128]{3,2,0,1:T(2,128)} %copy.33), calls=%async_computation.1 | async-start | bytes 262144 | tf_op jit(solution)/shard_map/all_to_all | solution.py:310
  128.8 4.0 %collective-permute-start.4 = (f32[4,16,128]{2,0,1:T(4,128)S(1)}, f32[4,16,128]{2,0,1:T(4,128)S(1)}, u32[]{:S(2)}, u32[]{:S(2)}) collective-permute-start(f32[4,16,128]{2,0,1:T(4,128)S(1)} %scatter_fusion), channel_id=1, source_target_pairs={{0,1},{1,0},{2,3},{3,2},{4,5},{5,4},{6,7},{7,6},{8,9},{9,8},{10,11... | collective-permute-start | bytes 98312 | tf_op jit(solution)/shard_map/ppermute | solution.py:256
  132.9 5.5 %collective-permute-start.5 = (f32[4,16,128]{2,0,1:T(4,128)S(1)}, f32[4,16,128]{2,0,1:T(4,128)S(1)}, u32[]{:S(2)}, u32[]{:S(2)}) collective-permute-start(f32[4,16,128]{2,0,1:T(4,128)S(1)} %add.96), channel_id=1, source_target_pairs={{0,2},{1,3},{2,0},{3,1},{4,6},{5,7},{6,4},{7,5},{8,10},{9,11},{10,... | collective-permute-start | bytes 98312 | tf_op jit(solution)/shard_map/ppermute | solution.py:256

commit v4 on v3

--- a/solution.py
+++ b/solution.py
@@ -33,11 +33,18 @@
     coast = land_mask.astype(jnp.float32)[None]
     stack = jnp.concatenate([planes, coast], axis=0)
     south, north = from_neighbours(stack, "lat", 1, width)
-    tall = jnp.concatenate([stack, south, north], axis=1)
-    east, west = from_neighbours(tall, "lon", 2, width)
+    east, west = from_neighbours(stack, "lon", 2, width)
+    sides = jnp.concatenate([east, west], axis=2)
+    corner_south, corner_north = from_neighbours(sides, "lat", 1, width)
     wide = -(-(cols + 2 * width) // 128) * 128
-    gap = jnp.zeros(tall.shape[:2] + (wide - cols - 2 * width,), jnp.float32)
-    ext = jnp.concatenate([tall, east, gap, west], axis=2)
+
+    def band(middle, edges):
+        gap = jnp.zeros(middle.shape[:2] + (wide - cols - 2 * width,), jnp.float32)
+        return jnp.concatenate([middle, edges[:, :, :width], gap, edges[:, :, width:]], axis=2)
+
+    ext = jnp.concatenate(
+        [band(stack, sides), band(south, corner_south), band(north, corner_north)], axis=1
+    )
     lat_count = lax.axis_size("lat")
     where_lat = lax.axis_index("lat")
     row = lax.broadcasted_iota(jnp.int32, ext.shape[1:], 0)
@@ -79,18 +86,17 @@
     rows, cols = out_ref.shape[2], out_ref.shape[3]
     tall, wide = mask_ref.shape
     marks = mask_ref[...]
-    marks_ref[0] = marks
-    marks_ref[1] = pltpu.roll(marks, 1, 0)
-    marks_ref[2] = pltpu.roll(marks, tall - 1, 0)
-    marks_ref[3] = pltpu.roll(marks, 1, 1)
-    marks_ref[4] = pltpu.roll(marks, wide - 1, 1)
+    marks_ref[0] = marks * pltpu.roll(marks, 1, 0)
+    marks_ref[1] = marks * pltpu.roll(marks, tall - 1, 0)
+    marks_ref[2] = marks * pltpu.roll(marks, 1, 1)
+    marks_ref[3] = marks * pltpu.roll(marks, wide - 1, 1)
 
     def laplace_ext(values):
-        north = marks_ref[1] * (pltpu.roll(values, 1, 0) - values)
-        south = marks_ref[2] * (pltpu.roll(values, tall - 1, 0) - values)
-        west = marks_ref[3] * (pltpu.roll(values, 1, 1) - values)
-        east = marks_ref[4] * (pltpu.roll(values, wide - 1, 1) - values)
-        return marks_ref[0] * (((north + south) + west) + east)
+        north = marks_ref[0] * (pltpu.roll(values, 1, 0) - values)
+        south = marks_ref[1] * (pltpu.roll(values, tall - 1, 0) - values)
+        west = marks_ref[2] * (pltpu.roll(values, 1, 1) - values)
+        east = marks_ref[3] * (pltpu.roll(values, wide - 1, 1) - values)
+        return ((north + south) + west) + east
 
     def smoothed(f, level):
         values = ext_ref[f * levels + level]
@@ -166,7 +172,7 @@
         out_specs=(pl.BlockSpec(memory_space=vmem), pl.BlockSpec(memory_space=vmem)),
         scratch_shapes=[
             pltpu.VMEM((len(set(FIELD_MIX)), levels) + shape[2:], jnp.float32),
-            pltpu.VMEM((5,) + mask.shape, jnp.float32),
+            pltpu.VMEM((4,) + mask.shape, jnp.float32),
         ],
     )(jnp.asarray(decay_table), ext, mask, mixing_base, surface, land)
 

time: 140 us -> 130 us (0.929)
  waiting for transfers between devices: 30.4 us -> 16.7 us
  starting transfers between devices: 20 us -> 27.7 us
  local copies, waits for them, and re-layouts: 20.2 us -> 16.5 us
  other arithmetic: 20.2 us -> 21.9 us
    ppermute x2 -> x3, waiting for transfers between devices: 5.98 us -> 0.01 us  [from_neighbours(): lax.ppermute(lax.slice_in_dim(block, 0, width, axis=dim), axis, to_prev)]
    ppermute x2 -> x3, waiting for transfers between devices: 7.6 us -> 2.4 us  [from_neighbours(): lax.ppermute(lax.slice_in_dim(block, size - width, size, axis=dim), axis,...]
    ppermute x2 -> x3, starting transfers between devices: 8.85 us -> 13.6 us  [from_neighbours(): lax.ppermute(lax.slice_in_dim(block, 0, width, axis=dim), axis, to_prev)]
    slice x2 -> x1, local copies, waits for them, and re-layouts: 5.9 us -> 1.92 us  [from_neighbours(): lax.slice_in_dim(block, 0, width, axis=dim)]
    slice x0 -> x6, local copies, waits for them, and re-layouts: none -> 3.81 us  [the longest x2 2.3 us: band(): edges[:, :, width:]]
    ppermute x2, starting transfers between devices: 0.52 us -> 3 us  [sum_over(): values = values + lax.ppermute(values, axis, pairs)]
    ppermute x2, waiting for transfers between devices: 8.96 us -> 6.5 us  [sum_over(): values = values + lax.ppermute(values, axis, pairs)]
    ppermute x1 -> x2, local copies, waits for them, and re-layouts: 2.9 us -> 1.57 us  [from_neighbours(): lax.ppermute(lax.slice_in_dim(block, size - width, size, axis=dim), axis,...]
  transfers between devices with their start and end apart: 8 -> 10, of which waited for: 6 -> 4; matrix products, arithmetic and copies ran while one was open for 13% -> 11% of each run, Pallas kernels for 0% -> 0%
where the time goes in v4:
time: 130 us
  Pallas kernels  46 us (35%)
  starting transfers between devices  27.7 us (21%)
  other arithmetic  21.9 us (17%)
  waiting for transfers between devices  16.7 us (13%)
  local copies, waits for them, and re-layouts  16.5 us (13%)
    pallas_call x1, Pallas kernels, tridiagonal(): pl.pallas_call(tridiagonal_kernel, out_shape=(jax.ShapeDtypeStruct(shape,...  33.1 us
    ppermute x3, starting transfers between devices, from_neighbours(): lax.ppermute(lax.slice_in_dim(block, 0, width, axis=dim), axis, to_prev)  13.6 us
    pallas_call x2, Pallas kernels, remap_call(): pl.pallas_call(kernel, out_shape=jax.ShapeDtypeStruct(out_shape, jnp.floa...  12.9 us
    concatenate x1, other arithmetic, extended_planes(): jnp.concatenate([band(stack, sides), band(south, corner_south), band(nort...  9.1 us
    all_to_all x1, waiting for transfers between devices, shards(): lax.all_to_all(buffer.reshape(received.shape), 'lat', split_axis=1, conca...  7.82 us
    all_to_all x1, starting transfers between devices, shards(): lax.all_to_all(outgoing, 'lat', split_axis=1, concat_axis=1, tiled=True)  6.73 us
    ppermute x2, waiting for transfers between devices, sum_over(): values = values + lax.ppermute(values, axis, pairs)  6.5 us
    concatenate x2, other arithmetic, extended_planes(): stack = jnp.concatenate([planes, coast], axis=0)  5.34 us
  transfers between devices with their start and end apart: 10, of which 4 were waited for; matrix products, arithmetic and copies ran while one was open for 11% of the time, Pallas kernels for 0%

profile of v4, /device:TPU:0, one launch (start us, length us, event | category | flops | bytes accessed | tf_op | source)
XLA Modules:
  0.0 129.6 jit_solution(13322147158171031833)
XLA Ops:
  1.9 3.5 %fusion.1 = (f32[301,8,4]{2,1,0:T(8,128)}, f32[301,8,4]{2,1,0:T(8,128)}) fusion(f32[300,8,256]{2,1,0:T(8,128)} %bitcast.39, f32[1,8,256]{2,1,0:T(8,128)S(1)} %get-tuple-element.25), kind=kLoop, calls=%fused_computation.11 | loop fusion | flops 19264 | bytes 2542848 | tf_op jit(solution)/shard_map/concatenate | solution.py:34
  5.4 1.9 %copy.32 = f32[301,8,4]{0,1,2:T(8,128)S(1)} copy(f32[301,8,4]{2,1,0:T(8,128)} %get-tuple-element.16) | data formatting | bytes 77056 | tf_op jit(solution)/shard_map/slice | solution.py:25
  7.4 2.9 %collective-permute-start = (f32[301,8,4]{0,1,2:T(8,128)S(1)}, f32[301,8,4]{0,1,2:T(8,128)S(1)}, u32[]{:S(2)}, u32[]{:S(2)}) collective-permute-start(f32[301,8,4]{0,1,2:T(8,128)S(1)} %copy.32), channel_id=1, source_target_pairs={{0,3},{1,0},{2,1},{3,2},{4,7},{5,4},{6,5},{7,6},{8,11},{9,8},{10,9... | collective-permute-start | bytes 115592 | tf_op jit(solution)/shard_map/ppermute | solution.py:25
  10.3 1.8 %copy.33 = f32[301,8,4]{0,1,2:T(8,128)S(1)} copy(f32[301,8,4]{2,1,0:T(8,128)} %get-tuple-element.17) | data formatting | bytes 77056 | tf_op jit(solution)/shard_map/slice | solution.py:26
  12.2 1.8 %fusion = (f32[301,4,256]{2,1,0:T(4,128)}, f32[301,4,256]{2,1,0:T(4,128)}) fusion(f32[300,8,256]{2,1,0:T(8,128)S(1)} %bitcast.40, f32[1,8,256]{2,1,0:T(8,128)S(1)} %get-tuple-element.25), kind=kLoop, calls=%fused_computation.10 | loop fusion | flops 616448 | bytes 4931584 | tf_op jit(solution)/shard_map/concatenate | solution.py:34
  14.0 5.6 %collective-permute-start.2 = (f32[301,4,256]{2,1,0:T(4,128)}, f32[301,4,256]{2,1,0:T(4,128)}, u32[]{:S(2)}, u32[]{:S(2)}) collective-permute-start(f32[301,4,256]{2,1,0:T(4,128)} %get-tuple-element.14), channel_id=1, source_target_pairs={{0,124},{4,0},{8,4},{12,8},{16,12},{20,16},{24,20},{28,24},{32,28}... | collective-permute-start | bytes 3698696 | tf_op jit(solution)/shard_map/ppermute | solution.py:25
  22.6 6.7 %all-to-all-start = ((f32[4,32,2,128]{3,2,0,1:T(2,128)}), f32[4,32,2,128]{3,2,0,1:T(2,128)S(1)}, u32[]{:S(2)}, u32[]{:S(2)}) async-start(f32[4,32,2,128]{3,2,0,1:T(2,128)} %bitcast.37), calls=%async_computation | async-start | bytes 262144 | tf_op jit(solution)/shard_map/all_to_all | solution.py:300
  29.5 5.0 %collective-permute-start.3 = (f32[301,4,8]{0,2,1:T(8,128)S(1)}, f32[301,4,8]{0,2,1:T(8,128)S(1)}, u32[]{:S(2)}, u32[]{:S(2)}) collective-permute-start(f32[301,4,8]{0,2,1:T(8,128)S(1)} %get-tuple-element.18), channel_id=1, source_target_pairs={{0,124},{4,0},{8,4},{12,8},{16,12},{20,16},{24,20},{28,24},{32,28}... | collective-permute-start | bytes 115592 | tf_op jit(solution)/shard_map/ppermute | solution.py:25
  34.6 1.6 %copy.34 = f32[301,8,4]{2,1,0:T(8,128)} copy(f32[301,8,4]{0,1,2:T(8,128)S(1)} %collective-permute-done) | data formatting | bytes 77056 | tf_op jit(solution)/shard_map/ppermute | solution.py:25
  36.2 1.6 %copy.35 = f32[301,8,4]{2,1,0:T(8,128)} copy(f32[301,8,4]{0,1,2:T(8,128)S(1)} %collective-permute-done.1) | data formatting | bytes 77056 | tf_op jit(solution)/shard_map/ppermute | solution.py:26
  39.2 2.4 %collective-permute-done.5 = f32[301,4,8]{0,2,1:T(8,128)S(1)} collective-permute-done((f32[301,4,8]{0,2,1:T(8,128)S(1)}, f32[301,4,8]{0,2,1:T(8,128)S(1)}, u32[]{:S(2)}, u32[]{:S(2)}) %collective-permute-start.5) | collective-permute-done | bytes 38560 | tf_op jit(solution)/shard_map/ppermute | solution.py:26
  44.7 9.1 %maximum_maximum_fusion.after_ref.ext_ref = f32[301,16,384]{2,1,0:T(8,128)} fusion(f32[301,4,4]{2,1,0:T(4,128)} %copy.41, f32[301,4,120]{2,1,0:T(4,128)S(1)} %broadcast.108, f32[301,4,4]{2,1,0:T(4,128)} %copy.40, f32[301,4,256]{2,1,0:T(4,128)} %collective-permute-done.4, f32[301,4,4]{2,1,0:T(4,128)} %copy.39, f32[301,4,4]{2,1,0:T(4,128)S(1)} %copy.38, ...), kind=kLoop, calls=%fused_computation.3 | loop fusion | flops 22192128 | bytes 13085568 | tf_op jit(solution)/shard_map/concatenate | solution.py:45
  53.8 6.3 %shard_map.104 = f32[4,8,256]{2,1,0:T(8,128)} custom-call(f32[256,128]{1,0:T(8,128)} %bitcast.42, s32[32,256]{1,0:T(8,128)} %bitcast.46, f32[32,256]{1,0:T(8,128)} %bitcast.48, f32[301,16,384]{2,1,0:T(8,128)} %maximum_maximum_fusion.after_ref.ext_ref), custom_call_target="tpu_custom_call" | custom-call | tf_op jit(solution)/shard_map/pallas_call | solution.py:246
  60.1 1.4 %fusion.5.surf_ref = f32[8,256]{1,0:T(8,128)} fusion(f32[4,8,256]{2,1,0:T(8,128)} %shard_map.104), kind=kLoop, calls=%fused_computation.26 | loop fusion | flops 22528 | bytes 40960 | tf_op jit(solution)/shard_map/add | solution.py:311
  61.5 1.4 %fusion.4.mask_ref = f32[16,384]{1,0:T(8,128)} fusion(f32[301,16,384]{2,1,0:T(8,128)} %maximum_maximum_fusion.after_ref.ext_ref, pred[16]{0:T(512)(128)(4,1)S(1)} %and_or_fusion), kind=kLoop, calls=%fused_computation.23 | loop fusion | flops 6144 | bytes 49168 | tf_op jit(solution)/shard_map/jit(_where)/select_n | solution.py:55
  62.9 33.1 %shard_map.105 = (f32[4,75,8,256]{3,2,1,0:T(8,128)}, f32[4,8,256]{2,1,0:T(8,128)}) custom-call(f32[75]{0:T(128)} %constant.8.clone.decay_ref, f32[301,16,384]{2,1,0:T(8,128)} %maximum_maximum_fusion.after_ref.ext_ref, f32[16,384]{1,0:T(8,128)} %fusion.4.mask_ref, f32[74,8,256]{2,1,0:T(8,128)} %base_ref.1, f32[8,256]{1,0:T(8,128)} %fusion.5.surf_ref, ...), custom_call_target="tpu_custom_call" | custom-call | tf_op jit(solution)/shard_map/pallas_call | solution.py:164
  96.0 6.6 %shard_map.106 = f32[256,128]{1,0:T(8,128)} custom-call(f32[4,8,256]{2,1,0:T(8,128)} %get-tuple-element.5.back_ref, s32[32,256]{1,0:T(8,128)} %bitcast.47, f32[32,256]{1,0:T(8,128)} %bitcast.49), custom_call_target="tpu_custom_call" | custom-call | tf_op jit(solution)/shard_map/pallas_call | solution.py:246
  102.6 1.6 %copy.45 = f32[4,32,2,128]{3,2,0,1:T(2,128)} copy(f32[4,32,2,128]{3,2,1,0:T(2,128)} %bitcast.44) | data formatting | bytes 262144 | tf_op jit(solution)/shard_map/reshape | solution.py:317
  104.2 4.3 %all-to-all-start.1 = ((f32[4,32,2,128]{3,2,0,1:T(2,128)}), f32[4,32,2,128]{3,2,0,1:T(2,128)S(1)}, u32[]{:S(2)}, u32[]{:S(2)}) async-start(f32[4,32,2,128]{3,2,0,1:T(2,128)} %copy.45), calls=%async_computation.1 | async-start | bytes 262144 | tf_op jit(solution)/shard_map/all_to_all | solution.py:316
  108.5 7.8 %all-to-all-done.1 = f32[4,32,2,128]{3,2,0,1:T(2,128)S(1)} async-done(((f32[4,32,2,128]{3,2,0,1:T(2,128)}), f32[4,32,2,128]{3,2,0,1:T(2,128)S(1)}, u32[]{:S(2)}, u32[]{:S(2)}) %all-to-all-start.1) | async-done | bytes 131104 | tf_op jit(solution)/shard_map/all_to_all | solution.py:316
  116.6 2.8 %scatter_fusion = f32[4,16,128]{2,0,1:T(4,128)S(1)} fusion(f32[4,16,128]{2,0,1:T(4,128)S(1)} %broadcast_in_dim.35, s32[64]{0:T(128)S(1)} %fusion.9, f32[64,4,128]{2,1,0:T(4,128)S(1)} %copy.47), kind=kCustom, calls=%fused_computation.2 | custom fusion | flops 32768 | bytes 393472 | tf_op jit(solution)/shard_map/scatter-add | solution.py:320
  120.0 3.5 %collective-permute-done.6 = f32[4,16,128]{2,0,1:T(4,128)S(1)} collective-permute-done((f32[4,16,128]{2,0,1:T(4,128)S(1)}, f32[4,16,128]{2,0,1:T(4,128)S(1)}, u32[]{:S(2)}, u32[]{:S(2)}) %collective-permute-start.6) | collective-permute-done | bytes 32800 | tf_op jit(solution)/shard_map/ppermute | solution.py:262
  123.5 2.5 %collective-permute-start.7 = (f32[4,16,128]{2,0,1:T(4,128)S(1)}, f32[4,16,128]{2,0,1:T(4,128)S(1)}, u32[]{:S(2)}, u32[]{:S(2)}) collective-permute-start(f32[4,16,128]{2,0,1:T(4,128)S(1)} %add.96), channel_id=1, source_target_pairs={{0,2},{1,3},{2,0},{3,1},{4,6},{5,7},{6,4},{7,5},{8,10},{9,11},{10,... | collective-permute-start | bytes 98312 | tf_op jit(solution)/shard_map/ppermute | solution.py:262
  125.9 3.0 %collective-permute-done.7 = f32[4,16,128]{2,0,1:T(4,128)S(1)} collective-permute-done((f32[4,16,128]{2,0,1:T(4,128)S(1)}, f32[4,16,128]{2,0,1:T(4,128)S(1)}, u32[]{:S(2)}, u32[]{:S(2)}) %collective-permute-start.7) | collective-permute-done | bytes 32800 | tf_op jit(solution)/shard_map/ppermute | solution.py:262
  (56 shorter events, 10.6 us)
Async XLA Ops:
  0.6 20.5 %copy-start = (f32[4,16,128]{2,1,0:T(8,128)S(1)}, f32[4,16,128]{2,1,0:T(8,128)}, u32[]{:S(2)}) copy-start(f32[4,16,128]{2,1,0:T(8,128)} %param.11) | copy-start | bytes 98308
  5.4 6.7 %copy-start.2 = (f32[4,75,8,256]{3,2,1,0:T(8,128)S(1)}, f32[4,75,8,256]{3,2,1,0:T(8,128)}, u32[]{:S(2)}) copy-start(f32[4,75,8,256]{3,2,1,0:T(8,128)} %param.9) | copy-start | bytes 7372804
  7.4 22.0 %collective-permute-start = (f32[301,8,4]{0,1,2:T(8,128)S(1)}, f32[301,8,4]{0,1,2:T(8,128)S(1)}, u32[]{:S(2)}, u32[]{:S(2)}) collective-permute-start(f32[301,8,4]{0,1,2:T(8,128)S(1)} %copy.32), channel_id=1, source_target_pairs={{0,3},{1,0},{2,1},{3,2},{4,7},{5,4},{6,5},{7,6},{8,11},{9,8},{10,9... | collective-permute-start | bytes 115592 | tf_op jit(solution)/shard_map/ppermute | solution.py:25
  12.1 7.6 %copy-start.3 = (s32[1,32]{1,0:T(1,128)S(1)}, s32[1,32]{1,0:T(1,128)}, u32[]{:S(2)}) copy-start(s32[1,32]{1,0:T(1,128)} %param.12) | copy-start | bytes 388
  12.1 8.1 %copy-start.1 = (s32[1,64]{1,0:T(1,128)S(1)}, s32[1,64]{1,0:T(1,128)}, u32[]{:S(2)}) copy-start(s32[1,64]{1,0:T(1,128)} %param.13) | copy-start | bytes 772
  12.1 17.4 %collective-permute-start.1 = (f32[301,8,4]{0,1,2:T(8,128)S(1)}, f32[301,8,4]{0,1,2:T(8,128)S(1)}, u32[]{:S(2)}, u32[]{:S(2)}) collective-permute-start(f32[301,8,4]{0,1,2:T(8,128)S(1)} %copy.33), channel_id=1, source_target_pairs={{0,1},{1,2},{2,3},{3,0},{4,5},{5,6},{6,7},{7,4},{8,9},{9,10},{10,1... | collective-permute-start | bytes 115592 | tf_op jit(solution)/shard_map/ppermute | solution.py:26
  14.0 30.6 %collective-permute-start.2 = (f32[301,4,256]{2,1,0:T(4,128)}, f32[301,4,256]{2,1,0:T(4,128)}, u32[]{:S(2)}, u32[]{:S(2)}) collective-permute-start(f32[301,4,256]{2,1,0:T(4,128)} %get-tuple-element.14), channel_id=1, source_target_pairs={{0,124},{4,0},{8,4},{12,8},{16,12},{20,16},{24,20},{28,24},{32,28}... | collective-permute-start | bytes 3698696 | tf_op jit(solution)/shard_map/ppermute | solution.py:25
  19.7 25.0 %collective-permute-start.4 = (f32[301,4,256]{2,1,0:T(4,128)}, f32[301,4,256]{2,1,0:T(4,128)}, u32[]{:S(2)}, u32[]{:S(2)}) collective-permute-start(f32[301,4,256]{2,1,0:T(4,128)} %get-tuple-element.15), channel_id=1, source_target_pairs={{0,4},{4,8},{8,12},{12,16},{16,20},{20,24},{24,28},{28,32},{32,36}... | collective-permute-start | bytes 3698696 | tf_op jit(solution)/shard_map/ppermute | solution.py:26
  22.6 21.3 %all-to-all-start = ((f32[4,32,2,128]{3,2,0,1:T(2,128)}), f32[4,32,2,128]{3,2,0,1:T(2,128)S(1)}, u32[]{:S(2)}, u32[]{:S(2)}) async-start(f32[4,32,2,128]{3,2,0,1:T(2,128)} %bitcast.37), calls=%async_computation | async-start | bytes 262144 | tf_op jit(solution)/shard_map/all_to_all | solution.py:300
  29.5 8.2 %collective-permute-start.3 = (f32[301,4,8]{0,2,1:T(8,128)S(1)}, f32[301,4,8]{0,2,1:T(8,128)S(1)}, u32[]{:S(2)}, u32[]{:S(2)}) collective-permute-start(f32[301,4,8]{0,2,1:T(8,128)S(1)} %get-tuple-element.18), channel_id=1, source_target_pairs={{0,124},{4,0},{8,4},{12,8},{16,12},{20,16},{24,20},{28,24},{32,28}... | collective-permute-start | bytes 115592 | tf_op jit(solution)/shard_map/ppermute | solution.py:25
  34.6 7.0 %collective-permute-start.5 = (f32[301,4,8]{0,2,1:T(8,128)S(1)}, f32[301,4,8]{0,2,1:T(8,128)S(1)}, u32[]{:S(2)}, u32[]{:S(2)}) collective-permute-start(f32[301,4,8]{0,2,1:T(8,128)S(1)} %get-tuple-element.19), channel_id=1, source_target_pairs={{0,4},{4,8},{8,12},{12,16},{16,20},{20,24},{24,28},{28,32},{32,36}... | collective-permute-start | bytes 115592 | tf_op jit(solution)/shard_map/ppermute | solution.py:26
  104.2 12.2 %all-to-all-start.1 = ((f32[4,32,2,128]{3,2,0,1:T(2,128)}), f32[4,32,2,128]{3,2,0,1:T(2,128)S(1)}, u32[]{:S(2)}, u32[]{:S(2)}) async-start(f32[4,32,2,128]{3,2,0,1:T(2,128)} %copy.45), calls=%async_computation.1 | async-start | bytes 262144 | tf_op jit(solution)/shard_map/all_to_all | solution.py:316
  119.5 4.0 %collective-permute-start.6 = (f32[4,16,128]{2,0,1:T(4,128)S(1)}, f32[4,16,128]{2,0,1:T(4,128)S(1)}, u32[]{:S(2)}, u32[]{:S(2)}) collective-permute-start(f32[4,16,128]{2,0,1:T(4,128)S(1)} %scatter_fusion), channel_id=1, source_target_pairs={{0,1},{1,0},{2,3},{3,2},{4,5},{5,4},{6,7},{7,6},{8,9},{9,8},{10,11... | collective-permute-start | bytes 98312 | tf_op jit(solution)/shard_map/ppermute | solution.py:262
  123.5 5.5 %collective-permute-start.7 = (f32[4,16,128]{2,0,1:T(4,128)S(1)}, f32[4,16,128]{2,0,1:T(4,128)S(1)}, u32[]{:S(2)}, u32[]{:S(2)}) collective-permute-start(f32[4,16,128]{2,0,1:T(4,128)S(1)} %add.96), channel_id=1, source_target_pairs={{0,2},{1,3},{2,0},{3,1},{4,6},{5,7},{6,4},{7,5},{8,10},{9,11},{10,... | collective-permute-start | bytes 98312 | tf_op jit(solution)/shard_map/ppermute | solution.py:262

commit v5 on v4

--- a/solution.py
+++ b/solution.py
@@ -36,24 +36,23 @@
     east, west = from_neighbours(stack, "lon", 2, width)
     sides = jnp.concatenate([east, west], axis=2)
     corner_south, corner_north = from_neighbours(sides, "lat", 1, width)
-    wide = -(-(cols + 2 * width) // 128) * 128
-
-    def band(middle, edges):
-        gap = jnp.zeros(middle.shape[:2] + (wide - cols - 2 * width,), jnp.float32)
-        return jnp.concatenate([middle, edges[:, :, :width], gap, edges[:, :, width:]], axis=2)
-
-    ext = jnp.concatenate(
-        [band(stack, sides), band(south, corner_south), band(north, corner_north)], axis=1
+    wide = -(-(2 * width) // 128) * 128
+    edges = jnp.concatenate([sides, corner_south, corner_north], axis=1)
+    gap = jnp.zeros(edges.shape[:2] + (wide - 2 * width,), jnp.float32)
+    edge_tile = jnp.concatenate([edges[:, :, :width], gap, edges[:, :, width:]], axis=2)
+    halo_rows = jnp.concatenate([south, north], axis=1)
+    coast_plane = jnp.concatenate(
+        [jnp.concatenate([stack[-1], halo_rows[-1]], axis=0), edge_tile[-1]], axis=1
     )
     lat_count = lax.axis_size("lat")
     where_lat = lax.axis_index("lat")
-    row = lax.broadcasted_iota(jnp.int32, ext.shape[1:], 0)
+    row = lax.broadcasted_iota(jnp.int32, coast_plane.shape, 0)
     outside = jnp.logical_or(
         jnp.logical_and(where_lat == 0, row >= rows + width),
         jnp.logical_and(where_lat == lat_count - 1, jnp.logical_and(row >= rows, row < rows + width)),
     )
-    mask = jnp.where(outside, 0.0, ext[-1])
-    return ext, mask
+    mask = jnp.where(outside, 0.0, coast_plane)
+    return planes, halo_rows, edge_tile, mask
 
 
 def with_halo(block, sides, width):
@@ -80,7 +79,8 @@
 
 
 def tridiagonal_kernel(
-    decay_ref, ext_ref, mask_ref, base_ref, surf_ref, land_ref, out_ref, back_ref, ratio_ref, marks_ref
+    decay_ref, inner_ref, rows_ref, edge_ref, mask_ref, base_ref, surf_ref, land_ref,
+    out_ref, back_ref, ratio_ref, marks_ref,
 ):
     fields, levels = out_ref.shape[0], out_ref.shape[1]
     rows, cols = out_ref.shape[2], out_ref.shape[3]
@@ -99,7 +99,9 @@
         return ((north + south) + west) + east
 
     def smoothed(f, level):
-        values = ext_ref[f * levels + level]
+        plane = f * levels + level
+        values = jnp.concatenate([inner_ref[plane], rows_ref[plane]], axis=0)
+        values = jnp.concatenate([values, edge_ref[plane]], axis=1)
         for turn in range(2):
             inner = laplace_ext(values)
             values = values - SMOOTHING * laplace_ext(inner)
@@ -155,7 +157,7 @@
         back_ref[f] = land * out_ref[f, 0]
 
 
-def tridiagonal(ext, mask, shape, mixing_base, surface, land):
+def tridiagonal(pieces, mask, shape, mixing_base, surface, land):
     fields, levels = shape[0], shape[1]
     decay_table = np.array(
         [math.exp(-level / DEPTH_SCALE) for level in range(levels)], dtype=np.float32
@@ -168,13 +170,13 @@
             jax.ShapeDtypeStruct((fields,) + shape[2:], jnp.float32),
         ),
         in_specs=[pl.BlockSpec(memory_space=pltpu.MemorySpace.SMEM)]
-        + [pl.BlockSpec(memory_space=vmem)] * 5,
+        + [pl.BlockSpec(memory_space=vmem)] * (len(pieces) + 4),
         out_specs=(pl.BlockSpec(memory_space=vmem), pl.BlockSpec(memory_space=vmem)),
         scratch_shapes=[
             pltpu.VMEM((len(set(FIELD_MIX)), levels) + shape[2:], jnp.float32),
             pltpu.VMEM((4,) + mask.shape, jnp.float32),
         ],
-    )(jnp.asarray(decay_table), ext, mask, mixing_base, surface, land)
+    )(jnp.asarray(decay_table), *pieces, mask, mixing_base, surface, land)
 
 
 def split_three(values):
@@ -194,7 +196,8 @@
     return total
 
 
-def gather_kernel(recv_ref, index_ref, weight_ref, after_ref, out_ref):
+def gather_kernel(recv_ref, index_ref, weight_ref, *after_and_out):
+    out_ref = after_and_out[-1]
     stacked, lanes = recv_ref.shape
     fields, rows, cols = out_ref.shape
     segments = stacked // fields
@@ -304,14 +307,14 @@
     index_rows = cover_index.reshape(items * rows, cols)
     weight_rows = cover_weight.reshape(items * rows, cols)
     land = land_mask.astype(jnp.float32)
-    ext, mask = extended_planes(adjoint_state, land_mask, HALO)
+    *pieces, mask = extended_planes(adjoint_state, land_mask, HALO)
     forcing = remap_call(
-        gather_kernel, (fields, rows, cols), flat_recv, index_rows, weight_rows, after=(ext,)
+        gather_kernel, (fields, rows, cols), flat_recv, index_rows, weight_rows, after=tuple(pieces[1:])
     )
     surface = WIND_GAIN * (forcing[2] * forcing[2] + forcing[3] * forcing[3]) + jax.nn.softplus(
         forcing[1] - forcing[0]
     )
-    state_adjoint, flux_back = tridiagonal(ext, mask, adjoint_state.shape, mixing_base, surface, land)
+    state_adjoint, flux_back = tridiagonal(pieces, mask, adjoint_state.shape, mixing_base, surface, land)
     buffer = remap_call(scatter_kernel, flat_recv.shape, flux_back, index_rows, weight_rows)
     returned = lax.all_to_all(
         buffer.reshape(received.shape), "lat", split_axis=1, concat_axis=1, tiled=True

time: 130 us -> 131 us (level)
  waiting for transfers between devices: 16.7 us -> 21.4 us
  other arithmetic: 21.9 us -> 19.1 us
    ppermute x3, waiting for transfers between devices: 2.4 us -> 5.33 us  [from_neighbours(): lax.ppermute(lax.slice_in_dim(block, size - width, size, axis=dim), axis,...]
    concatenate x1 -> x3, other arithmetic: 9.1 us -> 6.85 us  [the longest x1 3.69 us: extended_planes(): halo_rows = jnp.concatenate([south, north], axis=1)]
    slice x6 -> x3, local copies, waits for them, and re-layouts: 3.81 us -> 5.76 us  [the longest x2 2.9 us: extended_planes(): edges[:, :, :width]]
    ppermute x3, waiting for transfers between devices: 0.01 us -> 1.69 us  [from_neighbours(): lax.ppermute(lax.slice_in_dim(block, 0, width, axis=dim), axis, to_prev)]
    ppermute x2 -> x1, local copies, waits for them, and re-layouts: 1.57 us -> 0.01 us  [from_neighbours(): lax.ppermute(lax.slice_in_dim(block, size - width, size, axis=dim), axis,...]
    ppermute x2 -> x1, local copies, waits for them, and re-layouts: 1.57 us -> 0.01 us  [from_neighbours(): lax.ppermute(lax.slice_in_dim(block, 0, width, axis=dim), axis, to_prev)]
  transfers between devices with their start and end apart: 10 -> 10, of which waited for: 4 -> 5; matrix products, arithmetic and copies ran while one was open for 11% -> 13% of each run, Pallas kernels for 0% -> 0%
where the time goes in v5:
time: 131 us; the launch traced here: 130 us
  Pallas kernels  46 us (35%)
  starting transfers between devices  27.2 us (21%)
  waiting for transfers between devices  21.4 us (16%)
  other arithmetic  19.1 us (15%)
  local copies, waits for them, and re-layouts  15.3 us (12%)
    pallas_call x1, Pallas kernels, tridiagonal(): pl.pallas_call(tridiagonal_kernel, out_shape=(jax.ShapeDtypeStruct(shape,...  33.2 us
    ppermute x3, starting transfers between devices, from_neighbours(): lax.ppermute(lax.slice_in_dim(block, 0, width, axis=dim), axis, to_prev)  13.6 us
    pallas_call x2, Pallas kernels, remap_call(): pl.pallas_call(kernel, out_shape=jax.ShapeDtypeStruct(out_shape, jnp.floa...  12.9 us
    all_to_all x1, waiting for transfers between devices, shards(): lax.all_to_all(buffer.reshape(received.shape), 'lat', split_axis=1, conca...  7.82 us
    all_to_all x1, starting transfers between devices, shards(): lax.all_to_all(outgoing, 'lat', split_axis=1, concat_axis=1, tiled=True)  6.73 us
    ppermute x2, waiting for transfers between devices, sum_over(): values = values + lax.ppermute(values, axis, pairs)  6.51 us
    concatenate x2, other arithmetic, extended_planes(): stack = jnp.concatenate([planes, coast], axis=0)  5.42 us
    ppermute x3, waiting for transfers between devices, from_neighbours(): lax.ppermute(lax.slice_in_dim(block, size - width, size, axis=dim), axis,...  5.33 us
  transfers between devices with their start and end apart: 10, of which 5 were waited for; matrix products, arithmetic and copies ran while one was open for 13% of the time, Pallas kernels for 0%

profile of v5, /device:TPU:0, one launch (start us, length us, event | category | flops | bytes accessed | tf_op | source)
XLA Modules:
  0.0 129.9 jit_solution(17568730930763235384)
XLA Ops:
  1.4 3.5 %fusion = (f32[301,8,4]{2,1,0:T(8,128)}, f32[301,8,4]{2,1,0:T(8,128)}) fusion(f32[300,8,256]{2,1,0:T(8,128)} %bitcast.39, f32[1,8,256]{2,1,0:T(8,128)S(1)} %get-tuple-element.23), kind=kLoop, calls=%fused_computation.13 | loop fusion | flops 19264 | bytes 2542848 | tf_op jit(solution)/shard_map/concatenate | solution.py:34
  4.9 1.9 %copy.28 = f32[301,8,4]{0,1,2:T(8,128)S(1)} copy(f32[301,8,4]{2,1,0:T(8,128)} %get-tuple-element.14) | data formatting | bytes 77056 | tf_op jit(solution)/shard_map/slice | solution.py:25
  6.8 2.9 %collective-permute-start.2 = (f32[301,8,4]{0,1,2:T(8,128)S(1)}, f32[301,8,4]{0,1,2:T(8,128)S(1)}, u32[]{:S(2)}, u32[]{:S(2)}) collective-permute-start(f32[301,8,4]{0,1,2:T(8,128)S(1)} %copy.28), channel_id=1, source_target_pairs={{0,3},{1,0},{2,1},{3,2},{4,7},{5,4},{6,5},{7,6},{8,11},{9,8},{10,9... | collective-permute-start | bytes 115592 | tf_op jit(solution)/shard_map/ppermute | solution.py:25
  9.7 1.8 %copy.29 = f32[301,8,4]{0,1,2:T(8,128)S(1)} copy(f32[301,8,4]{2,1,0:T(8,128)} %get-tuple-element.15) | data formatting | bytes 77056 | tf_op jit(solution)/shard_map/slice | solution.py:26
  11.6 1.9 %fusion.1 = (f32[301,4,256]{2,1,0:T(4,128)}, f32[301,4,256]{2,1,0:T(4,128)}) fusion(f32[300,8,256]{2,1,0:T(8,128)S(1)} %bitcast.41, f32[1,8,256]{2,1,0:T(8,128)S(1)} %get-tuple-element.23), kind=kLoop, calls=%fused_computation.14 | loop fusion | flops 616448 | bytes 4931584 | tf_op jit(solution)/shard_map/concatenate | solution.py:34
  13.5 5.6 %collective-permute-start = (f32[301,4,256]{2,1,0:T(4,128)}, f32[301,4,256]{2,1,0:T(4,128)}, u32[]{:S(2)}, u32[]{:S(2)}) collective-permute-start(f32[301,4,256]{2,1,0:T(4,128)} %get-tuple-element.16), channel_id=1, source_target_pairs={{0,124},{4,0},{8,4},{12,8},{16,12},{20,16},{24,20},{28,24},{32,28}... | collective-permute-start | bytes 3698696 | tf_op jit(solution)/shard_map/ppermute | solution.py:25
  22.1 6.7 %all-to-all-start = ((f32[4,32,2,128]{3,2,0,1:T(2,128)}), f32[4,32,2,128]{3,2,0,1:T(2,128)S(1)}, u32[]{:S(2)}, u32[]{:S(2)}) async-start(f32[4,32,2,128]{3,2,0,1:T(2,128)} %bitcast.37), calls=%async_computation | async-start | bytes 262144 | tf_op jit(solution)/shard_map/all_to_all | solution.py:303
  29.0 5.0 %collective-permute-start.4 = (f32[301,4,8]{0,2,1:T(8,128)S(1)}, f32[301,4,8]{0,2,1:T(8,128)S(1)}, u32[]{:S(2)}, u32[]{:S(2)}) collective-permute-start(f32[301,4,8]{0,2,1:T(8,128)S(1)} %get-tuple-element.20), channel_id=1, source_target_pairs={{0,124},{4,0},{8,4},{12,8},{16,12},{20,16},{24,20},{28,24},{32,28}... | collective-permute-start | bytes 115592 | tf_op jit(solution)/shard_map/ppermute | solution.py:25
  34.1 1.7 %collective-permute-done.4 = f32[301,4,8]{0,2,1:T(8,128)S(1)} collective-permute-done((f32[301,4,8]{0,2,1:T(8,128)S(1)}, f32[301,4,8]{0,2,1:T(8,128)S(1)}, u32[]{:S(2)}, u32[]{:S(2)}) %collective-permute-start.4) | collective-permute-done | bytes 38560 | tf_op jit(solution)/shard_map/ppermute | solution.py:25
  35.8 5.3 %collective-permute-done.5 = f32[301,4,8]{0,2,1:T(8,128)S(1)} collective-permute-done((f32[301,4,8]{0,2,1:T(8,128)S(1)}, f32[301,4,8]{0,2,1:T(8,128)S(1)}, u32[]{:S(2)}, u32[]{:S(2)}) %collective-permute-start.5) | collective-permute-done | bytes 38560 | tf_op jit(solution)/shard_map/ppermute | solution.py:26
  41.2 2.9 %copy.32 = f32[301,16,4]{2,1,0:T(8,128)} copy(f32[301,16,4]{0,2,1:T(4,128)S(1)} %get-tuple-element.18) | data formatting | bytes 154112 | tf_op jit(solution)/shard_map/slice | solution.py:42
  44.0 2.9 %copy.33 = f32[301,16,4]{2,1,0:T(8,128)} copy(f32[301,16,4]{0,2,1:T(4,128)S(1)} %get-tuple-element.19) | data formatting | bytes 154112 | tf_op jit(solution)/shard_map/slice | solution.py:42
  46.9 3.1 %pad_maximum_fusion.1.after_and_out_1_.edge_ref = f32[301,16,128]{2,1,0:T(8,128)S(1)} fusion(f32[301,16,4]{2,1,0:T(8,128)} %copy.33, f32[301,16,4]{2,1,0:T(8,128)} %copy.32, f32[128]{0:T(128)S(1)} %pad.4.clone), kind=kLoop, calls=%fused_computation.9 | loop fusion | flops 1232896 | bytes 2620416 | tf_op jit(solution)/shard_map/concatenate | solution.py:42
  50.9 3.7 %pad_maximum_fusion.after_and_out_0_.rows_ref = f32[301,8,256]{2,1,0:T(8,128)} fusion(f32[301,4,256]{2,1,0:T(4,128)} %collective-permute-done.1, f32[301,4,256]{2,1,0:T(4,128)} %collective-permute-done), kind=kLoop, calls=%fused_computation.7 | loop fusion | flops 616448 | bytes 4931584 | tf_op jit(solution)/shard_map/concatenate | solution.py:43
  54.5 6.3 %shard_map.104 = f32[4,8,256]{2,1,0:T(8,128)} custom-call(f32[256,128]{1,0:T(8,128)} %bitcast.42, s32[32,256]{1,0:T(8,128)} %bitcast.46, f32[32,256]{1,0:T(8,128)} %bitcast.48, f32[301,8,256]{2,1,0:T(8,128)} %pad_maximum_fusion.after_and_out_0_.rows_ref, f32[301,16,128]{2,1,0:T(8,128)} %copy-done.2), custom_call_target="tpu_custom_call" | custom-call | tf_op jit(solution)/shard_map/pallas_call | solution.py:249
  63.6 33.2 %shard_map.105 = (f32[4,75,8,256]{3,2,1,0:T(8,128)}, f32[4,8,256]{2,1,0:T(8,128)}) custom-call(f32[75]{0:T(128)} %constant.9.clone.decay_ref, f32[300,8,256]{2,1,0:T(8,128)} %bitcast.40, f32[301,8,256]{2,1,0:T(8,128)} %pad_maximum_fusion.after_and_out_0_.rows_ref, f32[301,16,128]{2,1,0:T(8,128)} %copy-done.2, f32[16,384]{1,0:T(8,128)} %maximum_select_fusion.mask_ref, ...), custom_call_target="tpu_custom_call" | custom-call | tf_op jit(solution)/shard_map/pallas_call | solution.py:166
  96.8 6.6 %shard_map.106 = f32[256,128]{1,0:T(8,128)} custom-call(f32[4,8,256]{2,1,0:T(8,128)} %get-tuple-element.5.back_ref, s32[32,256]{1,0:T(8,128)} %bitcast.47, f32[32,256]{1,0:T(8,128)} %bitcast.49), custom_call_target="tpu_custom_call" | custom-call | tf_op jit(solution)/shard_map/pallas_call | solution.py:249
  103.3 1.6 %copy.37 = f32[4,32,2,128]{3,2,0,1:T(2,128)} copy(f32[4,32,2,128]{3,2,1,0:T(2,128)} %bitcast.44) | data formatting | bytes 262144 | tf_op jit(solution)/shard_map/reshape | solution.py:320
  104.9 3.8 %all-to-all-start.1 = ((f32[4,32,2,128]{3,2,0,1:T(2,128)}), f32[4,32,2,128]{3,2,0,1:T(2,128)S(1)}, u32[]{:S(2)}, u32[]{:S(2)}) async-start(f32[4,32,2,128]{3,2,0,1:T(2,128)} %copy.37), calls=%async_computation.1 | async-start | bytes 262144 | tf_op jit(solution)/shard_map/all_to_all | solution.py:319
  108.8 7.8 %all-to-all-done.1 = f32[4,32,2,128]{3,2,0,1:T(2,128)S(1)} async-done(((f32[4,32,2,128]{3,2,0,1:T(2,128)}), f32[4,32,2,128]{3,2,0,1:T(2,128)S(1)}, u32[]{:S(2)}, u32[]{:S(2)}) %all-to-all-start.1) | async-done | bytes 131104 | tf_op jit(solution)/shard_map/all_to_all | solution.py:319
  116.9 2.8 %scatter_fusion = f32[4,16,128]{2,0,1:T(4,128)S(1)} fusion(f32[4,16,128]{2,0,1:T(4,128)S(1)} %broadcast_in_dim.35, s32[64]{0:T(128)S(1)} %fusion.10, f32[64,4,128]{2,1,0:T(4,128)S(1)} %copy.39), kind=kCustom, calls=%fused_computation.2 | custom fusion | flops 32768 | bytes 393472 | tf_op jit(solution)/shard_map/scatter-add | solution.py:323
  120.3 3.5 %collective-permute-done.6 = f32[4,16,128]{2,0,1:T(4,128)S(1)} collective-permute-done((f32[4,16,128]{2,0,1:T(4,128)S(1)}, f32[4,16,128]{2,0,1:T(4,128)S(1)}, u32[]{:S(2)}, u32[]{:S(2)}) %collective-permute-start.6) | collective-permute-done | bytes 32800 | tf_op jit(solution)/shard_map/ppermute | solution.py:265
  123.7 2.4 %collective-permute-start.7 = (f32[4,16,128]{2,0,1:T(4,128)S(1)}, f32[4,16,128]{2,0,1:T(4,128)S(1)}, u32[]{:S(2)}, u32[]{:S(2)}) collective-permute-start(f32[4,16,128]{2,0,1:T(4,128)S(1)} %add.96), channel_id=1, source_target_pairs={{0,2},{1,3},{2,0},{3,1},{4,6},{5,7},{6,4},{7,5},{8,10},{9,11},{10,... | collective-permute-start | bytes 98312 | tf_op jit(solution)/shard_map/ppermute | solution.py:265
  126.2 3.1 %collective-permute-done.7 = f32[4,16,128]{2,0,1:T(4,128)S(1)} collective-permute-done((f32[4,16,128]{2,0,1:T(4,128)S(1)}, f32[4,16,128]{2,0,1:T(4,128)S(1)}, u32[]{:S(2)}, u32[]{:S(2)}) %collective-permute-start.7) | collective-permute-done | bytes 32800 | tf_op jit(solution)/shard_map/ppermute | solution.py:265
  (58 shorter events, 8.9 us)
Async XLA Ops:
  0.6 20.0 %copy-start = (f32[4,16,128]{2,1,0:T(8,128)S(1)}, f32[4,16,128]{2,1,0:T(8,128)}, u32[]{:S(2)}) copy-start(f32[4,16,128]{2,1,0:T(8,128)} %param.11) | copy-start | bytes 98308
  1.4 61.5 %copy-start.4 = (f32[8,256]{1,0:T(8,128)}, f32[8,256]{1,0:T(8,128)S(1)}, u32[]{:S(2)}) copy-start(f32[8,256]{1,0:T(8,128)S(1)} %get-tuple-element.22.land_ref) | copy-start | bytes 24580
  4.9 6.7 %copy-start.3 = (f32[4,75,8,256]{3,2,1,0:T(8,128)S(1)}, f32[4,75,8,256]{3,2,1,0:T(8,128)}, u32[]{:S(2)}) copy-start(f32[4,75,8,256]{3,2,1,0:T(8,128)} %param.9) | copy-start | bytes 7372804
  6.8 22.1 %collective-permute-start.2 = (f32[301,8,4]{0,1,2:T(8,128)S(1)}, f32[301,8,4]{0,1,2:T(8,128)S(1)}, u32[]{:S(2)}, u32[]{:S(2)}) collective-permute-start(f32[301,8,4]{0,1,2:T(8,128)S(1)} %copy.28), channel_id=1, source_target_pairs={{0,3},{1,0},{2,1},{3,2},{4,7},{5,4},{6,5},{7,6},{8,11},{9,8},{10,9... | collective-permute-start | bytes 115592 | tf_op jit(solution)/shard_map/ppermute | solution.py:25
  11.5 7.7 %copy-start.5 = (s32[1,32]{1,0:T(1,128)S(1)}, s32[1,32]{1,0:T(1,128)}, u32[]{:S(2)}) copy-start(s32[1,32]{1,0:T(1,128)} %param.12) | copy-start | bytes 388
  11.5 8.1 %copy-start.1 = (s32[1,64]{1,0:T(1,128)S(1)}, s32[1,64]{1,0:T(1,128)}, u32[]{:S(2)}) copy-start(s32[1,64]{1,0:T(1,128)} %param.13) | copy-start | bytes 772
  11.5 17.4 %collective-permute-start.3 = (f32[301,8,4]{0,1,2:T(8,128)S(1)}, f32[301,8,4]{0,1,2:T(8,128)S(1)}, u32[]{:S(2)}, u32[]{:S(2)}) collective-permute-start(f32[301,8,4]{0,1,2:T(8,128)S(1)} %copy.29), channel_id=1, source_target_pairs={{0,1},{1,2},{2,3},{3,0},{4,5},{5,6},{6,7},{7,4},{8,9},{9,10},{10,1... | collective-permute-start | bytes 115592 | tf_op jit(solution)/shard_map/ppermute | solution.py:26
  13.5 37.4 %collective-permute-start = (f32[301,4,256]{2,1,0:T(4,128)}, f32[301,4,256]{2,1,0:T(4,128)}, u32[]{:S(2)}, u32[]{:S(2)}) collective-permute-start(f32[301,4,256]{2,1,0:T(4,128)} %get-tuple-element.16), channel_id=1, source_target_pairs={{0,124},{4,0},{8,4},{12,8},{16,12},{20,16},{24,20},{28,24},{32,28}... | collective-permute-start | bytes 3698696 | tf_op jit(solution)/shard_map/ppermute | solution.py:25
  19.1 31.7 %collective-permute-start.1 = (f32[301,4,256]{2,1,0:T(4,128)}, f32[301,4,256]{2,1,0:T(4,128)}, u32[]{:S(2)}, u32[]{:S(2)}) collective-permute-start(f32[301,4,256]{2,1,0:T(4,128)} %get-tuple-element.17), channel_id=1, source_target_pairs={{0,4},{4,8},{8,12},{12,16},{16,20},{20,24},{24,28},{28,32},{32,36}... | collective-permute-start | bytes 3698696 | tf_op jit(solution)/shard_map/ppermute | solution.py:26
  22.1 28.0 %all-to-all-start = ((f32[4,32,2,128]{3,2,0,1:T(2,128)}), f32[4,32,2,128]{3,2,0,1:T(2,128)S(1)}, u32[]{:S(2)}, u32[]{:S(2)}) async-start(f32[4,32,2,128]{3,2,0,1:T(2,128)} %bitcast.37), calls=%async_computation | async-start | bytes 262144 | tf_op jit(solution)/shard_map/all_to_all | solution.py:303
  29.0 6.8 %collective-permute-start.4 = (f32[301,4,8]{0,2,1:T(8,128)S(1)}, f32[301,4,8]{0,2,1:T(8,128)S(1)}, u32[]{:S(2)}, u32[]{:S(2)}) collective-permute-start(f32[301,4,8]{0,2,1:T(8,128)S(1)} %get-tuple-element.20), channel_id=1, source_target_pairs={{0,124},{4,0},{8,4},{12,8},{16,12},{20,16},{24,20},{28,24},{32,28}... | collective-permute-start | bytes 115592 | tf_op jit(solution)/shard_map/ppermute | solution.py:25
  34.0 7.1 %collective-permute-start.5 = (f32[301,4,8]{0,2,1:T(8,128)S(1)}, f32[301,4,8]{0,2,1:T(8,128)S(1)}, u32[]{:S(2)}, u32[]{:S(2)}) collective-permute-start(f32[301,4,8]{0,2,1:T(8,128)S(1)} %get-tuple-element.21), channel_id=1, source_target_pairs={{0,4},{4,8},{8,12},{12,16},{16,20},{20,24},{24,28},{28,32},{32,36}... | collective-permute-start | bytes 115592 | tf_op jit(solution)/shard_map/ppermute | solution.py:26
  50.0 4.5 %copy-start.2 = (f32[301,16,128]{2,1,0:T(8,128)}, f32[301,16,128]{2,1,0:T(8,128)S(1)}, u32[]{:S(2)}) copy-start(f32[301,16,128]{2,1,0:T(8,128)S(1)} %pad_maximum_fusion.1.after_and_out_1_.edge_ref) | copy-start | bytes 7397380
  104.9 11.7 %all-to-all-start.1 = ((f32[4,32,2,128]{3,2,0,1:T(2,128)}), f32[4,32,2,128]{3,2,0,1:T(2,128)S(1)}, u32[]{:S(2)}, u32[]{:S(2)}) async-start(f32[4,32,2,128]{3,2,0,1:T(2,128)} %copy.37), calls=%async_computation.1 | async-start | bytes 262144 | tf_op jit(solution)/shard_map/all_to_all | solution.py:319
  119.7 4.0 %collective-permute-start.6 = (f32[4,16,128]{2,0,1:T(4,128)S(1)}, f32[4,16,128]{2,0,1:T(4,128)S(1)}, u32[]{:S(2)}, u32[]{:S(2)}) collective-permute-start(f32[4,16,128]{2,0,1:T(4,128)S(1)} %scatter_fusion), channel_id=1, source_target_pairs={{0,1},{1,0},{2,3},{3,2},{4,5},{5,4},{6,7},{7,6},{8,9},{9,8},{10,11... | collective-permute-start | bytes 98312 | tf_op jit(solution)/shard_map/ppermute | solution.py:265
  123.7 5.5 %collective-permute-start.7 = (f32[4,16,128]{2,0,1:T(4,128)S(1)}, f32[4,16,128]{2,0,1:T(4,128)S(1)}, u32[]{:S(2)}, u32[]{:S(2)}) collective-permute-start(f32[4,16,128]{2,0,1:T(4,128)S(1)} %add.96), channel_id=1, source_target_pairs={{0,2},{1,3},{2,0},{3,1},{4,6},{5,7},{6,4},{7,5},{8,10},{9,11},{10,... | collective-permute-start | bytes 98312 | tf_op jit(solution)/shard_map/ppermute | solution.py:265

commit v6 on v5

--- a/solution.py
+++ b/solution.py
@@ -90,22 +90,33 @@
     marks_ref[1] = marks * pltpu.roll(marks, tall - 1, 0)
     marks_ref[2] = marks * pltpu.roll(marks, 1, 1)
     marks_ref[3] = marks * pltpu.roll(marks, wide - 1, 1)
-
-    def laplace_ext(values):
-        north = marks_ref[0] * (pltpu.roll(values, 1, 0) - values)
-        south = marks_ref[1] * (pltpu.roll(values, tall - 1, 0) - values)
-        west = marks_ref[2] * (pltpu.roll(values, 1, 1) - values)
-        east = marks_ref[3] * (pltpu.roll(values, wide - 1, 1) - values)
-        return ((north + south) + west) + east
+    marks_ref[4] = (marks_ref[0] + marks_ref[1]) + (marks_ref[2] + marks_ref[3])
+
+    def laplace_ext(values, inner=False):
+        shifted = [
+            pltpu.roll(values, 1, 0),
+            pltpu.roll(values, tall - 1, 0),
+            pltpu.roll(values, 1, 1),
+            pltpu.roll(values, wide - 1, 1),
+        ]
+        if inner:
+            shifted = [part[:rows, :cols] for part in shifted]
+            values = values[:rows, :cols]
+            weight = [marks_ref[i, :rows, :cols] for i in range(5)]
+        else:
+            weight = [marks_ref[i] for i in range(5)]
+        vertical = weight[0] * shifted[0] + weight[1] * shifted[1]
+        across = weight[2] * shifted[2] + weight[3] * shifted[3]
+        return (vertical + across) - weight[4] * values
 
     def smoothed(f, level):
         plane = f * levels + level
         values = jnp.concatenate([inner_ref[plane], rows_ref[plane]], axis=0)
         values = jnp.concatenate([values, edge_ref[plane]], axis=1)
-        for turn in range(2):
-            inner = laplace_ext(values)
-            values = values - SMOOTHING * laplace_ext(inner)
-        return values[:rows, :cols]
+        inner = laplace_ext(values)
+        values = values - SMOOTHING * laplace_ext(inner)
+        inner = laplace_ext(values)
+        return values[:rows, :cols] - SMOOTHING * laplace_ext(inner, inner=True)
 
     gains = sorted(set(FIELD_MIX))
     groups = [[f for f in range(fields) if FIELD_MIX[f] == g] for g in gains]
@@ -174,7 +185,7 @@
         out_specs=(pl.BlockSpec(memory_space=vmem), pl.BlockSpec(memory_space=vmem)),
         scratch_shapes=[
             pltpu.VMEM((len(set(FIELD_MIX)), levels) + shape[2:], jnp.float32),
-            pltpu.VMEM((4,) + mask.shape, jnp.float32),
+            pltpu.VMEM((5,) + mask.shape, jnp.float32),
         ],
     )(jnp.asarray(decay_table), *pieces, mask, mixing_base, surface, land)
 

time: 131 us -> 129 us (0.985)
  Pallas kernels: 46 us -> 44.6 us
    pallas_call x1, Pallas kernels: 33.2 us -> 31.7 us  [tridiagonal(): pl.pallas_call(tridiagonal_kernel, out_shape=(jax.ShapeDtypeStruct(shape,...]
where the time goes in v6:
time: 129 us; the launch traced here: 128 us
  Pallas kernels  44.6 us (35%)
  starting transfers between devices  27.2 us (21%)
  waiting for transfers between devices  21.4 us (17%)
  other arithmetic  19.1 us (15%)
  local copies, waits for them, and re-layouts  15.3 us (12%)
    pallas_call x1, Pallas kernels, tridiagonal(): pl.pallas_call(tridiagonal_kernel, out_shape=(jax.ShapeDtypeStruct(shape,...  31.7 us
    ppermute x3, starting transfers between devices, from_neighbours(): lax.ppermute(lax.slice_in_dim(block, 0, width, axis=dim), axis, to_prev)  13.6 us
    pallas_call x2, Pallas kernels, remap_call(): pl.pallas_call(kernel, out_shape=jax.ShapeDtypeStruct(out_shape, jnp.floa...  12.9 us
    all_to_all x1, waiting for transfers between devices, shards(): lax.all_to_all(buffer.reshape(received.shape), 'lat', split_axis=1, conca...  7.82 us
    all_to_all x1, starting transfers between devices, shards(): lax.all_to_all(outgoing, 'lat', split_axis=1, concat_axis=1, tiled=True)  6.73 us
    ppermute x2, waiting for transfers between devices, sum_over(): values = values + lax.ppermute(values, axis, pairs)  6.53 us
    concatenate x2, other arithmetic, extended_planes(): stack = jnp.concatenate([planes, coast], axis=0)  5.42 us
    ppermute x3, waiting for transfers between devices, from_neighbours(): lax.ppermute(lax.slice_in_dim(block, size - width, size, axis=dim), axis,...  5.33 us
  transfers between devices with their start and end apart: 10, of which 5 were waited for; matrix products, arithmetic and copies ran while one was open for 13% of the time, Pallas kernels for 0%

profile of v6, /device:TPU:0, one launch (start us, length us, event | category | flops | bytes accessed | tf_op | source)
XLA Modules:
  0.0 128.4 jit_solution(10986219709984256254)
XLA Ops:
  1.4 3.5 %fusion = (f32[301,8,4]{2,1,0:T(8,128)}, f32[301,8,4]{2,1,0:T(8,128)}) fusion(f32[300,8,256]{2,1,0:T(8,128)} %bitcast.39, f32[1,8,256]{2,1,0:T(8,128)S(1)} %get-tuple-element.23), kind=kLoop, calls=%fused_computation.13 | loop fusion | flops 19264 | bytes 2542848 | tf_op jit(solution)/shard_map/concatenate | solution.py:34
  4.9 1.9 %copy.28 = f32[301,8,4]{0,1,2:T(8,128)S(1)} copy(f32[301,8,4]{2,1,0:T(8,128)} %get-tuple-element.14) | data formatting | bytes 77056 | tf_op jit(solution)/shard_map/slice | solution.py:25
  6.8 2.9 %collective-permute-start.2 = (f32[301,8,4]{0,1,2:T(8,128)S(1)}, f32[301,8,4]{0,1,2:T(8,128)S(1)}, u32[]{:S(2)}, u32[]{:S(2)}) collective-permute-start(f32[301,8,4]{0,1,2:T(8,128)S(1)} %copy.28), channel_id=1, source_target_pairs={{0,3},{1,0},{2,1},{3,2},{4,7},{5,4},{6,5},{7,6},{8,11},{9,8},{10,9... | collective-permute-start | bytes 115592 | tf_op jit(solution)/shard_map/ppermute | solution.py:25
  9.7 1.8 %copy.29 = f32[301,8,4]{0,1,2:T(8,128)S(1)} copy(f32[301,8,4]{2,1,0:T(8,128)} %get-tuple-element.15) | data formatting | bytes 77056 | tf_op jit(solution)/shard_map/slice | solution.py:26
  11.6 1.9 %fusion.1 = (f32[301,4,256]{2,1,0:T(4,128)}, f32[301,4,256]{2,1,0:T(4,128)}) fusion(f32[300,8,256]{2,1,0:T(8,128)S(1)} %bitcast.41, f32[1,8,256]{2,1,0:T(8,128)S(1)} %get-tuple-element.23), kind=kLoop, calls=%fused_computation.14 | loop fusion | flops 616448 | bytes 4931584 | tf_op jit(solution)/shard_map/concatenate | solution.py:34
  13.5 5.6 %collective-permute-start = (f32[301,4,256]{2,1,0:T(4,128)}, f32[301,4,256]{2,1,0:T(4,128)}, u32[]{:S(2)}, u32[]{:S(2)}) collective-permute-start(f32[301,4,256]{2,1,0:T(4,128)} %get-tuple-element.16), channel_id=1, source_target_pairs={{0,124},{4,0},{8,4},{12,8},{16,12},{20,16},{24,20},{28,24},{32,28}... | collective-permute-start | bytes 3698696 | tf_op jit(solution)/shard_map/ppermute | solution.py:25
  22.1 6.7 %all-to-all-start = ((f32[4,32,2,128]{3,2,0,1:T(2,128)}), f32[4,32,2,128]{3,2,0,1:T(2,128)S(1)}, u32[]{:S(2)}, u32[]{:S(2)}) async-start(f32[4,32,2,128]{3,2,0,1:T(2,128)} %bitcast.37), calls=%async_computation | async-start | bytes 262144 | tf_op jit(solution)/shard_map/all_to_all | solution.py:314
  29.0 5.0 %collective-permute-start.4 = (f32[301,4,8]{0,2,1:T(8,128)S(1)}, f32[301,4,8]{0,2,1:T(8,128)S(1)}, u32[]{:S(2)}, u32[]{:S(2)}) collective-permute-start(f32[301,4,8]{0,2,1:T(8,128)S(1)} %get-tuple-element.20), channel_id=1, source_target_pairs={{0,124},{4,0},{8,4},{12,8},{16,12},{20,16},{24,20},{28,24},{32,28}... | collective-permute-start | bytes 115592 | tf_op jit(solution)/shard_map/ppermute | solution.py:25
  34.1 1.7 %collective-permute-done.4 = f32[301,4,8]{0,2,1:T(8,128)S(1)} collective-permute-done((f32[301,4,8]{0,2,1:T(8,128)S(1)}, f32[301,4,8]{0,2,1:T(8,128)S(1)}, u32[]{:S(2)}, u32[]{:S(2)}) %collective-permute-start.4) | collective-permute-done | bytes 38560 | tf_op jit(solution)/shard_map/ppermute | solution.py:25
  35.8 5.3 %collective-permute-done.5 = f32[301,4,8]{0,2,1:T(8,128)S(1)} collective-permute-done((f32[301,4,8]{0,2,1:T(8,128)S(1)}, f32[301,4,8]{0,2,1:T(8,128)S(1)}, u32[]{:S(2)}, u32[]{:S(2)}) %collective-permute-start.5) | collective-permute-done | bytes 38560 | tf_op jit(solution)/shard_map/ppermute | solution.py:26
  41.2 2.9 %copy.32 = f32[301,16,4]{2,1,0:T(8,128)} copy(f32[301,16,4]{0,2,1:T(4,128)S(1)} %get-tuple-element.18) | data formatting | bytes 154112 | tf_op jit(solution)/shard_map/slice | solution.py:42
  44.0 2.9 %copy.33 = f32[301,16,4]{2,1,0:T(8,128)} copy(f32[301,16,4]{0,2,1:T(4,128)S(1)} %get-tuple-element.19) | data formatting | bytes 154112 | tf_op jit(solution)/shard_map/slice | solution.py:42
  46.9 3.1 %pad_maximum_fusion.1.after_and_out_1_.edge_ref = f32[301,16,128]{2,1,0:T(8,128)S(1)} fusion(f32[301,16,4]{2,1,0:T(8,128)} %copy.33, f32[301,16,4]{2,1,0:T(8,128)} %copy.32, f32[128]{0:T(128)S(1)} %pad.4.clone), kind=kLoop, calls=%fused_computation.9 | loop fusion | flops 1232896 | bytes 2620416 | tf_op jit(solution)/shard_map/concatenate | solution.py:42
  50.9 3.7 %pad_maximum_fusion.after_and_out_0_.rows_ref = f32[301,8,256]{2,1,0:T(8,128)} fusion(f32[301,4,256]{2,1,0:T(4,128)} %collective-permute-done.1, f32[301,4,256]{2,1,0:T(4,128)} %collective-permute-done), kind=kLoop, calls=%fused_computation.7 | loop fusion | flops 616448 | bytes 4931584 | tf_op jit(solution)/shard_map/concatenate | solution.py:43
  54.5 6.3 %shard_map.104 = f32[4,8,256]{2,1,0:T(8,128)} custom-call(f32[256,128]{1,0:T(8,128)} %bitcast.42, s32[32,256]{1,0:T(8,128)} %bitcast.46, f32[32,256]{1,0:T(8,128)} %bitcast.48, f32[301,8,256]{2,1,0:T(8,128)} %pad_maximum_fusion.after_and_out_0_.rows_ref, f32[301,16,128]{2,1,0:T(8,128)} %copy-done.2), custom_call_target="tpu_custom_call" | custom-call | tf_op jit(solution)/shard_map/pallas_call | solution.py:260
  63.6 31.7 %shard_map.105 = (f32[4,75,8,256]{3,2,1,0:T(8,128)}, f32[4,8,256]{2,1,0:T(8,128)}) custom-call(f32[75]{0:T(128)} %constant.9.clone.decay_ref, f32[300,8,256]{2,1,0:T(8,128)} %bitcast.40, f32[301,8,256]{2,1,0:T(8,128)} %pad_maximum_fusion.after_and_out_0_.rows_ref, f32[301,16,128]{2,1,0:T(8,128)} %copy-done.2, f32[16,384]{1,0:T(8,128)} %maximum_select_fusion.mask_ref, ...), custom_call_target="tpu_custom_call" | custom-call | tf_op jit(solution)/shard_map/pallas_call | solution.py:177
  95.3 6.6 %shard_map.106 = f32[256,128]{1,0:T(8,128)} custom-call(f32[4,8,256]{2,1,0:T(8,128)} %get-tuple-element.5.back_ref, s32[32,256]{1,0:T(8,128)} %bitcast.47, f32[32,256]{1,0:T(8,128)} %bitcast.49), custom_call_target="tpu_custom_call" | custom-call | tf_op jit(solution)/shard_map/pallas_call | solution.py:260
  101.9 1.6 %copy.37 = f32[4,32,2,128]{3,2,0,1:T(2,128)} copy(f32[4,32,2,128]{3,2,1,0:T(2,128)} %bitcast.44) | data formatting | bytes 262144 | tf_op jit(solution)/shard_map/reshape | solution.py:331
  103.5 3.8 %all-to-all-start.1 = ((f32[4,32,2,128]{3,2,0,1:T(2,128)}), f32[4,32,2,128]{3,2,0,1:T(2,128)S(1)}, u32[]{:S(2)}, u32[]{:S(2)}) async-start(f32[4,32,2,128]{3,2,0,1:T(2,128)} %copy.37), calls=%async_computation.1 | async-start | bytes 262144 | tf_op jit(solution)/shard_map/all_to_all | solution.py:330
  107.3 7.8 %all-to-all-done.1 = f32[4,32,2,128]{3,2,0,1:T(2,128)S(1)} async-done(((f32[4,32,2,128]{3,2,0,1:T(2,128)}), f32[4,32,2,128]{3,2,0,1:T(2,128)S(1)}, u32[]{:S(2)}, u32[]{:S(2)}) %all-to-all-start.1) | async-done | bytes 131104 | tf_op jit(solution)/shard_map/all_to_all | solution.py:330
  115.5 2.8 %scatter_fusion = f32[4,16,128]{2,0,1:T(4,128)S(1)} fusion(f32[4,16,128]{2,0,1:T(4,128)S(1)} %broadcast_in_dim.35, s32[64]{0:T(128)S(1)} %fusion.10, f32[64,4,128]{2,1,0:T(4,128)S(1)} %copy.39), kind=kCustom, calls=%fused_computation.2 | custom fusion | flops 32768 | bytes 393472 | tf_op jit(solution)/shard_map/scatter-add | solution.py:334
  118.8 3.5 %collective-permute-done.6 = f32[4,16,128]{2,0,1:T(4,128)S(1)} collective-permute-done((f32[4,16,128]{2,0,1:T(4,128)S(1)}, f32[4,16,128]{2,0,1:T(4,128)S(1)}, u32[]{:S(2)}, u32[]{:S(2)}) %collective-permute-start.6) | collective-permute-done | bytes 32800 | tf_op jit(solution)/shard_map/ppermute | solution.py:276
  122.3 2.4 %collective-permute-start.7 = (f32[4,16,128]{2,0,1:T(4,128)S(1)}, f32[4,16,128]{2,0,1:T(4,128)S(1)}, u32[]{:S(2)}, u32[]{:S(2)}) collective-permute-start(f32[4,16,128]{2,0,1:T(4,128)S(1)} %add.96), channel_id=1, source_target_pairs={{0,2},{1,3},{2,0},{3,1},{4,6},{5,7},{6,4},{7,5},{8,10},{9,11},{10,... | collective-permute-start | bytes 98312 | tf_op jit(solution)/shard_map/ppermute | solution.py:276
  124.7 3.1 %collective-permute-done.7 = f32[4,16,128]{2,0,1:T(4,128)S(1)} collective-permute-done((f32[4,16,128]{2,0,1:T(4,128)S(1)}, f32[4,16,128]{2,0,1:T(4,128)S(1)}, u32[]{:S(2)}, u32[]{:S(2)}) %collective-permute-start.7) | collective-permute-done | bytes 32800 | tf_op jit(solution)/shard_map/ppermute | solution.py:276
  (58 shorter events, 8.9 us)
Async XLA Ops:
  0.6 20.0 %copy-start = (f32[4,16,128]{2,1,0:T(8,128)S(1)}, f32[4,16,128]{2,1,0:T(8,128)}, u32[]{:S(2)}) copy-start(f32[4,16,128]{2,1,0:T(8,128)} %param.11) | copy-start | bytes 98308
  1.4 61.5 %copy-start.4 = (f32[8,256]{1,0:T(8,128)}, f32[8,256]{1,0:T(8,128)S(1)}, u32[]{:S(2)}) copy-start(f32[8,256]{1,0:T(8,128)S(1)} %get-tuple-element.22.land_ref) | copy-start | bytes 24580
  4.9 6.7 %copy-start.3 = (f32[4,75,8,256]{3,2,1,0:T(8,128)S(1)}, f32[4,75,8,256]{3,2,1,0:T(8,128)}, u32[]{:S(2)}) copy-start(f32[4,75,8,256]{3,2,1,0:T(8,128)} %param.9) | copy-start | bytes 7372804
  6.8 22.1 %collective-permute-start.2 = (f32[301,8,4]{0,1,2:T(8,128)S(1)}, f32[301,8,4]{0,1,2:T(8,128)S(1)}, u32[]{:S(2)}, u32[]{:S(2)}) collective-permute-start(f32[301,8,4]{0,1,2:T(8,128)S(1)} %copy.28), channel_id=1, source_target_pairs={{0,3},{1,0},{2,1},{3,2},{4,7},{5,4},{6,5},{7,6},{8,11},{9,8},{10,9... | collective-permute-start | bytes 115592 | tf_op jit(solution)/shard_map/ppermute | solution.py:25
  11.5 7.7 %copy-start.5 = (s32[1,32]{1,0:T(1,128)S(1)}, s32[1,32]{1,0:T(1,128)}, u32[]{:S(2)}) copy-start(s32[1,32]{1,0:T(1,128)} %param.12) | copy-start | bytes 388
  11.5 8.1 %copy-start.1 = (s32[1,64]{1,0:T(1,128)S(1)}, s32[1,64]{1,0:T(1,128)}, u32[]{:S(2)}) copy-start(s32[1,64]{1,0:T(1,128)} %param.13) | copy-start | bytes 772
  11.5 17.4 %collective-permute-start.3 = (f32[301,8,4]{0,1,2:T(8,128)S(1)}, f32[301,8,4]{0,1,2:T(8,128)S(1)}, u32[]{:S(2)}, u32[]{:S(2)}) collective-permute-start(f32[301,8,4]{0,1,2:T(8,128)S(1)} %copy.29), channel_id=1, source_target_pairs={{0,1},{1,2},{2,3},{3,0},{4,5},{5,6},{6,7},{7,4},{8,9},{9,10},{10,1... | collective-permute-start | bytes 115592 | tf_op jit(solution)/shard_map/ppermute | solution.py:26
  13.5 37.4 %collective-permute-start = (f32[301,4,256]{2,1,0:T(4,128)}, f32[301,4,256]{2,1,0:T(4,128)}, u32[]{:S(2)}, u32[]{:S(2)}) collective-permute-start(f32[301,4,256]{2,1,0:T(4,128)} %get-tuple-element.16), channel_id=1, source_target_pairs={{0,124},{4,0},{8,4},{12,8},{16,12},{20,16},{24,20},{28,24},{32,28}... | collective-permute-start | bytes 3698696 | tf_op jit(solution)/shard_map/ppermute | solution.py:25
  19.1 31.7 %collective-permute-start.1 = (f32[301,4,256]{2,1,0:T(4,128)}, f32[301,4,256]{2,1,0:T(4,128)}, u32[]{:S(2)}, u32[]{:S(2)}) collective-permute-start(f32[301,4,256]{2,1,0:T(4,128)} %get-tuple-element.17), channel_id=1, source_target_pairs={{0,4},{4,8},{8,12},{12,16},{16,20},{20,24},{24,28},{28,32},{32,36}... | collective-permute-start | bytes 3698696 | tf_op jit(solution)/shard_map/ppermute | solution.py:26
  22.1 28.0 %all-to-all-start = ((f32[4,32,2,128]{3,2,0,1:T(2,128)}), f32[4,32,2,128]{3,2,0,1:T(2,128)S(1)}, u32[]{:S(2)}, u32[]{:S(2)}) async-start(f32[4,32,2,128]{3,2,0,1:T(2,128)} %bitcast.37), calls=%async_computation | async-start | bytes 262144 | tf_op jit(solution)/shard_map/all_to_all | solution.py:314
  29.0 6.8 %collective-permute-start.4 = (f32[301,4,8]{0,2,1:T(8,128)S(1)}, f32[301,4,8]{0,2,1:T(8,128)S(1)}, u32[]{:S(2)}, u32[]{:S(2)}) collective-permute-start(f32[301,4,8]{0,2,1:T(8,128)S(1)} %get-tuple-element.20), channel_id=1, source_target_pairs={{0,124},{4,0},{8,4},{12,8},{16,12},{20,16},{24,20},{28,24},{32,28}... | collective-permute-start | bytes 115592 | tf_op jit(solution)/shard_map/ppermute | solution.py:25
  34.0 7.1 %collective-permute-start.5 = (f32[301,4,8]{0,2,1:T(8,128)S(1)}, f32[301,4,8]{0,2,1:T(8,128)S(1)}, u32[]{:S(2)}, u32[]{:S(2)}) collective-permute-start(f32[301,4,8]{0,2,1:T(8,128)S(1)} %get-tuple-element.21), channel_id=1, source_target_pairs={{0,4},{4,8},{8,12},{12,16},{16,20},{20,24},{24,28},{28,32},{32,36}... | collective-permute-start | bytes 115592 | tf_op jit(solution)/shard_map/ppermute | solution.py:26
  50.0 4.5 %copy-start.2 = (f32[301,16,128]{2,1,0:T(8,128)}, f32[301,16,128]{2,1,0:T(8,128)S(1)}, u32[]{:S(2)}) copy-start(f32[301,16,128]{2,1,0:T(8,128)S(1)} %pad_maximum_fusion.1.after_and_out_1_.edge_ref) | copy-start | bytes 7397380
  103.5 11.7 %all-to-all-start.1 = ((f32[4,32,2,128]{3,2,0,1:T(2,128)}), f32[4,32,2,128]{3,2,0,1:T(2,128)S(1)}, u32[]{:S(2)}, u32[]{:S(2)}) async-start(f32[4,32,2,128]{3,2,0,1:T(2,128)} %copy.37), calls=%async_computation.1 | async-start | bytes 262144 | tf_op jit(solution)/shard_map/all_to_all | solution.py:330
  118.3 4.0 %collective-permute-start.6 = (f32[4,16,128]{2,0,1:T(4,128)S(1)}, f32[4,16,128]{2,0,1:T(4,128)S(1)}, u32[]{:S(2)}, u32[]{:S(2)}) collective-permute-start(f32[4,16,128]{2,0,1:T(4,128)S(1)} %scatter_fusion), channel_id=1, source_target_pairs={{0,1},{1,0},{2,3},{3,2},{4,5},{5,4},{6,7},{7,6},{8,9},{9,8},{10,11... | collective-permute-start | bytes 98312 | tf_op jit(solution)/shard_map/ppermute | solution.py:276
  122.3 5.5 %collective-permute-start.7 = (f32[4,16,128]{2,0,1:T(4,128)S(1)}, f32[4,16,128]{2,0,1:T(4,128)S(1)}, u32[]{:S(2)}, u32[]{:S(2)}) collective-permute-start(f32[4,16,128]{2,0,1:T(4,128)S(1)} %add.96), channel_id=1, source_target_pairs={{0,2},{1,3},{2,0},{3,1},{4,6},{5,7},{6,4},{7,5},{8,10},{9,11},{10,... | collective-permute-start | bytes 98312 | tf_op jit(solution)/shard_map/ppermute | solution.py:276

commit v7 on v6

--- a/solution.py
+++ b/solution.py
@@ -129,12 +129,13 @@
             below = gain * below_mix
             above = gain * above_mix
             pivot = ((1.0 + below) + above) - below * ratios[gi]
+            scale = 1.0 / pivot
             if level is not None:
-                ratio = above / pivot
+                ratio = above * scale
                 ratio_ref[gi, level] = ratio
                 new_ratios.append(ratio)
             for f in groups[gi]:
-                value = (smoothed(f, level if level is not None else levels - 1) + below * parts[f]) / pivot
+                value = (smoothed(f, level if level is not None else levels - 1) + below * parts[f]) * scale
                 out_ref[f, level if level is not None else levels - 1] = value
                 new_parts[f] = value
         return tuple(new_ratios), tuple(new_parts)
@@ -190,12 +191,10 @@
     )(jnp.asarray(decay_table), *pieces, mask, mixing_base, surface, land)
 
 
-def split_three(values):
+def split_parts(values):
     high = values.astype(jnp.bfloat16)
-    rest = values - high.astype(jnp.float32)
-    middle = rest.astype(jnp.bfloat16)
-    low = (rest - middle.astype(jnp.float32)).astype(jnp.bfloat16)
-    return high, middle, low
+    low = (values - high.astype(jnp.float32)).astype(jnp.bfloat16)
+    return high, low
 
 
 def matmul_exact(parts, other, contract):
@@ -213,7 +212,7 @@
     fields, rows, cols = out_ref.shape
     segments = stacked // fields
     items = index_ref.shape[0] // rows
-    parts = split_three(recv_ref[...])
+    parts = split_parts(recv_ref[...])
     lane_iota = lax.broadcasted_iota(jnp.int32, (lanes, cols), 0)
     segment_iota = lax.broadcasted_iota(jnp.int32, (fields, segments, cols), 1)
 
@@ -249,7 +248,7 @@
             weighted = weight_ref[pl.ds(item * rows + y, 1), :][None] * back
             hit = segment_iota == (index // lanes)[None]
             spread = jnp.where(hit, weighted, 0.0).reshape(stacked, cols)
-            total = total + matmul_exact(split_three(spread), onehot, 1)
+            total = total + matmul_exact(split_parts(spread), onehot, 1)
         return total
 
     out_ref[...] = lax.fori_loop(0, rows, row_step, jnp.zeros((stacked, lanes), jnp.float32))
@@ -330,8 +329,11 @@
     returned = lax.all_to_all(
         buffer.reshape(received.shape), "lat", split_axis=1, concat_axis=1, tiled=True
     )
-    kept = jnp.where(live_slot[None, :, :, None], returned, 0.0).reshape(4, -1, 128)
-    owner_sum = jnp.zeros_like(atm_flux).at[:, chosen.reshape(-1), :].add(kept)
+    owned_ids = lax.broadcasted_iota(jnp.int32, (owned,) + chosen.shape, 0)
+    picks = jnp.logical_and(owned_ids == chosen[None], live_slot[None]).astype(jnp.float32)
+    owner_sum = jnp.einsum(
+        "sdc,fdck->fsk", picks, returned, precision=lax.Precision.HIGHEST
+    )
     flux_adjoint = sum_over(owner_sum, "lon")
     return (state_adjoint, flux_adjoint)
 

time: 129 us -> 124 us (0.961)
  other arithmetic: 19.1 us -> 16.7 us
  Pallas kernels: 44.6 us -> 42.5 us
    scatter-add x1 -> x0, other arithmetic: 2.83 us -> none  [shards(): owner_sum = jnp.zeros_like(atm_flux).at[:, chosen.reshape(-1), :].add(kept)]
    pallas_call x2, Pallas kernels: 12.9 us -> 10.8 us  [remap_call(): pl.pallas_call(kernel, out_shape=jax.ShapeDtypeStruct(out_shape, jnp.floa...]
where the time goes in v7:
time: 124 us; the launch traced here: 123 us
  Pallas kernels  42.5 us (34%)
  starting transfers between devices  27.1 us (22%)
  waiting for transfers between devices  21.2 us (17%)
  other arithmetic  16.7 us (13%)
  local copies, waits for them, and re-layouts  14.8 us (12%)
    pallas_call x1, Pallas kernels, tridiagonal(): pl.pallas_call(tridiagonal_kernel, out_shape=(jax.ShapeDtypeStruct(shape,...  31.7 us
    ppermute x3, starting transfers between devices, from_neighbours(): lax.ppermute(lax.slice_in_dim(block, 0, width, axis=dim), axis, to_prev)  13.6 us
    pallas_call x2, Pallas kernels, remap_call(): pl.pallas_call(kernel, out_shape=jax.ShapeDtypeStruct(out_shape, jnp.floa...  10.8 us
    all_to_all x1, waiting for transfers between devices, shards(): lax.all_to_all(buffer.reshape(received.shape), 'lat', split_axis=1, conca...  7.82 us
    all_to_all x1, starting transfers between devices, shards(): lax.all_to_all(outgoing, 'lat', split_axis=1, concat_axis=1, tiled=True)  6.73 us
    ppermute x2, waiting for transfers between devices, sum_over(): values = values + lax.ppermute(values, axis, pairs)  6.53 us
    concatenate x2, other arithmetic, extended_planes(): stack = jnp.concatenate([planes, coast], axis=0)  5.41 us
    ppermute x3, waiting for transfers between devices, from_neighbours(): lax.ppermute(lax.slice_in_dim(block, size - width, size, axis=dim), axis,...  5.33 us
  transfers between devices with their start and end apart: 10, of which 5 were waited for; matrix products, arithmetic and copies ran while one was open for 13% of the time, Pallas kernels for 0%

profile of v7, /device:TPU:0, one launch (start us, length us, event | category | flops | bytes accessed | tf_op | source)
XLA Modules:
  0.0 123.3 jit_solution(17123036239774631584)
XLA Ops:
  1.4 3.5 %fusion = (f32[301,8,4]{2,1,0:T(8,128)}, f32[301,8,4]{2,1,0:T(8,128)}) fusion(f32[300,8,256]{2,1,0:T(8,128)} %bitcast.40, f32[1,8,256]{2,1,0:T(8,128)S(1)} %get-tuple-element.15), kind=kLoop, calls=%fused_computation.12 | loop fusion | flops 19264 | bytes 2542848 | tf_op jit(solution)/shard_map/concatenate | solution.py:34
  4.9 1.9 %copy.17 = f32[301,8,4]{0,1,2:T(8,128)S(1)} copy(f32[301,8,4]{2,1,0:T(8,128)} %get-tuple-element.6) | data formatting | bytes 77056 | tf_op jit(solution)/shard_map/slice | solution.py:25
  6.8 2.9 %collective-permute-start.2 = (f32[301,8,4]{0,1,2:T(8,128)S(1)}, f32[301,8,4]{0,1,2:T(8,128)S(1)}, u32[]{:S(2)}, u32[]{:S(2)}) collective-permute-start(f32[301,8,4]{0,1,2:T(8,128)S(1)} %copy.17), channel_id=1, source_target_pairs={{0,3},{1,0},{2,1},{3,2},{4,7},{5,4},{6,5},{7,6},{8,11},{9,8},{10,9... | collective-permute-start | bytes 115592 | tf_op jit(solution)/shard_map/ppermute | solution.py:25
  9.7 1.8 %copy.18 = f32[301,8,4]{0,1,2:T(8,128)S(1)} copy(f32[301,8,4]{2,1,0:T(8,128)} %get-tuple-element.7) | data formatting | bytes 77056 | tf_op jit(solution)/shard_map/slice | solution.py:26
  11.6 1.9 %fusion.1 = (f32[301,4,256]{2,1,0:T(4,128)}, f32[301,4,256]{2,1,0:T(4,128)}) fusion(f32[300,8,256]{2,1,0:T(8,128)S(1)} %bitcast.42, f32[1,8,256]{2,1,0:T(8,128)S(1)} %get-tuple-element.15), kind=kLoop, calls=%fused_computation.13 | loop fusion | flops 616448 | bytes 4931584 | tf_op jit(solution)/shard_map/concatenate | solution.py:34
  13.5 5.6 %collective-permute-start = (f32[301,4,256]{2,1,0:T(4,128)}, f32[301,4,256]{2,1,0:T(4,128)}, u32[]{:S(2)}, u32[]{:S(2)}) collective-permute-start(f32[301,4,256]{2,1,0:T(4,128)} %get-tuple-element.8), channel_id=1, source_target_pairs={{0,124},{4,0},{8,4},{12,8},{16,12},{20,16},{24,20},{28,24},{32,28}... | collective-permute-start | bytes 3698696 | tf_op jit(solution)/shard_map/ppermute | solution.py:25
  22.1 6.7 %all-to-all-start = ((f32[4,32,2,128]{3,2,0,1:T(2,128)}), f32[4,32,2,128]{3,2,0,1:T(2,128)S(1)}, u32[]{:S(2)}, u32[]{:S(2)}) async-start(f32[4,32,2,128]{3,2,0,1:T(2,128)} %bitcast.38), calls=%async_computation | async-start | bytes 262144 | tf_op jit(solution)/shard_map/all_to_all | solution.py:313
  28.9 5.0 %collective-permute-start.4 = (f32[301,4,8]{0,2,1:T(8,128)S(1)}, f32[301,4,8]{0,2,1:T(8,128)S(1)}, u32[]{:S(2)}, u32[]{:S(2)}) collective-permute-start(f32[301,4,8]{0,2,1:T(8,128)S(1)} %get-tuple-element.12), channel_id=1, source_target_pairs={{0,124},{4,0},{8,4},{12,8},{16,12},{20,16},{24,20},{28,24},{32,28}... | collective-permute-start | bytes 115592 | tf_op jit(solution)/shard_map/ppermute | solution.py:25
  34.2 1.6 %collective-permute-done.4 = f32[301,4,8]{0,2,1:T(8,128)S(1)} collective-permute-done((f32[301,4,8]{0,2,1:T(8,128)S(1)}, f32[301,4,8]{0,2,1:T(8,128)S(1)}, u32[]{:S(2)}, u32[]{:S(2)}) %collective-permute-start.4) | collective-permute-done | bytes 38560 | tf_op jit(solution)/shard_map/ppermute | solution.py:25
  35.8 5.3 %collective-permute-done.5 = f32[301,4,8]{0,2,1:T(8,128)S(1)} collective-permute-done((f32[301,4,8]{0,2,1:T(8,128)S(1)}, f32[301,4,8]{0,2,1:T(8,128)S(1)}, u32[]{:S(2)}, u32[]{:S(2)}) %collective-permute-start.5) | collective-permute-done | bytes 38560 | tf_op jit(solution)/shard_map/ppermute | solution.py:26
  41.2 2.9 %copy.21 = f32[301,16,4]{2,1,0:T(8,128)} copy(f32[301,16,4]{0,2,1:T(4,128)S(1)} %get-tuple-element.10) | data formatting | bytes 154112 | tf_op jit(solution)/shard_map/slice | solution.py:42
  44.0 2.9 %copy.22 = f32[301,16,4]{2,1,0:T(8,128)} copy(f32[301,16,4]{0,2,1:T(4,128)S(1)} %get-tuple-element.11) | data formatting | bytes 154112 | tf_op jit(solution)/shard_map/slice | solution.py:42
  46.9 3.1 %pad_maximum_fusion.1.after_and_out_1_.edge_ref = f32[301,16,128]{2,1,0:T(8,128)S(1)} fusion(f32[301,16,4]{2,1,0:T(8,128)} %copy.22, f32[301,16,4]{2,1,0:T(8,128)} %copy.21, f32[128]{0:T(128)S(1)} %pad.4.clone), kind=kLoop, calls=%fused_computation.8 | loop fusion | flops 1232896 | bytes 2620416 | tf_op jit(solution)/shard_map/concatenate | solution.py:42
  50.9 3.7 %pad_maximum_fusion.after_and_out_0_.rows_ref = f32[301,8,256]{2,1,0:T(8,128)} fusion(f32[301,4,256]{2,1,0:T(4,128)} %collective-permute-done.1, f32[301,4,256]{2,1,0:T(4,128)} %collective-permute-done), kind=kLoop, calls=%fused_computation.6 | loop fusion | flops 616448 | bytes 4931584 | tf_op jit(solution)/shard_map/concatenate | solution.py:43
  54.5 5.2 %shard_map.104 = f32[4,8,256]{2,1,0:T(8,128)} custom-call(f32[256,128]{1,0:T(8,128)} %bitcast.43, s32[32,256]{1,0:T(8,128)} %bitcast.46, f32[32,256]{1,0:T(8,128)} %bitcast.48, f32[301,8,256]{2,1,0:T(8,128)} %pad_maximum_fusion.after_and_out_0_.rows_ref, f32[301,16,128]{2,1,0:T(8,128)} %copy-done.2), custom_call_target="tpu_custom_call" | custom-call | tf_op jit(solution)/shard_map/pallas_call | solution.py:259
  59.7 1.4 %fusion.9.surf_ref = f32[8,256]{1,0:T(8,128)} fusion(f32[4,8,256]{2,1,0:T(8,128)} %shard_map.104), kind=kLoop, calls=%fused_computation.32 | loop fusion | flops 22528 | bytes 40960 | tf_op jit(solution)/shard_map/add | solution.py:324
  62.5 31.7 %shard_map.105 = (f32[4,75,8,256]{3,2,1,0:T(8,128)}, f32[4,8,256]{2,1,0:T(8,128)}) custom-call(f32[75]{0:T(128)} %constant.31.clone.decay_ref, f32[300,8,256]{2,1,0:T(8,128)} %bitcast.41, f32[301,8,256]{2,1,0:T(8,128)} %pad_maximum_fusion.after_and_out_0_.rows_ref, f32[301,16,128]{2,1,0:T(8,128)} %copy-done.2, f32[16,384]{1,0:T(8,128)} %maximum_select_fusion.mask_ref, ...), custom_call_target="tpu_custom_call" | custom-call | tf_op jit(solution)/shard_map/pallas_call | solution.py:178
  94.2 5.6 %shard_map.106 = f32[256,128]{1,0:T(8,128)} custom-call(f32[4,8,256]{2,1,0:T(8,128)} %get-tuple-element.5.back_ref, s32[32,256]{1,0:T(8,128)} %bitcast.47, f32[32,256]{1,0:T(8,128)} %bitcast.49), custom_call_target="tpu_custom_call" | custom-call | tf_op jit(solution)/shard_map/pallas_call | solution.py:259
  99.8 1.6 %copy.26 = f32[4,32,2,128]{3,2,0,1:T(2,128)} copy(f32[4,32,2,128]{3,2,1,0:T(2,128)} %bitcast.45) | data formatting | bytes 262144 | tf_op jit(solution)/shard_map/reshape | solution.py:330
  101.4 3.9 %all-to-all-start.1 = ((f32[4,32,2,128]{3,2,0,1:T(2,128)}), f32[4,32,2,128]{3,2,0,1:T(2,128)S(1)}, u32[]{:S(2)}, u32[]{:S(2)}) async-start(f32[4,32,2,128]{3,2,0,1:T(2,128)} %copy.26), calls=%async_computation.1 | async-start | bytes 262144 | tf_op jit(solution)/shard_map/all_to_all | solution.py:329
  105.3 7.8 %all-to-all-done.1 = f32[4,32,2,128]{3,2,0,1:T(2,128)S(1)} async-done(((f32[4,32,2,128]{3,2,0,1:T(2,128)}), f32[4,32,2,128]{3,2,0,1:T(2,128)S(1)}, u32[]{:S(2)}, u32[]{:S(2)}) %all-to-all-start.1) | async-done | bytes 131104 | tf_op jit(solution)/shard_map/all_to_all | solution.py:329
  113.8 3.5 %collective-permute-done.6 = f32[4,16,128]{2,1,0:T(8,128)S(1)} collective-permute-done((f32[4,16,128]{2,1,0:T(8,128)S(1)}, f32[4,16,128]{2,1,0:T(8,128)S(1)}, u32[]{:S(2)}, u32[]{:S(2)}) %collective-permute-start.6) | collective-permute-done | bytes 32800 | tf_op jit(solution)/shard_map/ppermute | solution.py:275
  117.3 2.4 %collective-permute-start.7 = (f32[4,16,128]{2,1,0:T(8,128)S(1)}, f32[4,16,128]{2,1,0:T(8,128)S(1)}, u32[]{:S(2)}, u32[]{:S(2)}) collective-permute-start(f32[4,16,128]{2,1,0:T(8,128)S(1)} %add.79), channel_id=1, source_target_pairs={{0,2},{1,3},{2,0},{3,1},{4,6},{5,7},{6,4},{7,5},{8,10},{9,11},{10,... | collective-permute-start | bytes 98312 | tf_op jit(solution)/shard_map/ppermute | solution.py:275
  119.6 3.1 %collective-permute-done.7 = f32[4,16,128]{2,1,0:T(8,128)S(1)} collective-permute-done((f32[4,16,128]{2,1,0:T(8,128)S(1)}, f32[4,16,128]{2,1,0:T(8,128)S(1)}, u32[]{:S(2)}, u32[]{:S(2)}) %collective-permute-start.7) | collective-permute-done | bytes 32800 | tf_op jit(solution)/shard_map/ppermute | solution.py:275
  (54 shorter events, 7.6 us)
Async XLA Ops:
  0.6 20.0 %copy-start = (f32[4,16,128]{2,1,0:T(8,128)S(1)}, f32[4,16,128]{2,1,0:T(8,128)}, u32[]{:S(2)}) copy-start(f32[4,16,128]{2,1,0:T(8,128)} %param.11) | copy-start | bytes 98308
  1.4 60.5 %copy-start.4 = (f32[8,256]{1,0:T(8,128)}, f32[8,256]{1,0:T(8,128)S(1)}, u32[]{:S(2)}) copy-start(f32[8,256]{1,0:T(8,128)S(1)} %get-tuple-element.14.land_ref) | copy-start | bytes 24580
  4.9 6.7 %copy-start.3 = (f32[4,75,8,256]{3,2,1,0:T(8,128)S(1)}, f32[4,75,8,256]{3,2,1,0:T(8,128)}, u32[]{:S(2)}) copy-start(f32[4,75,8,256]{3,2,1,0:T(8,128)} %param.9) | copy-start | bytes 7372804
  6.8 22.1 %collective-permute-start.2 = (f32[301,8,4]{0,1,2:T(8,128)S(1)}, f32[301,8,4]{0,1,2:T(8,128)S(1)}, u32[]{:S(2)}, u32[]{:S(2)}) collective-permute-start(f32[301,8,4]{0,1,2:T(8,128)S(1)} %copy.17), channel_id=1, source_target_pairs={{0,3},{1,0},{2,1},{3,2},{4,7},{5,4},{6,5},{7,6},{8,11},{9,8},{10,9... | collective-permute-start | bytes 115592 | tf_op jit(solution)/shard_map/ppermute | solution.py:25
  11.5 7.7 %copy-start.5 = (s32[1,32]{1,0:T(1,128)S(1)}, s32[1,32]{1,0:T(1,128)}, u32[]{:S(2)}) copy-start(s32[1,32]{1,0:T(1,128)} %param.12) | copy-start | bytes 388
  11.5 8.1 %copy-start.1 = (s32[1,64]{1,0:T(1,128)S(1)}, s32[1,64]{1,0:T(1,128)}, u32[]{:S(2)}) copy-start(s32[1,64]{1,0:T(1,128)} %param.13) | copy-start | bytes 772
  11.5 17.4 %collective-permute-start.3 = (f32[301,8,4]{0,1,2:T(8,128)S(1)}, f32[301,8,4]{0,1,2:T(8,128)S(1)}, u32[]{:S(2)}, u32[]{:S(2)}) collective-permute-start(f32[301,8,4]{0,1,2:T(8,128)S(1)} %copy.18), channel_id=1, source_target_pairs={{0,1},{1,2},{2,3},{3,0},{4,5},{5,6},{6,7},{7,4},{8,9},{9,10},{10,1... | collective-permute-start | bytes 115592 | tf_op jit(solution)/shard_map/ppermute | solution.py:26
  13.5 37.4 %collective-permute-start = (f32[301,4,256]{2,1,0:T(4,128)}, f32[301,4,256]{2,1,0:T(4,128)}, u32[]{:S(2)}, u32[]{:S(2)}) collective-permute-start(f32[301,4,256]{2,1,0:T(4,128)} %get-tuple-element.8), channel_id=1, source_target_pairs={{0,124},{4,0},{8,4},{12,8},{16,12},{20,16},{24,20},{28,24},{32,28}... | collective-permute-start | bytes 3698696 | tf_op jit(solution)/shard_map/ppermute | solution.py:25
  19.1 31.7 %collective-permute-start.1 = (f32[301,4,256]{2,1,0:T(4,128)}, f32[301,4,256]{2,1,0:T(4,128)}, u32[]{:S(2)}, u32[]{:S(2)}) collective-permute-start(f32[301,4,256]{2,1,0:T(4,128)} %get-tuple-element.9), channel_id=1, source_target_pairs={{0,4},{4,8},{8,12},{12,16},{16,20},{20,24},{24,28},{28,32},{32,36}... | collective-permute-start | bytes 3698696 | tf_op jit(solution)/shard_map/ppermute | solution.py:26
  22.1 27.9 %all-to-all-start = ((f32[4,32,2,128]{3,2,0,1:T(2,128)}), f32[4,32,2,128]{3,2,0,1:T(2,128)S(1)}, u32[]{:S(2)}, u32[]{:S(2)}) async-start(f32[4,32,2,128]{3,2,0,1:T(2,128)} %bitcast.38), calls=%async_computation | async-start | bytes 262144 | tf_op jit(solution)/shard_map/all_to_all | solution.py:313
  28.9 6.8 %collective-permute-start.4 = (f32[301,4,8]{0,2,1:T(8,128)S(1)}, f32[301,4,8]{0,2,1:T(8,128)S(1)}, u32[]{:S(2)}, u32[]{:S(2)}) collective-permute-start(f32[301,4,8]{0,2,1:T(8,128)S(1)} %get-tuple-element.12), channel_id=1, source_target_pairs={{0,124},{4,0},{8,4},{12,8},{16,12},{20,16},{24,20},{28,24},{32,28}... | collective-permute-start | bytes 115592 | tf_op jit(solution)/shard_map/ppermute | solution.py:25
  33.9 7.2 %collective-permute-start.5 = (f32[301,4,8]{0,2,1:T(8,128)S(1)}, f32[301,4,8]{0,2,1:T(8,128)S(1)}, u32[]{:S(2)}, u32[]{:S(2)}) collective-permute-start(f32[301,4,8]{0,2,1:T(8,128)S(1)} %get-tuple-element.13), channel_id=1, source_target_pairs={{0,4},{4,8},{8,12},{12,16},{16,20},{20,24},{24,28},{28,32},{32,36}... | collective-permute-start | bytes 115592 | tf_op jit(solution)/shard_map/ppermute | solution.py:26
  50.0 4.5 %copy-start.2 = (f32[301,16,128]{2,1,0:T(8,128)}, f32[301,16,128]{2,1,0:T(8,128)S(1)}, u32[]{:S(2)}) copy-start(f32[301,16,128]{2,1,0:T(8,128)S(1)} %pad_maximum_fusion.1.after_and_out_1_.edge_ref) | copy-start | bytes 7397380
  101.4 11.7 %all-to-all-start.1 = ((f32[4,32,2,128]{3,2,0,1:T(2,128)}), f32[4,32,2,128]{3,2,0,1:T(2,128)S(1)}, u32[]{:S(2)}, u32[]{:S(2)}) async-start(f32[4,32,2,128]{3,2,0,1:T(2,128)} %copy.26), calls=%async_computation.1 | async-start | bytes 262144 | tf_op jit(solution)/shard_map/all_to_all | solution.py:329
  113.3 4.0 %collective-permute-start.6 = (f32[4,16,128]{2,1,0:T(8,128)S(1)}, f32[4,16,128]{2,1,0:T(8,128)S(1)}, u32[]{:S(2)}, u32[]{:S(2)}) collective-permute-start(f32[4,16,128]{2,1,0:T(8,128)S(1)} %convolution_bitcast_fusion), channel_id=1, source_target_pairs={{0,1},{1,0},{2,3},{3,2},{4,5},{5,4},{6,7},{7,6},{8,9},{9,8},{10,11... | collective-permute-start | bytes 98312 | tf_op jit(solution)/shard_map/ppermute | solution.py:275
  117.3 5.4 %collective-permute-start.7 = (f32[4,16,128]{2,1,0:T(8,128)S(1)}, f32[4,16,128]{2,1,0:T(8,128)S(1)}, u32[]{:S(2)}, u32[]{:S(2)}) collective-permute-start(f32[4,16,128]{2,1,0:T(8,128)S(1)} %add.79), channel_id=1, source_target_pairs={{0,2},{1,3},{2,0},{3,1},{4,6},{5,7},{6,4},{7,5},{8,10},{9,11},{10,... | collective-permute-start | bytes 98312 | tf_op jit(solution)/shard_map/ppermute | solution.py:275

commit v8 on v7

--- a/solution.py
+++ b/solution.py
@@ -147,7 +147,7 @@
         return (mix, ratios, parts)
 
     carry = (zero, tuple(zero for _ in gains), tuple(zero for _ in range(fields)))
-    last_mix, ratios, parts = lax.fori_loop(0, levels - 1, forward, carry)
+    last_mix, ratios, parts = lax.fori_loop(0, levels - 1, forward, carry, unroll=2)
     step(None, last_mix, zero, ratios, parts)
 
     def backward(i, later):
@@ -163,7 +163,7 @@
         return tuple(v for _, v in result)
 
     final = tuple(out_ref[f, levels - 1] for f in range(fields))
-    lax.fori_loop(0, levels - 1, backward, final)
+    lax.fori_loop(0, levels - 1, backward, final, unroll=2)
     land = land_ref[...]
     for f in range(fields):
         back_ref[f] = land * out_ref[f, 0]

time: 124 us -> 127 us (1.024)
  Pallas kernels: 42.5 us -> 46 us
    pallas_call x1, Pallas kernels: 31.7 us -> 35.2 us  [tridiagonal(): pl.pallas_call(tridiagonal_kernel, out_shape=(jax.ShapeDtypeStruct(shape,...]
where the time goes in v8:
time: 127 us
  Pallas kernels  46 us (36%)
  starting transfers between devices  27.1 us (21%)
  waiting for transfers between devices  21.2 us (17%)
  other arithmetic  16.7 us (13%)
  local copies, waits for them, and re-layouts  14.8 us (12%)
    pallas_call x1, Pallas kernels, tridiagonal(): pl.pallas_call(tridiagonal_kernel, out_shape=(jax.ShapeDtypeStruct(shape,...  35.2 us
    ppermute x3, starting transfers between devices, from_neighbours(): lax.ppermute(lax.slice_in_dim(block, 0, width, axis=dim), axis, to_prev)  13.6 us
    pallas_call x2, Pallas kernels, remap_call(): pl.pallas_call(kernel, out_shape=jax.ShapeDtypeStruct(out_shape, jnp.floa...  10.8 us
    all_to_all x1, waiting for transfers between devices, shards(): lax.all_to_all(buffer.reshape(received.shape), 'lat', split_axis=1, conca...  7.82 us
    all_to_all x1, starting transfers between devices, shards(): lax.all_to_all(outgoing, 'lat', split_axis=1, concat_axis=1, tiled=True)  6.73 us
    ppermute x2, waiting for transfers between devices, sum_over(): values = values + lax.ppermute(values, axis, pairs)  6.53 us
    concatenate x2, other arithmetic, extended_planes(): stack = jnp.concatenate([planes, coast], axis=0)  5.41 us
    ppermute x3, waiting for transfers between devices, from_neighbours(): lax.ppermute(lax.slice_in_dim(block, size - width, size, axis=dim), axis,...  5.33 us
  transfers between devices with their start and end apart: 10, of which 5 were waited for; matrix products, arithmetic and copies ran while one was open for 13% of the time, Pallas kernels for 0%

profile of v8, /device:TPU:0, one launch (start us, length us, event | category | flops | bytes accessed | tf_op | source)
XLA Modules:
  0.0 126.8 jit_solution(5060392013553361906)
XLA Ops:
  1.4 3.5 %fusion = (f32[301,8,4]{2,1,0:T(8,128)}, f32[301,8,4]{2,1,0:T(8,128)}) fusion(f32[300,8,256]{2,1,0:T(8,128)} %bitcast.40, f32[1,8,256]{2,1,0:T(8,128)S(1)} %get-tuple-element.15), kind=kLoop, calls=%fused_computation.12 | loop fusion | flops 19264 | bytes 2542848 | tf_op jit(solution)/shard_map/concatenate | solution.py:34
  4.9 1.9 %copy.17 = f32[301,8,4]{0,1,2:T(8,128)S(1)} copy(f32[301,8,4]{2,1,0:T(8,128)} %get-tuple-element.6) | data formatting | bytes 77056 | tf_op jit(solution)/shard_map/slice | solution.py:25
  6.8 2.9 %collective-permute-start.2 = (f32[301,8,4]{0,1,2:T(8,128)S(1)}, f32[301,8,4]{0,1,2:T(8,128)S(1)}, u32[]{:S(2)}, u32[]{:S(2)}) collective-permute-start(f32[301,8,4]{0,1,2:T(8,128)S(1)} %copy.17), channel_id=1, source_target_pairs={{0,3},{1,0},{2,1},{3,2},{4,7},{5,4},{6,5},{7,6},{8,11},{9,8},{10,9... | collective-permute-start | bytes 115592 | tf_op jit(solution)/shard_map/ppermute | solution.py:25
  9.7 1.8 %copy.18 = f32[301,8,4]{0,1,2:T(8,128)S(1)} copy(f32[301,8,4]{2,1,0:T(8,128)} %get-tuple-element.7) | data formatting | bytes 77056 | tf_op jit(solution)/shard_map/slice | solution.py:26
  11.6 1.9 %fusion.1 = (f32[301,4,256]{2,1,0:T(4,128)}, f32[301,4,256]{2,1,0:T(4,128)}) fusion(f32[300,8,256]{2,1,0:T(8,128)S(1)} %bitcast.42, f32[1,8,256]{2,1,0:T(8,128)S(1)} %get-tuple-element.15), kind=kLoop, calls=%fused_computation.13 | loop fusion | flops 616448 | bytes 4931584 | tf_op jit(solution)/shard_map/concatenate | solution.py:34
  13.5 5.6 %collective-permute-start = (f32[301,4,256]{2,1,0:T(4,128)}, f32[301,4,256]{2,1,0:T(4,128)}, u32[]{:S(2)}, u32[]{:S(2)}) collective-permute-start(f32[301,4,256]{2,1,0:T(4,128)} %get-tuple-element.8), channel_id=1, source_target_pairs={{0,124},{4,0},{8,4},{12,8},{16,12},{20,16},{24,20},{28,24},{32,28}... | collective-permute-start | bytes 3698696 | tf_op jit(solution)/shard_map/ppermute | solution.py:25
  22.1 6.7 %all-to-all-start = ((f32[4,32,2,128]{3,2,0,1:T(2,128)}), f32[4,32,2,128]{3,2,0,1:T(2,128)S(1)}, u32[]{:S(2)}, u32[]{:S(2)}) async-start(f32[4,32,2,128]{3,2,0,1:T(2,128)} %bitcast.38), calls=%async_computation | async-start | bytes 262144 | tf_op jit(solution)/shard_map/all_to_all | solution.py:313
  28.9 5.0 %collective-permute-start.4 = (f32[301,4,8]{0,2,1:T(8,128)S(1)}, f32[301,4,8]{0,2,1:T(8,128)S(1)}, u32[]{:S(2)}, u32[]{:S(2)}) collective-permute-start(f32[301,4,8]{0,2,1:T(8,128)S(1)} %get-tuple-element.12), channel_id=1, source_target_pairs={{0,124},{4,0},{8,4},{12,8},{16,12},{20,16},{24,20},{28,24},{32,28}... | collective-permute-start | bytes 115592 | tf_op jit(solution)/shard_map/ppermute | solution.py:25
  34.2 1.6 %collective-permute-done.4 = f32[301,4,8]{0,2,1:T(8,128)S(1)} collective-permute-done((f32[301,4,8]{0,2,1:T(8,128)S(1)}, f32[301,4,8]{0,2,1:T(8,128)S(1)}, u32[]{:S(2)}, u32[]{:S(2)}) %collective-permute-start.4) | collective-permute-done | bytes 38560 | tf_op jit(solution)/shard_map/ppermute | solution.py:25
  35.8 5.3 %collective-permute-done.5 = f32[301,4,8]{0,2,1:T(8,128)S(1)} collective-permute-done((f32[301,4,8]{0,2,1:T(8,128)S(1)}, f32[301,4,8]{0,2,1:T(8,128)S(1)}, u32[]{:S(2)}, u32[]{:S(2)}) %collective-permute-start.5) | collective-permute-done | bytes 38560 | tf_op jit(solution)/shard_map/ppermute | solution.py:26
  41.2 2.9 %copy.21 = f32[301,16,4]{2,1,0:T(8,128)} copy(f32[301,16,4]{0,2,1:T(4,128)S(1)} %get-tuple-element.10) | data formatting | bytes 154112 | tf_op jit(solution)/shard_map/slice | solution.py:42
  44.0 2.9 %copy.22 = f32[301,16,4]{2,1,0:T(8,128)} copy(f32[301,16,4]{0,2,1:T(4,128)S(1)} %get-tuple-element.11) | data formatting | bytes 154112 | tf_op jit(solution)/shard_map/slice | solution.py:42
  46.9 3.1 %pad_maximum_fusion.1.after_and_out_1_.edge_ref = f32[301,16,128]{2,1,0:T(8,128)S(1)} fusion(f32[301,16,4]{2,1,0:T(8,128)} %copy.22, f32[301,16,4]{2,1,0:T(8,128)} %copy.21, f32[128]{0:T(128)S(1)} %pad.4.clone), kind=kLoop, calls=%fused_computation.8 | loop fusion | flops 1232896 | bytes 2620416 | tf_op jit(solution)/shard_map/concatenate | solution.py:42
  50.9 3.7 %pad_maximum_fusion.after_and_out_0_.rows_ref = f32[301,8,256]{2,1,0:T(8,128)} fusion(f32[301,4,256]{2,1,0:T(4,128)} %collective-permute-done.1, f32[301,4,256]{2,1,0:T(4,128)} %collective-permute-done), kind=kLoop, calls=%fused_computation.6 | loop fusion | flops 616448 | bytes 4931584 | tf_op jit(solution)/shard_map/concatenate | solution.py:43
  54.5 5.2 %shard_map.104 = f32[4,8,256]{2,1,0:T(8,128)} custom-call(f32[256,128]{1,0:T(8,128)} %bitcast.43, s32[32,256]{1,0:T(8,128)} %bitcast.46, f32[32,256]{1,0:T(8,128)} %bitcast.48, f32[301,8,256]{2,1,0:T(8,128)} %pad_maximum_fusion.after_and_out_0_.rows_ref, f32[301,16,128]{2,1,0:T(8,128)} %copy-done.2), custom_call_target="tpu_custom_call" | custom-call | tf_op jit(solution)/shard_map/pallas_call | solution.py:259
  59.7 1.4 %fusion.9.surf_ref = f32[8,256]{1,0:T(8,128)} fusion(f32[4,8,256]{2,1,0:T(8,128)} %shard_map.104), kind=kLoop, calls=%fused_computation.32 | loop fusion | flops 22528 | bytes 40960 | tf_op jit(solution)/shard_map/add | solution.py:324
  62.5 35.2 %shard_map.105 = (f32[4,75,8,256]{3,2,1,0:T(8,128)}, f32[4,8,256]{2,1,0:T(8,128)}) custom-call(f32[75]{0:T(128)} %constant.31.clone.decay_ref, f32[300,8,256]{2,1,0:T(8,128)} %bitcast.41, f32[301,8,256]{2,1,0:T(8,128)} %pad_maximum_fusion.after_and_out_0_.rows_ref, f32[301,16,128]{2,1,0:T(8,128)} %copy-done.2, f32[16,384]{1,0:T(8,128)} %maximum_select_fusion.mask_ref, ...), custom_call_target="tpu_custom_call" | custom-call | tf_op jit(solution)/shard_map/pallas_call | solution.py:178
  97.7 5.6 %shard_map.106 = f32[256,128]{1,0:T(8,128)} custom-call(f32[4,8,256]{2,1,0:T(8,128)} %get-tuple-element.5.back_ref, s32[32,256]{1,0:T(8,128)} %bitcast.47, f32[32,256]{1,0:T(8,128)} %bitcast.49), custom_call_target="tpu_custom_call" | custom-call | tf_op jit(solution)/shard_map/pallas_call | solution.py:259
  103.3 1.6 %copy.26 = f32[4,32,2,128]{3,2,0,1:T(2,128)} copy(f32[4,32,2,128]{3,2,1,0:T(2,128)} %bitcast.45) | data formatting | bytes 262144 | tf_op jit(solution)/shard_map/reshape | solution.py:330
  104.9 3.9 %all-to-all-start.1 = ((f32[4,32,2,128]{3,2,0,1:T(2,128)}), f32[4,32,2,128]{3,2,0,1:T(2,128)S(1)}, u32[]{:S(2)}, u32[]{:S(2)}) async-start(f32[4,32,2,128]{3,2,0,1:T(2,128)} %copy.26), calls=%async_computation.1 | async-start | bytes 262144 | tf_op jit(solution)/shard_map/all_to_all | solution.py:329
  108.8 7.8 %all-to-all-done.1 = f32[4,32,2,128]{3,2,0,1:T(2,128)S(1)} async-done(((f32[4,32,2,128]{3,2,0,1:T(2,128)}), f32[4,32,2,128]{3,2,0,1:T(2,128)S(1)}, u32[]{:S(2)}, u32[]{:S(2)}) %all-to-all-start.1) | async-done | bytes 131104 | tf_op jit(solution)/shard_map/all_to_all | solution.py:329
  117.3 3.5 %collective-permute-done.6 = f32[4,16,128]{2,1,0:T(8,128)S(1)} collective-permute-done((f32[4,16,128]{2,1,0:T(8,128)S(1)}, f32[4,16,128]{2,1,0:T(8,128)S(1)}, u32[]{:S(2)}, u32[]{:S(2)}) %collective-permute-start.6) | collective-permute-done | bytes 32800 | tf_op jit(solution)/shard_map/ppermute | solution.py:275
  120.8 2.4 %collective-permute-start.7 = (f32[4,16,128]{2,1,0:T(8,128)S(1)}, f32[4,16,128]{2,1,0:T(8,128)S(1)}, u32[]{:S(2)}, u32[]{:S(2)}) collective-permute-start(f32[4,16,128]{2,1,0:T(8,128)S(1)} %add.79), channel_id=1, source_target_pairs={{0,2},{1,3},{2,0},{3,1},{4,6},{5,7},{6,4},{7,5},{8,10},{9,11},{10,... | collective-permute-start | bytes 98312 | tf_op jit(solution)/shard_map/ppermute | solution.py:275
  123.1 3.1 %collective-permute-done.7 = f32[4,16,128]{2,1,0:T(8,128)S(1)} collective-permute-done((f32[4,16,128]{2,1,0:T(8,128)S(1)}, f32[4,16,128]{2,1,0:T(8,128)S(1)}, u32[]{:S(2)}, u32[]{:S(2)}) %collective-permute-start.7) | collective-permute-done | bytes 32800 | tf_op jit(solution)/shard_map/ppermute | solution.py:275
  (54 shorter events, 7.6 us)
Async XLA Ops:
  0.6 20.0 %copy-start = (f32[4,16,128]{2,1,0:T(8,128)S(1)}, f32[4,16,128]{2,1,0:T(8,128)}, u32[]{:S(2)}) copy-start(f32[4,16,128]{2,1,0:T(8,128)} %param.11) | copy-start | bytes 98308
  1.4 60.5 %copy-start.4 = (f32[8,256]{1,0:T(8,128)}, f32[8,256]{1,0:T(8,128)S(1)}, u32[]{:S(2)}) copy-start(f32[8,256]{1,0:T(8,128)S(1)} %get-tuple-element.14.land_ref) | copy-start | bytes 24580
  4.9 6.7 %copy-start.3 = (f32[4,75,8,256]{3,2,1,0:T(8,128)S(1)}, f32[4,75,8,256]{3,2,1,0:T(8,128)}, u32[]{:S(2)}) copy-start(f32[4,75,8,256]{3,2,1,0:T(8,128)} %param.9) | copy-start | bytes 7372804
  6.8 22.1 %collective-permute-start.2 = (f32[301,8,4]{0,1,2:T(8,128)S(1)}, f32[301,8,4]{0,1,2:T(8,128)S(1)}, u32[]{:S(2)}, u32[]{:S(2)}) collective-permute-start(f32[301,8,4]{0,1,2:T(8,128)S(1)} %copy.17), channel_id=1, source_target_pairs={{0,3},{1,0},{2,1},{3,2},{4,7},{5,4},{6,5},{7,6},{8,11},{9,8},{10,9... | collective-permute-start | bytes 115592 | tf_op jit(solution)/shard_map/ppermute | solution.py:25
  11.5 7.7 %copy-start.5 = (s32[1,32]{1,0:T(1,128)S(1)}, s32[1,32]{1,0:T(1,128)}, u32[]{:S(2)}) copy-start(s32[1,32]{1,0:T(1,128)} %param.12) | copy-start | bytes 388
  11.5 8.1 %copy-start.1 = (s32[1,64]{1,0:T(1,128)S(1)}, s32[1,64]{1,0:T(1,128)}, u32[]{:S(2)}) copy-start(s32[1,64]{1,0:T(1,128)} %param.13) | copy-start | bytes 772
  11.5 17.4 %collective-permute-start.3 = (f32[301,8,4]{0,1,2:T(8,128)S(1)}, f32[301,8,4]{0,1,2:T(8,128)S(1)}, u32[]{:S(2)}, u32[]{:S(2)}) collective-permute-start(f32[301,8,4]{0,1,2:T(8,128)S(1)} %copy.18), channel_id=1, source_target_pairs={{0,1},{1,2},{2,3},{3,0},{4,5},{5,6},{6,7},{7,4},{8,9},{9,10},{10,1... | collective-permute-start | bytes 115592 | tf_op jit(solution)/shard_map/ppermute | solution.py:26
  13.5 37.4 %collective-permute-start = (f32[301,4,256]{2,1,0:T(4,128)}, f32[301,4,256]{2,1,0:T(4,128)}, u32[]{:S(2)}, u32[]{:S(2)}) collective-permute-start(f32[301,4,256]{2,1,0:T(4,128)} %get-tuple-element.8), channel_id=1, source_target_pairs={{0,124},{4,0},{8,4},{12,8},{16,12},{20,16},{24,20},{28,24},{32,28}... | collective-permute-start | bytes 3698696 | tf_op jit(solution)/shard_map/ppermute | solution.py:25
  19.1 31.7 %collective-permute-start.1 = (f32[301,4,256]{2,1,0:T(4,128)}, f32[301,4,256]{2,1,0:T(4,128)}, u32[]{:S(2)}, u32[]{:S(2)}) collective-permute-start(f32[301,4,256]{2,1,0:T(4,128)} %get-tuple-element.9), channel_id=1, source_target_pairs={{0,4},{4,8},{8,12},{12,16},{16,20},{20,24},{24,28},{28,32},{32,36}... | collective-permute-start | bytes 3698696 | tf_op jit(solution)/shard_map/ppermute | solution.py:26
  22.1 27.9 %all-to-all-start = ((f32[4,32,2,128]{3,2,0,1:T(2,128)}), f32[4,32,2,128]{3,2,0,1:T(2,128)S(1)}, u32[]{:S(2)}, u32[]{:S(2)}) async-start(f32[4,32,2,128]{3,2,0,1:T(2,128)} %bitcast.38), calls=%async_computation | async-start | bytes 262144 | tf_op jit(solution)/shard_map/all_to_all | solution.py:313
  28.9 6.8 %collective-permute-start.4 = (f32[301,4,8]{0,2,1:T(8,128)S(1)}, f32[301,4,8]{0,2,1:T(8,128)S(1)}, u32[]{:S(2)}, u32[]{:S(2)}) collective-permute-start(f32[301,4,8]{0,2,1:T(8,128)S(1)} %get-tuple-element.12), channel_id=1, source_target_pairs={{0,124},{4,0},{8,4},{12,8},{16,12},{20,16},{24,20},{28,24},{32,28}... | collective-permute-start | bytes 115592 | tf_op jit(solution)/shard_map/ppermute | solution.py:25
  33.9 7.2 %collective-permute-start.5 = (f32[301,4,8]{0,2,1:T(8,128)S(1)}, f32[301,4,8]{0,2,1:T(8,128)S(1)}, u32[]{:S(2)}, u32[]{:S(2)}) collective-permute-start(f32[301,4,8]{0,2,1:T(8,128)S(1)} %get-tuple-element.13), channel_id=1, source_target_pairs={{0,4},{4,8},{8,12},{12,16},{16,20},{20,24},{24,28},{28,32},{32,36}... | collective-permute-start | bytes 115592 | tf_op jit(solution)/shard_map/ppermute | solution.py:26
  50.0 4.5 %copy-start.2 = (f32[301,16,128]{2,1,0:T(8,128)}, f32[301,16,128]{2,1,0:T(8,128)S(1)}, u32[]{:S(2)}) copy-start(f32[301,16,128]{2,1,0:T(8,128)S(1)} %pad_maximum_fusion.1.after_and_out_1_.edge_ref) | copy-start | bytes 7397380
  104.9 11.7 %all-to-all-start.1 = ((f32[4,32,2,128]{3,2,0,1:T(2,128)}), f32[4,32,2,128]{3,2,0,1:T(2,128)S(1)}, u32[]{:S(2)}, u32[]{:S(2)}) async-start(f32[4,32,2,128]{3,2,0,1:T(2,128)} %copy.26), calls=%async_computation.1 | async-start | bytes 262144 | tf_op jit(solution)/shard_map/all_to_all | solution.py:329
  116.8 4.0 %collective-permute-start.6 = (f32[4,16,128]{2,1,0:T(8,128)S(1)}, f32[4,16,128]{2,1,0:T(8,128)S(1)}, u32[]{:S(2)}, u32[]{:S(2)}) collective-permute-start(f32[4,16,128]{2,1,0:T(8,128)S(1)} %convolution_bitcast_fusion), channel_id=1, source_target_pairs={{0,1},{1,0},{2,3},{3,2},{4,5},{5,4},{6,7},{7,6},{8,9},{9,8},{10,11... | collective-permute-start | bytes 98312 | tf_op jit(solution)/shard_map/ppermute | solution.py:275
  120.8 5.4 %collective-permute-start.7 = (f32[4,16,128]{2,1,0:T(8,128)S(1)}, f32[4,16,128]{2,1,0:T(8,128)S(1)}, u32[]{:S(2)}, u32[]{:S(2)}) collective-permute-start(f32[4,16,128]{2,1,0:T(8,128)S(1)} %add.79), channel_id=1, source_target_pairs={{0,2},{1,3},{2,0},{3,1},{4,6},{5,7},{6,4},{7,5},{8,10},{9,11},{10,... | collective-permute-start | bytes 98312 | tf_op jit(solution)/shard_map/ppermute | solution.py:275

commit v9 on v7

--- a/solution.py
+++ b/solution.py
@@ -135,7 +135,7 @@
                 ratio_ref[gi, level] = ratio
                 new_ratios.append(ratio)
             for f in groups[gi]:
-                value = (smoothed(f, level if level is not None else levels - 1) + below * parts[f]) * scale
+                value = (out_ref[f, level if level is not None else levels - 1] + below * parts[f]) * scale
                 out_ref[f, level if level is not None else levels - 1] = value
                 new_parts[f] = value
         return tuple(new_ratios), tuple(new_parts)
@@ -146,6 +146,13 @@
         ratios, parts = step(level, below_mix, mix, ratios, parts)
         return (mix, ratios, parts)
 
+    def smooth_plane(plane, carry):
+        f = plane // levels
+        level = plane % levels
+        out_ref[f, level] = smoothed(f, level)
+        return carry
+
+    lax.fori_loop(0, fields * levels, smooth_plane, 0)
     carry = (zero, tuple(zero for _ in gains), tuple(zero for _ in range(fields)))
     last_mix, ratios, parts = lax.fori_loop(0, levels - 1, forward, carry)
     step(None, last_mix, zero, ratios, parts)

time: 124 us -> 193 us (1.56)
  Pallas kernels: 42.5 us -> 112 us
    pallas_call x1, Pallas kernels: 31.7 us -> 101 us  [tridiagonal(): pl.pallas_call(tridiagonal_kernel, out_shape=(jax.ShapeDtypeStruct(shape,...]
  transfers between devices with their start and end apart: 10 -> 10, of which waited for: 5 -> 5; matrix products, arithmetic and copies ran while one was open for 13% -> 9% of each run, Pallas kernels for 0% -> 0%
where the time goes in v9:
time: 193 us
  Pallas kernels  112 us (58%)
  starting transfers between devices  27.1 us (14%)
  waiting for transfers between devices  21.2 us (11%)
  other arithmetic  16.7 us (9%)
  local copies, waits for them, and re-layouts  14.8 us (8%)
    pallas_call x1, Pallas kernels, tridiagonal(): pl.pallas_call(tridiagonal_kernel, out_shape=(jax.ShapeDtypeStruct(shape,...  101 us
    ppermute x3, starting transfers between devices, from_neighbours(): lax.ppermute(lax.slice_in_dim(block, 0, width, axis=dim), axis, to_prev)  13.6 us
    pallas_call x2, Pallas kernels, remap_call(): pl.pallas_call(kernel, out_shape=jax.ShapeDtypeStruct(out_shape, jnp.floa...  10.8 us
    all_to_all x1, waiting for transfers between devices, shards(): lax.all_to_all(buffer.reshape(received.shape), 'lat', split_axis=1, conca...  7.82 us
    all_to_all x1, starting transfers between devices, shards(): lax.all_to_all(outgoing, 'lat', split_axis=1, concat_axis=1, tiled=True)  6.73 us
    ppermute x2, waiting for transfers between devices, sum_over(): values = values + lax.ppermute(values, axis, pairs)  6.53 us
    concatenate x2, other arithmetic, extended_planes(): stack = jnp.concatenate([planes, coast], axis=0)  5.41 us
    ppermute x3, waiting for transfers between devices, from_neighbours(): lax.ppermute(lax.slice_in_dim(block, size - width, size, axis=dim), axis,...  5.33 us
  transfers between devices with their start and end apart: 10, of which 5 were waited for; matrix products, arithmetic and copies ran while one was open for 9% of the time, Pallas kernels for 0%

profile of v9, /device:TPU:0, one launch (start us, length us, event | category | flops | bytes accessed | tf_op | source)
XLA Modules:
  0.0 192.6 jit_solution(7438392591892628390)
XLA Ops:
  1.4 3.5 %fusion = (f32[301,8,4]{2,1,0:T(8,128)}, f32[301,8,4]{2,1,0:T(8,128)}) fusion(f32[300,8,256]{2,1,0:T(8,128)} %bitcast.40, f32[1,8,256]{2,1,0:T(8,128)S(1)} %get-tuple-element.15), kind=kLoop, calls=%fused_computation.12 | loop fusion | flops 19264 | bytes 2542848 | tf_op jit(solution)/shard_map/concatenate | solution.py:34
  4.9 1.9 copy.17
  6.8 2.9 %collective-permute-start.2 = (f32[301,8,4]{0,1,2:T(8,128)S(1)}, f32[301,8,4]{0,1,2:T(8,128)S(1)}, u32[]{:S(2)}, u32[]{:S(2)}) collective-permute-start(f32[301,8,4]{0,1,2:T(8,128)S(1)} %copy.17), channel_id=1, source_target_pairs={{0,3},{1,0},{2,1},{3,2},{4,7},{5,4},{6,5},{7,6},{8,11},{9,8},{10,9... | collective-permute-start | bytes 115592 | tf_op jit(solution)/shard_map/ppermute | solution.py:25
  9.7 1.8 copy.18
  11.6 1.9 fusion.1
  13.5 5.6 %collective-permute-start = (f32[301,4,256]{2,1,0:T(4,128)}, f32[301,4,256]{2,1,0:T(4,128)}, u32[]{:S(2)}, u32[]{:S(2)}) collective-permute-start(f32[301,4,256]{2,1,0:T(4,128)} %get-tuple-element.8), channel_id=1, source_target_pairs={{0,124},{4,0},{8,4},{12,8},{16,12},{20,16},{24,20},{28,24},{32,28}... | collective-permute-start | bytes 3698696 | tf_op jit(solution)/shard_map/ppermute | solution.py:25
  22.1 6.7 %all-to-all-start = ((f32[4,32,2,128]{3,2,0,1:T(2,128)}), f32[4,32,2,128]{3,2,0,1:T(2,128)S(1)}, u32[]{:S(2)}, u32[]{:S(2)}) async-start(f32[4,32,2,128]{3,2,0,1:T(2,128)} %bitcast.38), calls=%async_computation | async-start | bytes 262144 | tf_op jit(solution)/shard_map/all_to_all | solution.py:320
  28.9 5.0 %collective-permute-start.4 = (f32[301,4,8]{0,2,1:T(8,128)S(1)}, f32[301,4,8]{0,2,1:T(8,128)S(1)}, u32[]{:S(2)}, u32[]{:S(2)}) collective-permute-start(f32[301,4,8]{0,2,1:T(8,128)S(1)} %get-tuple-element.12), channel_id=1, source_target_pairs={{0,124},{4,0},{8,4},{12,8},{16,12},{20,16},{24,20},{28,24},{32,28}... | collective-permute-start | bytes 115592 | tf_op jit(solution)/shard_map/ppermute | solution.py:25
  34.2 1.6 collective-permute-done.4
  35.8 5.3 %collective-permute-done.5 = f32[301,4,8]{0,2,1:T(8,128)S(1)} collective-permute-done((f32[301,4,8]{0,2,1:T(8,128)S(1)}, f32[301,4,8]{0,2,1:T(8,128)S(1)}, u32[]{:S(2)}, u32[]{:S(2)}) %collective-permute-start.5) | collective-permute-done | bytes 38560 | tf_op jit(solution)/shard_map/ppermute | solution.py:26
  41.2 2.9 %copy.21 = f32[301,16,4]{2,1,0:T(8,128)} copy(f32[301,16,4]{0,2,1:T(4,128)S(1)} %get-tuple-element.10) | data formatting | bytes 154112 | tf_op jit(solution)/shard_map/slice | solution.py:42
  44.0 2.9 %copy.22 = f32[301,16,4]{2,1,0:T(8,128)} copy(f32[301,16,4]{0,2,1:T(4,128)S(1)} %get-tuple-element.11) | data formatting | bytes 154112 | tf_op jit(solution)/shard_map/slice | solution.py:42
  46.9 3.1 %pad_maximum_fusion.1.after_and_out_1_.edge_ref = f32[301,16,128]{2,1,0:T(8,128)S(1)} fusion(f32[301,16,4]{2,1,0:T(8,128)} %copy.22, f32[301,16,4]{2,1,0:T(8,128)} %copy.21, f32[128]{0:T(128)S(1)} %pad.4.clone), kind=kLoop, calls=%fused_computation.8 | loop fusion | flops 1232896 | bytes 2620416 | tf_op jit(solution)/shard_map/concatenate | solution.py:42
  50.9 3.7 %pad_maximum_fusion.after_and_out_0_.rows_ref = f32[301,8,256]{2,1,0:T(8,128)} fusion(f32[301,4,256]{2,1,0:T(4,128)} %collective-permute-done.1, f32[301,4,256]{2,1,0:T(4,128)} %collective-permute-done), kind=kLoop, calls=%fused_computation.6 | loop fusion | flops 616448 | bytes 4931584 | tf_op jit(solution)/shard_map/concatenate | solution.py:43
  54.5 5.2 %shard_map.104 = f32[4,8,256]{2,1,0:T(8,128)} custom-call(f32[256,128]{1,0:T(8,128)} %bitcast.43, s32[32,256]{1,0:T(8,128)} %bitcast.46, f32[32,256]{1,0:T(8,128)} %bitcast.48, f32[301,8,256]{2,1,0:T(8,128)} %pad_maximum_fusion.after_and_out_0_.rows_ref, f32[301,16,128]{2,1,0:T(8,128)} %copy-done.2), custom_call_target="tpu_custom_call" | custom-call | tf_op jit(solution)/shard_map/pallas_call | solution.py:266
  59.7 1.4 fusion.9.surf_ref
  62.5 101.0 %shard_map.105 = (f32[4,75,8,256]{3,2,1,0:T(8,128)}, f32[4,8,256]{2,1,0:T(8,128)}) custom-call(f32[75]{0:T(128)} %constant.31.clone.decay_ref, f32[300,8,256]{2,1,0:T(8,128)} %bitcast.41, f32[301,8,256]{2,1,0:T(8,128)} %pad_maximum_fusion.after_and_out_0_.rows_ref, f32[301,16,128]{2,1,0:T(8,128)} %copy-done.2, f32[16,384]{1,0:T(8,128)} %maximum_select_fusion.mask_ref, ...), custom_call_target="tpu_custom_call" | custom-call | tf_op jit(solution)/shard_map/pallas_call | solution.py:185
  163.5 5.6 %shard_map.106 = f32[256,128]{1,0:T(8,128)} custom-call(f32[4,8,256]{2,1,0:T(8,128)} %get-tuple-element.5.back_ref, s32[32,256]{1,0:T(8,128)} %bitcast.47, f32[32,256]{1,0:T(8,128)} %bitcast.49), custom_call_target="tpu_custom_call" | custom-call | tf_op jit(solution)/shard_map/pallas_call | solution.py:266
  169.1 1.6 copy.26
  170.7 3.9 %all-to-all-start.1 = ((f32[4,32,2,128]{3,2,0,1:T(2,128)}), f32[4,32,2,128]{3,2,0,1:T(2,128)S(1)}, u32[]{:S(2)}, u32[]{:S(2)}) async-start(f32[4,32,2,128]{3,2,0,1:T(2,128)} %copy.26), calls=%async_computation.1 | async-start | bytes 262144 | tf_op jit(solution)/shard_map/all_to_all | solution.py:336
  174.6 7.8 %all-to-all-done.1 = f32[4,32,2,128]{3,2,0,1:T(2,128)S(1)} async-done(((f32[4,32,2,128]{3,2,0,1:T(2,128)}), f32[4,32,2,128]{3,2,0,1:T(2,128)S(1)}, u32[]{:S(2)}, u32[]{:S(2)}) %all-to-all-start.1) | async-done | bytes 131104 | tf_op jit(solution)/shard_map/all_to_all | solution.py:336
  183.1 3.5 %collective-permute-done.6 = f32[4,16,128]{2,1,0:T(8,128)S(1)} collective-permute-done((f32[4,16,128]{2,1,0:T(8,128)S(1)}, f32[4,16,128]{2,1,0:T(8,128)S(1)}, u32[]{:S(2)}, u32[]{:S(2)}) %collective-permute-start.6) | collective-permute-done | bytes 32800 | tf_op jit(solution)/shard_map/ppermute | solution.py:282
  186.6 2.4 %collective-permute-start.7 = (f32[4,16,128]{2,1,0:T(8,128)S(1)}, f32[4,16,128]{2,1,0:T(8,128)S(1)}, u32[]{:S(2)}, u32[]{:S(2)}) collective-permute-start(f32[4,16,128]{2,1,0:T(8,128)S(1)} %add.79), channel_id=1, source_target_pairs={{0,2},{1,3},{2,0},{3,1},{4,6},{5,7},{6,4},{7,5},{8,10},{9,11},{10,... | collective-permute-start | bytes 98312 | tf_op jit(solution)/shard_map/ppermute | solution.py:282
  189.0 3.1 %collective-permute-done.7 = f32[4,16,128]{2,1,0:T(8,128)S(1)} collective-permute-done((f32[4,16,128]{2,1,0:T(8,128)S(1)}, f32[4,16,128]{2,1,0:T(8,128)S(1)}, u32[]{:S(2)}, u32[]{:S(2)}) %collective-permute-start.7) | collective-permute-done | bytes 32800 | tf_op jit(solution)/shard_map/ppermute | solution.py:282
  (54 shorter events, 7.6 us)
Async XLA Ops:
  0.6 20.0 %copy-start = (f32[4,16,128]{2,1,0:T(8,128)S(1)}, f32[4,16,128]{2,1,0:T(8,128)}, u32[]{:S(2)}) copy-start(f32[4,16,128]{2,1,0:T(8,128)} %param.11) | copy-start | bytes 98308
  1.4 60.5 %copy-start.4 = (f32[8,256]{1,0:T(8,128)}, f32[8,256]{1,0:T(8,128)S(1)}, u32[]{:S(2)}) copy-start(f32[8,256]{1,0:T(8,128)S(1)} %get-tuple-element.14.land_ref) | copy-start | bytes 24580
  4.9 6.7 %copy-start.3 = (f32[4,75,8,256]{3,2,1,0:T(8,128)S(1)}, f32[4,75,8,256]{3,2,1,0:T(8,128)}, u32[]{:S(2)}) copy-start(f32[4,75,8,256]{3,2,1,0:T(8,128)} %param.9) | copy-start | bytes 7372804
  6.8 22.1 %collective-permute-start.2 = (f32[301,8,4]{0,1,2:T(8,128)S(1)}, f32[301,8,4]{0,1,2:T(8,128)S(1)}, u32[]{:S(2)}, u32[]{:S(2)}) collective-permute-start(f32[301,8,4]{0,1,2:T(8,128)S(1)} %copy.17), channel_id=1, source_target_pairs={{0,3},{1,0},{2,1},{3,2},{4,7},{5,4},{6,5},{7,6},{8,11},{9,8},{10,9... | collective-permute-start | bytes 115592 | tf_op jit(solution)/shard_map/ppermute | solution.py:25
  11.5 7.7 %copy-start.5 = (s32[1,32]{1,0:T(1,128)S(1)}, s32[1,32]{1,0:T(1,128)}, u32[]{:S(2)}) copy-start(s32[1,32]{1,0:T(1,128)} %param.12) | copy-start | bytes 388
  11.5 8.1 %copy-start.1 = (s32[1,64]{1,0:T(1,128)S(1)}, s32[1,64]{1,0:T(1,128)}, u32[]{:S(2)}) copy-start(s32[1,64]{1,0:T(1,128)} %param.13) | copy-start | bytes 772
  11.5 17.4 %collective-permute-start.3 = (f32[301,8,4]{0,1,2:T(8,128)S(1)}, f32[301,8,4]{0,1,2:T(8,128)S(1)}, u32[]{:S(2)}, u32[]{:S(2)}) collective-permute-start(f32[301,8,4]{0,1,2:T(8,128)S(1)} %copy.18), channel_id=1, source_target_pairs={{0,1},{1,2},{2,3},{3,0},{4,5},{5,6},{6,7},{7,4},{8,9},{9,10},{10,1... | collective-permute-start | bytes 115592 | tf_op jit(solution)/shard_map/ppermute | solution.py:26
  13.5 37.4 %collective-permute-start = (f32[301,4,256]{2,1,0:T(4,128)}, f32[301,4,256]{2,1,0:T(4,128)}, u32[]{:S(2)}, u32[]{:S(2)}) collective-permute-start(f32[301,4,256]{2,1,0:T(4,128)} %get-tuple-element.8), channel_id=1, source_target_pairs={{0,124},{4,0},{8,4},{12,8},{16,12},{20,16},{24,20},{28,24},{32,28}... | collective-permute-start | bytes 3698696 | tf_op jit(solution)/shard_map/ppermute | solution.py:25
  19.1 31.7 %collective-permute-start.1 = (f32[301,4,256]{2,1,0:T(4,128)}, f32[301,4,256]{2,1,0:T(4,128)}, u32[]{:S(2)}, u32[]{:S(2)}) collective-permute-start(f32[301,4,256]{2,1,0:T(4,128)} %get-tuple-element.9), channel_id=1, source_target_pairs={{0,4},{4,8},{8,12},{12,16},{16,20},{20,24},{24,28},{28,32},{32,36}... | collective-permute-start | bytes 3698696 | tf_op jit(solution)/shard_map/ppermute | solution.py:26
  22.1 27.9 %all-to-all-start = ((f32[4,32,2,128]{3,2,0,1:T(2,128)}), f32[4,32,2,128]{3,2,0,1:T(2,128)S(1)}, u32[]{:S(2)}, u32[]{:S(2)}) async-start(f32[4,32,2,128]{3,2,0,1:T(2,128)} %bitcast.38), calls=%async_computation | async-start | bytes 262144 | tf_op jit(solution)/shard_map/all_to_all | solution.py:320
  28.9 6.8 %collective-permute-start.4 = (f32[301,4,8]{0,2,1:T(8,128)S(1)}, f32[301,4,8]{0,2,1:T(8,128)S(1)}, u32[]{:S(2)}, u32[]{:S(2)}) collective-permute-start(f32[301,4,8]{0,2,1:T(8,128)S(1)} %get-tuple-element.12), channel_id=1, source_target_pairs={{0,124},{4,0},{8,4},{12,8},{16,12},{20,16},{24,20},{28,24},{32,28}... | collective-permute-start | bytes 115592 | tf_op jit(solution)/shard_map/ppermute | solution.py:25
  33.9 7.2 %collective-permute-start.5 = (f32[301,4,8]{0,2,1:T(8,128)S(1)}, f32[301,4,8]{0,2,1:T(8,128)S(1)}, u32[]{:S(2)}, u32[]{:S(2)}) collective-permute-start(f32[301,4,8]{0,2,1:T(8,128)S(1)} %get-tuple-element.13), channel_id=1, source_target_pairs={{0,4},{4,8},{8,12},{12,16},{16,20},{20,24},{24,28},{28,32},{32,36}... | collective-permute-start | bytes 115592 | tf_op jit(solution)/shard_map/ppermute | solution.py:26
  50.0 4.5 %copy-start.2 = (f32[301,16,128]{2,1,0:T(8,128)}, f32[301,16,128]{2,1,0:T(8,128)S(1)}, u32[]{:S(2)}) copy-start(f32[301,16,128]{2,1,0:T(8,128)S(1)} %pad_maximum_fusion.1.after_and_out_1_.edge_ref) | copy-start | bytes 7397380
  170.7 11.7 %all-to-all-start.1 = ((f32[4,32,2,128]{3,2,0,1:T(2,128)}), f32[4,32,2,128]{3,2,0,1:T(2,128)S(1)}, u32[]{:S(2)}, u32[]{:S(2)}) async-start(f32[4,32,2,128]{3,2,0,1:T(2,128)} %copy.26), calls=%async_computation.1 | async-start | bytes 262144 | tf_op jit(solution)/shard_map/all_to_all | solution.py:336
  182.6 4.0 %collective-permute-start.6 = (f32[4,16,128]{2,1,0:T(8,128)S(1)}, f32[4,16,128]{2,1,0:T(8,128)S(1)}, u32[]{:S(2)}, u32[]{:S(2)}) collective-permute-start(f32[4,16,128]{2,1,0:T(8,128)S(1)} %convolution_bitcast_fusion), channel_id=1, source_target_pairs={{0,1},{1,0},{2,3},{3,2},{4,5},{5,4},{6,7},{7,6},{8,9},{9,8},{10,11... | collective-permute-start | bytes 98312 | tf_op jit(solution)/shard_map/ppermute | solution.py:282
  186.6 5.4 %collective-permute-start.7 = (f32[4,16,128]{2,1,0:T(8,128)S(1)}, f32[4,16,128]{2,1,0:T(8,128)S(1)}, u32[]{:S(2)}, u32[]{:S(2)}) collective-permute-start(f32[4,16,128]{2,1,0:T(8,128)S(1)} %add.79), channel_id=1, source_target_pairs={{0,2},{1,3},{2,0},{3,1},{4,6},{5,7},{6,4},{7,5},{8,10},{9,11},{10,... | collective-permute-start | bytes 98312 | tf_op jit(solution)/shard_map/ppermute | solution.py:282

commit v10 on v7

--- a/solution.py
+++ b/solution.py
@@ -123,7 +123,7 @@
     surf = surf_ref[...]
     zero = jnp.zeros_like(surf)
 
-    def step(level, below_mix, above_mix, ratios, parts):
+    def step(level, below_mix, above_mix, ratios, parts, sources):
         new_ratios, new_parts = [], list(parts)
         for gi, gain in enumerate(gains):
             below = gain * below_mix
@@ -135,20 +135,22 @@
                 ratio_ref[gi, level] = ratio
                 new_ratios.append(ratio)
             for f in groups[gi]:
-                value = (smoothed(f, level if level is not None else levels - 1) + below * parts[f]) * scale
+                value = (sources[f] + below * parts[f]) * scale
                 out_ref[f, level if level is not None else levels - 1] = value
                 new_parts[f] = value
         return tuple(new_ratios), tuple(new_parts)
 
     def forward(level, carry):
-        below_mix, ratios, parts = carry
+        below_mix, ratios, parts, sources = carry
+        upcoming = tuple(smoothed(f, level + 1) for f in range(fields))
         mix = base_ref[level] + surf * decay_ref[level]
-        ratios, parts = step(level, below_mix, mix, ratios, parts)
-        return (mix, ratios, parts)
-
-    carry = (zero, tuple(zero for _ in gains), tuple(zero for _ in range(fields)))
-    last_mix, ratios, parts = lax.fori_loop(0, levels - 1, forward, carry)
-    step(None, last_mix, zero, ratios, parts)
+        ratios, parts = step(level, below_mix, mix, ratios, parts, sources)
+        return (mix, ratios, parts, upcoming)
+
+    first = tuple(smoothed(f, 0) for f in range(fields))
+    carry = (zero, tuple(zero for _ in gains), tuple(zero for _ in range(fields)), first)
+    last_mix, ratios, parts, sources = lax.fori_loop(0, levels - 1, forward, carry)
+    step(None, last_mix, zero, ratios, parts, sources)
 
     def backward(i, later):
         level = levels - 2 - i

time: 124 us -> 124 us (level)
  no operation moved by 1% of the time
where the time goes in v10:
time: 124 us; the launch traced here: 123 us
  Pallas kernels  42.3 us (34%)
  starting transfers between devices  27.1 us (22%)
  waiting for transfers between devices  21.2 us (17%)
  other arithmetic  16.7 us (13%)
  local copies, waits for them, and re-layouts  14.8 us (12%)
    pallas_call x1, Pallas kernels, tridiagonal(): pl.pallas_call(tridiagonal_kernel, out_shape=(jax.ShapeDtypeStruct(shape,...  31.5 us
    ppermute x3, starting transfers between devices, from_neighbours(): lax.ppermute(lax.slice_in_dim(block, 0, width, axis=dim), axis, to_prev)  13.6 us
    pallas_call x2, Pallas kernels, remap_call(): pl.pallas_call(kernel, out_shape=jax.ShapeDtypeStruct(out_shape, jnp.floa...  10.8 us
    all_to_all x1, waiting for transfers between devices, shards(): lax.all_to_all(buffer.reshape(received.shape), 'lat', split_axis=1, conca...  7.82 us
    all_to_all x1, starting transfers between devices, shards(): lax.all_to_all(outgoing, 'lat', split_axis=1, concat_axis=1, tiled=True)  6.73 us
    ppermute x2, waiting for transfers between devices, sum_over(): values = values + lax.ppermute(values, axis, pairs)  6.53 us
    concatenate x2, other arithmetic, extended_planes(): stack = jnp.concatenate([planes, coast], axis=0)  5.41 us
    ppermute x3, waiting for transfers between devices, from_neighbours(): lax.ppermute(lax.slice_in_dim(block, size - width, size, axis=dim), axis,...  5.33 us
  transfers between devices with their start and end apart: 10, of which 5 were waited for; matrix products, arithmetic and copies ran while one was open for 13% of the time, Pallas kernels for 0%

profile of v10, /device:TPU:0, one launch (start us, length us, event | category | flops | bytes accessed | tf_op | source)
XLA Modules:
  0.0 123.1 jit_solution(10578560466036048128)
XLA Ops:
  1.4 3.5 %fusion = (f32[301,8,4]{2,1,0:T(8,128)}, f32[301,8,4]{2,1,0:T(8,128)}) fusion(f32[300,8,256]{2,1,0:T(8,128)} %bitcast.40, f32[1,8,256]{2,1,0:T(8,128)S(1)} %get-tuple-element.15), kind=kLoop, calls=%fused_computation.12 | loop fusion | flops 19264 | bytes 2542848 | tf_op jit(solution)/shard_map/concatenate | solution.py:34
  4.9 1.9 %copy.17 = f32[301,8,4]{0,1,2:T(8,128)S(1)} copy(f32[301,8,4]{2,1,0:T(8,128)} %get-tuple-element.6) | data formatting | bytes 77056 | tf_op jit(solution)/shard_map/slice | solution.py:25
  6.8 2.9 %collective-permute-start.2 = (f32[301,8,4]{0,1,2:T(8,128)S(1)}, f32[301,8,4]{0,1,2:T(8,128)S(1)}, u32[]{:S(2)}, u32[]{:S(2)}) collective-permute-start(f32[301,8,4]{0,1,2:T(8,128)S(1)} %copy.17), channel_id=1, source_target_pairs={{0,3},{1,0},{2,1},{3,2},{4,7},{5,4},{6,5},{7,6},{8,11},{9,8},{10,9... | collective-permute-start | bytes 115592 | tf_op jit(solution)/shard_map/ppermute | solution.py:25
  9.7 1.8 %copy.18 = f32[301,8,4]{0,1,2:T(8,128)S(1)} copy(f32[301,8,4]{2,1,0:T(8,128)} %get-tuple-element.7) | data formatting | bytes 77056 | tf_op jit(solution)/shard_map/slice | solution.py:26
  11.6 1.9 %fusion.1 = (f32[301,4,256]{2,1,0:T(4,128)}, f32[301,4,256]{2,1,0:T(4,128)}) fusion(f32[300,8,256]{2,1,0:T(8,128)S(1)} %bitcast.42, f32[1,8,256]{2,1,0:T(8,128)S(1)} %get-tuple-element.15), kind=kLoop, calls=%fused_computation.13 | loop fusion | flops 616448 | bytes 4931584 | tf_op jit(solution)/shard_map/concatenate | solution.py:34
  13.5 5.6 %collective-permute-start = (f32[301,4,256]{2,1,0:T(4,128)}, f32[301,4,256]{2,1,0:T(4,128)}, u32[]{:S(2)}, u32[]{:S(2)}) collective-permute-start(f32[301,4,256]{2,1,0:T(4,128)} %get-tuple-element.8), channel_id=1, source_target_pairs={{0,124},{4,0},{8,4},{12,8},{16,12},{20,16},{24,20},{28,24},{32,28}... | collective-permute-start | bytes 3698696 | tf_op jit(solution)/shard_map/ppermute | solution.py:25
  22.1 6.7 %all-to-all-start = ((f32[4,32,2,128]{3,2,0,1:T(2,128)}), f32[4,32,2,128]{3,2,0,1:T(2,128)S(1)}, u32[]{:S(2)}, u32[]{:S(2)}) async-start(f32[4,32,2,128]{3,2,0,1:T(2,128)} %bitcast.38), calls=%async_computation | async-start | bytes 262144 | tf_op jit(solution)/shard_map/all_to_all | solution.py:315
  28.9 5.0 %collective-permute-start.4 = (f32[301,4,8]{0,2,1:T(8,128)S(1)}, f32[301,4,8]{0,2,1:T(8,128)S(1)}, u32[]{:S(2)}, u32[]{:S(2)}) collective-permute-start(f32[301,4,8]{0,2,1:T(8,128)S(1)} %get-tuple-element.12), channel_id=1, source_target_pairs={{0,124},{4,0},{8,4},{12,8},{16,12},{20,16},{24,20},{28,24},{32,28}... | collective-permute-start | bytes 115592 | tf_op jit(solution)/shard_map/ppermute | solution.py:25
  34.2 1.6 %collective-permute-done.4 = f32[301,4,8]{0,2,1:T(8,128)S(1)} collective-permute-done((f32[301,4,8]{0,2,1:T(8,128)S(1)}, f32[301,4,8]{0,2,1:T(8,128)S(1)}, u32[]{:S(2)}, u32[]{:S(2)}) %collective-permute-start.4) | collective-permute-done | bytes 38560 | tf_op jit(solution)/shard_map/ppermute | solution.py:25
  35.8 5.3 %collective-permute-done.5 = f32[301,4,8]{0,2,1:T(8,128)S(1)} collective-permute-done((f32[301,4,8]{0,2,1:T(8,128)S(1)}, f32[301,4,8]{0,2,1:T(8,128)S(1)}, u32[]{:S(2)}, u32[]{:S(2)}) %collective-permute-start.5) | collective-permute-done | bytes 38560 | tf_op jit(solution)/shard_map/ppermute | solution.py:26
  41.2 2.9 %copy.21 = f32[301,16,4]{2,1,0:T(8,128)} copy(f32[301,16,4]{0,2,1:T(4,128)S(1)} %get-tuple-element.10) | data formatting | bytes 154112 | tf_op jit(solution)/shard_map/slice | solution.py:42
  44.0 2.9 %copy.22 = f32[301,16,4]{2,1,0:T(8,128)} copy(f32[301,16,4]{0,2,1:T(4,128)S(1)} %get-tuple-element.11) | data formatting | bytes 154112 | tf_op jit(solution)/shard_map/slice | solution.py:42
  46.9 3.1 %pad_maximum_fusion.1.after_and_out_1_.edge_ref = f32[301,16,128]{2,1,0:T(8,128)S(1)} fusion(f32[301,16,4]{2,1,0:T(8,128)} %copy.22, f32[301,16,4]{2,1,0:T(8,128)} %copy.21, f32[128]{0:T(128)S(1)} %pad.4.clone), kind=kLoop, calls=%fused_computation.8 | loop fusion | flops 1232896 | bytes 2620416 | tf_op jit(solution)/shard_map/concatenate | solution.py:42
  50.9 3.7 %pad_maximum_fusion.after_and_out_0_.rows_ref = f32[301,8,256]{2,1,0:T(8,128)} fusion(f32[301,4,256]{2,1,0:T(4,128)} %collective-permute-done.1, f32[301,4,256]{2,1,0:T(4,128)} %collective-permute-done), kind=kLoop, calls=%fused_computation.6 | loop fusion | flops 616448 | bytes 4931584 | tf_op jit(solution)/shard_map/concatenate | solution.py:43
  54.5 5.2 %shard_map.104 = f32[4,8,256]{2,1,0:T(8,128)} custom-call(f32[256,128]{1,0:T(8,128)} %bitcast.43, s32[32,256]{1,0:T(8,128)} %bitcast.46, f32[32,256]{1,0:T(8,128)} %bitcast.48, f32[301,8,256]{2,1,0:T(8,128)} %pad_maximum_fusion.after_and_out_0_.rows_ref, f32[301,16,128]{2,1,0:T(8,128)} %copy-done.2), custom_call_target="tpu_custom_call" | custom-call | tf_op jit(solution)/shard_map/pallas_call | solution.py:261
  59.7 1.4 %fusion.9.surf_ref = f32[8,256]{1,0:T(8,128)} fusion(f32[4,8,256]{2,1,0:T(8,128)} %shard_map.104), kind=kLoop, calls=%fused_computation.32 | loop fusion | flops 22528 | bytes 40960 | tf_op jit(solution)/shard_map/add | solution.py:326
  62.5 31.5 %shard_map.105 = (f32[4,75,8,256]{3,2,1,0:T(8,128)}, f32[4,8,256]{2,1,0:T(8,128)}) custom-call(f32[75]{0:T(128)} %constant.31.clone.decay_ref, f32[300,8,256]{2,1,0:T(8,128)} %bitcast.41, f32[301,8,256]{2,1,0:T(8,128)} %pad_maximum_fusion.after_and_out_0_.rows_ref, f32[301,16,128]{2,1,0:T(8,128)} %copy-done.2, f32[16,384]{1,0:T(8,128)} %maximum_select_fusion.mask_ref, ...), custom_call_target="tpu_custom_call" | custom-call | tf_op jit(solution)/shard_map/pallas_call | solution.py:180
  94.0 5.6 %shard_map.106 = f32[256,128]{1,0:T(8,128)} custom-call(f32[4,8,256]{2,1,0:T(8,128)} %get-tuple-element.5.back_ref, s32[32,256]{1,0:T(8,128)} %bitcast.47, f32[32,256]{1,0:T(8,128)} %bitcast.49), custom_call_target="tpu_custom_call" | custom-call | tf_op jit(solution)/shard_map/pallas_call | solution.py:261
  99.6 1.6 %copy.26 = f32[4,32,2,128]{3,2,0,1:T(2,128)} copy(f32[4,32,2,128]{3,2,1,0:T(2,128)} %bitcast.45) | data formatting | bytes 262144 | tf_op jit(solution)/shard_map/reshape | solution.py:332
  101.2 3.9 %all-to-all-start.1 = ((f32[4,32,2,128]{3,2,0,1:T(2,128)}), f32[4,32,2,128]{3,2,0,1:T(2,128)S(1)}, u32[]{:S(2)}, u32[]{:S(2)}) async-start(f32[4,32,2,128]{3,2,0,1:T(2,128)} %copy.26), calls=%async_computation.1 | async-start | bytes 262144 | tf_op jit(solution)/shard_map/all_to_all | solution.py:331
  105.1 7.8 %all-to-all-done.1 = f32[4,32,2,128]{3,2,0,1:T(2,128)S(1)} async-done(((f32[4,32,2,128]{3,2,0,1:T(2,128)}), f32[4,32,2,128]{3,2,0,1:T(2,128)S(1)}, u32[]{:S(2)}, u32[]{:S(2)}) %all-to-all-start.1) | async-done | bytes 131104 | tf_op jit(solution)/shard_map/all_to_all | solution.py:331
  113.6 3.5 %collective-permute-done.6 = f32[4,16,128]{2,1,0:T(8,128)S(1)} collective-permute-done((f32[4,16,128]{2,1,0:T(8,128)S(1)}, f32[4,16,128]{2,1,0:T(8,128)S(1)}, u32[]{:S(2)}, u32[]{:S(2)}) %collective-permute-start.6) | collective-permute-done | bytes 32800 | tf_op jit(solution)/shard_map/ppermute | solution.py:277
  117.1 2.4 %collective-permute-start.7 = (f32[4,16,128]{2,1,0:T(8,128)S(1)}, f32[4,16,128]{2,1,0:T(8,128)S(1)}, u32[]{:S(2)}, u32[]{:S(2)}) collective-permute-start(f32[4,16,128]{2,1,0:T(8,128)S(1)} %add.79), channel_id=1, source_target_pairs={{0,2},{1,3},{2,0},{3,1},{4,6},{5,7},{6,4},{7,5},{8,10},{9,11},{10,... | collective-permute-start | bytes 98312 | tf_op jit(solution)/shard_map/ppermute | solution.py:277
  119.5 3.1 %collective-permute-done.7 = f32[4,16,128]{2,1,0:T(8,128)S(1)} collective-permute-done((f32[4,16,128]{2,1,0:T(8,128)S(1)}, f32[4,16,128]{2,1,0:T(8,128)S(1)}, u32[]{:S(2)}, u32[]{:S(2)}) %collective-permute-start.7) | collective-permute-done | bytes 32800 | tf_op jit(solution)/shard_map/ppermute | solution.py:277
  (54 shorter events, 7.6 us)
Async XLA Ops:
  0.6 20.0 %copy-start = (f32[4,16,128]{2,1,0:T(8,128)S(1)}, f32[4,16,128]{2,1,0:T(8,128)}, u32[]{:S(2)}) copy-start(f32[4,16,128]{2,1,0:T(8,128)} %param.11) | copy-start | bytes 98308
  1.4 60.5 %copy-start.4 = (f32[8,256]{1,0:T(8,128)}, f32[8,256]{1,0:T(8,128)S(1)}, u32[]{:S(2)}) copy-start(f32[8,256]{1,0:T(8,128)S(1)} %get-tuple-element.14.land_ref) | copy-start | bytes 24580
  4.9 6.7 %copy-start.3 = (f32[4,75,8,256]{3,2,1,0:T(8,128)S(1)}, f32[4,75,8,256]{3,2,1,0:T(8,128)}, u32[]{:S(2)}) copy-start(f32[4,75,8,256]{3,2,1,0:T(8,128)} %param.9) | copy-start | bytes 7372804
  6.8 22.1 %collective-permute-start.2 = (f32[301,8,4]{0,1,2:T(8,128)S(1)}, f32[301,8,4]{0,1,2:T(8,128)S(1)}, u32[]{:S(2)}, u32[]{:S(2)}) collective-permute-start(f32[301,8,4]{0,1,2:T(8,128)S(1)} %copy.17), channel_id=1, source_target_pairs={{0,3},{1,0},{2,1},{3,2},{4,7},{5,4},{6,5},{7,6},{8,11},{9,8},{10,9... | collective-permute-start | bytes 115592 | tf_op jit(solution)/shard_map/ppermute | solution.py:25
  11.5 7.7 %copy-start.5 = (s32[1,32]{1,0:T(1,128)S(1)}, s32[1,32]{1,0:T(1,128)}, u32[]{:S(2)}) copy-start(s32[1,32]{1,0:T(1,128)} %param.12) | copy-start | bytes 388
  11.5 8.1 %copy-start.1 = (s32[1,64]{1,0:T(1,128)S(1)}, s32[1,64]{1,0:T(1,128)}, u32[]{:S(2)}) copy-start(s32[1,64]{1,0:T(1,128)} %param.13) | copy-start | bytes 772
  11.5 17.4 %collective-permute-start.3 = (f32[301,8,4]{0,1,2:T(8,128)S(1)}, f32[301,8,4]{0,1,2:T(8,128)S(1)}, u32[]{:S(2)}, u32[]{:S(2)}) collective-permute-start(f32[301,8,4]{0,1,2:T(8,128)S(1)} %copy.18), channel_id=1, source_target_pairs={{0,1},{1,2},{2,3},{3,0},{4,5},{5,6},{6,7},{7,4},{8,9},{9,10},{10,1... | collective-permute-start | bytes 115592 | tf_op jit(solution)/shard_map/ppermute | solution.py:26
  13.5 37.4 %collective-permute-start = (f32[301,4,256]{2,1,0:T(4,128)}, f32[301,4,256]{2,1,0:T(4,128)}, u32[]{:S(2)}, u32[]{:S(2)}) collective-permute-start(f32[301,4,256]{2,1,0:T(4,128)} %get-tuple-element.8), channel_id=1, source_target_pairs={{0,124},{4,0},{8,4},{12,8},{16,12},{20,16},{24,20},{28,24},{32,28}... | collective-permute-start | bytes 3698696 | tf_op jit(solution)/shard_map/ppermute | solution.py:25
  19.1 31.7 %collective-permute-start.1 = (f32[301,4,256]{2,1,0:T(4,128)}, f32[301,4,256]{2,1,0:T(4,128)}, u32[]{:S(2)}, u32[]{:S(2)}) collective-permute-start(f32[301,4,256]{2,1,0:T(4,128)} %get-tuple-element.9), channel_id=1, source_target_pairs={{0,4},{4,8},{8,12},{12,16},{16,20},{20,24},{24,28},{28,32},{32,36}... | collective-permute-start | bytes 3698696 | tf_op jit(solution)/shard_map/ppermute | solution.py:26
  22.1 27.9 %all-to-all-start = ((f32[4,32,2,128]{3,2,0,1:T(2,128)}), f32[4,32,2,128]{3,2,0,1:T(2,128)S(1)}, u32[]{:S(2)}, u32[]{:S(2)}) async-start(f32[4,32,2,128]{3,2,0,1:T(2,128)} %bitcast.38), calls=%async_computation | async-start | bytes 262144 | tf_op jit(solution)/shard_map/all_to_all | solution.py:315
  28.9 6.8 %collective-permute-start.4 = (f32[301,4,8]{0,2,1:T(8,128)S(1)}, f32[301,4,8]{0,2,1:T(8,128)S(1)}, u32[]{:S(2)}, u32[]{:S(2)}) collective-permute-start(f32[301,4,8]{0,2,1:T(8,128)S(1)} %get-tuple-element.12), channel_id=1, source_target_pairs={{0,124},{4,0},{8,4},{12,8},{16,12},{20,16},{24,20},{28,24},{32,28}... | collective-permute-start | bytes 115592 | tf_op jit(solution)/shard_map/ppermute | solution.py:25
  33.9 7.2 %collective-permute-start.5 = (f32[301,4,8]{0,2,1:T(8,128)S(1)}, f32[301,4,8]{0,2,1:T(8,128)S(1)}, u32[]{:S(2)}, u32[]{:S(2)}) collective-permute-start(f32[301,4,8]{0,2,1:T(8,128)S(1)} %get-tuple-element.13), channel_id=1, source_target_pairs={{0,4},{4,8},{8,12},{12,16},{16,20},{20,24},{24,28},{28,32},{32,36}... | collective-permute-start | bytes 115592 | tf_op jit(solution)/shard_map/ppermute | solution.py:26
  50.0 4.5 %copy-start.2 = (f32[301,16,128]{2,1,0:T(8,128)}, f32[301,16,128]{2,1,0:T(8,128)S(1)}, u32[]{:S(2)}) copy-start(f32[301,16,128]{2,1,0:T(8,128)S(1)} %pad_maximum_fusion.1.after_and_out_1_.edge_ref) | copy-start | bytes 7397380
  101.2 11.7 %all-to-all-start.1 = ((f32[4,32,2,128]{3,2,0,1:T(2,128)}), f32[4,32,2,128]{3,2,0,1:T(2,128)S(1)}, u32[]{:S(2)}, u32[]{:S(2)}) async-start(f32[4,32,2,128]{3,2,0,1:T(2,128)} %copy.26), calls=%async_computation.1 | async-start | bytes 262144 | tf_op jit(solution)/shard_map/all_to_all | solution.py:331
  113.1 4.0 %collective-permute-start.6 = (f32[4,16,128]{2,1,0:T(8,128)S(1)}, f32[4,16,128]{2,1,0:T(8,128)S(1)}, u32[]{:S(2)}, u32[]{:S(2)}) collective-permute-start(f32[4,16,128]{2,1,0:T(8,128)S(1)} %convolution_bitcast_fusion), channel_id=1, source_target_pairs={{0,1},{1,0},{2,3},{3,2},{4,5},{5,4},{6,7},{7,6},{8,9},{9,8},{10,11... | collective-permute-start | bytes 98312 | tf_op jit(solution)/shard_map/ppermute | solution.py:277
  117.1 5.4 %collective-permute-start.7 = (f32[4,16,128]{2,1,0:T(8,128)S(1)}, f32[4,16,128]{2,1,0:T(8,128)S(1)}, u32[]{:S(2)}, u32[]{:S(2)}) collective-permute-start(f32[4,16,128]{2,1,0:T(8,128)S(1)} %add.79), channel_id=1, source_target_pairs={{0,2},{1,3},{2,0},{3,1},{4,6},{5,7},{6,4},{7,5},{8,10},{9,11},{10,... | collective-permute-start | bytes 98312 | tf_op jit(solution)/shard_map/ppermute | solution.py:277

commit v11 on v10

--- a/solution.py
+++ b/solution.py
@@ -321,7 +321,7 @@
     land = land_mask.astype(jnp.float32)
     *pieces, mask = extended_planes(adjoint_state, land_mask, HALO)
     forcing = remap_call(
-        gather_kernel, (fields, rows, cols), flat_recv, index_rows, weight_rows, after=tuple(pieces[1:])
+        gather_kernel, (fields, rows, cols), flat_recv, index_rows, weight_rows
     )
     surface = WIND_GAIN * (forcing[2] * forcing[2] + forcing[3] * forcing[3]) + jax.nn.softplus(
         forcing[1] - forcing[0]

time: 124 us -> 124 us (level)
  transfers between devices with their start and end apart: 10 -> 10, of which waited for: 5 -> 5; matrix products, arithmetic and copies ran while one was open for 13% -> 15% of each run, Pallas kernels for 0% -> 4%
where the time goes in v11:
time: 124 us; the launch traced here: 123 us
  Pallas kernels  42.4 us (34%)
  starting transfers between devices  27.1 us (22%)
  waiting for transfers between devices  21.2 us (17%)
  other arithmetic  16.6 us (13%)
  local copies, waits for them, and re-layouts  14.8 us (12%)
    pallas_call x1, Pallas kernels, tridiagonal(): pl.pallas_call(tridiagonal_kernel, out_shape=(jax.ShapeDtypeStruct(shape,...  31.5 us
    ppermute x3, starting transfers between devices, from_neighbours(): lax.ppermute(lax.slice_in_dim(block, 0, width, axis=dim), axis, to_prev)  13.6 us
    pallas_call x2, Pallas kernels, remap_call(): pl.pallas_call(kernel, out_shape=jax.ShapeDtypeStruct(out_shape, jnp.floa...  10.8 us
    all_to_all x1, waiting for transfers between devices, shards(): lax.all_to_all(buffer.reshape(received.shape), 'lat', split_axis=1, conca...  7.82 us
    all_to_all x1, starting transfers between devices, shards(): lax.all_to_all(outgoing, 'lat', split_axis=1, concat_axis=1, tiled=True)  6.73 us
    ppermute x2, waiting for transfers between devices, sum_over(): values = values + lax.ppermute(values, axis, pairs)  6.53 us
    concatenate x2, other arithmetic, extended_planes(): stack = jnp.concatenate([planes, coast], axis=0)  5.41 us
    ppermute x3, waiting for transfers between devices, from_neighbours(): lax.ppermute(lax.slice_in_dim(block, size - width, size, axis=dim), axis,...  5.33 us
  transfers between devices with their start and end apart: 10, of which 5 were waited for; matrix products, arithmetic and copies ran while one was open for 15% of the time, Pallas kernels for 4%

profile of v11, /device:TPU:0, one launch (start us, length us, event | category | flops | bytes accessed | tf_op | source)
XLA Modules:
  0.0 123.2 jit_solution(325348380080663068)
XLA Ops:
  1.4 3.5 %fusion = (f32[301,8,4]{2,1,0:T(8,128)}, f32[301,8,4]{2,1,0:T(8,128)}) fusion(f32[300,8,256]{2,1,0:T(8,128)} %bitcast.40, f32[1,8,256]{2,1,0:T(8,128)S(1)} %get-tuple-element.15), kind=kLoop, calls=%fused_computation.12 | loop fusion | flops 19264 | bytes 2542848 | tf_op jit(solution)/shard_map/concatenate | solution.py:34
  4.9 1.9 %copy.17 = f32[301,8,4]{0,1,2:T(8,128)S(1)} copy(f32[301,8,4]{2,1,0:T(8,128)} %get-tuple-element.6) | data formatting | bytes 77056 | tf_op jit(solution)/shard_map/slice | solution.py:25
  6.8 2.9 %collective-permute-start.2 = (f32[301,8,4]{0,1,2:T(8,128)S(1)}, f32[301,8,4]{0,1,2:T(8,128)S(1)}, u32[]{:S(2)}, u32[]{:S(2)}) collective-permute-start(f32[301,8,4]{0,1,2:T(8,128)S(1)} %copy.17), channel_id=1, source_target_pairs={{0,3},{1,0},{2,1},{3,2},{4,7},{5,4},{6,5},{7,6},{8,11},{9,8},{10,9... | collective-permute-start | bytes 115592 | tf_op jit(solution)/shard_map/ppermute | solution.py:25
  9.7 1.8 %copy.18 = f32[301,8,4]{0,1,2:T(8,128)S(1)} copy(f32[301,8,4]{2,1,0:T(8,128)} %get-tuple-element.7) | data formatting | bytes 77056 | tf_op jit(solution)/shard_map/slice | solution.py:26
  11.6 1.9 %fusion.1 = (f32[301,4,256]{2,1,0:T(4,128)}, f32[301,4,256]{2,1,0:T(4,128)}) fusion(f32[300,8,256]{2,1,0:T(8,128)S(1)} %bitcast.42, f32[1,8,256]{2,1,0:T(8,128)S(1)} %get-tuple-element.15), kind=kLoop, calls=%fused_computation.13 | loop fusion | flops 616448 | bytes 4931584 | tf_op jit(solution)/shard_map/concatenate | solution.py:34
  13.5 5.6 %collective-permute-start = (f32[301,4,256]{2,1,0:T(4,128)}, f32[301,4,256]{2,1,0:T(4,128)}, u32[]{:S(2)}, u32[]{:S(2)}) collective-permute-start(f32[301,4,256]{2,1,0:T(4,128)} %get-tuple-element.8), channel_id=1, source_target_pairs={{0,124},{4,0},{8,4},{12,8},{16,12},{20,16},{24,20},{28,24},{32,28}... | collective-permute-start | bytes 3698696 | tf_op jit(solution)/shard_map/ppermute | solution.py:25
  22.1 6.7 %all-to-all-start = ((f32[4,32,2,128]{3,2,0,1:T(2,128)}), f32[4,32,2,128]{3,2,0,1:T(2,128)S(1)}, u32[]{:S(2)}, u32[]{:S(2)}) async-start(f32[4,32,2,128]{3,2,0,1:T(2,128)} %bitcast.38), calls=%async_computation | async-start | bytes 262144 | tf_op jit(solution)/shard_map/all_to_all | solution.py:315
  28.9 5.0 %collective-permute-start.4 = (f32[301,4,8]{0,2,1:T(8,128)S(1)}, f32[301,4,8]{0,2,1:T(8,128)S(1)}, u32[]{:S(2)}, u32[]{:S(2)}) collective-permute-start(f32[301,4,8]{0,2,1:T(8,128)S(1)} %get-tuple-element.12), channel_id=1, source_target_pairs={{0,124},{4,0},{8,4},{12,8},{16,12},{20,16},{24,20},{28,24},{32,28}... | collective-permute-start | bytes 115592 | tf_op jit(solution)/shard_map/ppermute | solution.py:25
  34.2 1.6 %collective-permute-done.4 = f32[301,4,8]{0,2,1:T(8,128)S(1)} collective-permute-done((f32[301,4,8]{0,2,1:T(8,128)S(1)}, f32[301,4,8]{0,2,1:T(8,128)S(1)}, u32[]{:S(2)}, u32[]{:S(2)}) %collective-permute-start.4) | collective-permute-done | bytes 38560 | tf_op jit(solution)/shard_map/ppermute | solution.py:25
  35.8 5.3 %collective-permute-done.5 = f32[301,4,8]{0,2,1:T(8,128)S(1)} collective-permute-done((f32[301,4,8]{0,2,1:T(8,128)S(1)}, f32[301,4,8]{0,2,1:T(8,128)S(1)}, u32[]{:S(2)}, u32[]{:S(2)}) %collective-permute-start.5) | collective-permute-done | bytes 38560 | tf_op jit(solution)/shard_map/ppermute | solution.py:26
  41.2 2.9 %copy.21 = f32[301,16,4]{2,1,0:T(8,128)} copy(f32[301,16,4]{0,2,1:T(4,128)S(1)} %get-tuple-element.10) | data formatting | bytes 154112 | tf_op jit(solution)/shard_map/slice | solution.py:42
  44.0 2.9 %copy.22 = f32[301,16,4]{2,1,0:T(8,128)} copy(f32[301,16,4]{0,2,1:T(4,128)S(1)} %get-tuple-element.11) | data formatting | bytes 154112 | tf_op jit(solution)/shard_map/slice | solution.py:42
  46.9 3.1 %pad_maximum_fusion.1.edge_ref = f32[301,16,128]{2,1,0:T(8,128)S(1)} fusion(f32[301,16,4]{2,1,0:T(8,128)} %copy.22, f32[301,16,4]{2,1,0:T(8,128)} %copy.21, f32[128]{0:T(128)S(1)} %pad.4.clone), kind=kLoop, calls=%fused_computation.8 | loop fusion | flops 1232896 | bytes 2620416 | tf_op jit(solution)/shard_map/concatenate | solution.py:42
  50.8 5.3 %shard_map.104 = f32[4,8,256]{2,1,0:T(8,128)} custom-call(f32[256,128]{1,0:T(8,128)} %bitcast.44, s32[32,256]{1,0:T(8,128)} %bitcast.46, f32[32,256]{1,0:T(8,128)} %bitcast.48), custom_call_target="tpu_custom_call" | custom-call | tf_op jit(solution)/shard_map/pallas_call | solution.py:261
  56.1 1.4 %fusion.9.surf_ref = f32[8,256]{1,0:T(8,128)} fusion(f32[4,8,256]{2,1,0:T(8,128)} %shard_map.104), kind=kLoop, calls=%fused_computation.32 | loop fusion | flops 22528 | bytes 40960 | tf_op jit(solution)/shard_map/add | solution.py:326
  58.9 3.6 %pad_maximum_fusion.rows_ref = f32[301,8,256]{2,1,0:T(8,128)} fusion(f32[301,4,256]{2,1,0:T(4,128)} %collective-permute-done.1, f32[301,4,256]{2,1,0:T(4,128)} %collective-permute-done), kind=kLoop, calls=%fused_computation.6 | loop fusion | flops 616448 | bytes 4931584 | tf_op jit(solution)/shard_map/concatenate | solution.py:43
  62.5 31.5 %shard_map.105 = (f32[4,75,8,256]{3,2,1,0:T(8,128)}, f32[4,8,256]{2,1,0:T(8,128)}) custom-call(f32[75]{0:T(128)} %constant.31.clone.decay_ref, f32[300,8,256]{2,1,0:T(8,128)} %bitcast.41, f32[301,8,256]{2,1,0:T(8,128)} %pad_maximum_fusion.rows_ref, f32[301,16,128]{2,1,0:T(8,128)} %copy-done.3, f32[16,384]{1,0:T(8,128)} %maximum_select_fusion.mask_ref, ...), custom_call_target="tpu_custom_call" | custom-call | tf_op jit(solution)/shard_map/pallas_call | solution.py:180
  94.1 5.6 %shard_map.106 = f32[256,128]{1,0:T(8,128)} custom-call(f32[4,8,256]{2,1,0:T(8,128)} %get-tuple-element.5.back_ref, s32[32,256]{1,0:T(8,128)} %bitcast.47, f32[32,256]{1,0:T(8,128)} %bitcast.49), custom_call_target="tpu_custom_call" | custom-call | tf_op jit(solution)/shard_map/pallas_call | solution.py:261
  99.6 1.6 %copy.26 = f32[4,32,2,128]{3,2,0,1:T(2,128)} copy(f32[4,32,2,128]{3,2,1,0:T(2,128)} %bitcast.45) | data formatting | bytes 262144 | tf_op jit(solution)/shard_map/reshape | solution.py:332
  101.2 3.9 %all-to-all-start.1 = ((f32[4,32,2,128]{3,2,0,1:T(2,128)}), f32[4,32,2,128]{3,2,0,1:T(2,128)S(1)}, u32[]{:S(2)}, u32[]{:S(2)}) async-start(f32[4,32,2,128]{3,2,0,1:T(2,128)} %copy.26), calls=%async_computation.1 | async-start | bytes 262144 | tf_op jit(solution)/shard_map/all_to_all | solution.py:331
  105.1 7.8 %all-to-all-done.1 = f32[4,32,2,128]{3,2,0,1:T(2,128)S(1)} async-done(((f32[4,32,2,128]{3,2,0,1:T(2,128)}), f32[4,32,2,128]{3,2,0,1:T(2,128)S(1)}, u32[]{:S(2)}, u32[]{:S(2)}) %all-to-all-start.1) | async-done | bytes 131104 | tf_op jit(solution)/shard_map/all_to_all | solution.py:331
  113.6 3.5 %collective-permute-done.6 = f32[4,16,128]{2,1,0:T(8,128)S(1)} collective-permute-done((f32[4,16,128]{2,1,0:T(8,128)S(1)}, f32[4,16,128]{2,1,0:T(8,128)S(1)}, u32[]{:S(2)}, u32[]{:S(2)}) %collective-permute-start.6) | collective-permute-done | bytes 32800 | tf_op jit(solution)/shard_map/ppermute | solution.py:277
  117.1 2.4 %collective-permute-start.7 = (f32[4,16,128]{2,1,0:T(8,128)S(1)}, f32[4,16,128]{2,1,0:T(8,128)S(1)}, u32[]{:S(2)}, u32[]{:S(2)}) collective-permute-start(f32[4,16,128]{2,1,0:T(8,128)S(1)} %add.79), channel_id=1, source_target_pairs={{0,2},{1,3},{2,0},{3,1},{4,6},{5,7},{6,4},{7,5},{8,10},{9,11},{10,... | collective-permute-start | bytes 98312 | tf_op jit(solution)/shard_map/ppermute | solution.py:277
  119.5 3.1 %collective-permute-done.7 = f32[4,16,128]{2,1,0:T(8,128)S(1)} collective-permute-done((f32[4,16,128]{2,1,0:T(8,128)S(1)}, f32[4,16,128]{2,1,0:T(8,128)S(1)}, u32[]{:S(2)}, u32[]{:S(2)}) %collective-permute-start.7) | collective-permute-done | bytes 32800 | tf_op jit(solution)/shard_map/ppermute | solution.py:277
  (54 shorter events, 7.6 us)
Async XLA Ops:
  0.6 20.0 %copy-start = (f32[4,16,128]{2,1,0:T(8,128)S(1)}, f32[4,16,128]{2,1,0:T(8,128)}, u32[]{:S(2)}) copy-start(f32[4,16,128]{2,1,0:T(8,128)} %param.11) | copy-start | bytes 98308
  1.4 56.9 %copy-start.4 = (f32[8,256]{1,0:T(8,128)}, f32[8,256]{1,0:T(8,128)S(1)}, u32[]{:S(2)}) copy-start(f32[8,256]{1,0:T(8,128)S(1)} %get-tuple-element.14.land_ref) | copy-start | bytes 24580
  4.9 6.7 %copy-start.2 = (f32[4,75,8,256]{3,2,1,0:T(8,128)S(1)}, f32[4,75,8,256]{3,2,1,0:T(8,128)}, u32[]{:S(2)}) copy-start(f32[4,75,8,256]{3,2,1,0:T(8,128)} %param.9) | copy-start | bytes 7372804
  6.8 22.1 %collective-permute-start.2 = (f32[301,8,4]{0,1,2:T(8,128)S(1)}, f32[301,8,4]{0,1,2:T(8,128)S(1)}, u32[]{:S(2)}, u32[]{:S(2)}) collective-permute-start(f32[301,8,4]{0,1,2:T(8,128)S(1)} %copy.17), channel_id=1, source_target_pairs={{0,3},{1,0},{2,1},{3,2},{4,7},{5,4},{6,5},{7,6},{8,11},{9,8},{10,9... | collective-permute-start | bytes 115592 | tf_op jit(solution)/shard_map/ppermute | solution.py:25
  11.5 7.7 %copy-start.5 = (s32[1,32]{1,0:T(1,128)S(1)}, s32[1,32]{1,0:T(1,128)}, u32[]{:S(2)}) copy-start(s32[1,32]{1,0:T(1,128)} %param.12) | copy-start | bytes 388
  11.5 8.1 %copy-start.1 = (s32[1,64]{1,0:T(1,128)S(1)}, s32[1,64]{1,0:T(1,128)}, u32[]{:S(2)}) copy-start(s32[1,64]{1,0:T(1,128)} %param.13) | copy-start | bytes 772
  11.5 17.4 %collective-permute-start.3 = (f32[301,8,4]{0,1,2:T(8,128)S(1)}, f32[301,8,4]{0,1,2:T(8,128)S(1)}, u32[]{:S(2)}, u32[]{:S(2)}) collective-permute-start(f32[301,8,4]{0,1,2:T(8,128)S(1)} %copy.18), channel_id=1, source_target_pairs={{0,1},{1,2},{2,3},{3,0},{4,5},{5,6},{6,7},{7,4},{8,9},{9,10},{10,1... | collective-permute-start | bytes 115592 | tf_op jit(solution)/shard_map/ppermute | solution.py:26
  13.5 44.0 %collective-permute-start = (f32[301,4,256]{2,1,0:T(4,128)}, f32[301,4,256]{2,1,0:T(4,128)}, u32[]{:S(2)}, u32[]{:S(2)}) collective-permute-start(f32[301,4,256]{2,1,0:T(4,128)} %get-tuple-element.8), channel_id=1, source_target_pairs={{0,124},{4,0},{8,4},{12,8},{16,12},{20,16},{24,20},{28,24},{32,28}... | collective-permute-start | bytes 3698696 | tf_op jit(solution)/shard_map/ppermute | solution.py:25
  19.1 38.3 %collective-permute-start.1 = (f32[301,4,256]{2,1,0:T(4,128)}, f32[301,4,256]{2,1,0:T(4,128)}, u32[]{:S(2)}, u32[]{:S(2)}) collective-permute-start(f32[301,4,256]{2,1,0:T(4,128)} %get-tuple-element.9), channel_id=1, source_target_pairs={{0,4},{4,8},{8,12},{12,16},{16,20},{20,24},{24,28},{28,32},{32,36}... | collective-permute-start | bytes 3698696 | tf_op jit(solution)/shard_map/ppermute | solution.py:26
  22.1 27.9 %all-to-all-start = ((f32[4,32,2,128]{3,2,0,1:T(2,128)}), f32[4,32,2,128]{3,2,0,1:T(2,128)S(1)}, u32[]{:S(2)}, u32[]{:S(2)}) async-start(f32[4,32,2,128]{3,2,0,1:T(2,128)} %bitcast.38), calls=%async_computation | async-start | bytes 262144 | tf_op jit(solution)/shard_map/all_to_all | solution.py:315
  28.9 6.8 %collective-permute-start.4 = (f32[301,4,8]{0,2,1:T(8,128)S(1)}, f32[301,4,8]{0,2,1:T(8,128)S(1)}, u32[]{:S(2)}, u32[]{:S(2)}) collective-permute-start(f32[301,4,8]{0,2,1:T(8,128)S(1)} %get-tuple-element.12), channel_id=1, source_target_pairs={{0,124},{4,0},{8,4},{12,8},{16,12},{20,16},{24,20},{28,24},{32,28}... | collective-permute-start | bytes 115592 | tf_op jit(solution)/shard_map/ppermute | solution.py:25
  33.9 7.2 %collective-permute-start.5 = (f32[301,4,8]{0,2,1:T(8,128)S(1)}, f32[301,4,8]{0,2,1:T(8,128)S(1)}, u32[]{:S(2)}, u32[]{:S(2)}) collective-permute-start(f32[301,4,8]{0,2,1:T(8,128)S(1)} %get-tuple-element.13), channel_id=1, source_target_pairs={{0,4},{4,8},{8,12},{12,16},{16,20},{20,24},{24,28},{28,32},{32,36}... | collective-permute-start | bytes 115592 | tf_op jit(solution)/shard_map/ppermute | solution.py:26
  50.0 12.5 %copy-start.3 = (f32[301,16,128]{2,1,0:T(8,128)}, f32[301,16,128]{2,1,0:T(8,128)S(1)}, u32[]{:S(2)}) copy-start(f32[301,16,128]{2,1,0:T(8,128)S(1)} %pad_maximum_fusion.1.edge_ref) | copy-start | bytes 7397380
  101.2 11.7 %all-to-all-start.1 = ((f32[4,32,2,128]{3,2,0,1:T(2,128)}), f32[4,32,2,128]{3,2,0,1:T(2,128)S(1)}, u32[]{:S(2)}, u32[]{:S(2)}) async-start(f32[4,32,2,128]{3,2,0,1:T(2,128)} %copy.26), calls=%async_computation.1 | async-start | bytes 262144 | tf_op jit(solution)/shard_map/all_to_all | solution.py:331
  113.1 4.0 %collective-permute-start.6 = (f32[4,16,128]{2,1,0:T(8,128)S(1)}, f32[4,16,128]{2,1,0:T(8,128)S(1)}, u32[]{:S(2)}, u32[]{:S(2)}) collective-permute-start(f32[4,16,128]{2,1,0:T(8,128)S(1)} %convolution_bitcast_fusion), channel_id=1, source_target_pairs={{0,1},{1,0},{2,3},{3,2},{4,5},{5,4},{6,7},{7,6},{8,9},{9,8},{10,11... | collective-permute-start | bytes 98312 | tf_op jit(solution)/shard_map/ppermute | solution.py:277
  117.1 5.4 %collective-permute-start.7 = (f32[4,16,128]{2,1,0:T(8,128)S(1)}, f32[4,16,128]{2,1,0:T(8,128)S(1)}, u32[]{:S(2)}, u32[]{:S(2)}) collective-permute-start(f32[4,16,128]{2,1,0:T(8,128)S(1)} %add.79), channel_id=1, source_target_pairs={{0,2},{1,3},{2,0},{3,1},{4,6},{5,7},{6,4},{7,5},{8,10},{9,11},{10,... | collective-permute-start | bytes 98312 | tf_op jit(solution)/shard_map/ppermute | solution.py:277

commit v12 on v10

--- a/solution.py
+++ b/solution.py
@@ -231,7 +231,7 @@
         out_ref[:, pl.ds(y, 1), :] = total[:, None, :]
         return carry
 
-    lax.fori_loop(0, rows, row_step, 0)
+    lax.fori_loop(0, rows, row_step, 0, unroll=True)
 
 
 def scatter_kernel(back_ref, index_ref, weight_ref, out_ref):
@@ -253,7 +253,9 @@
             total = total + matmul_exact(split_parts(spread), onehot, 1)
         return total
 
-    out_ref[...] = lax.fori_loop(0, rows, row_step, jnp.zeros((stacked, lanes), jnp.float32))
+    out_ref[...] = lax.fori_loop(
+        0, rows, row_step, jnp.zeros((stacked, lanes), jnp.float32), unroll=True
+    )
 
 
 def remap_call(kernel, out_shape, *operands, after=()):

time: 124 us -> 122 us (0.984)
  Pallas kernels: 42.3 us -> 40.3 us
    pallas_call x2, Pallas kernels: 10.8 us -> 8.75 us  [remap_call(): pl.pallas_call(kernel, out_shape=jax.ShapeDtypeStruct(out_shape, jnp.floa...]
  transfers between devices with their start and end apart: 10 -> 10, of which waited for: 5 -> 5; matrix products, arithmetic and copies ran while one was open for 13% -> 14% of each run, Pallas kernels for 0% -> 0%
where the time goes in v12:
time: 122 us; the launch traced here: 121 us
  Pallas kernels  40.3 us (33%)
  starting transfers between devices  27.1 us (22%)
  waiting for transfers between devices  21.2 us (17%)
  other arithmetic  16.7 us (14%)
  local copies, waits for them, and re-layouts  14.8 us (12%)
    pallas_call x1, Pallas kernels, tridiagonal(): pl.pallas_call(tridiagonal_kernel, out_shape=(jax.ShapeDtypeStruct(shape,...  31.5 us
    ppermute x3, starting transfers between devices, from_neighbours(): lax.ppermute(lax.slice_in_dim(block, 0, width, axis=dim), axis, to_prev)  13.6 us
    pallas_call x2, Pallas kernels, remap_call(): pl.pallas_call(kernel, out_shape=jax.ShapeDtypeStruct(out_shape, jnp.floa...  8.75 us
    all_to_all x1, waiting for transfers between devices, shards(): lax.all_to_all(buffer.reshape(received.shape), 'lat', split_axis=1, conca...  7.82 us
    all_to_all x1, starting transfers between devices, shards(): lax.all_to_all(outgoing, 'lat', split_axis=1, concat_axis=1, tiled=True)  6.73 us
    ppermute x2, waiting for transfers between devices, sum_over(): values = values + lax.ppermute(values, axis, pairs)  6.53 us
    concatenate x2, other arithmetic, extended_planes(): stack = jnp.concatenate([planes, coast], axis=0)  5.41 us
    ppermute x3, waiting for transfers between devices, from_neighbours(): lax.ppermute(lax.slice_in_dim(block, size - width, size, axis=dim), axis,...  5.33 us
  transfers between devices with their start and end apart: 10, of which 5 were waited for; matrix products, arithmetic and copies ran while one was open for 14% of the time, Pallas kernels for 0%

profile of v12, /device:TPU:0, one launch (start us, length us, event | category | flops | bytes accessed | tf_op | source)
XLA Modules:
  0.0 121.1 jit_solution(6741873200363744670)
XLA Ops:
  1.4 3.5 %fusion = (f32[301,8,4]{2,1,0:T(8,128)}, f32[301,8,4]{2,1,0:T(8,128)}) fusion(f32[300,8,256]{2,1,0:T(8,128)} %bitcast.40, f32[1,8,256]{2,1,0:T(8,128)S(1)} %get-tuple-element.15), kind=kLoop, calls=%fused_computation.12 | loop fusion | flops 19264 | bytes 2542848 | tf_op jit(solution)/shard_map/concatenate | solution.py:34
  4.9 1.9 %copy.17 = f32[301,8,4]{0,1,2:T(8,128)S(1)} copy(f32[301,8,4]{2,1,0:T(8,128)} %get-tuple-element.6) | data formatting | bytes 77056 | tf_op jit(solution)/shard_map/slice | solution.py:25
  6.8 2.9 %collective-permute-start.2 = (f32[301,8,4]{0,1,2:T(8,128)S(1)}, f32[301,8,4]{0,1,2:T(8,128)S(1)}, u32[]{:S(2)}, u32[]{:S(2)}) collective-permute-start(f32[301,8,4]{0,1,2:T(8,128)S(1)} %copy.17), channel_id=1, source_target_pairs={{0,3},{1,0},{2,1},{3,2},{4,7},{5,4},{6,5},{7,6},{8,11},{9,8},{10,9... | collective-permute-start | bytes 115592 | tf_op jit(solution)/shard_map/ppermute | solution.py:25
  9.7 1.8 %copy.18 = f32[301,8,4]{0,1,2:T(8,128)S(1)} copy(f32[301,8,4]{2,1,0:T(8,128)} %get-tuple-element.7) | data formatting | bytes 77056 | tf_op jit(solution)/shard_map/slice | solution.py:26
  11.6 1.9 %fusion.1 = (f32[301,4,256]{2,1,0:T(4,128)}, f32[301,4,256]{2,1,0:T(4,128)}) fusion(f32[300,8,256]{2,1,0:T(8,128)S(1)} %bitcast.42, f32[1,8,256]{2,1,0:T(8,128)S(1)} %get-tuple-element.15), kind=kLoop, calls=%fused_computation.13 | loop fusion | flops 616448 | bytes 4931584 | tf_op jit(solution)/shard_map/concatenate | solution.py:34
  13.5 5.6 %collective-permute-start = (f32[301,4,256]{2,1,0:T(4,128)}, f32[301,4,256]{2,1,0:T(4,128)}, u32[]{:S(2)}, u32[]{:S(2)}) collective-permute-start(f32[301,4,256]{2,1,0:T(4,128)} %get-tuple-element.8), channel_id=1, source_target_pairs={{0,124},{4,0},{8,4},{12,8},{16,12},{20,16},{24,20},{28,24},{32,28}... | collective-permute-start | bytes 3698696 | tf_op jit(solution)/shard_map/ppermute | solution.py:25
  22.1 6.7 %all-to-all-start = ((f32[4,32,2,128]{3,2,0,1:T(2,128)}), f32[4,32,2,128]{3,2,0,1:T(2,128)S(1)}, u32[]{:S(2)}, u32[]{:S(2)}) async-start(f32[4,32,2,128]{3,2,0,1:T(2,128)} %bitcast.38), calls=%async_computation | async-start | bytes 262144 | tf_op jit(solution)/shard_map/all_to_all | solution.py:317
  28.9 5.0 %collective-permute-start.4 = (f32[301,4,8]{0,2,1:T(8,128)S(1)}, f32[301,4,8]{0,2,1:T(8,128)S(1)}, u32[]{:S(2)}, u32[]{:S(2)}) collective-permute-start(f32[301,4,8]{0,2,1:T(8,128)S(1)} %get-tuple-element.12), channel_id=1, source_target_pairs={{0,124},{4,0},{8,4},{12,8},{16,12},{20,16},{24,20},{28,24},{32,28}... | collective-permute-start | bytes 115592 | tf_op jit(solution)/shard_map/ppermute | solution.py:25
  34.2 1.6 %collective-permute-done.4 = f32[301,4,8]{0,2,1:T(8,128)S(1)} collective-permute-done((f32[301,4,8]{0,2,1:T(8,128)S(1)}, f32[301,4,8]{0,2,1:T(8,128)S(1)}, u32[]{:S(2)}, u32[]{:S(2)}) %collective-permute-start.4) | collective-permute-done | bytes 38560 | tf_op jit(solution)/shard_map/ppermute | solution.py:25
  35.8 5.3 %collective-permute-done.5 = f32[301,4,8]{0,2,1:T(8,128)S(1)} collective-permute-done((f32[301,4,8]{0,2,1:T(8,128)S(1)}, f32[301,4,8]{0,2,1:T(8,128)S(1)}, u32[]{:S(2)}, u32[]{:S(2)}) %collective-permute-start.5) | collective-permute-done | bytes 38560 | tf_op jit(solution)/shard_map/ppermute | solution.py:26
  41.2 2.9 %copy.21 = f32[301,16,4]{2,1,0:T(8,128)} copy(f32[301,16,4]{0,2,1:T(4,128)S(1)} %get-tuple-element.10) | data formatting | bytes 154112 | tf_op jit(solution)/shard_map/slice | solution.py:42
  44.0 2.9 %copy.22 = f32[301,16,4]{2,1,0:T(8,128)} copy(f32[301,16,4]{0,2,1:T(4,128)S(1)} %get-tuple-element.11) | data formatting | bytes 154112 | tf_op jit(solution)/shard_map/slice | solution.py:42
  46.9 3.1 %pad_maximum_fusion.1.after_and_out_1_.edge_ref = f32[301,16,128]{2,1,0:T(8,128)S(1)} fusion(f32[301,16,4]{2,1,0:T(8,128)} %copy.22, f32[301,16,4]{2,1,0:T(8,128)} %copy.21, f32[128]{0:T(128)S(1)} %pad.4.clone), kind=kLoop, calls=%fused_computation.8 | loop fusion | flops 1232896 | bytes 2620416 | tf_op jit(solution)/shard_map/concatenate | solution.py:42
  50.9 3.7 %pad_maximum_fusion.after_and_out_0_.rows_ref = f32[301,8,256]{2,1,0:T(8,128)} fusion(f32[301,4,256]{2,1,0:T(4,128)} %collective-permute-done.1, f32[301,4,256]{2,1,0:T(4,128)} %collective-permute-done), kind=kLoop, calls=%fused_computation.6 | loop fusion | flops 616448 | bytes 4931584 | tf_op jit(solution)/shard_map/concatenate | solution.py:43
  54.5 4.5 %shard_map.104 = f32[4,8,256]{2,1,0:T(8,128)} custom-call(f32[256,128]{1,0:T(8,128)} %bitcast.43, s32[32,256]{1,0:T(8,128)} %bitcast.46, f32[32,256]{1,0:T(8,128)} %bitcast.48, f32[301,8,256]{2,1,0:T(8,128)} %pad_maximum_fusion.after_and_out_0_.rows_ref, f32[301,16,128]{2,1,0:T(8,128)} %copy-done.2), custom_call_target="tpu_custom_call" | custom-call | tf_op jit(solution)/shard_map/pallas_call | solution.py:263
  59.1 1.4 %fusion.9.surf_ref = f32[8,256]{1,0:T(8,128)} fusion(f32[4,8,256]{2,1,0:T(8,128)} %shard_map.104), kind=kLoop, calls=%fused_computation.32 | loop fusion | flops 22528 | bytes 40960 | tf_op jit(solution)/shard_map/add | solution.py:328
  61.8 31.5 %shard_map.105 = (f32[4,75,8,256]{3,2,1,0:T(8,128)}, f32[4,8,256]{2,1,0:T(8,128)}) custom-call(f32[75]{0:T(128)} %constant.31.clone.decay_ref, f32[300,8,256]{2,1,0:T(8,128)} %bitcast.41, f32[301,8,256]{2,1,0:T(8,128)} %pad_maximum_fusion.after_and_out_0_.rows_ref, f32[301,16,128]{2,1,0:T(8,128)} %copy-done.2, f32[16,384]{1,0:T(8,128)} %maximum_select_fusion.mask_ref, ...), custom_call_target="tpu_custom_call" | custom-call | tf_op jit(solution)/shard_map/pallas_call | solution.py:180
  93.4 4.2 %shard_map.106 = f32[256,128]{1,0:T(8,128)} custom-call(f32[4,8,256]{2,1,0:T(8,128)} %get-tuple-element.5.back_ref, s32[32,256]{1,0:T(8,128)} %bitcast.47, f32[32,256]{1,0:T(8,128)} %bitcast.49), custom_call_target="tpu_custom_call" | custom-call | tf_op jit(solution)/shard_map/pallas_call | solution.py:263
  97.6 1.6 %copy.26 = f32[4,32,2,128]{3,2,0,1:T(2,128)} copy(f32[4,32,2,128]{3,2,1,0:T(2,128)} %bitcast.45) | data formatting | bytes 262144 | tf_op jit(solution)/shard_map/reshape | solution.py:334
  99.2 3.9 %all-to-all-start.1 = ((f32[4,32,2,128]{3,2,0,1:T(2,128)}), f32[4,32,2,128]{3,2,0,1:T(2,128)S(1)}, u32[]{:S(2)}, u32[]{:S(2)}) async-start(f32[4,32,2,128]{3,2,0,1:T(2,128)} %copy.26), calls=%async_computation.1 | async-start | bytes 262144 | tf_op jit(solution)/shard_map/all_to_all | solution.py:333
  103.1 7.8 %all-to-all-done.1 = f32[4,32,2,128]{3,2,0,1:T(2,128)S(1)} async-done(((f32[4,32,2,128]{3,2,0,1:T(2,128)}), f32[4,32,2,128]{3,2,0,1:T(2,128)S(1)}, u32[]{:S(2)}, u32[]{:S(2)}) %all-to-all-start.1) | async-done | bytes 131104 | tf_op jit(solution)/shard_map/all_to_all | solution.py:333
  111.6 3.5 %collective-permute-done.6 = f32[4,16,128]{2,1,0:T(8,128)S(1)} collective-permute-done((f32[4,16,128]{2,1,0:T(8,128)S(1)}, f32[4,16,128]{2,1,0:T(8,128)S(1)}, u32[]{:S(2)}, u32[]{:S(2)}) %collective-permute-start.6) | collective-permute-done | bytes 32800 | tf_op jit(solution)/shard_map/ppermute | solution.py:279
  115.1 2.4 %collective-permute-start.7 = (f32[4,16,128]{2,1,0:T(8,128)S(1)}, f32[4,16,128]{2,1,0:T(8,128)S(1)}, u32[]{:S(2)}, u32[]{:S(2)}) collective-permute-start(f32[4,16,128]{2,1,0:T(8,128)S(1)} %add.79), channel_id=1, source_target_pairs={{0,2},{1,3},{2,0},{3,1},{4,6},{5,7},{6,4},{7,5},{8,10},{9,11},{10,... | collective-permute-start | bytes 98312 | tf_op jit(solution)/shard_map/ppermute | solution.py:279
  117.4 3.1 %collective-permute-done.7 = f32[4,16,128]{2,1,0:T(8,128)S(1)} collective-permute-done((f32[4,16,128]{2,1,0:T(8,128)S(1)}, f32[4,16,128]{2,1,0:T(8,128)S(1)}, u32[]{:S(2)}, u32[]{:S(2)}) %collective-permute-start.7) | collective-permute-done | bytes 32800 | tf_op jit(solution)/shard_map/ppermute | solution.py:279
  (54 shorter events, 7.6 us)
Async XLA Ops:
  0.6 20.0 %copy-start = (f32[4,16,128]{2,1,0:T(8,128)S(1)}, f32[4,16,128]{2,1,0:T(8,128)}, u32[]{:S(2)}) copy-start(f32[4,16,128]{2,1,0:T(8,128)} %param.11) | copy-start | bytes 98308
  1.4 59.8 %copy-start.4 = (f32[8,256]{1,0:T(8,128)}, f32[8,256]{1,0:T(8,128)S(1)}, u32[]{:S(2)}) copy-start(f32[8,256]{1,0:T(8,128)S(1)} %get-tuple-element.14.land_ref) | copy-start | bytes 24580
  4.9 6.7 %copy-start.3 = (f32[4,75,8,256]{3,2,1,0:T(8,128)S(1)}, f32[4,75,8,256]{3,2,1,0:T(8,128)}, u32[]{:S(2)}) copy-start(f32[4,75,8,256]{3,2,1,0:T(8,128)} %param.9) | copy-start | bytes 7372804
  6.8 22.1 %collective-permute-start.2 = (f32[301,8,4]{0,1,2:T(8,128)S(1)}, f32[301,8,4]{0,1,2:T(8,128)S(1)}, u32[]{:S(2)}, u32[]{:S(2)}) collective-permute-start(f32[301,8,4]{0,1,2:T(8,128)S(1)} %copy.17), channel_id=1, source_target_pairs={{0,3},{1,0},{2,1},{3,2},{4,7},{5,4},{6,5},{7,6},{8,11},{9,8},{10,9... | collective-permute-start | bytes 115592 | tf_op jit(solution)/shard_map/ppermute | solution.py:25
  11.5 7.7 %copy-start.5 = (s32[1,32]{1,0:T(1,128)S(1)}, s32[1,32]{1,0:T(1,128)}, u32[]{:S(2)}) copy-start(s32[1,32]{1,0:T(1,128)} %param.12) | copy-start | bytes 388
  11.5 8.1 %copy-start.1 = (s32[1,64]{1,0:T(1,128)S(1)}, s32[1,64]{1,0:T(1,128)}, u32[]{:S(2)}) copy-start(s32[1,64]{1,0:T(1,128)} %param.13) | copy-start | bytes 772
  11.5 17.4 %collective-permute-start.3 = (f32[301,8,4]{0,1,2:T(8,128)S(1)}, f32[301,8,4]{0,1,2:T(8,128)S(1)}, u32[]{:S(2)}, u32[]{:S(2)}) collective-permute-start(f32[301,8,4]{0,1,2:T(8,128)S(1)} %copy.18), channel_id=1, source_target_pairs={{0,1},{1,2},{2,3},{3,0},{4,5},{5,6},{6,7},{7,4},{8,9},{9,10},{10,1... | collective-permute-start | bytes 115592 | tf_op jit(solution)/shard_map/ppermute | solution.py:26
  13.5 37.4 %collective-permute-start = (f32[301,4,256]{2,1,0:T(4,128)}, f32[301,4,256]{2,1,0:T(4,128)}, u32[]{:S(2)}, u32[]{:S(2)}) collective-permute-start(f32[301,4,256]{2,1,0:T(4,128)} %get-tuple-element.8), channel_id=1, source_target_pairs={{0,124},{4,0},{8,4},{12,8},{16,12},{20,16},{24,20},{28,24},{32,28}... | collective-permute-start | bytes 3698696 | tf_op jit(solution)/shard_map/ppermute | solution.py:25
  19.1 31.7 %collective-permute-start.1 = (f32[301,4,256]{2,1,0:T(4,128)}, f32[301,4,256]{2,1,0:T(4,128)}, u32[]{:S(2)}, u32[]{:S(2)}) collective-permute-start(f32[301,4,256]{2,1,0:T(4,128)} %get-tuple-element.9), channel_id=1, source_target_pairs={{0,4},{4,8},{8,12},{12,16},{16,20},{20,24},{24,28},{28,32},{32,36}... | collective-permute-start | bytes 3698696 | tf_op jit(solution)/shard_map/ppermute | solution.py:26
  22.1 27.9 %all-to-all-start = ((f32[4,32,2,128]{3,2,0,1:T(2,128)}), f32[4,32,2,128]{3,2,0,1:T(2,128)S(1)}, u32[]{:S(2)}, u32[]{:S(2)}) async-start(f32[4,32,2,128]{3,2,0,1:T(2,128)} %bitcast.38), calls=%async_computation | async-start | bytes 262144 | tf_op jit(solution)/shard_map/all_to_all | solution.py:317
  28.9 6.8 %collective-permute-start.4 = (f32[301,4,8]{0,2,1:T(8,128)S(1)}, f32[301,4,8]{0,2,1:T(8,128)S(1)}, u32[]{:S(2)}, u32[]{:S(2)}) collective-permute-start(f32[301,4,8]{0,2,1:T(8,128)S(1)} %get-tuple-element.12), channel_id=1, source_target_pairs={{0,124},{4,0},{8,4},{12,8},{16,12},{20,16},{24,20},{28,24},{32,28}... | collective-permute-start | bytes 115592 | tf_op jit(solution)/shard_map/ppermute | solution.py:25
  33.9 7.2 %collective-permute-start.5 = (f32[301,4,8]{0,2,1:T(8,128)S(1)}, f32[301,4,8]{0,2,1:T(8,128)S(1)}, u32[]{:S(2)}, u32[]{:S(2)}) collective-permute-start(f32[301,4,8]{0,2,1:T(8,128)S(1)} %get-tuple-element.13), channel_id=1, source_target_pairs={{0,4},{4,8},{8,12},{12,16},{16,20},{20,24},{24,28},{28,32},{32,36}... | collective-permute-start | bytes 115592 | tf_op jit(solution)/shard_map/ppermute | solution.py:26
  50.0 4.5 %copy-start.2 = (f32[301,16,128]{2,1,0:T(8,128)}, f32[301,16,128]{2,1,0:T(8,128)S(1)}, u32[]{:S(2)}) copy-start(f32[301,16,128]{2,1,0:T(8,128)S(1)} %pad_maximum_fusion.1.after_and_out_1_.edge_ref) | copy-start | bytes 7397380
  99.2 11.7 %all-to-all-start.1 = ((f32[4,32,2,128]{3,2,0,1:T(2,128)}), f32[4,32,2,128]{3,2,0,1:T(2,128)S(1)}, u32[]{:S(2)}, u32[]{:S(2)}) async-start(f32[4,32,2,128]{3,2,0,1:T(2,128)} %copy.26), calls=%async_computation.1 | async-start | bytes 262144 | tf_op jit(solution)/shard_map/all_to_all | solution.py:333
  111.1 4.0 %collective-permute-start.6 = (f32[4,16,128]{2,1,0:T(8,128)S(1)}, f32[4,16,128]{2,1,0:T(8,128)S(1)}, u32[]{:S(2)}, u32[]{:S(2)}) collective-permute-start(f32[4,16,128]{2,1,0:T(8,128)S(1)} %convolution_bitcast_fusion), channel_id=1, source_target_pairs={{0,1},{1,0},{2,3},{3,2},{4,5},{5,4},{6,7},{7,6},{8,9},{9,8},{10,11... | collective-permute-start | bytes 98312 | tf_op jit(solution)/shard_map/ppermute | solution.py:279
  115.1 5.4 %collective-permute-start.7 = (f32[4,16,128]{2,1,0:T(8,128)S(1)}, f32[4,16,128]{2,1,0:T(8,128)S(1)}, u32[]{:S(2)}, u32[]{:S(2)}) collective-permute-start(f32[4,16,128]{2,1,0:T(8,128)S(1)} %add.79), channel_id=1, source_target_pairs={{0,2},{1,3},{2,0},{3,1},{4,6},{5,7},{6,4},{7,5},{8,10},{9,11},{10,... | collective-permute-start | bytes 98312 | tf_op jit(solution)/shard_map/ppermute | solution.py:279

commit v13 on v12

--- a/solution.py
+++ b/solution.py
@@ -165,7 +165,7 @@
         return tuple(v for _, v in result)
 
     final = tuple(out_ref[f, levels - 1] for f in range(fields))
-    lax.fori_loop(0, levels - 1, backward, final)
+    lax.fori_loop(0, levels - 1, backward, final, unroll=2)
     land = land_ref[...]
     for f in range(fields):
         back_ref[f] = land * out_ref[f, 0]

time: 122 us -> 122 us (level)
  no operation moved by 1% of the time
where the time goes in v13:
time: 122 us; the launch traced here: 121 us
  Pallas kernels  40.2 us (33%)
  starting transfers between devices  27.1 us (22%)
  waiting for transfers between devices  21.2 us (17%)
  other arithmetic  16.7 us (14%)
  local copies, waits for them, and re-layouts  14.8 us (12%)
    pallas_call x1, Pallas kernels, tridiagonal(): pl.pallas_call(tridiagonal_kernel, out_shape=(jax.ShapeDtypeStruct(shape,...  31.4 us
    ppermute x3, starting transfers between devices, from_neighbours(): lax.ppermute(lax.slice_in_dim(block, 0, width, axis=dim), axis, to_prev)  13.6 us
    pallas_call x2, Pallas kernels, remap_call(): pl.pallas_call(kernel, out_shape=jax.ShapeDtypeStruct(out_shape, jnp.floa...  8.75 us
    all_to_all x1, waiting for transfers between devices, shards(): lax.all_to_all(buffer.reshape(received.shape), 'lat', split_axis=1, conca...  7.82 us
    all_to_all x1, starting transfers between devices, shards(): lax.all_to_all(outgoing, 'lat', split_axis=1, concat_axis=1, tiled=True)  6.73 us
    ppermute x2, waiting for transfers between devices, sum_over(): values = values + lax.ppermute(values, axis, pairs)  6.53 us
    concatenate x2, other arithmetic, extended_planes(): stack = jnp.concatenate([planes, coast], axis=0)  5.41 us
    ppermute x3, waiting for transfers between devices, from_neighbours(): lax.ppermute(lax.slice_in_dim(block, size - width, size, axis=dim), axis,...  5.33 us
  transfers between devices with their start and end apart: 10, of which 5 were waited for; matrix products, arithmetic and copies ran while one was open for 14% of the time, Pallas kernels for 0%

profile of v13, /device:TPU:0, one launch (start us, length us, event | category | flops | bytes accessed | tf_op | source)
XLA Modules:
  0.0 121.0 jit_solution(644390299961746702)
XLA Ops:
  1.4 3.5 %fusion = (f32[301,8,4]{2,1,0:T(8,128)}, f32[301,8,4]{2,1,0:T(8,128)}) fusion(f32[300,8,256]{2,1,0:T(8,128)} %bitcast.40, f32[1,8,256]{2,1,0:T(8,128)S(1)} %get-tuple-element.15), kind=kLoop, calls=%fused_computation.12 | loop fusion | flops 19264 | bytes 2542848 | tf_op jit(solution)/shard_map/concatenate | solution.py:34
  4.9 1.9 %copy.17 = f32[301,8,4]{0,1,2:T(8,128)S(1)} copy(f32[301,8,4]{2,1,0:T(8,128)} %get-tuple-element.6) | data formatting | bytes 77056 | tf_op jit(solution)/shard_map/slice | solution.py:25
  6.8 2.9 %collective-permute-start.2 = (f32[301,8,4]{0,1,2:T(8,128)S(1)}, f32[301,8,4]{0,1,2:T(8,128)S(1)}, u32[]{:S(2)}, u32[]{:S(2)}) collective-permute-start(f32[301,8,4]{0,1,2:T(8,128)S(1)} %copy.17), channel_id=1, source_target_pairs={{0,3},{1,0},{2,1},{3,2},{4,7},{5,4},{6,5},{7,6},{8,11},{9,8},{10,9... | collective-permute-start | bytes 115592 | tf_op jit(solution)/shard_map/ppermute | solution.py:25
  9.7 1.8 %copy.18 = f32[301,8,4]{0,1,2:T(8,128)S(1)} copy(f32[301,8,4]{2,1,0:T(8,128)} %get-tuple-element.7) | data formatting | bytes 77056 | tf_op jit(solution)/shard_map/slice | solution.py:26
  11.6 1.9 %fusion.1 = (f32[301,4,256]{2,1,0:T(4,128)}, f32[301,4,256]{2,1,0:T(4,128)}) fusion(f32[300,8,256]{2,1,0:T(8,128)S(1)} %bitcast.42, f32[1,8,256]{2,1,0:T(8,128)S(1)} %get-tuple-element.15), kind=kLoop, calls=%fused_computation.13 | loop fusion | flops 616448 | bytes 4931584 | tf_op jit(solution)/shard_map/concatenate | solution.py:34
  13.5 5.6 %collective-permute-start = (f32[301,4,256]{2,1,0:T(4,128)}, f32[301,4,256]{2,1,0:T(4,128)}, u32[]{:S(2)}, u32[]{:S(2)}) collective-permute-start(f32[301,4,256]{2,1,0:T(4,128)} %get-tuple-element.8), channel_id=1, source_target_pairs={{0,124},{4,0},{8,4},{12,8},{16,12},{20,16},{24,20},{28,24},{32,28}... | collective-permute-start | bytes 3698696 | tf_op jit(solution)/shard_map/ppermute | solution.py:25
  22.1 6.7 %all-to-all-start = ((f32[4,32,2,128]{3,2,0,1:T(2,128)}), f32[4,32,2,128]{3,2,0,1:T(2,128)S(1)}, u32[]{:S(2)}, u32[]{:S(2)}) async-start(f32[4,32,2,128]{3,2,0,1:T(2,128)} %bitcast.38), calls=%async_computation | async-start | bytes 262144 | tf_op jit(solution)/shard_map/all_to_all | solution.py:317
  28.9 5.0 %collective-permute-start.4 = (f32[301,4,8]{0,2,1:T(8,128)S(1)}, f32[301,4,8]{0,2,1:T(8,128)S(1)}, u32[]{:S(2)}, u32[]{:S(2)}) collective-permute-start(f32[301,4,8]{0,2,1:T(8,128)S(1)} %get-tuple-element.12), channel_id=1, source_target_pairs={{0,124},{4,0},{8,4},{12,8},{16,12},{20,16},{24,20},{28,24},{32,28}... | collective-permute-start | bytes 115592 | tf_op jit(solution)/shard_map/ppermute | solution.py:25
  34.2 1.6 %collective-permute-done.4 = f32[301,4,8]{0,2,1:T(8,128)S(1)} collective-permute-done((f32[301,4,8]{0,2,1:T(8,128)S(1)}, f32[301,4,8]{0,2,1:T(8,128)S(1)}, u32[]{:S(2)}, u32[]{:S(2)}) %collective-permute-start.4) | collective-permute-done | bytes 38560 | tf_op jit(solution)/shard_map/ppermute | solution.py:25
  35.8 5.3 %collective-permute-done.5 = f32[301,4,8]{0,2,1:T(8,128)S(1)} collective-permute-done((f32[301,4,8]{0,2,1:T(8,128)S(1)}, f32[301,4,8]{0,2,1:T(8,128)S(1)}, u32[]{:S(2)}, u32[]{:S(2)}) %collective-permute-start.5) | collective-permute-done | bytes 38560 | tf_op jit(solution)/shard_map/ppermute | solution.py:26
  41.2 2.9 %copy.21 = f32[301,16,4]{2,1,0:T(8,128)} copy(f32[301,16,4]{0,2,1:T(4,128)S(1)} %get-tuple-element.10) | data formatting | bytes 154112 | tf_op jit(solution)/shard_map/slice | solution.py:42
  44.0 2.9 %copy.22 = f32[301,16,4]{2,1,0:T(8,128)} copy(f32[301,16,4]{0,2,1:T(4,128)S(1)} %get-tuple-element.11) | data formatting | bytes 154112 | tf_op jit(solution)/shard_map/slice | solution.py:42
  46.9 3.1 %pad_maximum_fusion.1.after_and_out_1_.edge_ref = f32[301,16,128]{2,1,0:T(8,128)S(1)} fusion(f32[301,16,4]{2,1,0:T(8,128)} %copy.22, f32[301,16,4]{2,1,0:T(8,128)} %copy.21, f32[128]{0:T(128)S(1)} %pad.4.clone), kind=kLoop, calls=%fused_computation.8 | loop fusion | flops 1232896 | bytes 2620416 | tf_op jit(solution)/shard_map/concatenate | solution.py:42
  50.9 3.7 %pad_maximum_fusion.after_and_out_0_.rows_ref = f32[301,8,256]{2,1,0:T(8,128)} fusion(f32[301,4,256]{2,1,0:T(4,128)} %collective-permute-done.1, f32[301,4,256]{2,1,0:T(4,128)} %collective-permute-done), kind=kLoop, calls=%fused_computation.6 | loop fusion | flops 616448 | bytes 4931584 | tf_op jit(solution)/shard_map/concatenate | solution.py:43
  54.5 4.5 %shard_map.104 = f32[4,8,256]{2,1,0:T(8,128)} custom-call(f32[256,128]{1,0:T(8,128)} %bitcast.43, s32[32,256]{1,0:T(8,128)} %bitcast.46, f32[32,256]{1,0:T(8,128)} %bitcast.48, f32[301,8,256]{2,1,0:T(8,128)} %pad_maximum_fusion.after_and_out_0_.rows_ref, f32[301,16,128]{2,1,0:T(8,128)} %copy-done.2), custom_call_target="tpu_custom_call" | custom-call | tf_op jit(solution)/shard_map/pallas_call | solution.py:263
  59.1 1.4 %fusion.9.surf_ref = f32[8,256]{1,0:T(8,128)} fusion(f32[4,8,256]{2,1,0:T(8,128)} %shard_map.104), kind=kLoop, calls=%fused_computation.32 | loop fusion | flops 22528 | bytes 40960 | tf_op jit(solution)/shard_map/add | solution.py:328
  61.8 31.4 %shard_map.105 = (f32[4,75,8,256]{3,2,1,0:T(8,128)}, f32[4,8,256]{2,1,0:T(8,128)}) custom-call(f32[75]{0:T(128)} %constant.31.clone.decay_ref, f32[300,8,256]{2,1,0:T(8,128)} %bitcast.41, f32[301,8,256]{2,1,0:T(8,128)} %pad_maximum_fusion.after_and_out_0_.rows_ref, f32[301,16,128]{2,1,0:T(8,128)} %copy-done.2, f32[16,384]{1,0:T(8,128)} %maximum_select_fusion.mask_ref, ...), custom_call_target="tpu_custom_call" | custom-call | tf_op jit(solution)/shard_map/pallas_call | solution.py:180
  93.3 4.2 %shard_map.106 = f32[256,128]{1,0:T(8,128)} custom-call(f32[4,8,256]{2,1,0:T(8,128)} %get-tuple-element.5.back_ref, s32[32,256]{1,0:T(8,128)} %bitcast.47, f32[32,256]{1,0:T(8,128)} %bitcast.49), custom_call_target="tpu_custom_call" | custom-call | tf_op jit(solution)/shard_map/pallas_call | solution.py:263
  97.5 1.6 %copy.26 = f32[4,32,2,128]{3,2,0,1:T(2,128)} copy(f32[4,32,2,128]{3,2,1,0:T(2,128)} %bitcast.45) | data formatting | bytes 262144 | tf_op jit(solution)/shard_map/reshape | solution.py:334
  99.1 3.9 %all-to-all-start.1 = ((f32[4,32,2,128]{3,2,0,1:T(2,128)}), f32[4,32,2,128]{3,2,0,1:T(2,128)S(1)}, u32[]{:S(2)}, u32[]{:S(2)}) async-start(f32[4,32,2,128]{3,2,0,1:T(2,128)} %copy.26), calls=%async_computation.1 | async-start | bytes 262144 | tf_op jit(solution)/shard_map/all_to_all | solution.py:333
  103.0 7.8 %all-to-all-done.1 = f32[4,32,2,128]{3,2,0,1:T(2,128)S(1)} async-done(((f32[4,32,2,128]{3,2,0,1:T(2,128)}), f32[4,32,2,128]{3,2,0,1:T(2,128)S(1)}, u32[]{:S(2)}, u32[]{:S(2)}) %all-to-all-start.1) | async-done | bytes 131104 | tf_op jit(solution)/shard_map/all_to_all | solution.py:333
  111.5 3.5 %collective-permute-done.6 = f32[4,16,128]{2,1,0:T(8,128)S(1)} collective-permute-done((f32[4,16,128]{2,1,0:T(8,128)S(1)}, f32[4,16,128]{2,1,0:T(8,128)S(1)}, u32[]{:S(2)}, u32[]{:S(2)}) %collective-permute-start.6) | collective-permute-done | bytes 32800 | tf_op jit(solution)/shard_map/ppermute | solution.py:279
  115.0 2.4 %collective-permute-start.7 = (f32[4,16,128]{2,1,0:T(8,128)S(1)}, f32[4,16,128]{2,1,0:T(8,128)S(1)}, u32[]{:S(2)}, u32[]{:S(2)}) collective-permute-start(f32[4,16,128]{2,1,0:T(8,128)S(1)} %add.79), channel_id=1, source_target_pairs={{0,2},{1,3},{2,0},{3,1},{4,6},{5,7},{6,4},{7,5},{8,10},{9,11},{10,... | collective-permute-start | bytes 98312 | tf_op jit(solution)/shard_map/ppermute | solution.py:279
  117.3 3.1 %collective-permute-done.7 = f32[4,16,128]{2,1,0:T(8,128)S(1)} collective-permute-done((f32[4,16,128]{2,1,0:T(8,128)S(1)}, f32[4,16,128]{2,1,0:T(8,128)S(1)}, u32[]{:S(2)}, u32[]{:S(2)}) %collective-permute-start.7) | collective-permute-done | bytes 32800 | tf_op jit(solution)/shard_map/ppermute | solution.py:279
  (54 shorter events, 7.6 us)
Async XLA Ops:
  0.6 20.0 %copy-start = (f32[4,16,128]{2,1,0:T(8,128)S(1)}, f32[4,16,128]{2,1,0:T(8,128)}, u32[]{:S(2)}) copy-start(f32[4,16,128]{2,1,0:T(8,128)} %param.11) | copy-start | bytes 98308
  1.4 59.8 %copy-start.4 = (f32[8,256]{1,0:T(8,128)}, f32[8,256]{1,0:T(8,128)S(1)}, u32[]{:S(2)}) copy-start(f32[8,256]{1,0:T(8,128)S(1)} %get-tuple-element.14.land_ref) | copy-start | bytes 24580
  4.9 6.7 %copy-start.3 = (f32[4,75,8,256]{3,2,1,0:T(8,128)S(1)}, f32[4,75,8,256]{3,2,1,0:T(8,128)}, u32[]{:S(2)}) copy-start(f32[4,75,8,256]{3,2,1,0:T(8,128)} %param.9) | copy-start | bytes 7372804
  6.8 22.1 %collective-permute-start.2 = (f32[301,8,4]{0,1,2:T(8,128)S(1)}, f32[301,8,4]{0,1,2:T(8,128)S(1)}, u32[]{:S(2)}, u32[]{:S(2)}) collective-permute-start(f32[301,8,4]{0,1,2:T(8,128)S(1)} %copy.17), channel_id=1, source_target_pairs={{0,3},{1,0},{2,1},{3,2},{4,7},{5,4},{6,5},{7,6},{8,11},{9,8},{10,9... | collective-permute-start | bytes 115592 | tf_op jit(solution)/shard_map/ppermute | solution.py:25
  11.5 7.7 %copy-start.5 = (s32[1,32]{1,0:T(1,128)S(1)}, s32[1,32]{1,0:T(1,128)}, u32[]{:S(2)}) copy-start(s32[1,32]{1,0:T(1,128)} %param.12) | copy-start | bytes 388
  11.5 8.1 %copy-start.1 = (s32[1,64]{1,0:T(1,128)S(1)}, s32[1,64]{1,0:T(1,128)}, u32[]{:S(2)}) copy-start(s32[1,64]{1,0:T(1,128)} %param.13) | copy-start | bytes 772
  11.5 17.4 %collective-permute-start.3 = (f32[301,8,4]{0,1,2:T(8,128)S(1)}, f32[301,8,4]{0,1,2:T(8,128)S(1)}, u32[]{:S(2)}, u32[]{:S(2)}) collective-permute-start(f32[301,8,4]{0,1,2:T(8,128)S(1)} %copy.18), channel_id=1, source_target_pairs={{0,1},{1,2},{2,3},{3,0},{4,5},{5,6},{6,7},{7,4},{8,9},{9,10},{10,1... | collective-permute-start | bytes 115592 | tf_op jit(solution)/shard_map/ppermute | solution.py:26
  13.5 37.4 %collective-permute-start = (f32[301,4,256]{2,1,0:T(4,128)}, f32[301,4,256]{2,1,0:T(4,128)}, u32[]{:S(2)}, u32[]{:S(2)}) collective-permute-start(f32[301,4,256]{2,1,0:T(4,128)} %get-tuple-element.8), channel_id=1, source_target_pairs={{0,124},{4,0},{8,4},{12,8},{16,12},{20,16},{24,20},{28,24},{32,28}... | collective-permute-start | bytes 3698696 | tf_op jit(solution)/shard_map/ppermute | solution.py:25
  19.1 31.7 %collective-permute-start.1 = (f32[301,4,256]{2,1,0:T(4,128)}, f32[301,4,256]{2,1,0:T(4,128)}, u32[]{:S(2)}, u32[]{:S(2)}) collective-permute-start(f32[301,4,256]{2,1,0:T(4,128)} %get-tuple-element.9), channel_id=1, source_target_pairs={{0,4},{4,8},{8,12},{12,16},{16,20},{20,24},{24,28},{28,32},{32,36}... | collective-permute-start | bytes 3698696 | tf_op jit(solution)/shard_map/ppermute | solution.py:26
  22.1 27.9 %all-to-all-start = ((f32[4,32,2,128]{3,2,0,1:T(2,128)}), f32[4,32,2,128]{3,2,0,1:T(2,128)S(1)}, u32[]{:S(2)}, u32[]{:S(2)}) async-start(f32[4,32,2,128]{3,2,0,1:T(2,128)} %bitcast.38), calls=%async_computation | async-start | bytes 262144 | tf_op jit(solution)/shard_map/all_to_all | solution.py:317
  28.9 6.8 %collective-permute-start.4 = (f32[301,4,8]{0,2,1:T(8,128)S(1)}, f32[301,4,8]{0,2,1:T(8,128)S(1)}, u32[]{:S(2)}, u32[]{:S(2)}) collective-permute-start(f32[301,4,8]{0,2,1:T(8,128)S(1)} %get-tuple-element.12), channel_id=1, source_target_pairs={{0,124},{4,0},{8,4},{12,8},{16,12},{20,16},{24,20},{28,24},{32,28}... | collective-permute-start | bytes 115592 | tf_op jit(solution)/shard_map/ppermute | solution.py:25
  33.9 7.2 %collective-permute-start.5 = (f32[301,4,8]{0,2,1:T(8,128)S(1)}, f32[301,4,8]{0,2,1:T(8,128)S(1)}, u32[]{:S(2)}, u32[]{:S(2)}) collective-permute-start(f32[301,4,8]{0,2,1:T(8,128)S(1)} %get-tuple-element.13), channel_id=1, source_target_pairs={{0,4},{4,8},{8,12},{12,16},{16,20},{20,24},{24,28},{28,32},{32,36}... | collective-permute-start | bytes 115592 | tf_op jit(solution)/shard_map/ppermute | solution.py:26
  50.0 4.5 %copy-start.2 = (f32[301,16,128]{2,1,0:T(8,128)}, f32[301,16,128]{2,1,0:T(8,128)S(1)}, u32[]{:S(2)}) copy-start(f32[301,16,128]{2,1,0:T(8,128)S(1)} %pad_maximum_fusion.1.after_and_out_1_.edge_ref) | copy-start | bytes 7397380
  99.1 11.7 %all-to-all-start.1 = ((f32[4,32,2,128]{3,2,0,1:T(2,128)}), f32[4,32,2,128]{3,2,0,1:T(2,128)S(1)}, u32[]{:S(2)}, u32[]{:S(2)}) async-start(f32[4,32,2,128]{3,2,0,1:T(2,128)} %copy.26), calls=%async_computation.1 | async-start | bytes 262144 | tf_op jit(solution)/shard_map/all_to_all | solution.py:333
  111.0 4.0 %collective-permute-start.6 = (f32[4,16,128]{2,1,0:T(8,128)S(1)}, f32[4,16,128]{2,1,0:T(8,128)S(1)}, u32[]{:S(2)}, u32[]{:S(2)}) collective-permute-start(f32[4,16,128]{2,1,0:T(8,128)S(1)} %convolution_bitcast_fusion), channel_id=1, source_target_pairs={{0,1},{1,0},{2,3},{3,2},{4,5},{5,4},{6,7},{7,6},{8,9},{9,8},{10,11... | collective-permute-start | bytes 98312 | tf_op jit(solution)/shard_map/ppermute | solution.py:279
  115.0 5.4 %collective-permute-start.7 = (f32[4,16,128]{2,1,0:T(8,128)S(1)}, f32[4,16,128]{2,1,0:T(8,128)S(1)}, u32[]{:S(2)}, u32[]{:S(2)}) collective-permute-start(f32[4,16,128]{2,1,0:T(8,128)S(1)} %add.79), channel_id=1, source_target_pairs={{0,2},{1,3},{2,0},{3,1},{4,6},{5,7},{6,4},{7,5},{8,10},{9,11},{10,... | collective-permute-start | bytes 98312 | tf_op jit(solution)/shard_map/ppermute | solution.py:279

commit v14 on v13

--- a/solution.py
+++ b/solution.py
@@ -33,13 +33,12 @@
     coast = land_mask.astype(jnp.float32)[None]
     stack = jnp.concatenate([planes, coast], axis=0)
     south, north = from_neighbours(stack, "lat", 1, width)
-    east, west = from_neighbours(stack, "lon", 2, width)
-    sides = jnp.concatenate([east, west], axis=2)
+    tile = 128
+    east_tile, west_tile = from_neighbours(stack, "lon", 2, tile)
+    lane = lax.broadcasted_iota(jnp.int32, east_tile.shape, 2)
+    sides = jnp.where(lane < width, east_tile, west_tile)
     corner_south, corner_north = from_neighbours(sides, "lat", 1, width)
-    wide = -(-(2 * width) // 128) * 128
-    edges = jnp.concatenate([sides, corner_south, corner_north], axis=1)
-    gap = jnp.zeros(edges.shape[:2] + (wide - 2 * width,), jnp.float32)
-    edge_tile = jnp.concatenate([edges[:, :, :width], gap, edges[:, :, width:]], axis=2)
+    edge_tile = jnp.concatenate([sides, corner_south, corner_north], axis=1)
     halo_rows = jnp.concatenate([south, north], axis=1)
     coast_plane = jnp.concatenate(
         [jnp.concatenate([stack[-1], halo_rows[-1]], axis=0), edge_tile[-1]], axis=1

time: 122 us -> 132 us (1.082)
  waiting for transfers between devices: 21.2 us -> 39.7 us
  local copies, waits for them, and re-layouts: 14.8 us -> 8.02 us
  other arithmetic: 16.7 us -> 14.1 us
    ppermute x3, waiting for transfers between devices: 5.33 us -> 18.4 us  [from_neighbours(): lax.ppermute(lax.slice_in_dim(block, size - width, size, axis=dim), axis,...]
    all_to_all x1, waiting for transfers between devices: 0.01 us -> 7.63 us  [shards(): lax.all_to_all(outgoing, 'lat', split_axis=1, concat_axis=1, tiled=True)]
    slice x4 -> x0, local copies, waits for them, and re-layouts: 7.52 us -> none  [the longest x2 2.9 us: extended_planes(): edges[:, :, :width]]
    concatenate x3 -> x1, other arithmetic: 3.19 us -> 1.4 us  [extended_planes(): edge_tile = jnp.concatenate([sides, corner_south, corner_north], axis=1)]
    select_n x0 -> x1, other arithmetic: none -> 1.78 us  [extended_planes(): sides = jnp.where(lane < width, east_tile, west_tile)]
    concatenate x1, other arithmetic: 3.67 us -> 2.06 us  [extended_planes(): halo_rows = jnp.concatenate([south, north], axis=1)]
    ppermute x3, starting transfers between devices: 0.08 us -> 1.61 us  [from_neighbours(): lax.ppermute(lax.slice_in_dim(block, size - width, size, axis=dim), axis,...]
    unnamed x12 -> x16, local copies, waits for them, and re-layouts: 0.03 us -> 1.52 us
  transfers between devices with their start and end apart: 10 -> 10, of which waited for: 5 -> 6; matrix products, arithmetic and copies ran while one was open for 14% -> 8% of each run, Pallas kernels for 0% -> 0%
where the time goes in v14:
time: 132 us; the launch traced here: 131 us
  Pallas kernels  40.2 us (30%)
  waiting for transfers between devices  39.7 us (30%)
  starting transfers between devices  28 us (21%)
  other arithmetic  14.1 us (11%)
  local copies, waits for them, and re-layouts  8.02 us (6%)
    pallas_call x1, Pallas kernels, tridiagonal(): pl.pallas_call(tridiagonal_kernel, out_shape=(jax.ShapeDtypeStruct(shape,...  31.4 us
    ppermute x3, waiting for transfers between devices, from_neighbours(): lax.ppermute(lax.slice_in_dim(block, size - width, size, axis=dim), axis,...  18.4 us
    ppermute x3, starting transfers between devices, from_neighbours(): lax.ppermute(lax.slice_in_dim(block, 0, width, axis=dim), axis, to_prev)  12.2 us
    pallas_call x2, Pallas kernels, remap_call(): pl.pallas_call(kernel, out_shape=jax.ShapeDtypeStruct(out_shape, jnp.floa...  8.74 us
    all_to_all x1, waiting for transfers between devices, shards(): lax.all_to_all(buffer.reshape(received.shape), 'lat', split_axis=1, conca...  7.82 us
    all_to_all x1, waiting for transfers between devices, shards(): lax.all_to_all(outgoing, 'lat', split_axis=1, concat_axis=1, tiled=True)  7.63 us
    all_to_all x1, starting transfers between devices, shards(): lax.all_to_all(outgoing, 'lat', split_axis=1, concat_axis=1, tiled=True)  6.73 us
    ppermute x2, waiting for transfers between devices, sum_over(): values = values + lax.ppermute(values, axis, pairs)  5.71 us
  transfers between devices with their start and end apart: 10, of which 6 were waited for; matrix products, arithmetic and copies ran while one was open for 8% of the time, Pallas kernels for 0%

profile of v14, /device:TPU:0, one launch (start us, length us, event | category | flops | bytes accessed | tf_op | source)
XLA Modules:
  0.0 131.1 jit_solution(16896823694802323273)
XLA Ops:
  1.4 3.4 %pad_maximum_fusion.2 = (f32[301,8,128]{2,1,0:T(8,128)}, f32[301,8,128]{2,1,0:T(8,128)}) fusion(f32[1,8,256]{2,1,0:T(8,128)S(1)} %get-tuple-element.13, f32[300,8,256]{2,1,0:T(8,128)} %bitcast.40), kind=kLoop, calls=%fused_computation.15 | loop fusion | flops 616448 | bytes 4931584 | tf_op jit(solution)/shard_map/concatenate | solution.py:34
  4.7 1.6 %collective-permute-start.3 = (f32[301,8,128]{2,1,0:T(8,128)}, f32[301,8,128]{2,1,0:T(8,128)}, u32[]{:S(2)}, u32[]{:S(2)}) collective-permute-start(f32[301,8,128]{2,1,0:T(8,128)} %get-tuple-element.6), channel_id=1, source_target_pairs={{0,1},{1,2},{2,3},{3,0},{4,5},{5,6},{6,7},{7,4},{8,9},{9,10},{10,1... | collective-permute-start | bytes 3698696 | tf_op jit(solution)/shard_map/ppermute | solution.py:26
  6.3 1.6 %collective-permute-start.2 = (f32[301,8,128]{2,1,0:T(8,128)}, f32[301,8,128]{2,1,0:T(8,128)}, u32[]{:S(2)}, u32[]{:S(2)}) collective-permute-start(f32[301,8,128]{2,1,0:T(8,128)} %get-tuple-element.7), channel_id=1, source_target_pairs={{0,3},{1,0},{2,1},{3,2},{4,7},{5,4},{6,5},{7,6},{8,11},{9,8},{10,9... | collective-permute-start | bytes 3698696 | tf_op jit(solution)/shard_map/ppermute | solution.py:25
  8.0 1.8 %fusion.1 = (f32[301,4,256]{2,1,0:T(4,128)}, f32[301,4,256]{2,1,0:T(4,128)}) fusion(f32[300,8,256]{2,1,0:T(8,128)S(1)} %bitcast.42, f32[1,8,256]{2,1,0:T(8,128)S(1)} %get-tuple-element.13), kind=kLoop, calls=%fused_computation.13 | loop fusion | flops 616448 | bytes 4931584 | tf_op jit(solution)/shard_map/concatenate | solution.py:34
  9.8 5.5 %collective-permute-start = (f32[301,4,256]{2,1,0:T(4,128)}, f32[301,4,256]{2,1,0:T(4,128)S(1)}, u32[]{:S(2)}, u32[]{:S(2)}) collective-permute-start(f32[301,4,256]{2,1,0:T(4,128)} %get-tuple-element.8), channel_id=1, source_target_pairs={{0,124},{4,0},{8,4},{12,8},{16,12},{20,16},{24,20},{28,24},{32,28}... | collective-permute-start | bytes 3698696 | tf_op jit(solution)/shard_map/ppermute | solution.py:25
  16.7 18.4 %collective-permute-done.3 = f32[301,8,128]{2,1,0:T(8,128)} collective-permute-done((f32[301,8,128]{2,1,0:T(8,128)}, f32[301,8,128]{2,1,0:T(8,128)}, u32[]{:S(2)}, u32[]{:S(2)}) %collective-permute-start.3) | collective-permute-done | bytes 1232928 | tf_op jit(solution)/shard_map/ppermute | solution.py:26
  35.2 1.8 %broadcast_select_fusion = f32[301,8,128]{2,1,0:T(8,128)S(1)} fusion(f32[301,8,128]{2,1,0:T(8,128)} %collective-permute-done.2, f32[301,8,128]{2,1,0:T(8,128)} %collective-permute-done.3, pred[128]{0:T(512)(128)(4,1)S(1)} %iota_compare_fusion.2), kind=kLoop, calls=%fused_computation.17 | loop fusion | flops 308224 | bytes 3698816 | tf_op jit(solution)/shard_map/jit(_where)/select_n | solution.py:39
  37.0 1.4 %fusion.15 = (f32[301,4,128]{2,1,0:T(4,128)}, f32[301,4,128]{2,1,0:T(4,128)}) fusion(f32[301,8,128]{2,1,0:T(8,128)S(1)} %broadcast_select_fusion), kind=kLoop, calls=%fused_computation.46 | loop fusion | bytes 2465792 | tf_op jit(solution)/shard_map/slice | solution.py:25
  38.5 5.1 %collective-permute-start.4 = (f32[301,4,128]{2,1,0:T(4,128)}, f32[301,4,128]{2,1,0:T(4,128)S(1)}, u32[]{:S(2)}, u32[]{:S(2)}) collective-permute-start(f32[301,4,128]{2,1,0:T(4,128)} %get-tuple-element.10), channel_id=1, source_target_pairs={{0,124},{4,0},{8,4},{12,8},{16,12},{20,16},{24,20},{28,24},{32,28}... | collective-permute-start | bytes 1849352 | tf_op jit(solution)/shard_map/ppermute | solution.py:25
  45.1 6.7 %all-to-all-start = ((f32[4,32,2,128]{3,2,0,1:T(2,128)}), f32[4,32,2,128]{3,2,0,1:T(2,128)S(1)}, u32[]{:S(2)}, u32[]{:S(2)}) async-start(f32[4,32,2,128]{3,2,0,1:T(2,128)} %bitcast.38), calls=%async_computation | async-start | bytes 262144 | tf_op jit(solution)/shard_map/all_to_all | solution.py:316
  52.1 7.6 %all-to-all-done = f32[4,32,2,128]{3,2,0,1:T(2,128)S(1)} async-done(((f32[4,32,2,128]{3,2,0,1:T(2,128)}), f32[4,32,2,128]{3,2,0,1:T(2,128)S(1)}, u32[]{:S(2)}, u32[]{:S(2)}) %all-to-all-start) | async-done | bytes 131104 | tf_op jit(solution)/shard_map/all_to_all | solution.py:316
  60.4 2.1 %pad_maximum_fusion.after_and_out_0_.rows_ref = f32[301,8,256]{2,1,0:T(8,128)} fusion(f32[301,4,256]{2,1,0:T(4,128)S(1)} %collective-permute-done.1, f32[301,4,256]{2,1,0:T(4,128)S(1)} %collective-permute-done), kind=kLoop, calls=%fused_computation.6 | loop fusion | flops 616448 | bytes 4931584 | tf_op jit(solution)/shard_map/concatenate | solution.py:42
  62.5 1.4 %pad_maximum_fusion.1.after_and_out_1_.edge_ref = f32[301,16,128]{2,1,0:T(8,128)S(1)} fusion(f32[301,4,128]{2,1,0:T(4,128)} %collective-permute-done.5, f32[301,4,128]{2,1,0:T(4,128)S(1)} %collective-permute-done.4, f32[301,8,128]{2,1,0:T(8,128)S(1)} %copy-done.5), kind=kLoop, calls=%fused_computation.8 | loop fusion | flops 1232896 | bytes 4931584 | tf_op jit(solution)/shard_map/concatenate | solution.py:41
  63.9 1.5 %copy-done.2 = f32[301,16,128]{2,1,0:T(8,128)} copy-done((f32[301,16,128]{2,1,0:T(8,128)}, f32[301,16,128]{2,1,0:T(8,128)S(1)}, u32[]{:S(2)}) %copy-start.2) | copy-done | bytes 2465816
  65.4 4.6 %shard_map.104 = f32[4,8,256]{2,1,0:T(8,128)} custom-call(f32[256,128]{1,0:T(8,128)} %bitcast.43, s32[32,256]{1,0:T(8,128)} %bitcast.46, f32[32,256]{1,0:T(8,128)} %bitcast.48, f32[301,8,256]{2,1,0:T(8,128)} %pad_maximum_fusion.after_and_out_0_.rows_ref, f32[301,16,128]{2,1,0:T(8,128)} %copy-done.2), custom_call_target="tpu_custom_call" | custom-call | tf_op jit(solution)/shard_map/pallas_call | solution.py:262
  69.9 1.4 %fusion.8.surf_ref = f32[8,256]{1,0:T(8,128)} fusion(f32[4,8,256]{2,1,0:T(8,128)} %shard_map.104), kind=kLoop, calls=%fused_computation.28 | loop fusion | flops 22528 | bytes 40960 | tf_op jit(solution)/shard_map/add | solution.py:327
  72.0 31.4 %shard_map.105 = (f32[4,75,8,256]{3,2,1,0:T(8,128)}, f32[4,8,256]{2,1,0:T(8,128)}) custom-call(f32[75]{0:T(128)} %constant.32.clone.decay_ref, f32[300,8,256]{2,1,0:T(8,128)} %bitcast.41, f32[301,8,256]{2,1,0:T(8,128)} %pad_maximum_fusion.after_and_out_0_.rows_ref, f32[301,16,128]{2,1,0:T(8,128)} %copy-done.2, f32[16,384]{1,0:T(8,128)} %maximum_select_fusion.mask_ref, ...), custom_call_target="tpu_custom_call" | custom-call | tf_op jit(solution)/shard_map/pallas_call | solution.py:179
  103.4 4.2 %shard_map.106 = f32[256,128]{1,0:T(8,128)} custom-call(f32[4,8,256]{2,1,0:T(8,128)} %get-tuple-element.5.back_ref, s32[32,256]{1,0:T(8,128)} %bitcast.47, f32[32,256]{1,0:T(8,128)} %bitcast.49), custom_call_target="tpu_custom_call" | custom-call | tf_op jit(solution)/shard_map/pallas_call | solution.py:262
  107.6 1.6 %copy.20 = f32[4,32,2,128]{3,2,0,1:T(2,128)} copy(f32[4,32,2,128]{3,2,1,0:T(2,128)} %bitcast.45) | data formatting | bytes 262144 | tf_op jit(solution)/shard_map/reshape | solution.py:333
  109.2 3.8 %all-to-all-start.1 = ((f32[4,32,2,128]{3,2,0,1:T(2,128)}), f32[4,32,2,128]{3,2,0,1:T(2,128)S(1)}, u32[]{:S(2)}, u32[]{:S(2)}) async-start(f32[4,32,2,128]{3,2,0,1:T(2,128)} %copy.20), calls=%async_computation.1 | async-start | bytes 262144 | tf_op jit(solution)/shard_map/all_to_all | solution.py:332
  113.1 7.8 %all-to-all-done.1 = f32[4,32,2,128]{3,2,0,1:T(2,128)S(1)} async-done(((f32[4,32,2,128]{3,2,0,1:T(2,128)}), f32[4,32,2,128]{3,2,0,1:T(2,128)S(1)}, u32[]{:S(2)}, u32[]{:S(2)}) %all-to-all-start.1) | async-done | bytes 131104 | tf_op jit(solution)/shard_map/all_to_all | solution.py:332
  122.3 2.7 %collective-permute-done.6 = f32[4,16,128]{2,1,0:T(8,128)S(1)} collective-permute-done((f32[4,16,128]{2,1,0:T(8,128)S(1)}, f32[4,16,128]{2,1,0:T(8,128)S(1)}, u32[]{:S(2)}, u32[]{:S(2)}) %collective-permute-start.6) | collective-permute-done | bytes 32800 | tf_op jit(solution)/shard_map/ppermute | solution.py:278
  125.1 2.4 %collective-permute-start.7 = (f32[4,16,128]{2,1,0:T(8,128)S(1)}, f32[4,16,128]{2,1,0:T(8,128)S(1)}, u32[]{:S(2)}, u32[]{:S(2)}) collective-permute-start(f32[4,16,128]{2,1,0:T(8,128)S(1)} %add.79), channel_id=1, source_target_pairs={{0,2},{1,3},{2,0},{3,1},{4,6},{5,7},{6,4},{7,5},{8,10},{9,11},{10,... | collective-permute-start | bytes 98312 | tf_op jit(solution)/shard_map/ppermute | solution.py:278
  127.5 3.0 %collective-permute-done.7 = f32[4,16,128]{2,1,0:T(8,128)S(1)} collective-permute-done((f32[4,16,128]{2,1,0:T(8,128)S(1)}, f32[4,16,128]{2,1,0:T(8,128)S(1)}, u32[]{:S(2)}, u32[]{:S(2)}) %collective-permute-start.7) | collective-permute-done | bytes 32800 | tf_op jit(solution)/shard_map/ppermute | solution.py:278
  (50 shorter events, 7.5 us)
Async XLA Ops:
  0.6 43.0 %copy-start = (f32[4,16,128]{2,1,0:T(8,128)S(1)}, f32[4,16,128]{2,1,0:T(8,128)}, u32[]{:S(2)}) copy-start(f32[4,16,128]{2,1,0:T(8,128)} %param.11) | copy-start | bytes 98308
  1.4 69.9 %copy-start.6 = (f32[8,256]{1,0:T(8,128)}, f32[8,256]{1,0:T(8,128)S(1)}, u32[]{:S(2)}) copy-start(f32[8,256]{1,0:T(8,128)S(1)} %get-tuple-element.12.land_ref) | copy-start | bytes 24580
  1.4 6.6 %copy-start.3 = (f32[4,75,8,256]{3,2,1,0:T(8,128)S(1)}, f32[4,75,8,256]{3,2,1,0:T(8,128)}, u32[]{:S(2)}) copy-start(f32[4,75,8,256]{3,2,1,0:T(8,128)} %param.9) | copy-start | bytes 7372804
  4.7 30.3 %collective-permute-start.3 = (f32[301,8,128]{2,1,0:T(8,128)}, f32[301,8,128]{2,1,0:T(8,128)}, u32[]{:S(2)}, u32[]{:S(2)}) collective-permute-start(f32[301,8,128]{2,1,0:T(8,128)} %get-tuple-element.6), channel_id=1, source_target_pairs={{0,1},{1,2},{2,3},{3,0},{4,5},{5,6},{6,7},{7,4},{8,9},{9,10},{10,1... | collective-permute-start | bytes 3698696 | tf_op jit(solution)/shard_map/ppermute | solution.py:26
  6.3 9.0 %copy-start.7 = (s32[1,32]{1,0:T(1,128)S(1)}, s32[1,32]{1,0:T(1,128)}, u32[]{:S(2)}) copy-start(s32[1,32]{1,0:T(1,128)} %param.12) | copy-start | bytes 388
  6.3 28.9 %collective-permute-start.2 = (f32[301,8,128]{2,1,0:T(8,128)}, f32[301,8,128]{2,1,0:T(8,128)}, u32[]{:S(2)}, u32[]{:S(2)}) collective-permute-start(f32[301,8,128]{2,1,0:T(8,128)} %get-tuple-element.7), channel_id=1, source_target_pairs={{0,3},{1,0},{2,1},{3,2},{4,7},{5,4},{6,5},{7,6},{8,11},{9,8},{10,9... | collective-permute-start | bytes 3698696 | tf_op jit(solution)/shard_map/ppermute | solution.py:25
  9.8 6.0 %copy-start.1 = (s32[1,64]{1,0:T(1,128)S(1)}, s32[1,64]{1,0:T(1,128)}, u32[]{:S(2)}) copy-start(s32[1,64]{1,0:T(1,128)} %param.13) | copy-start | bytes 772
  9.8 50.6 %collective-permute-start = (f32[301,4,256]{2,1,0:T(4,128)}, f32[301,4,256]{2,1,0:T(4,128)S(1)}, u32[]{:S(2)}, u32[]{:S(2)}) collective-permute-start(f32[301,4,256]{2,1,0:T(4,128)} %get-tuple-element.8), channel_id=1, source_target_pairs={{0,124},{4,0},{8,4},{12,8},{16,12},{20,16},{24,20},{28,24},{32,28}... | collective-permute-start | bytes 3698696 | tf_op jit(solution)/shard_map/ppermute | solution.py:25
  15.3 45.1 %collective-permute-start.1 = (f32[301,4,256]{2,1,0:T(4,128)}, f32[301,4,256]{2,1,0:T(4,128)S(1)}, u32[]{:S(2)}, u32[]{:S(2)}) collective-permute-start(f32[301,4,256]{2,1,0:T(4,128)} %get-tuple-element.9), channel_id=1, source_target_pairs={{0,4},{4,8},{8,12},{12,16},{16,20},{20,24},{24,28},{28,32},{32,36}... | collective-permute-start | bytes 3698696 | tf_op jit(solution)/shard_map/ppermute | solution.py:26
  37.0 1.5 %copy-start.4 = (f32[301,8,128]{2,1,0:T(8,128)}, f32[301,8,128]{2,1,0:T(8,128)S(1)}, u32[]{:S(2)}) copy-start(f32[301,8,128]{2,1,0:T(8,128)S(1)} %broadcast_select_fusion) | copy-start | bytes 3698692
  38.5 24.0 %collective-permute-start.4 = (f32[301,4,128]{2,1,0:T(4,128)}, f32[301,4,128]{2,1,0:T(4,128)S(1)}, u32[]{:S(2)}, u32[]{:S(2)}) collective-permute-start(f32[301,4,128]{2,1,0:T(4,128)} %get-tuple-element.10), channel_id=1, source_target_pairs={{0,124},{4,0},{8,4},{12,8},{16,12},{20,16},{24,20},{28,24},{32,28}... | collective-permute-start | bytes 1849352 | tf_op jit(solution)/shard_map/ppermute | solution.py:25
  43.5 18.9 %collective-permute-start.5 = (f32[301,4,128]{2,1,0:T(4,128)}, f32[301,4,128]{2,1,0:T(4,128)}, u32[]{:S(2)}, u32[]{:S(2)}) collective-permute-start(f32[301,4,128]{2,1,0:T(4,128)} %get-tuple-element.11), channel_id=1, source_target_pairs={{0,4},{4,8},{8,12},{12,16},{16,20},{20,24},{24,28},{28,32},{32,36}... | collective-permute-start | bytes 1849352 | tf_op jit(solution)/shard_map/ppermute | solution.py:26
  45.1 14.6 %all-to-all-start = ((f32[4,32,2,128]{3,2,0,1:T(2,128)}), f32[4,32,2,128]{3,2,0,1:T(2,128)S(1)}, u32[]{:S(2)}, u32[]{:S(2)}) async-start(f32[4,32,2,128]{3,2,0,1:T(2,128)} %bitcast.38), calls=%async_computation | async-start | bytes 262144 | tf_op jit(solution)/shard_map/all_to_all | solution.py:316
  60.4 2.1 %copy-start.5 = (f32[301,8,128]{2,1,0:T(8,128)S(1)}, f32[301,8,128]{2,1,0:T(8,128)}, u32[]{:S(2)}) copy-start(f32[301,8,128]{2,1,0:T(8,128)} %copy-done.4) | copy-start | bytes 3698692
  63.9 1.5 %copy-start.2 = (f32[301,16,128]{2,1,0:T(8,128)}, f32[301,16,128]{2,1,0:T(8,128)S(1)}, u32[]{:S(2)}) copy-start(f32[301,16,128]{2,1,0:T(8,128)S(1)} %pad_maximum_fusion.1.after_and_out_1_.edge_ref) | copy-start | bytes 7397380
  109.2 11.7 %all-to-all-start.1 = ((f32[4,32,2,128]{3,2,0,1:T(2,128)}), f32[4,32,2,128]{3,2,0,1:T(2,128)S(1)}, u32[]{:S(2)}, u32[]{:S(2)}) async-start(f32[4,32,2,128]{3,2,0,1:T(2,128)} %copy.20), calls=%async_computation.1 | async-start | bytes 262144 | tf_op jit(solution)/shard_map/all_to_all | solution.py:332
  121.1 4.0 %collective-permute-start.6 = (f32[4,16,128]{2,1,0:T(8,128)S(1)}, f32[4,16,128]{2,1,0:T(8,128)S(1)}, u32[]{:S(2)}, u32[]{:S(2)}) collective-permute-start(f32[4,16,128]{2,1,0:T(8,128)S(1)} %convolution_bitcast_fusion), channel_id=1, source_target_pairs={{0,1},{1,0},{2,3},{3,2},{4,5},{5,4},{6,7},{7,6},{8,9},{9,8},{10,11... | collective-permute-start | bytes 98312 | tf_op jit(solution)/shard_map/ppermute | solution.py:278
  125.1 5.4 %collective-permute-start.7 = (f32[4,16,128]{2,1,0:T(8,128)S(1)}, f32[4,16,128]{2,1,0:T(8,128)S(1)}, u32[]{:S(2)}, u32[]{:S(2)}) collective-permute-start(f32[4,16,128]{2,1,0:T(8,128)S(1)} %add.79), channel_id=1, source_target_pairs={{0,2},{1,3},{2,0},{3,1},{4,6},{5,7},{6,4},{7,5},{8,10},{9,11},{10,... | collective-permute-start | bytes 98312 | tf_op jit(solution)/shard_map/ppermute | solution.py:278

commit v15 on v13

--- a/solution.py
+++ b/solution.py
@@ -271,14 +271,20 @@
 
 def sum_over(values, axis):
     count = lax.axis_size(axis)
-    if count & (count - 1):
-        return lax.psum(values, axis)
-    step = 1
-    while step < count:
-        pairs = [(i, i ^ step) for i in range(count)]
-        values = values + lax.ppermute(values, axis, pairs)
-        step *= 2
-    return values
+    where = lax.axis_index(axis)
+    copies = [values] + [
+        lax.ppermute(values, axis, [(i, (i + shift) % count) for i in range(count)])
+        for shift in range(1, count)
+    ]
+    stacked = jnp.stack(copies)
+    ordered = [
+        lax.dynamic_index_in_dim(stacked, (where - owner) % count, 0, keepdims=False)
+        for owner in range(count)
+    ]
+    while len(ordered) > 1:
+        paired = [ordered[i] + ordered[i + 1] for i in range(0, len(ordered) - 1, 2)]
+        ordered = paired + ordered[len(ordered) - len(ordered) % 2:]
+    return ordered[0]
 
 
 def lat_edges(marks, width):

time: 122 us -> 121 us (level)
  waiting for transfers between devices: 21.2 us -> 18.4 us
  starting transfers between devices: 27.1 us -> 28.9 us
    ppermute x2 -> x3, waiting for transfers between devices: 6.53 us -> 3.69 us  [sum_over(): lax.ppermute(values, axis, [(i, (i + shift) % count) for i in range(count)])]
    ppermute x2 -> x3, starting transfers between devices: 2.86 us -> 4.65 us  [sum_over(): lax.ppermute(values, axis, [(i, (i + shift) % count) for i in range(count)])]
  transfers between devices with their start and end apart: 10 -> 11, of which waited for: 5 -> 6; matrix products, arithmetic and copies ran while one was open for 14% -> 14% of each run, Pallas kernels for 0% -> 0%
where the time goes in v15:
time: 121 us; the launch traced here: 120 us
  Pallas kernels  40.2 us (33%)
  starting transfers between devices  28.9 us (24%)
  waiting for transfers between devices  18.4 us (15%)
  other arithmetic  16.6 us (14%)
  local copies, waits for them, and re-layouts  14.8 us (12%)
    pallas_call x1, Pallas kernels, tridiagonal(): pl.pallas_call(tridiagonal_kernel, out_shape=(jax.ShapeDtypeStruct(shape,...  31.4 us
    ppermute x3, starting transfers between devices, from_neighbours(): lax.ppermute(lax.slice_in_dim(block, 0, width, axis=dim), axis, to_prev)  13.6 us
    pallas_call x2, Pallas kernels, remap_call(): pl.pallas_call(kernel, out_shape=jax.ShapeDtypeStruct(out_shape, jnp.floa...  8.73 us
    all_to_all x1, waiting for transfers between devices, shards(): lax.all_to_all(buffer.reshape(received.shape), 'lat', split_axis=1, conca...  7.82 us
    all_to_all x1, starting transfers between devices, shards(): lax.all_to_all(outgoing, 'lat', split_axis=1, concat_axis=1, tiled=True)  6.73 us
    concatenate x2, other arithmetic, extended_planes(): stack = jnp.concatenate([planes, coast], axis=0)  5.42 us
    ppermute x3, waiting for transfers between devices, from_neighbours(): lax.ppermute(lax.slice_in_dim(block, size - width, size, axis=dim), axis,...  5.33 us
    ppermute x3, starting transfers between devices, sum_over(): lax.ppermute(values, axis, [(i, (i + shift) % count) for i in range(count)])  4.65 us
  transfers between devices with their start and end apart: 11, of which 6 were waited for; matrix products, arithmetic and copies ran while one was open for 14% of the time, Pallas kernels for 0%

profile of v15, /device:TPU:0, one launch (start us, length us, event | category | flops | bytes accessed | tf_op | source)
XLA Modules:
  0.0 119.9 jit_solution(16709476285695516461)
XLA Ops:
  1.4 3.5 %fusion = (f32[301,8,4]{2,1,0:T(8,128)}, f32[301,8,4]{2,1,0:T(8,128)}) fusion(f32[300,8,256]{2,1,0:T(8,128)} %bitcast.46, f32[1,8,256]{2,1,0:T(8,128)S(1)} %get-tuple-element.15), kind=kLoop, calls=%fused_computation.12 | loop fusion | flops 19264 | bytes 2542848 | tf_op jit(solution)/shard_map/concatenate | solution.py:34
  4.9 1.9 %copy.17 = f32[301,8,4]{0,1,2:T(8,128)S(1)} copy(f32[301,8,4]{2,1,0:T(8,128)} %get-tuple-element.6) | data formatting | bytes 77056 | tf_op jit(solution)/shard_map/slice | solution.py:25
  6.8 2.9 %collective-permute-start.2 = (f32[301,8,4]{0,1,2:T(8,128)S(1)}, f32[301,8,4]{0,1,2:T(8,128)S(1)}, u32[]{:S(2)}, u32[]{:S(2)}) collective-permute-start(f32[301,8,4]{0,1,2:T(8,128)S(1)} %copy.17), channel_id=1, source_target_pairs={{0,3},{1,0},{2,1},{3,2},{4,7},{5,4},{6,5},{7,6},{8,11},{9,8},{10,9... | collective-permute-start | bytes 115592 | tf_op jit(solution)/shard_map/ppermute | solution.py:25
  9.7 1.8 %copy.18 = f32[301,8,4]{0,1,2:T(8,128)S(1)} copy(f32[301,8,4]{2,1,0:T(8,128)} %get-tuple-element.7) | data formatting | bytes 77056 | tf_op jit(solution)/shard_map/slice | solution.py:26
  11.6 1.9 %fusion.1 = (f32[301,4,256]{2,1,0:T(4,128)}, f32[301,4,256]{2,1,0:T(4,128)}) fusion(f32[300,8,256]{2,1,0:T(8,128)S(1)} %bitcast.48, f32[1,8,256]{2,1,0:T(8,128)S(1)} %get-tuple-element.15), kind=kLoop, calls=%fused_computation.13 | loop fusion | flops 616448 | bytes 4931584 | tf_op jit(solution)/shard_map/concatenate | solution.py:34
  13.5 5.6 %collective-permute-start = (f32[301,4,256]{2,1,0:T(4,128)}, f32[301,4,256]{2,1,0:T(4,128)}, u32[]{:S(2)}, u32[]{:S(2)}) collective-permute-start(f32[301,4,256]{2,1,0:T(4,128)} %get-tuple-element.8), channel_id=1, source_target_pairs={{0,124},{4,0},{8,4},{12,8},{16,12},{20,16},{24,20},{28,24},{32,28}... | collective-permute-start | bytes 3698696 | tf_op jit(solution)/shard_map/ppermute | solution.py:25
  22.1 6.7 %all-to-all-start = ((f32[4,32,2,128]{3,2,0,1:T(2,128)}), f32[4,32,2,128]{3,2,0,1:T(2,128)S(1)}, u32[]{:S(2)}, u32[]{:S(2)}) async-start(f32[4,32,2,128]{3,2,0,1:T(2,128)} %bitcast.44), calls=%async_computation | async-start | bytes 262144 | tf_op jit(solution)/shard_map/all_to_all | solution.py:323
  28.9 5.0 %collective-permute-start.4 = (f32[301,4,8]{0,2,1:T(8,128)S(1)}, f32[301,4,8]{0,2,1:T(8,128)S(1)}, u32[]{:S(2)}, u32[]{:S(2)}) collective-permute-start(f32[301,4,8]{0,2,1:T(8,128)S(1)} %get-tuple-element.12), channel_id=1, source_target_pairs={{0,124},{4,0},{8,4},{12,8},{16,12},{20,16},{24,20},{28,24},{32,28}... | collective-permute-start | bytes 115592 | tf_op jit(solution)/shard_map/ppermute | solution.py:25
  34.2 1.6 %collective-permute-done.4 = f32[301,4,8]{0,2,1:T(8,128)S(1)} collective-permute-done((f32[301,4,8]{0,2,1:T(8,128)S(1)}, f32[301,4,8]{0,2,1:T(8,128)S(1)}, u32[]{:S(2)}, u32[]{:S(2)}) %collective-permute-start.4) | collective-permute-done | bytes 38560 | tf_op jit(solution)/shard_map/ppermute | solution.py:25
  35.8 5.3 %collective-permute-done.5 = f32[301,4,8]{0,2,1:T(8,128)S(1)} collective-permute-done((f32[301,4,8]{0,2,1:T(8,128)S(1)}, f32[301,4,8]{0,2,1:T(8,128)S(1)}, u32[]{:S(2)}, u32[]{:S(2)}) %collective-permute-start.5) | collective-permute-done | bytes 38560 | tf_op jit(solution)/shard_map/ppermute | solution.py:26
  41.2 2.9 %copy.21 = f32[301,16,4]{2,1,0:T(8,128)} copy(f32[301,16,4]{0,2,1:T(4,128)S(1)} %get-tuple-element.10) | data formatting | bytes 154112 | tf_op jit(solution)/shard_map/slice | solution.py:42
  44.0 2.9 %copy.22 = f32[301,16,4]{2,1,0:T(8,128)} copy(f32[301,16,4]{0,2,1:T(4,128)S(1)} %get-tuple-element.11) | data formatting | bytes 154112 | tf_op jit(solution)/shard_map/slice | solution.py:42
  46.9 3.1 %pad_maximum_fusion.1.after_and_out_1_.edge_ref = f32[301,16,128]{2,1,0:T(8,128)S(1)} fusion(f32[301,16,4]{2,1,0:T(8,128)} %copy.22, f32[301,16,4]{2,1,0:T(8,128)} %copy.21, f32[128]{0:T(128)S(1)} %pad.8.clone), kind=kLoop, calls=%fused_computation.8 | loop fusion | flops 1232896 | bytes 2620416 | tf_op jit(solution)/shard_map/concatenate | solution.py:42
  50.9 3.7 %pad_maximum_fusion.after_and_out_0_.rows_ref = f32[301,8,256]{2,1,0:T(8,128)} fusion(f32[301,4,256]{2,1,0:T(4,128)} %collective-permute-done.1, f32[301,4,256]{2,1,0:T(4,128)} %collective-permute-done), kind=kLoop, calls=%fused_computation.6 | loop fusion | flops 616448 | bytes 4931584 | tf_op jit(solution)/shard_map/concatenate | solution.py:43
  54.5 4.6 %shard_map.104 = f32[4,8,256]{2,1,0:T(8,128)} custom-call(f32[256,128]{1,0:T(8,128)} %bitcast.49, s32[32,256]{1,0:T(8,128)} %bitcast.52, f32[32,256]{1,0:T(8,128)} %bitcast.54, f32[301,8,256]{2,1,0:T(8,128)} %pad_maximum_fusion.after_and_out_0_.rows_ref, f32[301,16,128]{2,1,0:T(8,128)} %copy-done.2), custom_call_target="tpu_custom_call" | custom-call | tf_op jit(solution)/shard_map/pallas_call | solution.py:263
  59.1 1.4 %fusion.10.surf_ref = f32[8,256]{1,0:T(8,128)} fusion(f32[4,8,256]{2,1,0:T(8,128)} %shard_map.104), kind=kLoop, calls=%fused_computation.34 | loop fusion | flops 22528 | bytes 40960 | tf_op jit(solution)/shard_map/add | solution.py:334
  61.8 31.4 %shard_map.105 = (f32[4,75,8,256]{3,2,1,0:T(8,128)}, f32[4,8,256]{2,1,0:T(8,128)}) custom-call(f32[75]{0:T(128)} %constant.77.clone.decay_ref, f32[300,8,256]{2,1,0:T(8,128)} %bitcast.47, f32[301,8,256]{2,1,0:T(8,128)} %pad_maximum_fusion.after_and_out_0_.rows_ref, f32[301,16,128]{2,1,0:T(8,128)} %copy-done.2, f32[16,384]{1,0:T(8,128)} %maximum_select_fusion.mask_ref, ...), custom_call_target="tpu_custom_call" | custom-call | tf_op jit(solution)/shard_map/pallas_call | solution.py:180
  93.3 4.2 %shard_map.106 = f32[256,128]{1,0:T(8,128)} custom-call(f32[4,8,256]{2,1,0:T(8,128)} %get-tuple-element.5.back_ref, s32[32,256]{1,0:T(8,128)} %bitcast.53, f32[32,256]{1,0:T(8,128)} %bitcast.55), custom_call_target="tpu_custom_call" | custom-call | tf_op jit(solution)/shard_map/pallas_call | solution.py:263
  97.5 1.6 %copy.26 = f32[4,32,2,128]{3,2,0,1:T(2,128)} copy(f32[4,32,2,128]{3,2,1,0:T(2,128)} %bitcast.51) | data formatting | bytes 262144 | tf_op jit(solution)/shard_map/reshape | solution.py:340
  99.0 3.8 %all-to-all-start.1 = ((f32[4,32,2,128]{3,2,0,1:T(2,128)}), f32[4,32,2,128]{3,2,0,1:T(2,128)S(1)}, u32[]{:S(2)}, u32[]{:S(2)}) async-start(f32[4,32,2,128]{3,2,0,1:T(2,128)} %copy.26), calls=%async_computation.1 | async-start | bytes 262144 | tf_op jit(solution)/shard_map/all_to_all | solution.py:339
  102.9 7.8 %all-to-all-done.1 = f32[4,32,2,128]{3,2,0,1:T(2,128)S(1)} async-done(((f32[4,32,2,128]{3,2,0,1:T(2,128)}), f32[4,32,2,128]{3,2,0,1:T(2,128)S(1)}, u32[]{:S(2)}, u32[]{:S(2)}) %all-to-all-start.1) | async-done | bytes 131104 | tf_op jit(solution)/shard_map/all_to_all | solution.py:339
  111.4 3.9 %collective-permute-start.7 = (f32[4,16,128]{2,1,0:T(8,128)S(1)}, f32[4,16,128]{2,1,0:T(8,128)S(1)}, u32[]{:S(2)}, u32[]{:S(2)}) collective-permute-start(f32[4,16,128]{2,1,0:T(8,128)S(1)} %bitcast.57), channel_id=1, source_target_pairs={{0,2},{1,3},{2,0},{3,1},{4,6},{5,7},{6,4},{7,5},{8,10},{9,11},{10,... | collective-permute-start | bytes 98312 | tf_op jit(solution)/shard_map/ppermute | solution.py:276
  116.1 1.5 %collective-permute-done.7 = f32[4,16,128]{2,1,0:T(8,128)S(1)} collective-permute-done((f32[4,16,128]{2,1,0:T(8,128)S(1)}, f32[4,16,128]{2,1,0:T(8,128)S(1)}, u32[]{:S(2)}, u32[]{:S(2)}) %collective-permute-start.7) | collective-permute-done | bytes 32800 | tf_op jit(solution)/shard_map/ppermute | solution.py:276
  117.6 1.7 %collective-permute-done.8 = f32[4,16,128]{2,1,0:T(8,128)S(1)} collective-permute-done((f32[4,16,128]{2,1,0:T(8,128)S(1)}, f32[4,16,128]{2,1,0:T(8,128)S(1)}, u32[]{:S(2)}, u32[]{:S(2)}) %collective-permute-start.8) | collective-permute-done | bytes 32800 | tf_op jit(solution)/shard_map/ppermute | solution.py:276
  (56 shorter events, 8.3 us)
Async XLA Ops:
  0.6 20.0 %copy-start = (f32[4,16,128]{2,1,0:T(8,128)S(1)}, f32[4,16,128]{2,1,0:T(8,128)}, u32[]{:S(2)}) copy-start(f32[4,16,128]{2,1,0:T(8,128)} %param.11) | copy-start | bytes 98308
  1.4 59.8 %copy-start.4 = (f32[8,256]{1,0:T(8,128)}, f32[8,256]{1,0:T(8,128)S(1)}, u32[]{:S(2)}) copy-start(f32[8,256]{1,0:T(8,128)S(1)} %get-tuple-element.14.land_ref) | copy-start | bytes 24580
  4.9 6.7 %copy-start.3 = (f32[4,75,8,256]{3,2,1,0:T(8,128)S(1)}, f32[4,75,8,256]{3,2,1,0:T(8,128)}, u32[]{:S(2)}) copy-start(f32[4,75,8,256]{3,2,1,0:T(8,128)} %param.9) | copy-start | bytes 7372804
  6.8 22.1 %collective-permute-start.2 = (f32[301,8,4]{0,1,2:T(8,128)S(1)}, f32[301,8,4]{0,1,2:T(8,128)S(1)}, u32[]{:S(2)}, u32[]{:S(2)}) collective-permute-start(f32[301,8,4]{0,1,2:T(8,128)S(1)} %copy.17), channel_id=1, source_target_pairs={{0,3},{1,0},{2,1},{3,2},{4,7},{5,4},{6,5},{7,6},{8,11},{9,8},{10,9... | collective-permute-start | bytes 115592 | tf_op jit(solution)/shard_map/ppermute | solution.py:25
  11.5 7.7 %copy-start.5 = (s32[1,32]{1,0:T(1,128)S(1)}, s32[1,32]{1,0:T(1,128)}, u32[]{:S(2)}) copy-start(s32[1,32]{1,0:T(1,128)} %param.12) | copy-start | bytes 388
  11.5 8.1 %copy-start.1 = (s32[1,64]{1,0:T(1,128)S(1)}, s32[1,64]{1,0:T(1,128)}, u32[]{:S(2)}) copy-start(s32[1,64]{1,0:T(1,128)} %param.13) | copy-start | bytes 772
  11.5 17.4 %collective-permute-start.3 = (f32[301,8,4]{0,1,2:T(8,128)S(1)}, f32[301,8,4]{0,1,2:T(8,128)S(1)}, u32[]{:S(2)}, u32[]{:S(2)}) collective-permute-start(f32[301,8,4]{0,1,2:T(8,128)S(1)} %copy.18), channel_id=1, source_target_pairs={{0,1},{1,2},{2,3},{3,0},{4,5},{5,6},{6,7},{7,4},{8,9},{9,10},{10,1... | collective-permute-start | bytes 115592 | tf_op jit(solution)/shard_map/ppermute | solution.py:26
  13.5 37.4 %collective-permute-start = (f32[301,4,256]{2,1,0:T(4,128)}, f32[301,4,256]{2,1,0:T(4,128)}, u32[]{:S(2)}, u32[]{:S(2)}) collective-permute-start(f32[301,4,256]{2,1,0:T(4,128)} %get-tuple-element.8), channel_id=1, source_target_pairs={{0,124},{4,0},{8,4},{12,8},{16,12},{20,16},{24,20},{28,24},{32,28}... | collective-permute-start | bytes 3698696 | tf_op jit(solution)/shard_map/ppermute | solution.py:25
  19.1 31.7 %collective-permute-start.1 = (f32[301,4,256]{2,1,0:T(4,128)}, f32[301,4,256]{2,1,0:T(4,128)}, u32[]{:S(2)}, u32[]{:S(2)}) collective-permute-start(f32[301,4,256]{2,1,0:T(4,128)} %get-tuple-element.9), channel_id=1, source_target_pairs={{0,4},{4,8},{8,12},{12,16},{16,20},{20,24},{24,28},{28,32},{32,36}... | collective-permute-start | bytes 3698696 | tf_op jit(solution)/shard_map/ppermute | solution.py:26
  22.1 28.0 %all-to-all-start = ((f32[4,32,2,128]{3,2,0,1:T(2,128)}), f32[4,32,2,128]{3,2,0,1:T(2,128)S(1)}, u32[]{:S(2)}, u32[]{:S(2)}) async-start(f32[4,32,2,128]{3,2,0,1:T(2,128)} %bitcast.44), calls=%async_computation | async-start | bytes 262144 | tf_op jit(solution)/shard_map/all_to_all | solution.py:323
  28.9 6.8 %collective-permute-start.4 = (f32[301,4,8]{0,2,1:T(8,128)S(1)}, f32[301,4,8]{0,2,1:T(8,128)S(1)}, u32[]{:S(2)}, u32[]{:S(2)}) collective-permute-start(f32[301,4,8]{0,2,1:T(8,128)S(1)} %get-tuple-element.12), channel_id=1, source_target_pairs={{0,124},{4,0},{8,4},{12,8},{16,12},{20,16},{24,20},{28,24},{32,28}... | collective-permute-start | bytes 115592 | tf_op jit(solution)/shard_map/ppermute | solution.py:25
  33.9 7.2 %collective-permute-start.5 = (f32[301,4,8]{0,2,1:T(8,128)S(1)}, f32[301,4,8]{0,2,1:T(8,128)S(1)}, u32[]{:S(2)}, u32[]{:S(2)}) collective-permute-start(f32[301,4,8]{0,2,1:T(8,128)S(1)} %get-tuple-element.13), channel_id=1, source_target_pairs={{0,4},{4,8},{8,12},{12,16},{16,20},{20,24},{24,28},{28,32},{32,36}... | collective-permute-start | bytes 115592 | tf_op jit(solution)/shard_map/ppermute | solution.py:26
  50.0 4.5 %copy-start.2 = (f32[301,16,128]{2,1,0:T(8,128)}, f32[301,16,128]{2,1,0:T(8,128)S(1)}, u32[]{:S(2)}) copy-start(f32[301,16,128]{2,1,0:T(8,128)S(1)} %pad_maximum_fusion.1.after_and_out_1_.edge_ref) | copy-start | bytes 7397380
  99.0 11.7 %all-to-all-start.1 = ((f32[4,32,2,128]{3,2,0,1:T(2,128)}), f32[4,32,2,128]{3,2,0,1:T(2,128)S(1)}, u32[]{:S(2)}, u32[]{:S(2)}) async-start(f32[4,32,2,128]{3,2,0,1:T(2,128)} %copy.26), calls=%async_computation.1 | async-start | bytes 262144 | tf_op jit(solution)/shard_map/all_to_all | solution.py:339
  110.9 5.2 %collective-permute-start.6 = (f32[4,16,128]{2,1,0:T(8,128)S(1)}, f32[4,16,128]{2,1,0:T(8,128)S(1)}, u32[]{:S(2)}, u32[]{:S(2)}) collective-permute-start(f32[4,16,128]{2,1,0:T(8,128)S(1)} %bitcast.56), channel_id=1, source_target_pairs={{0,1},{1,2},{2,3},{3,0},{4,5},{5,6},{6,7},{7,4},{8,9},{9,10},{10,1... | collective-permute-start | bytes 98312 | tf_op jit(solution)/shard_map/ppermute | solution.py:276
  111.4 6.2 %collective-permute-start.7 = (f32[4,16,128]{2,1,0:T(8,128)S(1)}, f32[4,16,128]{2,1,0:T(8,128)S(1)}, u32[]{:S(2)}, u32[]{:S(2)}) collective-permute-start(f32[4,16,128]{2,1,0:T(8,128)S(1)} %bitcast.57), channel_id=1, source_target_pairs={{0,2},{1,3},{2,0},{3,1},{4,6},{5,7},{6,4},{7,5},{8,10},{9,11},{10,... | collective-permute-start | bytes 98312 | tf_op jit(solution)/shard_map/ppermute | solution.py:276
  115.4 3.9 %collective-permute-start.8 = (f32[4,16,128]{2,1,0:T(8,128)S(1)}, f32[4,16,128]{2,1,0:T(8,128)S(1)}, u32[]{:S(2)}, u32[]{:S(2)}) collective-permute-start(f32[4,16,128]{2,1,0:T(8,128)S(1)} %bitcast.58), channel_id=1, source_target_pairs={{0,3},{1,0},{2,1},{3,2},{4,7},{5,4},{6,5},{7,6},{8,11},{9,8},{10,9... | collective-permute-start | bytes 98312 | tf_op jit(solution)/shard_map/ppermute | solution.py:276

commit v16 on v15

--- a/solution.py
+++ b/solution.py
@@ -32,10 +32,12 @@
     planes = values.reshape(fields * levels, rows, cols)
     coast = land_mask.astype(jnp.float32)[None]
     stack = jnp.concatenate([planes, coast], axis=0)
-    south, north = from_neighbours(stack, "lat", 1, width)
     east, west = from_neighbours(stack, "lon", 2, width)
     sides = jnp.concatenate([east, west], axis=2)
-    corner_south, corner_north = from_neighbours(sides, "lat", 1, width)
+    wide_rows = jnp.concatenate([stack, sides], axis=2)
+    south_wide, north_wide = from_neighbours(wide_rows, "lat", 1, width)
+    south, corner_south = south_wide[:, :, :cols], south_wide[:, :, cols:]
+    north, corner_north = north_wide[:, :, :cols], north_wide[:, :, cols:]
     wide = -(-(2 * width) // 128) * 128
     edges = jnp.concatenate([sides, corner_south, corner_north], axis=1)
     gap = jnp.zeros(edges.shape[:2] + (wide - 2 * width,), jnp.float32)

time: 121 us -> 142 us (1.17)
  local copies, waits for them, and re-layouts: 14.8 us -> 35.9 us
  waiting for transfers between devices: 18.4 us -> 25.1 us
  starting transfers between devices: 28.9 us -> 23.7 us
  other arithmetic: 16.6 us -> 14.5 us
    all_to_all x1, waiting for transfers between devices: 0.01 us -> 11.4 us  [shards(): lax.all_to_all(outgoing, 'lat', split_axis=1, concat_axis=1, tiled=True)]
    slice x0 -> x4, local copies, waits for them, and re-layouts: none -> 5.77 us  [the longest x2 3.46 us: extended_planes(): south, corner_south = (south_wide[:, :, :cols], south_wide[:, :, cols:])]
    ppermute x3 -> x2, starting transfers between devices: 13.6 us -> 7.96 us  [from_neighbours(): lax.ppermute(lax.slice_in_dim(block, 0, width, axis=dim), axis, to_prev)]
    slice x1 -> x3, local copies, waits for them, and re-layouts: 1.92 us -> 6.09 us  [from_neighbours(): lax.slice_in_dim(block, 0, width, axis=dim)]
    unnamed x12 -> x26, local copies, waits for them, and re-layouts: 0.03 us -> 4.18 us
    all_to_all x1, starting transfers between devices: 3.84 us -> 7.06 us  [shards(): lax.all_to_all(buffer.reshape(received.shape), 'lat', split_axis=1, conca...]
    slice x1 -> x2, local copies, waits for them, and re-layouts: 1.77 us -> 4.56 us  [from_neighbours(): lax.slice_in_dim(block, size - width, size, axis=dim)]
    ppermute x1 -> x2, local copies, waits for them, and re-layouts: 0.01 us -> 2.22 us  [from_neighbours(): lax.ppermute(lax.slice_in_dim(block, 0, width, axis=dim), axis, to_prev)]
  transfers between devices with their start and end apart: 11 -> 9, of which waited for: 6 -> 5; matrix products, arithmetic and copies ran while one was open for 14% -> 9% of each run, Pallas kernels for 0% -> 0%
where the time goes in v16:
time: 142 us; the launch traced here: 141 us
  Pallas kernels  40.2 us (28%)
  local copies, waits for them, and re-layouts  35.9 us (25%)
  waiting for transfers between devices  25.1 us (18%)
  starting transfers between devices  23.7 us (17%)
  other arithmetic  14.5 us (10%)
    pallas_call x1, Pallas kernels, tridiagonal(): pl.pallas_call(tridiagonal_kernel, out_shape=(jax.ShapeDtypeStruct(shape,...  31.4 us
    all_to_all x1, waiting for transfers between devices, shards(): lax.all_to_all(outgoing, 'lat', split_axis=1, concat_axis=1, tiled=True)  11.4 us
    pallas_call x2, Pallas kernels, remap_call(): pl.pallas_call(kernel, out_shape=jax.ShapeDtypeStruct(out_shape, jnp.floa...  8.73 us
    ppermute x2, starting transfers between devices, from_neighbours(): lax.ppermute(lax.slice_in_dim(block, 0, width, axis=dim), axis, to_prev)  7.96 us
    all_to_all x1, waiting for transfers between devices, shards(): lax.all_to_all(buffer.reshape(received.shape), 'lat', split_axis=1, conca...  7.82 us
    all_to_all x1, starting transfers between devices, shards(): lax.all_to_all(buffer.reshape(received.shape), 'lat', split_axis=1, conca...  7.06 us
    slice x3, local copies, waits for them, and re-layouts, from_neighbours(): lax.slice_in_dim(block, 0, width, axis=dim)  6.09 us
    all_to_all x1, starting transfers between devices, shards(): lax.all_to_all(outgoing, 'lat', split_axis=1, concat_axis=1, tiled=True)  5.19 us
  transfers between devices with their start and end apart: 9, of which 5 were waited for; matrix products, arithmetic and copies ran while one was open for 9% of the time, Pallas kernels for 0%

profile of v16, /device:TPU:0, one launch (start us, length us, event | category | flops | bytes accessed | tf_op | source)
XLA Modules:
  0.0 140.5 jit_solution(5531358591373918119)
XLA Ops:
  1.4 3.5 %fusion = (f32[301,8,4]{2,1,0:T(8,128)}, f32[301,8,4]{2,1,0:T(8,128)}) fusion(f32[300,8,256]{2,1,0:T(8,128)} %bitcast.46, f32[1,8,256]{2,1,0:T(8,128)S(1)} %get-tuple-element.13), kind=kLoop, calls=%fused_computation.9 | loop fusion | flops 19264 | bytes 2542848 | tf_op jit(solution)/shard_map/concatenate | solution.py:34
  4.9 1.9 %copy.17 = f32[301,8,4]{0,1,2:T(8,128)S(1)} copy(f32[301,8,4]{2,1,0:T(8,128)} %get-tuple-element.8) | data formatting | bytes 77056 | tf_op jit(solution)/shard_map/slice | solution.py:25
  6.8 2.9 %collective-permute-start = (f32[301,8,4]{0,1,2:T(8,128)S(1)}, f32[301,8,4]{0,1,2:T(8,128)S(1)}, u32[]{:S(2)}, u32[]{:S(2)}) collective-permute-start(f32[301,8,4]{0,1,2:T(8,128)S(1)} %copy.17), channel_id=1, source_target_pairs={{0,3},{1,0},{2,1},{3,2},{4,7},{5,4},{6,5},{7,6},{8,11},{9,8},{10,9... | collective-permute-start | bytes 115592 | tf_op jit(solution)/shard_map/ppermute | solution.py:25
  13.2 3.7 %collective-permute-done.1 = f32[301,8,4]{0,1,2:T(8,128)S(1)} collective-permute-done((f32[301,8,4]{0,1,2:T(8,128)S(1)}, f32[301,8,4]{0,1,2:T(8,128)S(1)}, u32[]{:S(2)}, u32[]{:S(2)}) %collective-permute-start.1) | collective-permute-done | bytes 38560 | tf_op jit(solution)/shard_map/ppermute | solution.py:26
  18.4 2.1 %pad_maximum_fusion = f32[301,8,264]{2,1,0:T(8,128)S(1)} fusion(f32[301,8,4]{2,1,0:T(8,128)} %copy.20, f32[301,8,4]{2,1,0:T(8,128)} %copy.19, f32[1,8,256]{2,1,0:T(8,128)S(1)} %get-tuple-element.13, f32[300,8,256]{2,1,0:T(8,128)S(1)} %bitcast.48), kind=kLoop, calls=%fused_computation.2 | loop fusion | flops 1907136 | bytes 5085696 | tf_op jit(solution)/shard_map/concatenate | solution.py:37
  20.6 1.8 %fusion.14 = (f32[301,4,264]{2,1,0:T(4,128)S(1)}, f32[301,4,264]{2,1,0:T(4,128)}) fusion(f32[301,8,264]{2,1,0:T(8,128)S(1)} %pad_maximum_fusion), kind=kLoop, calls=%fused_computation.42 | loop fusion | bytes 5085696 | tf_op jit(solution)/shard_map/slice | solution.py:25
  22.4 2.8 %copy.23 = f32[301,4,264]{0,2,1:T(8,128)S(1)} copy(f32[301,4,264]{2,1,0:T(4,128)} %get-tuple-element.7) | data formatting | bytes 2542848 | tf_op jit(solution)/shard_map/slice | solution.py:26
  25.3 2.4 %copy.21 = f32[301,4,264]{0,2,1:T(8,128)} copy(f32[301,4,264]{2,1,0:T(4,128)S(1)} %get-tuple-element.6) | data formatting | bytes 2542848 | tf_op jit(solution)/shard_map/slice | solution.py:25
  27.6 5.0 %collective-permute-start.2 = (f32[301,4,264]{0,2,1:T(8,128)}, f32[301,4,264]{0,2,1:T(8,128)}, u32[]{:S(2)}, u32[]{:S(2)}) collective-permute-start(f32[301,4,264]{0,2,1:T(8,128)} %copy.21), channel_id=1, source_target_pairs={{0,124},{4,0},{8,4},{12,8},{16,12},{20,16},{24,20},{28,24},{32,28}... | collective-permute-start | bytes 3814280 | tf_op jit(solution)/shard_map/ppermute | solution.py:25
  35.7 5.2 %all-to-all-start = ((f32[4,32,2,128]{3,2,0,1:T(2,128)}), f32[4,32,2,128]{3,2,0,1:T(2,128)S(1)}, u32[]{:S(2)}, u32[]{:S(2)}) async-start(f32[4,32,2,128]{3,2,0,1:T(2,128)} %bitcast.44), calls=%async_computation | async-start | bytes 262144 | tf_op jit(solution)/shard_map/all_to_all | solution.py:325
  42.4 11.4 %all-to-all-done = f32[4,32,2,128]{3,2,0,1:T(2,128)S(1)} async-done(((f32[4,32,2,128]{3,2,0,1:T(2,128)}), f32[4,32,2,128]{3,2,0,1:T(2,128)S(1)}, u32[]{:S(2)}, u32[]{:S(2)}) %all-to-all-start) | async-done | bytes 131104 | tf_op jit(solution)/shard_map/all_to_all | solution.py:325
  56.8 2.7 %slice.73 = f32[301,4,256]{0,2,1:T(8,128)} slice(f32[301,4,264]{0,2,1:T(8,128)} %collective-permute-done.2), slice={[0:301], [0:4], [0:256]} | slice | bytes 2465792 | tf_op jit(solution)/shard_map/slice | solution.py:39
  59.5 1.8 %copy.36 = f32[301,4,256]{2,1,0:T(4,128)S(1)} copy(f32[301,4,256]{0,2,1:T(8,128)} %slice.73) | data formatting | bytes 2465792
  61.4 2.0 %pad_maximum_fusion.1.after_and_out_0_.rows_ref = f32[301,8,256]{2,1,0:T(8,128)} fusion(f32[301,4,256]{2,1,0:T(4,128)S(1)} %copy.37, f32[301,4,256]{2,1,0:T(4,128)S(1)} %copy.36), kind=kLoop, calls=%fused_computation.4 | loop fusion | flops 616448 | bytes 4931584 | tf_op jit(solution)/shard_map/concatenate | solution.py:45
  65.0 2.8 %copy.27 = f32[301,16,4]{2,1,0:T(8,128)} copy(f32[301,16,4]{0,2,1:T(4,128)S(1)} %get-tuple-element.10) | data formatting | bytes 154112 | tf_op jit(solution)/shard_map/slice | solution.py:44
  67.9 2.8 %copy.28 = f32[301,16,4]{2,1,0:T(8,128)} copy(f32[301,16,4]{0,2,1:T(4,128)S(1)} %get-tuple-element.11) | data formatting | bytes 154112 | tf_op jit(solution)/shard_map/slice | solution.py:44
  70.7 3.1 %pad_maximum_fusion.2.after_and_out_1_.edge_ref = f32[301,16,128]{2,1,0:T(8,128)S(1)} fusion(f32[301,16,4]{2,1,0:T(8,128)} %copy.28, f32[301,16,4]{2,1,0:T(8,128)} %copy.27, f32[128]{0:T(128)S(1)} %pad.8.clone), kind=kLoop, calls=%fused_computation.8 | loop fusion | flops 1232896 | bytes 2620416 | tf_op jit(solution)/shard_map/concatenate | solution.py:44
  75.3 4.5 %shard_map.104 = f32[4,8,256]{2,1,0:T(8,128)} custom-call(f32[256,128]{1,0:T(8,128)} %bitcast.49, s32[32,256]{1,0:T(8,128)} %bitcast.52, f32[32,256]{1,0:T(8,128)} %bitcast.54, f32[301,8,256]{2,1,0:T(8,128)} %pad_maximum_fusion.1.after_and_out_0_.rows_ref, f32[301,16,128]{2,1,0:T(8,128)} %copy-done.2), custom_call_target="tpu_custom_call" | custom-call | tf_op jit(solution)/shard_map/pallas_call | solution.py:265
  81.9 31.4 %shard_map.105 = (f32[4,75,8,256]{3,2,1,0:T(8,128)}, f32[4,8,256]{2,1,0:T(8,128)}) custom-call(f32[75]{0:T(128)} %constant.77.clone.decay_ref, f32[300,8,256]{2,1,0:T(8,128)} %bitcast.47, f32[301,8,256]{2,1,0:T(8,128)} %pad_maximum_fusion.1.after_and_out_0_.rows_ref, f32[301,16,128]{2,1,0:T(8,128)} %copy-done.2, f32[16,384]{1,0:T(8,128)} %maximum_select_fusion.mask_ref, ...), custom_call_target="tpu_custom_call" | custom-call | tf_op jit(solution)/shard_map/pallas_call | solution.py:182
  113.4 4.2 %shard_map.106 = f32[256,128]{1,0:T(8,128)} custom-call(f32[4,8,256]{2,1,0:T(8,128)} %get-tuple-element.5.back_ref, s32[32,256]{1,0:T(8,128)} %bitcast.53, f32[32,256]{1,0:T(8,128)} %bitcast.55), custom_call_target="tpu_custom_call" | custom-call | tf_op jit(solution)/shard_map/pallas_call | solution.py:265
  119.2 7.1 %all-to-all-start.1 = ((f32[4,32,2,128]{3,2,0,1:T(2,128)}), f32[4,32,2,128]{3,2,0,1:T(2,128)S(1)}, u32[]{:S(2)}, u32[]{:S(2)}) async-start(f32[4,32,2,128]{3,2,0,1:T(2,128)} %copy.32), calls=%async_computation.1 | async-start | bytes 262144 | tf_op jit(solution)/shard_map/all_to_all | solution.py:341
  126.2 7.8 %all-to-all-done.1 = f32[4,32,2,128]{3,2,0,1:T(2,128)S(1)} async-done(((f32[4,32,2,128]{3,2,0,1:T(2,128)}), f32[4,32,2,128]{3,2,0,1:T(2,128)S(1)}, u32[]{:S(2)}, u32[]{:S(2)}) %all-to-all-start.1) | async-done | bytes 131104 | tf_op jit(solution)/shard_map/all_to_all | solution.py:341
  134.9 2.7 %collective-permute-start.6 = (f32[4,16,128]{2,1,0:T(8,128)S(1)}, f32[4,16,128]{2,1,0:T(8,128)S(1)}, u32[]{:S(2)}, u32[]{:S(2)}) collective-permute-start(f32[4,16,128]{2,1,0:T(8,128)S(1)} %bitcast.58), channel_id=1, source_target_pairs={{0,3},{1,0},{2,1},{3,2},{4,7},{5,4},{6,5},{7,6},{8,11},{9,8},{10,9... | collective-permute-start | bytes 98312 | tf_op jit(solution)/shard_map/ppermute | solution.py:278
  137.6 2.1 %collective-permute-done.5 = f32[4,16,128]{2,1,0:T(8,128)S(1)} collective-permute-done((f32[4,16,128]{2,1,0:T(8,128)S(1)}, f32[4,16,128]{2,1,0:T(8,128)S(1)}, u32[]{:S(2)}, u32[]{:S(2)}) %collective-permute-start.5) | collective-permute-done | bytes 32800 | tf_op jit(solution)/shard_map/ppermute | solution.py:278
  (74 shorter events, 21.7 us)
Async XLA Ops:
  0.6 33.6 %copy-start = (f32[4,16,128]{2,1,0:T(8,128)S(1)}, f32[4,16,128]{2,1,0:T(8,128)}, u32[]{:S(2)}) copy-start(f32[4,16,128]{2,1,0:T(8,128)} %param.11) | copy-start | bytes 98308
  1.4 79.9 %copy-start.10 = (f32[8,256]{1,0:T(8,128)}, f32[8,256]{1,0:T(8,128)S(1)}, u32[]{:S(2)}) copy-start(f32[8,256]{1,0:T(8,128)S(1)} %get-tuple-element.12.land_ref) | copy-start | bytes 24580
  4.9 13.5 %copy-start.3 = (f32[4,75,8,256]{3,2,1,0:T(8,128)S(1)}, f32[4,75,8,256]{3,2,1,0:T(8,128)}, u32[]{:S(2)}) copy-start(f32[4,75,8,256]{3,2,1,0:T(8,128)} %param.9) | copy-start | bytes 7372804
  6.8 4.8 %collective-permute-start = (f32[301,8,4]{0,1,2:T(8,128)S(1)}, f32[301,8,4]{0,1,2:T(8,128)S(1)}, u32[]{:S(2)}, u32[]{:S(2)}) collective-permute-start(f32[301,8,4]{0,1,2:T(8,128)S(1)} %copy.17), channel_id=1, source_target_pairs={{0,3},{1,0},{2,1},{3,2},{4,7},{5,4},{6,5},{7,6},{8,11},{9,8},{10,9... | collective-permute-start | bytes 115592 | tf_op jit(solution)/shard_map/ppermute | solution.py:25
  11.5 5.4 %collective-permute-start.1 = (f32[301,8,4]{0,1,2:T(8,128)S(1)}, f32[301,8,4]{0,1,2:T(8,128)S(1)}, u32[]{:S(2)}, u32[]{:S(2)}) collective-permute-start(f32[301,8,4]{0,1,2:T(8,128)S(1)} %copy.18), channel_id=1, source_target_pairs={{0,1},{1,2},{2,3},{3,0},{4,5},{5,6},{6,7},{7,4},{8,9},{9,10},{10,1... | collective-permute-start | bytes 115592 | tf_op jit(solution)/shard_map/ppermute | solution.py:26
  11.6 9.0 %copy-start.4 = (f32[301,8,4]{0,1,2:T(8,128)}, f32[301,8,4]{0,1,2:T(8,128)S(1)}, u32[]{:S(2)}) copy-start(f32[301,8,4]{0,1,2:T(8,128)S(1)} %collective-permute-done) | copy-start | bytes 115588
  16.9 3.7 %copy-start.6 = (f32[301,8,4]{0,1,2:T(8,128)}, f32[301,8,4]{0,1,2:T(8,128)S(1)}, u32[]{:S(2)}) copy-start(f32[301,8,4]{0,1,2:T(8,128)S(1)} %collective-permute-done.1) | copy-start | bytes 115588
  25.2 7.5 %copy-start.11 = (s32[1,32]{1,0:T(1,128)S(1)}, s32[1,32]{1,0:T(1,128)}, u32[]{:S(2)}) copy-start(s32[1,32]{1,0:T(1,128)} %param.12) | copy-start | bytes 388
  25.2 8.0 %copy-start.1 = (s32[1,64]{1,0:T(1,128)S(1)}, s32[1,64]{1,0:T(1,128)}, u32[]{:S(2)}) copy-start(s32[1,64]{1,0:T(1,128)} %param.13) | copy-start | bytes 772
  25.2 29.3 %collective-permute-start.3 = (f32[301,4,264]{0,2,1:T(8,128)S(1)}, f32[301,4,264]{0,2,1:T(8,128)}, u32[]{:S(2)}, u32[]{:S(2)}) collective-permute-start(f32[301,4,264]{0,2,1:T(8,128)S(1)} %copy.23), channel_id=1, source_target_pairs={{0,4},{4,8},{8,12},{12,16},{16,20},{20,24},{24,28},{28,32},{32,36}... | collective-permute-start | bytes 3814280 | tf_op jit(solution)/shard_map/ppermute | solution.py:26
  27.6 29.2 %collective-permute-start.2 = (f32[301,4,264]{0,2,1:T(8,128)}, f32[301,4,264]{0,2,1:T(8,128)}, u32[]{:S(2)}, u32[]{:S(2)}) collective-permute-start(f32[301,4,264]{0,2,1:T(8,128)} %copy.21), channel_id=1, source_target_pairs={{0,124},{4,0},{8,4},{12,8},{16,12},{20,16},{24,20},{28,24},{32,28}... | collective-permute-start | bytes 3814280 | tf_op jit(solution)/shard_map/ppermute | solution.py:25
  33.2 8.0 %copy-start.7 = (f32[301,8,4]{0,1,2:T(8,128)S(1)}, f32[301,8,4]{0,1,2:T(8,128)}, u32[]{:S(2)}) copy-start(f32[301,8,4]{0,1,2:T(8,128)} %copy-done.6) | copy-start | bytes 115588
  33.2 8.6 %copy-start.5 = (f32[301,8,4]{0,1,2:T(8,128)S(1)}, f32[301,8,4]{0,1,2:T(8,128)}, u32[]{:S(2)}) copy-start(f32[301,8,4]{0,1,2:T(8,128)} %copy-done.4) | copy-start | bytes 115588
  35.7 18.1 %all-to-all-start = ((f32[4,32,2,128]{3,2,0,1:T(2,128)}), f32[4,32,2,128]{3,2,0,1:T(2,128)S(1)}, u32[]{:S(2)}, u32[]{:S(2)}) async-start(f32[4,32,2,128]{3,2,0,1:T(2,128)} %bitcast.44), calls=%async_computation | async-start | bytes 262144 | tf_op jit(solution)/shard_map/all_to_all | solution.py:325
  61.4 3.6 %copy-start.8 = (f32[301,8,4]{0,2,1:T(4,128)S(1)}, f32[301,8,4]{0,2,1:T(4,128)}, u32[]{:S(2)}) copy-start(f32[301,8,4]{0,2,1:T(4,128)} %copy.26) | copy-start | bytes 115588
  61.4 3.6 %copy-start.9 = (f32[301,8,4]{0,2,1:T(4,128)S(1)}, f32[301,8,4]{0,2,1:T(4,128)}, u32[]{:S(2)}) copy-start(f32[301,8,4]{0,2,1:T(4,128)} %copy.25) | copy-start | bytes 115588
  73.9 1.5 %copy-start.2 = (f32[301,16,128]{2,1,0:T(8,128)}, f32[301,16,128]{2,1,0:T(8,128)S(1)}, u32[]{:S(2)}) copy-start(f32[301,16,128]{2,1,0:T(8,128)S(1)} %pad_maximum_fusion.2.after_and_out_1_.edge_ref) | copy-start | bytes 7397380
  119.2 14.9 %all-to-all-start.1 = ((f32[4,32,2,128]{3,2,0,1:T(2,128)}), f32[4,32,2,128]{3,2,0,1:T(2,128)S(1)}, u32[]{:S(2)}, u32[]{:S(2)}) async-start(f32[4,32,2,128]{3,2,0,1:T(2,128)} %copy.32), calls=%async_computation.1 | async-start | bytes 262144 | tf_op jit(solution)/shard_map/all_to_all | solution.py:341
  134.3 5.5 %collective-permute-start.5 = (f32[4,16,128]{2,1,0:T(8,128)S(1)}, f32[4,16,128]{2,1,0:T(8,128)S(1)}, u32[]{:S(2)}, u32[]{:S(2)}) collective-permute-start(f32[4,16,128]{2,1,0:T(8,128)S(1)} %bitcast.56), channel_id=1, source_target_pairs={{0,2},{1,3},{2,0},{3,1},{4,6},{5,7},{6,4},{7,5},{8,10},{9,11},{10,... | collective-permute-start | bytes 98312 | tf_op jit(solution)/shard_map/ppermute | solution.py:278
  134.3 5.5 %collective-permute-start.4 = (f32[4,16,128]{2,1,0:T(8,128)S(1)}, f32[4,16,128]{2,1,0:T(8,128)S(1)}, u32[]{:S(2)}, u32[]{:S(2)}) collective-permute-start(f32[4,16,128]{2,1,0:T(8,128)S(1)} %bitcast.57), channel_id=1, source_target_pairs={{0,1},{1,2},{2,3},{3,0},{4,5},{5,6},{6,7},{7,4},{8,9},{9,10},{10,1... | collective-permute-start | bytes 98312 | tf_op jit(solution)/shard_map/ppermute | solution.py:278
  134.9 5.0 %collective-permute-start.6 = (f32[4,16,128]{2,1,0:T(8,128)S(1)}, f32[4,16,128]{2,1,0:T(8,128)S(1)}, u32[]{:S(2)}, u32[]{:S(2)}) collective-permute-start(f32[4,16,128]{2,1,0:T(8,128)S(1)} %bitcast.58), channel_id=1, source_target_pairs={{0,3},{1,0},{2,1},{3,2},{4,7},{5,4},{6,5},{7,6},{8,11},{9,8},{10,9... | collective-permute-start | bytes 98312 | tf_op jit(solution)/shard_map/ppermute | solution.py:278

commit v17 on v15

--- a/solution.py
+++ b/solution.py
@@ -15,6 +15,7 @@
 
 
 HALO = 4
+SLOTS = 2
 
 
 def from_neighbours(block, axis, dim, width):
@@ -253,9 +254,15 @@
             total = total + matmul_exact(split_parts(spread), onehot, 1)
         return total
 
-    out_ref[...] = lax.fori_loop(
+    total = lax.fori_loop(
         0, rows, row_step, jnp.zeros((stacked, lanes), jnp.float32), unroll=True
     )
+    pair = SLOTS
+    owners = segments // pair
+    for owner in range(owners):
+        for f in range(fields):
+            start = f * segments + owner * pair
+            out_ref[pl.ds((owner * fields + f) * pair, pair), :] = total[start:start + pair, :]
 
 
 def remap_call(kernel, out_shape, *operands, after=()):
@@ -336,13 +343,14 @@
     )
     state_adjoint, flux_back = tridiagonal(pieces, mask, adjoint_state.shape, mixing_base, surface, land)
     buffer = remap_call(scatter_kernel, flat_recv.shape, flux_back, index_rows, weight_rows)
+    slots = received.shape[2]
     returned = lax.all_to_all(
-        buffer.reshape(received.shape), "lat", split_axis=1, concat_axis=1, tiled=True
+        buffer.reshape(received.shape[1], fields, slots, -1), "lat", split_axis=0, concat_axis=0, tiled=True
     )
     owned_ids = lax.broadcasted_iota(jnp.int32, (owned,) + chosen.shape, 0)
     picks = jnp.logical_and(owned_ids == chosen[None], live_slot[None]).astype(jnp.float32)
     owner_sum = jnp.einsum(
-        "sdc,fdck->fsk", picks, returned, precision=lax.Precision.HIGHEST
+        "sdc,dfck->fsk", picks, returned, precision=lax.Precision.HIGHEST
     )
     flux_adjoint = sum_over(owner_sum, "lon")
     return (state_adjoint, flux_adjoint)

time: 121 us -> 119 us (0.983)
  local copies, waits for them, and re-layouts: 14.8 us -> 13.2 us
    reshape x1 -> x0, local copies, waits for them, and re-layouts: 1.6 us -> none  [shards(): buffer.reshape(received.shape)]
where the time goes in v17:
time: 119 us; the launch traced here: 118 us
  Pallas kernels  40.2 us (34%)
  starting transfers between devices  28.9 us (24%)
  waiting for transfers between devices  18.4 us (15%)
  other arithmetic  16.6 us (14%)
  local copies, waits for them, and re-layouts  13.2 us (11%)
    pallas_call x1, Pallas kernels, tridiagonal(): pl.pallas_call(tridiagonal_kernel, out_shape=(jax.ShapeDtypeStruct(shape,...  31.4 us
    ppermute x3, starting transfers between devices, from_neighbours(): lax.ppermute(lax.slice_in_dim(block, 0, width, axis=dim), axis, to_prev)  13.6 us
    pallas_call x2, Pallas kernels, remap_call(): pl.pallas_call(kernel, out_shape=jax.ShapeDtypeStruct(out_shape, jnp.floa...  8.73 us
    all_to_all x1, waiting for transfers between devices, shards(): lax.all_to_all(buffer.reshape(received.shape[1], fields, slots, -1), 'lat...  7.82 us
    all_to_all x1, starting transfers between devices, shards(): lax.all_to_all(outgoing, 'lat', split_axis=1, concat_axis=1, tiled=True)  6.73 us
    concatenate x2, other arithmetic, extended_planes(): stack = jnp.concatenate([planes, coast], axis=0)  5.42 us
    ppermute x3, waiting for transfers between devices, from_neighbours(): lax.ppermute(lax.slice_in_dim(block, size - width, size, axis=dim), axis,...  5.33 us
    ppermute x3, starting transfers between devices, sum_over(): lax.ppermute(values, axis, [(i, (i + shift) % count) for i in range(count)])  4.65 us
  transfers between devices with their start and end apart: 11, of which 6 were waited for; matrix products, arithmetic and copies ran while one was open for 14% of the time, Pallas kernels for 0%

profile of v17, /device:TPU:0, one launch (start us, length us, event | category | flops | bytes accessed | tf_op | source)
XLA Modules:
  0.0 118.3 jit_solution(12393023456191314000)
XLA Ops:
  1.4 3.5 %fusion = (f32[301,8,4]{2,1,0:T(8,128)}, f32[301,8,4]{2,1,0:T(8,128)}) fusion(f32[300,8,256]{2,1,0:T(8,128)} %bitcast.46, f32[1,8,256]{2,1,0:T(8,128)S(1)} %get-tuple-element.15), kind=kLoop, calls=%fused_computation.12 | loop fusion | flops 19264 | bytes 2542848 | tf_op jit(solution)/shard_map/concatenate | solution.py:35
  4.9 1.9 %copy.17 = f32[301,8,4]{0,1,2:T(8,128)S(1)} copy(f32[301,8,4]{2,1,0:T(8,128)} %get-tuple-element.6) | data formatting | bytes 77056 | tf_op jit(solution)/shard_map/slice | solution.py:26
  6.8 2.9 %collective-permute-start.2 = (f32[301,8,4]{0,1,2:T(8,128)S(1)}, f32[301,8,4]{0,1,2:T(8,128)S(1)}, u32[]{:S(2)}, u32[]{:S(2)}) collective-permute-start(f32[301,8,4]{0,1,2:T(8,128)S(1)} %copy.17), channel_id=1, source_target_pairs={{0,3},{1,0},{2,1},{3,2},{4,7},{5,4},{6,5},{7,6},{8,11},{9,8},{10,9... | collective-permute-start | bytes 115592 | tf_op jit(solution)/shard_map/ppermute | solution.py:26
  9.7 1.8 %copy.18 = f32[301,8,4]{0,1,2:T(8,128)S(1)} copy(f32[301,8,4]{2,1,0:T(8,128)} %get-tuple-element.7) | data formatting | bytes 77056 | tf_op jit(solution)/shard_map/slice | solution.py:27
  11.6 1.9 %fusion.1 = (f32[301,4,256]{2,1,0:T(4,128)}, f32[301,4,256]{2,1,0:T(4,128)}) fusion(f32[300,8,256]{2,1,0:T(8,128)S(1)} %bitcast.48, f32[1,8,256]{2,1,0:T(8,128)S(1)} %get-tuple-element.15), kind=kLoop, calls=%fused_computation.13 | loop fusion | flops 616448 | bytes 4931584 | tf_op jit(solution)/shard_map/concatenate | solution.py:35
  13.5 5.6 %collective-permute-start = (f32[301,4,256]{2,1,0:T(4,128)}, f32[301,4,256]{2,1,0:T(4,128)}, u32[]{:S(2)}, u32[]{:S(2)}) collective-permute-start(f32[301,4,256]{2,1,0:T(4,128)} %get-tuple-element.8), channel_id=1, source_target_pairs={{0,124},{4,0},{8,4},{12,8},{16,12},{20,16},{24,20},{28,24},{32,28}... | collective-permute-start | bytes 3698696 | tf_op jit(solution)/shard_map/ppermute | solution.py:26
  22.1 6.7 %all-to-all-start = ((f32[4,32,2,128]{3,2,0,1:T(2,128)}), f32[4,32,2,128]{3,2,0,1:T(2,128)S(1)}, u32[]{:S(2)}, u32[]{:S(2)}) async-start(f32[4,32,2,128]{3,2,0,1:T(2,128)} %bitcast.44), calls=%async_computation | async-start | bytes 262144 | tf_op jit(solution)/shard_map/all_to_all | solution.py:330
  28.9 5.0 %collective-permute-start.4 = (f32[301,4,8]{0,2,1:T(8,128)S(1)}, f32[301,4,8]{0,2,1:T(8,128)S(1)}, u32[]{:S(2)}, u32[]{:S(2)}) collective-permute-start(f32[301,4,8]{0,2,1:T(8,128)S(1)} %get-tuple-element.12), channel_id=1, source_target_pairs={{0,124},{4,0},{8,4},{12,8},{16,12},{20,16},{24,20},{28,24},{32,28}... | collective-permute-start | bytes 115592 | tf_op jit(solution)/shard_map/ppermute | solution.py:26
  34.2 1.6 %collective-permute-done.4 = f32[301,4,8]{0,2,1:T(8,128)S(1)} collective-permute-done((f32[301,4,8]{0,2,1:T(8,128)S(1)}, f32[301,4,8]{0,2,1:T(8,128)S(1)}, u32[]{:S(2)}, u32[]{:S(2)}) %collective-permute-start.4) | collective-permute-done | bytes 38560 | tf_op jit(solution)/shard_map/ppermute | solution.py:26
  35.8 5.3 %collective-permute-done.5 = f32[301,4,8]{0,2,1:T(8,128)S(1)} collective-permute-done((f32[301,4,8]{0,2,1:T(8,128)S(1)}, f32[301,4,8]{0,2,1:T(8,128)S(1)}, u32[]{:S(2)}, u32[]{:S(2)}) %collective-permute-start.5) | collective-permute-done | bytes 38560 | tf_op jit(solution)/shard_map/ppermute | solution.py:27
  41.2 2.9 %copy.21 = f32[301,16,4]{2,1,0:T(8,128)} copy(f32[301,16,4]{0,2,1:T(4,128)S(1)} %get-tuple-element.10) | data formatting | bytes 154112 | tf_op jit(solution)/shard_map/slice | solution.py:43
  44.0 2.9 %copy.22 = f32[301,16,4]{2,1,0:T(8,128)} copy(f32[301,16,4]{0,2,1:T(4,128)S(1)} %get-tuple-element.11) | data formatting | bytes 154112 | tf_op jit(solution)/shard_map/slice | solution.py:43
  46.9 3.1 %pad_maximum_fusion.1.after_and_out_1_.edge_ref = f32[301,16,128]{2,1,0:T(8,128)S(1)} fusion(f32[301,16,4]{2,1,0:T(8,128)} %copy.22, f32[301,16,4]{2,1,0:T(8,128)} %copy.21, f32[128]{0:T(128)S(1)} %pad.8.clone), kind=kLoop, calls=%fused_computation.8 | loop fusion | flops 1232896 | bytes 2620416 | tf_op jit(solution)/shard_map/concatenate | solution.py:43
  50.1 0.8 copy.25
  50.9 3.7 %pad_maximum_fusion.after_and_out_0_.rows_ref = f32[301,8,256]{2,1,0:T(8,128)} fusion(f32[301,4,256]{2,1,0:T(4,128)} %collective-permute-done.1, f32[301,4,256]{2,1,0:T(4,128)} %collective-permute-done), kind=kLoop, calls=%fused_computation.6 | loop fusion | flops 616448 | bytes 4931584 | tf_op jit(solution)/shard_map/concatenate | solution.py:44
  54.5 4.6 %shard_map.104 = f32[4,8,256]{2,1,0:T(8,128)} custom-call(f32[256,128]{1,0:T(8,128)} %bitcast.49, s32[32,256]{1,0:T(8,128)} %bitcast.52, f32[32,256]{1,0:T(8,128)} %bitcast.54, f32[301,8,256]{2,1,0:T(8,128)} %pad_maximum_fusion.after_and_out_0_.rows_ref, f32[301,16,128]{2,1,0:T(8,128)} %copy-done.2), custom_call_target="tpu_custom_call" | custom-call | tf_op jit(solution)/shard_map/pallas_call | solution.py:270
  59.1 1.4 %fusion.10.surf_ref = f32[8,256]{1,0:T(8,128)} fusion(f32[4,8,256]{2,1,0:T(8,128)} %shard_map.104), kind=kLoop, calls=%fused_computation.34 | loop fusion | flops 22528 | bytes 40960 | tf_op jit(solution)/shard_map/add | solution.py:341
  61.8 31.4 %shard_map.105 = (f32[4,75,8,256]{3,2,1,0:T(8,128)}, f32[4,8,256]{2,1,0:T(8,128)}) custom-call(f32[75]{0:T(128)} %constant.77.clone.decay_ref, f32[300,8,256]{2,1,0:T(8,128)} %bitcast.47, f32[301,8,256]{2,1,0:T(8,128)} %pad_maximum_fusion.after_and_out_0_.rows_ref, f32[301,16,128]{2,1,0:T(8,128)} %copy-done.2, f32[16,384]{1,0:T(8,128)} %maximum_select_fusion.mask_ref, ...), custom_call_target="tpu_custom_call" | custom-call | tf_op jit(solution)/shard_map/pallas_call | solution.py:181
  93.3 4.2 %shard_map.106 = f32[256,128]{1,0:T(8,128)} custom-call(f32[4,8,256]{2,1,0:T(8,128)} %get-tuple-element.5.back_ref, s32[32,256]{1,0:T(8,128)} %bitcast.53, f32[32,256]{1,0:T(8,128)} %bitcast.55), custom_call_target="tpu_custom_call" | custom-call | tf_op jit(solution)/shard_map/pallas_call | solution.py:270
  97.5 3.9 %all-to-all-start.1 = ((f32[32,4,2,128]{3,2,1,0:T(2,128)}), f32[32,4,2,128]{3,2,1,0:T(2,128)S(1)}, u32[]{:S(2)}, u32[]{:S(2)}) async-start(f32[32,4,2,128]{3,2,1,0:T(2,128)} %bitcast.51), calls=%async_computation.1 | async-start | bytes 262144 | tf_op jit(solution)/shard_map/all_to_all | solution.py:347
  101.3 7.8 %all-to-all-done.1 = f32[32,4,2,128]{3,2,1,0:T(2,128)S(1)} async-done(((f32[32,4,2,128]{3,2,1,0:T(2,128)}), f32[32,4,2,128]{3,2,1,0:T(2,128)S(1)}, u32[]{:S(2)}, u32[]{:S(2)}) %all-to-all-start.1) | async-done | bytes 131104 | tf_op jit(solution)/shard_map/all_to_all | solution.py:347
  109.8 3.9 %collective-permute-start.7 = (f32[4,16,128]{2,1,0:T(8,128)S(1)}, f32[4,16,128]{2,1,0:T(8,128)S(1)}, u32[]{:S(2)}, u32[]{:S(2)}) collective-permute-start(f32[4,16,128]{2,1,0:T(8,128)S(1)} %bitcast.57), channel_id=1, source_target_pairs={{0,2},{1,3},{2,0},{3,1},{4,6},{5,7},{6,4},{7,5},{8,10},{9,11},{10,... | collective-permute-start | bytes 98312 | tf_op jit(solution)/shard_map/ppermute | solution.py:283
  114.5 1.5 %collective-permute-done.7 = f32[4,16,128]{2,1,0:T(8,128)S(1)} collective-permute-done((f32[4,16,128]{2,1,0:T(8,128)S(1)}, f32[4,16,128]{2,1,0:T(8,128)S(1)}, u32[]{:S(2)}, u32[]{:S(2)}) %collective-permute-start.7) | collective-permute-done | bytes 32800 | tf_op jit(solution)/shard_map/ppermute | solution.py:283
  116.0 1.7 %collective-permute-done.8 = f32[4,16,128]{2,1,0:T(8,128)S(1)} collective-permute-done((f32[4,16,128]{2,1,0:T(8,128)S(1)}, f32[4,16,128]{2,1,0:T(8,128)S(1)}, u32[]{:S(2)}, u32[]{:S(2)}) %collective-permute-start.8) | collective-permute-done | bytes 32800 | tf_op jit(solution)/shard_map/ppermute | solution.py:283
  (55 shorter events, 7.5 us)
Async XLA Ops:
  0.6 20.0 %copy-start = (f32[4,16,128]{2,1,0:T(8,128)S(1)}, f32[4,16,128]{2,1,0:T(8,128)}, u32[]{:S(2)}) copy-start(f32[4,16,128]{2,1,0:T(8,128)} %param.11) | copy-start | bytes 98308
  1.4 59.8 %copy-start.4 = (f32[8,256]{1,0:T(8,128)}, f32[8,256]{1,0:T(8,128)S(1)}, u32[]{:S(2)}) copy-start(f32[8,256]{1,0:T(8,128)S(1)} %get-tuple-element.14.land_ref) | copy-start | bytes 24580
  4.9 6.7 %copy-start.3 = (f32[4,75,8,256]{3,2,1,0:T(8,128)S(1)}, f32[4,75,8,256]{3,2,1,0:T(8,128)}, u32[]{:S(2)}) copy-start(f32[4,75,8,256]{3,2,1,0:T(8,128)} %param.9) | copy-start | bytes 7372804
  6.8 22.1 %collective-permute-start.2 = (f32[301,8,4]{0,1,2:T(8,128)S(1)}, f32[301,8,4]{0,1,2:T(8,128)S(1)}, u32[]{:S(2)}, u32[]{:S(2)}) collective-permute-start(f32[301,8,4]{0,1,2:T(8,128)S(1)} %copy.17), channel_id=1, source_target_pairs={{0,3},{1,0},{2,1},{3,2},{4,7},{5,4},{6,5},{7,6},{8,11},{9,8},{10,9... | collective-permute-start | bytes 115592 | tf_op jit(solution)/shard_map/ppermute | solution.py:26
  11.5 7.7 %copy-start.5 = (s32[1,32]{1,0:T(1,128)S(1)}, s32[1,32]{1,0:T(1,128)}, u32[]{:S(2)}) copy-start(s32[1,32]{1,0:T(1,128)} %param.12) | copy-start | bytes 388
  11.5 8.1 %copy-start.1 = (s32[1,64]{1,0:T(1,128)S(1)}, s32[1,64]{1,0:T(1,128)}, u32[]{:S(2)}) copy-start(s32[1,64]{1,0:T(1,128)} %param.13) | copy-start | bytes 772
  11.5 17.4 %collective-permute-start.3 = (f32[301,8,4]{0,1,2:T(8,128)S(1)}, f32[301,8,4]{0,1,2:T(8,128)S(1)}, u32[]{:S(2)}, u32[]{:S(2)}) collective-permute-start(f32[301,8,4]{0,1,2:T(8,128)S(1)} %copy.18), channel_id=1, source_target_pairs={{0,1},{1,2},{2,3},{3,0},{4,5},{5,6},{6,7},{7,4},{8,9},{9,10},{10,1... | collective-permute-start | bytes 115592 | tf_op jit(solution)/shard_map/ppermute | solution.py:27
  13.5 37.4 %collective-permute-start = (f32[301,4,256]{2,1,0:T(4,128)}, f32[301,4,256]{2,1,0:T(4,128)}, u32[]{:S(2)}, u32[]{:S(2)}) collective-permute-start(f32[301,4,256]{2,1,0:T(4,128)} %get-tuple-element.8), channel_id=1, source_target_pairs={{0,124},{4,0},{8,4},{12,8},{16,12},{20,16},{24,20},{28,24},{32,28}... | collective-permute-start | bytes 3698696 | tf_op jit(solution)/shard_map/ppermute | solution.py:26
  19.1 31.7 %collective-permute-start.1 = (f32[301,4,256]{2,1,0:T(4,128)}, f32[301,4,256]{2,1,0:T(4,128)}, u32[]{:S(2)}, u32[]{:S(2)}) collective-permute-start(f32[301,4,256]{2,1,0:T(4,128)} %get-tuple-element.9), channel_id=1, source_target_pairs={{0,4},{4,8},{8,12},{12,16},{16,20},{20,24},{24,28},{28,32},{32,36}... | collective-permute-start | bytes 3698696 | tf_op jit(solution)/shard_map/ppermute | solution.py:27
  22.1 28.0 %all-to-all-start = ((f32[4,32,2,128]{3,2,0,1:T(2,128)}), f32[4,32,2,128]{3,2,0,1:T(2,128)S(1)}, u32[]{:S(2)}, u32[]{:S(2)}) async-start(f32[4,32,2,128]{3,2,0,1:T(2,128)} %bitcast.44), calls=%async_computation | async-start | bytes 262144 | tf_op jit(solution)/shard_map/all_to_all | solution.py:330
  28.9 6.8 %collective-permute-start.4 = (f32[301,4,8]{0,2,1:T(8,128)S(1)}, f32[301,4,8]{0,2,1:T(8,128)S(1)}, u32[]{:S(2)}, u32[]{:S(2)}) collective-permute-start(f32[301,4,8]{0,2,1:T(8,128)S(1)} %get-tuple-element.12), channel_id=1, source_target_pairs={{0,124},{4,0},{8,4},{12,8},{16,12},{20,16},{24,20},{28,24},{32,28}... | collective-permute-start | bytes 115592 | tf_op jit(solution)/shard_map/ppermute | solution.py:26
  33.9 7.2 %collective-permute-start.5 = (f32[301,4,8]{0,2,1:T(8,128)S(1)}, f32[301,4,8]{0,2,1:T(8,128)S(1)}, u32[]{:S(2)}, u32[]{:S(2)}) collective-permute-start(f32[301,4,8]{0,2,1:T(8,128)S(1)} %get-tuple-element.13), channel_id=1, source_target_pairs={{0,4},{4,8},{8,12},{12,16},{16,20},{20,24},{24,28},{28,32},{32,36}... | collective-permute-start | bytes 115592 | tf_op jit(solution)/shard_map/ppermute | solution.py:27
  50.0 4.5 %copy-start.2 = (f32[301,16,128]{2,1,0:T(8,128)}, f32[301,16,128]{2,1,0:T(8,128)S(1)}, u32[]{:S(2)}) copy-start(f32[301,16,128]{2,1,0:T(8,128)S(1)} %pad_maximum_fusion.1.after_and_out_1_.edge_ref) | copy-start | bytes 7397380
  97.5 11.7 %all-to-all-start.1 = ((f32[32,4,2,128]{3,2,1,0:T(2,128)}), f32[32,4,2,128]{3,2,1,0:T(2,128)S(1)}, u32[]{:S(2)}, u32[]{:S(2)}) async-start(f32[32,4,2,128]{3,2,1,0:T(2,128)} %bitcast.51), calls=%async_computation.1 | async-start | bytes 262144 | tf_op jit(solution)/shard_map/all_to_all | solution.py:347
  109.3 5.2 %collective-permute-start.6 = (f32[4,16,128]{2,1,0:T(8,128)S(1)}, f32[4,16,128]{2,1,0:T(8,128)S(1)}, u32[]{:S(2)}, u32[]{:S(2)}) collective-permute-start(f32[4,16,128]{2,1,0:T(8,128)S(1)} %bitcast.56), channel_id=1, source_target_pairs={{0,1},{1,2},{2,3},{3,0},{4,5},{5,6},{6,7},{7,4},{8,9},{9,10},{10,1... | collective-permute-start | bytes 98312 | tf_op jit(solution)/shard_map/ppermute | solution.py:283
  109.8 6.2 %collective-permute-start.7 = (f32[4,16,128]{2,1,0:T(8,128)S(1)}, f32[4,16,128]{2,1,0:T(8,128)S(1)}, u32[]{:S(2)}, u32[]{:S(2)}) collective-permute-start(f32[4,16,128]{2,1,0:T(8,128)S(1)} %bitcast.57), channel_id=1, source_target_pairs={{0,2},{1,3},{2,0},{3,1},{4,6},{5,7},{6,4},{7,5},{8,10},{9,11},{10,... | collective-permute-start | bytes 98312 | tf_op jit(solution)/shard_map/ppermute | solution.py:283
  113.8 3.9 %collective-permute-start.8 = (f32[4,16,128]{2,1,0:T(8,128)S(1)}, f32[4,16,128]{2,1,0:T(8,128)S(1)}, u32[]{:S(2)}, u32[]{:S(2)}) collective-permute-start(f32[4,16,128]{2,1,0:T(8,128)S(1)} %bitcast.58), channel_id=1, source_target_pairs={{0,3},{1,0},{2,1},{3,2},{4,7},{5,4},{6,5},{7,6},{8,11},{9,8},{10,9... | collective-permute-start | bytes 98312 | tf_op jit(solution)/shard_map/ppermute | solution.py:283
